TPU v7x, 32 devices: a whole 2x2x4 slice. The times are simulated.
32 devices in a mesh: slab: 8 (over z, x), cross: 4 (over y, core).
Axes of the slice: x: 2, y: 2, z: 4, core: 2. Of those that a mesh axis runs over, the one named last changes fastest.
Arguments:
- les_state: float32 [54, 64, 16, 128], P(None, 'slab', 'cross'), may hold values from -6 to 6
- cmc_state: float32 [54, 128, 1024], P(None, 'cross', 'slab'), may hold values from -6 to 6
- cmc_map: int32 [64, 16, 128], P('slab', 'cross'), may hold values from 0 to 1023, as said below
- pdf_index: int32 [64, 16, 128], P('slab', 'cross'), may hold values from 0 to 127
- pdf_table: float32 [128, 128], replicated, may hold values from 0.001 to 0.05
- diffusion: float32 [54], replicated, may hold values from 0.02 to 0.15
- chem_matrix: float32 [54, 54], replicated, may hold values from -0.875 to 0.875
- dissipation: float32 [128, 1024], P('cross', 'slab'), may hold values from 0.05 to 0.2
- reaction_rate: float32 [128, 1024], P('cross', 'slab'), may hold values from 0.05 to 0.5
- substeps: int32 [1024], P('slab'), may hold values from 1 to 4
Outputs:
- les_out: float32 [54, 64, 16, 128], P(None, 'slab', 'cross')
- cmc_out: float32 [54, 128, 1024], P(None, 'cross', 'slab')
Inputs may be any that keep to these rules, and one draw needn't show every extreme that they name: `cmc_map`: an LES cell in plane x along the jet axis maps to a CMC cell whose index divided by 128 differs from x divided by 8 (both rounded down) by at most one.
All inputs are finite; a program needn't handle non-finite values.
Results may differ from a plain program's by a relative error of at most 0.0001.
Values sent between devices are 32-bit elements; how exact they have to be, the bound alone decides.
A program may use at most 128 MiB of HBM per device.

v0:
```python
import functools

import jax
import jax.numpy as jnp
from jax import lax
from jax.experimental import pallas as pl
from jax.experimental.pallas import tpu as pltpu
from jax.sharding import PartitionSpec as P

KMAX = 4
F32 = jnp.float32
BF16 = jnp.bfloat16
NT = (((1,), (1,)), ((), ()))
NN = (((1,), (0,)), ((), ()))


def shift(array, axis, by):
    count = lax.axis_size(axis)
    return lax.ppermute(array, axis, [(i, i + by) for i in range(count) if 0 <= i + by < count])


def swap(array, axis, bit):
    count = lax.axis_size(axis)
    return lax.ppermute(array, axis, [(i, i ^ bit) for i in range(count)])


def halves(x):
    high = x.astype(BF16)
    return high, (x - high.astype(F32)).astype(BF16)


def decode(row, nshape):
    cell = jnp.floor((row + 0.5) * (1.0 / nshape))
    return cell.astype(jnp.int32), (row - cell * nshape).astype(jnp.int32)


def rows_equal(targets, row):
    return jnp.where(targets == row, 1.0, 0.0).astype(BF16)


def bin_kernel(bins, sp, cells, nshape, outer, first, *refs):
    if outer:
        t_ref, w_ref, *refs = refs
        acc_ref = None if first else refs.pop(0)
        out_ref, wc_ref, lhs = refs
    else:
        t_ref, wc_ref, *refs = refs
        acc_ref = None if first else refs.pop(0)
        out_ref, lhs = refs
    ct = t_ref.shape[1]

    @pl.when(pl.program_id(0) == 0)
    def _():
        out_ref[...] = jnp.zeros_like(out_ref) if first else acc_ref[...]

    t = t_ref[...]
    cell, shape = decode(t[sp - 1 : sp, :], nshape)
    if outer:
        ids = lax.broadcasted_iota(jnp.int32, (nshape, ct), 0)
        table = w_ref[...]
        high, low = halves(table)
        rest = (table - high.astype(F32) - low.astype(F32)).astype(BF16)
        split = jnp.concatenate([high.astype(F32), low.astype(F32), rest.astype(F32)], axis=0).astype(BF16)
        parts = lax.dot_general(split, rows_equal(ids, shape), NN, preferred_element_type=F32)
        wb = table.shape[0]
        wc = parts[:wb] + parts[wb : 2 * wb] + parts[2 * wb :]
        wc_ref[...] = wc
        targets = lax.broadcasted_iota(jnp.int32, (2 * cells, ct), 0)
        targets = jnp.where(targets >= cells, targets + cells, targets)
    else:
        wc = wc_ref[...]
        targets = lax.broadcasted_iota(jnp.int32, (cells, ct), 0) + cells
    for b in range(0, bins, 2):
        prod = jnp.concatenate([t * wc[b : b + 1, :], t * wc[b + 1 : b + 2, :]], axis=0)
        high, low = halves(prod)
        lhs[b * sp : (b + 2) * sp, :ct] = high
        lhs[b * sp : (b + 2) * sp, ct:] = low
    hot = rows_equal(targets, cell)
    hot = jnp.concatenate([hot, hot], axis=1)
    out_ref[...] += lax.dot_general(lhs[...], hot, NT, preferred_element_type=F32)


def bin_call(t, w, wc, acc, bins, cells, nshape, ct=512):
    sp, count = t.shape
    outer = wc is None
    width = (2 if outer else 1) * cells
    rows = bins * sp
    whole = lambda shape: pl.BlockSpec(shape, lambda i: (0,) * len(shape))
    col = lambda r: pl.BlockSpec((r, ct), lambda i: (0, i))
    wb = w.shape[0]
    args, specs = [t], [col(sp)]
    if outer:
        args.append(w)
        specs.append(whole(w.shape))
    else:
        args.append(wc)
        specs.append(col(wb))
    if acc is not None:
        args.append(acc)
        specs.append(whole(acc.shape))
    shapes = [jax.ShapeDtypeStruct((rows, width), F32)]
    outs = [whole((rows, width))]
    if outer:
        shapes.append(jax.ShapeDtypeStruct((wb, count), F32))
        outs.append(col(wb))
    flops = rows * width * count // 4
    res = pl.pallas_call(
        functools.partial(bin_kernel, bins, sp, cells, nshape, outer, acc is None),
        grid=(count // ct,),
        out_shape=shapes,
        in_specs=specs,
        out_specs=outs,
        scratch_shapes=[pltpu.VMEM((rows, 2 * ct), BF16)],
        compiler_params=pltpu.CompilerParams(vmem_limit_bytes=40 << 20),
        cost_estimate=pl.CostEstimate(flops=flops, bytes_accessed=4 * sp * count, transcendentals=0),
        name="bin_outer" if outer else "bin_own",
    )(*args)
    return res if outer else res[0]


def chem_kernel(species, sp, own_ref, above_ref, below_ref, moved_ref, diss_ref, rate_ref, count_ref, matrix_ref, out_ref):
    bins, _, cells = out_ref.shape
    third = matrix_ref.shape[1] // 3
    high, low = halves(matrix_ref[...])
    column = lax.broadcasted_iota(jnp.int32, matrix_ref.shape, 1)
    matrix = jnp.where(column < 2 * third, high.astype(F32), low.astype(F32)).astype(BF16)
    group = next(g for g in (4, 2, 1) if bins % g == 0)
    count = jnp.concatenate([count_ref[...]] * group, axis=1)
    row = lax.broadcasted_iota(jnp.int32, (sp, group * cells), 0)
    gap = [jnp.zeros((third - sp, group * cells), F32)] * (third > sp)

    def blend(b):
        total = own_ref[b] + above_ref[b] + below_ref[b]
        return (total + moved_ref[b]) / (total[species : species + 1, :] + 1.0)

    def wide(ref, b):
        return jnp.concatenate([ref[b + n : b + n + 1, :] for n in range(group)], axis=1)

    for b in range(0, bins, group):
        blends = [blend(b + n) for n in range(group + 2)]
        before, here, after = (jnp.concatenate(blends[n : n + group], axis=1) for n in range(3))
        state = here + wide(diss_ref, b) * (after - 2.0 * here + before)
        half = 0.5 * wide(rate_ref, b)
        for k in range(KMAX):
            high, low = (part.astype(F32) for part in halves(state))
            stack = jnp.concatenate([high, *gap, low, *gap, high, *gap], axis=0).astype(BF16)
            rate = lax.dot_general(matrix, stack, NN, preferred_element_type=F32)
            state = jnp.where(k < count, state + half * jnp.tanh(rate), state)
        state = jnp.where(row == species, 1.0, state)
        for n in range(group):
            out_ref[b + n] = state[:, n * cells : (n + 1) * cells]


def project_kernel(bins, sp, cells, nshape, groups, accumulate, *refs):
    xs, refs = refs[: len(groups)], refs[len(groups) :]
    key_ref, wc_ref, *refs = refs
    acc_ref = refs.pop(0) if accumulate else None
    out_ref, lhs = refs
    ct = out_ref.shape[1]

    @pl.when(pl.program_id(0) == 0)
    def _():
        for n, x_ref in enumerate(xs):
            high, low = halves(x_ref[...])
            lhs[:, 2 * n * cells : (2 * n + 1) * cells] = high
            lhs[:, (2 * n + 1) * cells : (2 * n + 2) * cells] = low

    cell, _ = decode(key_ref[7:8, :], nshape)
    ids = lax.broadcasted_iota(jnp.int32, (cells, ct), 0)
    hots = []
    for g in groups:
        hot = rows_equal(ids + g * cells, cell)
        hots += [hot, hot]
    y = lax.dot_general(lhs[...], jnp.concatenate(hots, axis=0), NN, preferred_element_type=F32)
    total = acc_ref[...] if accumulate else jnp.zeros((sp, ct), F32)
    for b in range(bins):
        total = total + wc_ref[b + 1 : b + 2, :] * y[b * sp : (b + 1) * sp]
    out_ref[...] = total


def project_call(xs, groups, t, wc, acc, place, count, bins, cells, nshape, ct=256):
    sp, skip = t.shape[0], place // ct
    rows = bins * sp
    whole = lambda shape: pl.BlockSpec(shape, lambda i: (0,) * len(shape))
    col = lambda r: pl.BlockSpec((r, ct), lambda i: (0, i))
    args = list(xs) + [t, wc]
    specs = [whole(x.shape) for x in xs]
    specs.append(pl.BlockSpec((8, ct), lambda i: (sp // 8 - 1, i + skip)))
    specs.append(pl.BlockSpec((wc.shape[0], ct), lambda i: (0, i + skip)))
    if acc is not None:
        args.append(acc)
        specs.append(col(sp))
    return pl.pallas_call(
        functools.partial(project_kernel, bins, sp, cells, nshape, groups, acc is not None),
        grid=(count // ct,),
        out_shape=jax.ShapeDtypeStruct((sp, count), F32),
        in_specs=specs,
        out_specs=col(sp),
        scratch_shapes=[pltpu.VMEM((rows, 2 * len(groups) * cells), BF16)],
        compiler_params=pltpu.CompilerParams(vmem_limit_bytes=40 << 20),
        cost_estimate=pl.CostEstimate(flops=rows * cells * len(groups) * count // 4, bytes_accessed=8 * sp * count, transcendentals=0),
        name="project",
    )(*args)


def on_device(
    les_state, cmc_state, cmc_map, pdf_index, pdf_table, diffusion, chem_matrix, dissipation, reaction_rate, substeps
):
    species = les_state.shape[0]
    sp = -(-(species + 2) // 8) * 8
    own_bins, cells = cmc_state.shape[1:]
    bins = own_bins + 2
    nshape = pdf_table.shape[0]
    count = cmc_map.size
    ncross = lax.axis_size("cross")

    below = shift(les_state[:, -1:], "slab", 1)
    above = shift(les_state[:, :1], "slab", -1)
    behind = shift(les_state[:, :, -1:], "cross", 1)
    ahead = shift(les_state[:, :, :1], "cross", -1)
    xs = jnp.concatenate([below, les_state, above], axis=1)
    ys = jnp.concatenate([behind, les_state, ahead], axis=2)
    zs = jnp.pad(les_state, ((0, 0), (0, 0), (0, 0), (1, 1)))
    around = xs[:, 2:] + xs[:, :-2] + ys[:, :, 2:] + ys[:, :, :-2] + zs[..., 2:] + zs[..., :-2]
    transported = les_state + diffusion[:, None, None, None] * (around - 6.0 * les_state)
    flat = transported.reshape(species, count)
    offset = cmc_map.reshape(1, count) - (lax.axis_index("slab") - 1) * cells
    key = (offset * nshape + pdf_index.reshape(1, count)).astype(F32)
    rows = [flat] + [jnp.ones((1, count), F32)] + [jnp.zeros((sp - species - 2, count), F32)] * (sp > species + 2) + [key]
    t_own = jnp.concatenate(rows, axis=0)

    wb = -(-bins // 8) * 8
    table = jnp.pad(pdf_table.T, ((1, wb - own_bins - 1), (0, 0)))
    table = lax.dynamic_slice_in_dim(table, lax.axis_index("cross") * own_bins, wb, axis=0)
    used = lax.broadcasted_iota(jnp.int32, (wb, 1), 0) < bins
    table = jnp.where(used, table, 0.0)

    cmc_state, t_own = lax.optimization_barrier((cmc_state, t_own))
    left_cells = jnp.concatenate([shift(cmc_state[:, :, -1:], "slab", 1), cmc_state[:, :, :-1]], axis=2)
    right_cells = jnp.concatenate([cmc_state[:, :, 1:], shift(cmc_state[:, :, :1], "slab", -1)], axis=2)
    moved = cmc_state - 0.4 * (cmc_state - left_cells) + 0.1 * (right_cells - 2.0 * cmc_state + left_cells)
    moved = jnp.concatenate(
        [shift(moved[:, -1:], "cross", 1), moved, shift(moved[:, :1], "cross", -1)], axis=1
    )
    moved = jnp.pad(moved.transpose(1, 0, 2), ((0, 0), (0, sp - species), (0, 0)))

    blocks = [t_own]
    bits = [1 << k for k in range(ncross.bit_length() - 1)][::-1]
    for bit in bits:
        got = swap(jnp.concatenate(blocks, axis=1) if len(blocks) > 1 else blocks[0], "cross", bit)
        if len(blocks) == 1:
            got, moved = lax.optimization_barrier((got, moved))
        blocks.append(got)

    acc, wcs = None, []
    for block in blocks:
        acc, wc = bin_call(block, table, None, acc, bins, cells, nshape)
        wcs.append(wc)
    up = shift(acc[:, cells:], "slab", 1)
    down = shift(acc[:, :cells], "slab", -1)
    acc, *wcs = lax.optimization_barrier((acc, *wcs))
    mine = None
    for block, wc in zip(blocks, wcs):
        mine = bin_call(block, table, wc, mine, bins, cells, nshape)

    cube = lambda a: a.reshape(bins, sp, cells)
    extra = sp - species
    fresh = pl.pallas_call(
        functools.partial(chem_kernel, species, sp),
        out_shape=jax.ShapeDtypeStruct((own_bins, sp, cells), F32),
        compiler_params=pltpu.CompilerParams(vmem_limit_bytes=40 << 20),
        name="chem",
    )(
        cube(mine), cube(up), cube(down), moved, dissipation, reaction_rate, substeps[None, :],
        jnp.tile(jnp.pad(chem_matrix, ((0, extra), (0, -(-sp // 16) * 16 - species))), (1, 3)),
    )
    cmc_out = fresh[:, :species].transpose(1, 0, 2)
    fresh = fresh.reshape(own_bins * sp, cells)
    from_below = shift(fresh, "slab", 1)
    from_above = shift(fresh, "slab", -1)

    args = (count, own_bins, cells, nshape)
    where = [(blocks[0], wcs[0], 0)]
    for bit, block, wc in zip(bits, blocks[1:], wcs[1:]):
        held = {r: n for n, r in enumerate(order)} if bit != bits[0] else {0: 0}
        order = list(held) + [r ^ bit for r in held]
        where += [(block, wc, n * count) for n in range(len(held))]
    order = order if bits else [0]
    places = dict(zip(order, where))
    own_part = {r: project_call([fresh], (1,), *places[r][:2], None, places[r][2], *args) for r in order}
    from_below, from_above, own_part = lax.optimization_barrier((from_below, from_above, own_part))

    def reduced(who, bits, sides):
        if not bits:
            block, wc, place = places[who]
            return project_call(sides, (0, 2), block, wc, own_part[who], place, *args)
        far = reduced(who ^ bits[0], bits[1:], sides)
        if len(bits) > 1:
            far, sides = lax.optimization_barrier((far, sides))
        got = swap(far, "cross", bits[0])
        return reduced(who, bits[1:], sides) + got

    total = reduced(0, bits, [from_below, from_above])
    conditional = (total[:species] / total[species : species + 1]).reshape(transported.shape)
    les_out = transported + 0.5 * (conditional - transported)
    return (les_out, cmc_out)


def solution(mesh):
    return jax.shard_map(
        on_device,
        mesh=mesh,
        in_specs=(
            P(None, "slab", "cross", None),
            P(None, "cross", "slab"),
            P("slab", "cross", None),
            P("slab", "cross", None),
            P(),
            P(),
            P(),
            P("cross", "slab"),
            P("cross", "slab"),
            P("slab"),
        ),
        out_specs=(P(None, "slab", "cross", None), P(None, "cross", "slab")),
        check_vma=False,
    )
```

profile of v0, /device:TPU:2, one launch (start us, length us, event | category | flops | bytes accessed | tf_op | source)
XLA Modules:
  0.0 253.8 jit_solution(7995631748291764512)
XLA Ops:
  0.6 1.0 fusion.16
  1.7 1.9 collective-permute-start
  3.6 4.8 %collective-permute-start.1 = (f32[54,1,4,128]{3,2,1,0:T(4,128)S(1)}, f32[54,1,4,128]{3,2,1,0:T(4,128)S(1)}, u32[]{:S(2)}, u32[]{:S(2)}) collective-permute-start(f32[54,1,4,128]{3,2,1,0:T(4,128)S(1)} %get-tuple-element.61), channel_id=1, source_target_pairs={{0,4},{4,8},{8,12},{12,16},{16,20},{20,24},{24,28},{1,5},{5,9},{9,... | collective-permute-start | bytes 331784 | tf_op jit(solution)/shard_map/ppermute | solution.py:19
  8.4 2.0 fusion.17
  10.4 1.3 collective-permute-start.3
  11.7 1.3 collective-permute-start.2
  13.9 3.0 %collective-permute-done.2 = f32[54,8,1,128]{3,1,2,0:T(8,128)S(1)} collective-permute-done((f32[54,8,1,128]{3,1,2,0:T(8,128)S(1)}, f32[54,8,1,128]{3,1,2,0:T(8,128)S(1)}, u32[]{:S(2)}, u32[]{:S(2)}) %collective-permute-start.2) | collective-permute-done | bytes 221216 | tf_op jit(solution)/shard_map/ppermute | solution.py:19
  16.9 2.3 fusion.7
  20.9 2.9 %copy.34 = f32[54,32,128]{0,1,2:T(8,128)} copy(f32[54,32,128]{2,1,0:T(8,128)S(1)} %copy-done.15) | data formatting | bytes 1769472 | tf_op jit(solution)/shard_map/optimization_barrier | solution.py:238
  23.8 4.1 %collective-permute-start.4 = (f32[56,4096]{1,0:T(8,128)S(1)}, f32[56,4096]{1,0:T(8,128)S(1)}, u32[]{:S(2)}, u32[]{:S(2)}) collective-permute-start(f32[56,4096]{1,0:T(8,128)S(1)} %pad_maximum_fusion.1.refs_0_.refs_1_.refs_2_), channel_id=1, source_target_pairs={{0,2},{1,3},{2,0},{3,1},{4,6},{5,7},{6,4},{7,5},{8,10},{9,11},{10,... | collective-permute-start | bytes 2752520 | tf_op jit(solution)/shard_map/ppermute | solution.py:24
  28.7 2.5 %collective-permute-start.5 = (f32[54,32,1]{0,1,2:T(8,128)S(1)}, f32[54,32,1]{0,1,2:T(8,128)S(1)}, u32[]{:S(2)}, u32[]{:S(2)}) collective-permute-start(f32[54,32,1]{0,1,2:T(8,128)S(1)} %get-tuple-element.52), channel_id=1, source_target_pairs={{0,4},{4,8},{8,12},{12,16},{16,20},{20,24},{24,28},{1,5},{5,9},{9,... | collective-permute-start | bytes 20744 | tf_op jit(solution)/shard_map/ppermute | solution.py:19
  31.2 3.3 %collective-permute-start.6 = (f32[54,32,1]{0,1,2:T(8,128)S(1)}, f32[54,32,1]{0,1,2:T(8,128)S(1)}, u32[]{:S(2)}, u32[]{:S(2)}) collective-permute-start(f32[54,32,1]{0,1,2:T(8,128)S(1)} %get-tuple-element.53), channel_id=1, source_target_pairs={{4,0},{8,4},{12,8},{16,12},{20,16},{24,20},{28,24},{5,1},{9,5},{13... | collective-permute-start | bytes 20744 | tf_op jit(solution)/shard_map/ppermute | solution.py:19
  34.5 1.5 fusion.15
  36.0 1.7 collective-permute-done.6
  37.8 1.4 copy.41
  39.1 1.4 copy.36
  40.5 2.9 %fusion.2 = f32[54,32,128]{2,0,1:T(8,128)S(1)} fusion(f32[54,32,1]{2,0,1:T(8,128)} %copy.41, f32[54,32,127]{2,0,1:T(8,128)} %get-tuple-element.59, f32[54,32,127]{2,0,1:T(8,128)} %get-tuple-element.58, f32[54,32,1]{2,0,1:T(8,128)} %copy.36, f32[54,32,128]{2,1,0:T(8,128)S(1)} %copy-done.16), kind=kLoop, calls=%fused_computation.11 | loop fusion | flops 2211840 | bytes 3538944 | tf_op jit(solution)/shard_map/add | solution.py:241
  43.4 1.3 collective-permute-start.7
  44.7 1.3 collective-permute-start.8
  46.0 2.0 collective-permute-done.8
  48.1 1.0 pad.17.moved_ref
  49.1 1.4 pad_maximum_fusion
  51.4 2.6 %collective-permute-start.9 = (f32[56,8192]{1,0:T(8,128)}, f32[56,8192]{1,0:T(8,128)S(1)}, u32[]{:S(2)}, u32[]{:S(2)}) collective-permute-start(f32[56,8192]{1,0:T(8,128)} %pad_maximum_fusion), channel_id=1, source_target_pairs={{0,1},{1,0},{2,3},{3,2},{4,5},{5,4},{6,7},{7,6},{8,9},{9,8},{10,11... | collective-permute-start | bytes 5505032 | tf_op jit(solution)/shard_map/ppermute | solution.py:24
  54.2 11.4 %bin_outer.3 = (f32[1904,256]{1,0:T(8,128)S(1)}, f32[40,4096]{1,0:T(8,128)S(1)}) custom-call(f32[56,4096]{1,0:T(8,128)S(1)} %pad_maximum_fusion.1.refs_0_.refs_1_.refs_2_, f32[40,128]{1,0:T(8,128)S(1)} %fusion.11.refs_1_), custom_call_target="tpu_custom_call" | custom-call | flops 499122176 | bytes 917504 | tf_op jit(solution)/shard_map/bin_outer/pallas_call | solution.py:107
  66.5 11.4 %bin_outer.4 = (f32[1904,256]{1,0:T(8,128)S(1)}, f32[40,4096]{1,0:T(8,128)S(1)}) custom-call(f32[56,4096]{1,0:T(8,128)S(1)} %copy-done.4, f32[40,128]{1,0:T(8,128)S(1)} %fusion.11.refs_1_, f32[1904,256]{1,0:T(8,128)S(1)} %get-tuple-element.27.refs_2_), custom_call_target="tpu_custom_call" | custom-call | flops 499122176 | bytes 917504 | tf_op jit(solution)/shard_map/bin_outer/pallas_call | solution.py:107
  78.7 22.7 %bin_outer.5 = (f32[1904,256]{1,0:T(8,128)S(1)}, f32[40,8192]{1,0:T(8,128)S(1)}) custom-call(f32[56,8192]{1,0:T(8,128)S(1)} %collective-permute-done.9.refs_0_.refs_1_.refs_2_, f32[40,128]{1,0:T(8,128)S(1)} %fusion.11.refs_1_, f32[1904,256]{1,0:T(8,128)S(1)} %get-tuple-element.28.refs_2_), custom_call_target="tpu_custom_call" | custom-call | flops 998244352 | bytes 1835008 | tf_op jit(solution)/shard_map/bin_outer/pallas_call | solution.py:107
  101.4 1.4 fusion.13
  102.8 2.4 collective-permute-start.11
  105.2 4.5 %collective-permute-start.10 = (f32[1904,128]{1,0:T(8,128)}, f32[1904,128]{1,0:T(8,128)}, u32[]{:S(2)}, u32[]{:S(2)}) collective-permute-start(f32[1904,128]{1,0:T(8,128)} %get-tuple-element.55), channel_id=1, source_target_pairs={{0,4},{4,8},{8,12},{12,16},{16,20},{20,24},{24,28},{1,5},{5,9},{9,... | collective-permute-start | bytes 2924552 | tf_op jit(solution)/shard_map/ppermute | solution.py:19
  109.9 1.2 copy-done.1
  111.1 1.1 copy-done.7
  112.2 9.9 %bin_own.3.refs_2_ = f32[1904,128]{1,0:T(8,128)S(1)} custom-call(f32[56,4096]{1,0:T(8,128)S(1)} %copy-done.1, f32[40,4096]{1,0:T(8,128)S(1)} %copy-done.7), custom_call_target="tpu_custom_call" | custom-call | flops 249561088 | bytes 917504 | tf_op jit(solution)/shard_map/bin_own/pallas_call | solution.py:107
  122.1 10.1 %bin_own.4.refs_2_ = f32[1904,128]{1,0:T(8,128)S(1)} custom-call(f32[56,4096]{1,0:T(8,128)S(1)} %copy-done.5, f32[40,4096]{1,0:T(8,128)S(1)} %copy-done.10, f32[1904,128]{1,0:T(8,128)S(1)} %bin_own.3.refs_2_), custom_call_target="tpu_custom_call" | custom-call | flops 249561088 | bytes 917504 | tf_op jit(solution)/shard_map/bin_own/pallas_call | solution.py:107
  132.3 19.7 %bin_own.5 = f32[1904,128]{1,0:T(8,128)S(1)} custom-call(f32[56,8192]{1,0:T(8,128)S(1)} %collective-permute-done.9.refs_0_.refs_1_.refs_2_, f32[40,8192]{1,0:T(8,128)S(1)} %get-tuple-element.33.refs_1_.refs_2_.refs_3_, f32[1904,128]{1,0:T(8,128)S(1)} %bin_own.4.refs_2_), custom_call_target="tpu_custom_call" | custom-call | flops 499122176 | bytes 1835008 | tf_op jit(solution)/shard_map/bin_own/pallas_call | solution.py:107
  152.1 6.0 %chem.1 = f32[32,56,128]{2,1,0:T(8,128)S(1)} custom-call(f32[34,56,128]{2,1,0:T(8,128)S(1)} %bitcast.23, f32[34,56,128]{2,1,0:T(8,128)} %bitcast.6.above_ref, f32[34,56,128]{2,1,0:T(8,128)} %bitcast.7.below_ref, f32[34,56,128]{2,1,0:T(8,128)S(1)} %copy-done.11, f32[32,128]{1,0:T(8,128)S(1)} %copy-done.12, f32[32,128]{1,0:T(8,128)S(1)} %copy-done.13, ...), custom_call_target="tpu_custom_call" | custom-call | tf_op jit(solution)/shard_map/chem/pallas_call | solution.py:268
  158.1 2.4 collective-permute-start.13
  160.5 4.7 %collective-permute-start.12 = (f32[1792,128]{1,0:T(8,128)S(1)}, f32[1792,128]{1,0:T(8,128)S(1)}, u32[]{:S(2)}, u32[]{:S(2)}) collective-permute-start(f32[1792,128]{1,0:T(8,128)S(1)} %bitcast.18), channel_id=1, source_target_pairs={{0,4},{4,8},{8,12},{12,16},{16,20},{20,24},{24,28},{1,5},{5,9},{9,... | collective-permute-start | bytes 2752520 | tf_op jit(solution)/shard_map/ppermute | solution.py:19
  165.2 7.8 %project.10.refs_4_ = f32[56,4096]{1,0:T(8,128)S(1)} custom-call(f32[1792,128]{1,0:T(8,128)S(1)} %bitcast.19, f32[56,4096]{1,0:T(8,128)S(1)} %copy-done.5, f32[40,4096]{1,0:T(8,128)S(1)} %copy-done.10), custom_call_target="tpu_custom_call" | custom-call | flops 234881024 | bytes 1835008 | tf_op jit(solution)/shard_map/project/pallas_call | solution.py:193
  173.0 7.8 %project.8.refs_4_ = f32[56,4096]{1,0:T(8,128)S(1)} custom-call(f32[1792,128]{1,0:T(8,128)S(1)} %bitcast.20, f32[56,4096]{1,0:T(8,128)S(1)} %copy-done.2, f32[40,4096]{1,0:T(8,128)S(1)} %copy-done.8), custom_call_target="tpu_custom_call" | custom-call | flops 234881024 | bytes 1835008 | tf_op jit(solution)/shard_map/project/pallas_call | solution.py:193
  180.8 7.9 %project.11.refs_4_ = f32[56,4096]{1,0:T(8,128)S(1)} custom-call(f32[1792,128]{1,0:T(8,128)S(1)} %bitcast.21, f32[56,8192]{1,0:T(8,128)S(1)} %collective-permute-done.9.refs_0_.refs_1_.refs_2_, f32[40,8192]{1,0:T(8,128)S(1)} %get-tuple-element.33.refs_1_.refs_2_.refs_3_), custom_call_target="tpu_custom_call" | custom-call | flops 234881024 | bytes 1835008 | tf_op jit(solution)/shard_map/project/pallas_call | solution.py:193
  188.7 7.7 %project.9.refs_4_ = f32[56,4096]{1,0:T(8,128)S(1)} custom-call(f32[1792,128]{1,0:T(8,128)S(1)} %bitcast.22, f32[56,8192]{1,0:T(8,128)S(1)} %collective-permute-done.9.refs_0_.refs_1_.refs_2_, f32[40,8192]{1,0:T(8,128)S(1)} %get-tuple-element.33.refs_1_.refs_2_.refs_3_), custom_call_target="tpu_custom_call" | custom-call | flops 234881024 | bytes 1835008 | tf_op jit(solution)/shard_map/project/pallas_call | solution.py:193
  196.4 5.9 %collective-permute-done.12.refs_0_ = f32[1792,128]{1,0:T(8,128)S(1)} collective-permute-done((f32[1792,128]{1,0:T(8,128)S(1)}, f32[1792,128]{1,0:T(8,128)S(1)}, u32[]{:S(2)}, u32[]{:S(2)}) %collective-permute-start.12) | collective-permute-done | bytes 917536 | tf_op jit(solution)/shard_map/ppermute | solution.py:19
  202.4 11.3 %project.13 = f32[56,4096]{1,0:T(8,128)S(1)} custom-call(f32[1792,128]{1,0:T(8,128)S(1)} %collective-permute-done.12.refs_0_, f32[1792,128]{1,0:T(8,128)S(1)} %collective-permute-done.13.refs_1_, f32[56,8192]{1,0:T(8,128)S(1)} %collective-permute-done.9.refs_0_.refs_1_.refs_2_, f32[40,8192]{1,0:T(8,128)S(1)} %get-tuple-element.33.refs_1_.refs_2_.refs_3_, ...), custom_call_target="tpu_custom_call" | custom-call | flops 469762048 | bytes 1835008 | tf_op jit(solution)/shard_map/project/pallas_call | solution.py:193
  213.7 11.2 %project.12 = f32[56,4096]{1,0:T(8,128)S(1)} custom-call(f32[1792,128]{1,0:T(8,128)S(1)} %collective-permute-done.12.refs_0_, f32[1792,128]{1,0:T(8,128)S(1)} %collective-permute-done.13.refs_1_, f32[56,4096]{1,0:T(8,128)S(1)} %copy-done.5, f32[40,4096]{1,0:T(8,128)S(1)} %copy-done.10, f32[56,4096]{1,0:T(8,128)S(1)} %project.10.refs_4_), custom_call_target="tpu_custom_call" | custom-call | flops 469762048 | bytes 1835008 | tf_op jit(solution)/shard_map/project/pallas_call | solution.py:193
  226.1 11.1 %project.15 = f32[56,4096]{1,0:T(8,128)S(1)} custom-call(f32[1792,128]{1,0:T(8,128)S(1)} %collective-permute-done.12.refs_0_, f32[1792,128]{1,0:T(8,128)S(1)} %collective-permute-done.13.refs_1_, f32[56,8192]{1,0:T(8,128)S(1)} %collective-permute-done.9.refs_0_.refs_1_.refs_2_, f32[40,8192]{1,0:T(8,128)S(1)} %get-tuple-element.33.refs_1_.refs_2_.refs_3_, ...), custom_call_target="tpu_custom_call" | custom-call | flops 469762048 | bytes 1835008 | tf_op jit(solution)/shard_map/project/pallas_call | solution.py:193
  237.6 1.1 copy.44
  238.7 11.1 %project.14 = f32[56,4096]{1,0:T(8,128)S(1)} custom-call(f32[1792,128]{1,0:T(8,128)S(1)} %collective-permute-done.12.refs_0_, f32[1792,128]{1,0:T(8,128)S(1)} %collective-permute-done.13.refs_1_, f32[56,4096]{1,0:T(8,128)S(1)} %copy-done.2, f32[40,4096]{1,0:T(8,128)S(1)} %copy-done.8, f32[56,4096]{1,0:T(8,128)S(1)} %project.8.refs_4_), custom_call_target="tpu_custom_call" | custom-call | flops 469762048 | bytes 1835008 | tf_op jit(solution)/shard_map/project/pallas_call | solution.py:193
  251.3 2.5 multiply_add_fusion
  (90 shorter events, 9.2 us)
Async XLA Ops:
  0.6 16.2 %copy-start.17 = (f32[54,8,4,128]{3,2,1,0:T(4,128)S(1)}, f32[54,8,4,128]{3,2,1,0:T(4,128)}, u32[]{:S(2)}) copy-start(f32[54,8,4,128]{3,2,1,0:T(4,128)} %param.10) | copy-start | bytes 2654212
  1.7 12.2 %collective-permute-start = (f32[54,1,4,128]{3,2,1,0:T(4,128)S(1)}, f32[54,1,4,128]{3,2,1,0:T(4,128)S(1)}, u32[]{:S(2)}, u32[]{:S(2)}) collective-permute-start(f32[54,1,4,128]{3,2,1,0:T(4,128)S(1)} %get-tuple-element.60), channel_id=1, source_target_pairs={{4,0},{8,4},{12,8},{16,12},{20,16},{24,20},{28,24},{5,1},{9,5},{13... | collective-permute-start | bytes 331784 | tf_op jit(solution)/shard_map/ppermute | solution.py:19
  3.6 10.3 %collective-permute-start.1 = (f32[54,1,4,128]{3,2,1,0:T(4,128)S(1)}, f32[54,1,4,128]{3,2,1,0:T(4,128)S(1)}, u32[]{:S(2)}, u32[]{:S(2)}) collective-permute-start(f32[54,1,4,128]{3,2,1,0:T(4,128)S(1)} %get-tuple-element.61), channel_id=1, source_target_pairs={{0,4},{4,8},{8,12},{12,16},{16,20},{20,24},{24,28},{1,5},{5,9},{9,... | collective-permute-start | bytes 331784 | tf_op jit(solution)/shard_map/ppermute | solution.py:19
  10.4 3.5 %collective-permute-start.3 = (f32[54,8,1,128]{3,1,2,0:T(8,128)S(1)}, f32[54,8,1,128]{3,1,2,0:T(8,128)S(1)}, u32[]{:S(2)}, u32[]{:S(2)}) collective-permute-start(f32[54,8,1,128]{3,1,2,0:T(8,128)S(1)} %bitcast.31), channel_id=1, source_target_pairs={{0,1},{1,2},{2,3},{4,5},{5,6},{6,7},{8,9},{9,10},{10,11},{12,13},{... | collective-permute-start | bytes 663560 | tf_op jit(solution)/shard_map/ppermute | solution.py:19
  11.7 5.1 %collective-permute-start.2 = (f32[54,8,1,128]{3,1,2,0:T(8,128)S(1)}, f32[54,8,1,128]{3,1,2,0:T(8,128)S(1)}, u32[]{:S(2)}, u32[]{:S(2)}) collective-permute-start(f32[54,8,1,128]{3,1,2,0:T(8,128)S(1)} %bitcast.30), channel_id=1, source_target_pairs={{1,0},{2,1},{3,2},{5,4},{6,5},{7,6},{9,8},{10,9},{11,10},{13,12},{... | collective-permute-start | bytes 663560 | tf_op jit(solution)/shard_map/ppermute | solution.py:19
  13.9 5.7 %copy-start.21 = (f32[54,1,4,128]{3,2,1,0:T(4,128)}, f32[54,1,4,128]{3,2,1,0:T(4,128)S(1)}, u32[]{:S(2)}) copy-start(f32[54,1,4,128]{3,2,1,0:T(4,128)S(1)} %collective-permute-done) | copy-start | bytes 331780
  13.9 5.7 %copy-start.23 = (f32[54,1,4,128]{3,2,1,0:T(4,128)}, f32[54,1,4,128]{3,2,1,0:T(4,128)S(1)}, u32[]{:S(2)}) copy-start(f32[54,1,4,128]{3,2,1,0:T(4,128)S(1)} %collective-permute-done.1) | copy-start | bytes 331780
  16.9 2.8 %copy-start.19 = (f32[54,8,1,128]{3,1,2,0:T(8,128)}, f32[54,8,1,128]{3,1,2,0:T(8,128)S(1)}, u32[]{:S(2)}) copy-start(f32[54,8,1,128]{3,1,2,0:T(8,128)S(1)} %collective-permute-done.2) | copy-start | bytes 663556
  19.2 1.2 copy-start.15
  20.4 33.8 %copy-start = (f32[56,4096]{1,0:T(8,128)}, f32[56,4096]{1,0:T(8,128)S(1)}, u32[]{:S(2)}) copy-start(f32[56,4096]{1,0:T(8,128)S(1)} %pad_maximum_fusion.1.refs_0_.refs_1_.refs_2_) | copy-start | bytes 2752516
  23.8 25.3 %collective-permute-start.4 = (f32[56,4096]{1,0:T(8,128)S(1)}, f32[56,4096]{1,0:T(8,128)S(1)}, u32[]{:S(2)}, u32[]{:S(2)}) collective-permute-start(f32[56,4096]{1,0:T(8,128)S(1)} %pad_maximum_fusion.1.refs_0_.refs_1_.refs_2_), channel_id=1, source_target_pairs={{0,2},{1,3},{2,0},{3,1},{4,6},{5,7},{6,4},{7,5},{8,10},{9,11},{10,... | collective-permute-start | bytes 2752520 | tf_op jit(solution)/shard_map/ppermute | solution.py:24
  28.7 10.4 %collective-permute-start.5 = (f32[54,32,1]{0,1,2:T(8,128)S(1)}, f32[54,32,1]{0,1,2:T(8,128)S(1)}, u32[]{:S(2)}, u32[]{:S(2)}) collective-permute-start(f32[54,32,1]{0,1,2:T(8,128)S(1)} %get-tuple-element.52), channel_id=1, source_target_pairs={{0,4},{4,8},{8,12},{12,16},{16,20},{20,24},{24,28},{1,5},{5,9},{9,... | collective-permute-start | bytes 20744 | tf_op jit(solution)/shard_map/ppermute | solution.py:19
  31.2 6.5 %collective-permute-start.6 = (f32[54,32,1]{0,1,2:T(8,128)S(1)}, f32[54,32,1]{0,1,2:T(8,128)S(1)}, u32[]{:S(2)}, u32[]{:S(2)}) collective-permute-start(f32[54,32,1]{0,1,2:T(8,128)S(1)} %get-tuple-element.53), channel_id=1, source_target_pairs={{4,0},{8,4},{12,8},{16,12},{20,16},{24,20},{28,24},{5,1},{9,5},{13... | collective-permute-start | bytes 20744 | tf_op jit(solution)/shard_map/ppermute | solution.py:19
  36.0 4.4 %copy-start.16 = (f32[54,32,128]{2,1,0:T(8,128)S(1)}, f32[54,32,128]{2,1,0:T(8,128)}, u32[]{:S(2)}) copy-start(f32[54,32,128]{2,1,0:T(8,128)} %param.11) | copy-start | bytes 2654212
  43.4 2.6 %collective-permute-start.7 = (f32[54,1,128]{2,0,1:T(8,128)S(1)}, f32[54,1,128]{2,0,1:T(8,128)S(1)}, u32[]{:S(2)}, u32[]{:S(2)}) collective-permute-start(f32[54,1,128]{2,0,1:T(8,128)S(1)} %get-tuple-element.56), channel_id=1, source_target_pairs={{0,1},{1,2},{2,3},{4,5},{5,6},{6,7},{8,9},{9,10},{10,11},{12,13},{... | collective-permute-start | bytes 82952 | tf_op jit(solution)/shard_map/ppermute | solution.py:19
  44.7 3.3 %collective-permute-start.8 = (f32[54,1,128]{2,0,1:T(8,128)S(1)}, f32[54,1,128]{2,0,1:T(8,128)S(1)}, u32[]{:S(2)}, u32[]{:S(2)}) collective-permute-start(f32[54,1,128]{2,0,1:T(8,128)S(1)} %get-tuple-element.57), channel_id=1, source_target_pairs={{1,0},{2,1},{3,2},{5,4},{6,5},{7,6},{9,8},{10,9},{11,10},{13,12},{... | collective-permute-start | bytes 82952 | tf_op jit(solution)/shard_map/ppermute | solution.py:19
  49.1 4.9 %copy-start.25 = (f32[128,128]{1,0:T(8,128)S(1)}, f32[128,128]{1,0:T(8,128)}, u32[]{:S(2)}) copy-start(f32[128,128]{1,0:T(8,128)} %param.14) | copy-start | bytes 196612
  50.5 1.0 copy-start.3
  51.4 27.3 %collective-permute-start.9 = (f32[56,8192]{1,0:T(8,128)}, f32[56,8192]{1,0:T(8,128)S(1)}, u32[]{:S(2)}, u32[]{:S(2)}) collective-permute-start(f32[56,8192]{1,0:T(8,128)} %pad_maximum_fusion), channel_id=1, source_target_pairs={{0,1},{1,0},{2,3},{3,2},{4,5},{5,4},{6,7},{7,6},{8,9},{9,8},{10,11... | collective-permute-start | bytes 5505032 | tf_op jit(solution)/shard_map/ppermute | solution.py:24
  54.1 12.3 %copy-start.4 = (f32[56,4096]{1,0:T(8,128)S(1)}, f32[56,4096]{1,0:T(8,128)}, u32[]{:S(2)}) copy-start(f32[56,4096]{1,0:T(8,128)} %copy-done.3) | copy-start | bytes 2752516
  65.6 0.8 copy-start.6
  77.9 0.8 copy-start.9
  101.4 8.3 %copy-start.26 = (f32[54,54]{1,0:T(8,128)S(1)}, f32[54,54]{1,0:T(8,128)}, u32[]{:S(2)}) copy-start(f32[54,54]{1,0:T(8,128)} %param.16) | copy-start | bytes 34996
  102.8 49.2 %collective-permute-start.11 = (f32[1904,128]{1,0:T(8,128)}, f32[1904,128]{1,0:T(8,128)}, u32[]{:S(2)}, u32[]{:S(2)}) collective-permute-start(f32[1904,128]{1,0:T(8,128)} %get-tuple-element.54), channel_id=1, source_target_pairs={{4,0},{8,4},{12,8},{16,12},{20,16},{24,20},{28,24},{5,1},{9,5},{13... | collective-permute-start | bytes 2924552 | tf_op jit(solution)/shard_map/ppermute | solution.py:19
  105.2 46.8 %collective-permute-start.10 = (f32[1904,128]{1,0:T(8,128)}, f32[1904,128]{1,0:T(8,128)}, u32[]{:S(2)}, u32[]{:S(2)}) collective-permute-start(f32[1904,128]{1,0:T(8,128)} %get-tuple-element.55), channel_id=1, source_target_pairs={{0,4},{4,8},{8,12},{12,16},{16,20},{20,24},{24,28},{1,5},{5,9},{9,... | collective-permute-start | bytes 2924552 | tf_op jit(solution)/shard_map/ppermute | solution.py:19
  109.9 1.2 copy-start.1
  111.1 1.1 copy-start.7
  112.2 9.9 %copy-start.5 = (f32[56,4096]{1,0:T(8,128)S(1)}, f32[56,4096]{1,0:T(8,128)}, u32[]{:S(2)}) copy-start(f32[56,4096]{1,0:T(8,128)} %copy-done.3) | copy-start | bytes 2752516
  112.2 9.9 %copy-start.10 = (f32[40,4096]{1,0:T(8,128)S(1)}, f32[40,4096]{1,0:T(8,128)}, u32[]{:S(2)}) copy-start(f32[40,4096]{1,0:T(8,128)} %copy-done.9) | copy-start | bytes 1966084
  132.2 19.8 %copy-start.11 = (f32[34,56,128]{2,1,0:T(8,128)S(1)}, f32[34,56,128]{2,1,0:T(8,128)}, u32[]{:S(2)}) copy-start(f32[34,56,128]{2,1,0:T(8,128)} %pad.17.moved_ref) | copy-start | bytes 2924548
  132.2 19.8 %copy-start.12 = (f32[32,128]{1,0:T(8,128)S(1)}, f32[32,128]{1,0:T(8,128)}, u32[]{:S(2)}) copy-start(f32[32,128]{1,0:T(8,128)} %diss_ref.1) | copy-start | bytes 49156
  132.3 19.8 %copy-start.13 = (f32[32,128]{1,0:T(8,128)S(1)}, f32[32,128]{1,0:T(8,128)}, u32[]{:S(2)}) copy-start(f32[32,128]{1,0:T(8,128)} %rate_ref.1) | copy-start | bytes 49156
  132.3 19.8 %copy-start.14 = (s32[128]{0:T(128)S(1)}, s32[128]{0:T(128)}, u32[]{:S(2)}) copy-start(s32[128]{0:T(128)} %param.19) | copy-start | bytes 1540
  158.1 14.9 %copy-start.2 = (f32[56,4096]{1,0:T(8,128)S(1)}, f32[56,4096]{1,0:T(8,128)}, u32[]{:S(2)}) copy-start(f32[56,4096]{1,0:T(8,128)} %copy-done) | copy-start | bytes 2752516
  158.1 14.9 %copy-start.8 = (f32[40,4096]{1,0:T(8,128)S(1)}, f32[40,4096]{1,0:T(8,128)}, u32[]{:S(2)}) copy-start(f32[40,4096]{1,0:T(8,128)} %copy-done.6) | copy-start | bytes 1966084
  158.1 38.4 %collective-permute-start.13 = (f32[1792,128]{1,0:T(8,128)S(1)}, f32[1792,128]{1,0:T(8,128)S(1)}, u32[]{:S(2)}, u32[]{:S(2)}) collective-permute-start(f32[1792,128]{1,0:T(8,128)S(1)} %bitcast.17), channel_id=1, source_target_pairs={{4,0},{8,4},{12,8},{16,12},{20,16},{24,20},{28,24},{5,1},{9,5},{13... | collective-permute-start | bytes 2752520 | tf_op jit(solution)/shard_map/ppermute | solution.py:19
  160.5 41.9 %collective-permute-start.12 = (f32[1792,128]{1,0:T(8,128)S(1)}, f32[1792,128]{1,0:T(8,128)S(1)}, u32[]{:S(2)}, u32[]{:S(2)}) collective-permute-start(f32[1792,128]{1,0:T(8,128)S(1)} %bitcast.18), channel_id=1, source_target_pairs={{0,4},{4,8},{8,12},{12,16},{16,20},{20,24},{24,28},{1,5},{5,9},{9,... | collective-permute-start | bytes 2752520 | tf_op jit(solution)/shard_map/ppermute | solution.py:19
  213.7 11.3 %collective-permute-start.14 = (f32[56,4096]{1,0:T(8,128)S(1)}, f32[56,4096]{1,0:T(8,128)S(1)}, u32[]{:S(2)}, u32[]{:S(2)}) collective-permute-start(f32[56,4096]{1,0:T(8,128)S(1)} %project.13), channel_id=1, source_target_pairs={{0,1},{1,0},{2,3},{3,2},{4,5},{5,4},{6,7},{7,6},{8,9},{9,8},{10,11... | collective-permute-start | bytes 2752520 | tf_op jit(solution)/shard_map/ppermute | solution.py:24
  225.1 24.7 %collective-permute-start.16 = (f32[56,4096]{1,0:T(8,128)S(1)}, f32[56,4096]{1,0:T(8,128)S(1)}, u32[]{:S(2)}, u32[]{:S(2)}) collective-permute-start(f32[56,4096]{1,0:T(8,128)S(1)} %add.70), channel_id=1, source_target_pairs={{0,2},{1,3},{2,0},{3,1},{4,6},{5,7},{6,4},{7,5},{8,10},{9,11},{10,... | collective-permute-start | bytes 2752520 | tf_op jit(solution)/shard_map/ppermute | solution.py:24
  237.2 12.6 %collective-permute-start.15 = (f32[56,4096]{1,0:T(8,128)S(1)}, f32[56,4096]{1,0:T(8,128)S(1)}, u32[]{:S(2)}, u32[]{:S(2)}) collective-permute-start(f32[56,4096]{1,0:T(8,128)S(1)} %project.15), channel_id=1, source_target_pairs={{0,1},{1,0},{2,3},{3,2},{4,5},{5,4},{6,7},{7,6},{8,9},{9,8},{10,11... | collective-permute-start | bytes 2752520 | tf_op jit(solution)/shard_map/ppermute | solution.py:24
  250.0 1.2 copy-start.18
  250.0 1.2 copy-start.20
  250.0 1.2 copy-start.22
  250.0 1.3 copy-start.24
  250.0 1.3 copy-start.27
where the time goes:
time: 255 us; the launch traced here: 254 us
  Pallas kernels  167 us (65%)
  starting transfers between devices  39.8 us (16%)
  local copies, waits for them, and re-layouts  22.4 us (9%)
  waiting for transfers between devices  12.7 us (5%)
  other arithmetic  10.4 us (4%)
    pallas_call x6, Pallas kernels, bin_call(): pl.pallas_call(functools.partial(bin_kernel, bins, sp, cells, nshape, out...  85.2 us
    pallas_call x8, Pallas kernels, project_call(): pl.pallas_call(functools.partial(project_kernel, bins, sp, cells, nshape,...  76 us
    ppermute x12, starting transfers between devices, shift(): lax.ppermute(array, axis, [(i, i + by) for i in range(count) if 0 <= i +...  31.8 us
    ppermute x12, waiting for transfers between devices, shift(): lax.ppermute(array, axis, [(i, i + by) for i in range(count) if 0 <= i +...  12.7 us
    ppermute x5, starting transfers between devices, swap(): return lax.ppermute(array, axis, [(i, i ^ bit) for i in range(count)])  8.04 us
    unnamed x58, local copies, waits for them, and re-layouts  7.32 us
    pallas_call x1, Pallas kernels, on_device(): pl.pallas_call(functools.partial(chem_kernel, species, sp), out_shape=jax...  5.97 us
  transfers between devices with their start and end apart: 17, of which 4 were waited for; matrix products, arithmetic and copies ran while one was open for 5% of the time, Pallas kernels for 50%

commit v1 on v0

v1 whole, which is shorter than its diff:
```python
import functools

import jax
import jax.numpy as jnp
from jax import lax
from jax.experimental import pallas as pl
from jax.experimental.pallas import tpu as pltpu
from jax.sharding import PartitionSpec as P

KMAX = 4
F32 = jnp.float32
BF16 = jnp.bfloat16
NT = (((1,), (1,)), ((), ()))
NN = (((1,), (0,)), ((), ()))
LANES = 128
TILE = 256
HALF = 64
GROUP = 8
LIMIT = 56 << 20


def shift(array, axis, by):
    count = lax.axis_size(axis)
    return lax.ppermute(array, axis, [(i, i + by) for i in range(count) if 0 <= i + by < count])


def swap(array, axis, bit):
    count = lax.axis_size(axis)
    return lax.ppermute(array, axis, [(i, i ^ bit) for i in range(count)])


def hop(array, axis, outward):
    count = lax.axis_size(axis)
    step = lambda i: 2 if (i % 2 == 1) == outward else -2
    return lax.ppermute(array, axis, [(i, i + step(i)) for i in range(count) if 0 <= i + step(i) < count])


def halves(x):
    high = x.astype(BF16)
    return high, (x - high.astype(F32)).astype(BF16)


def padded_halves(x):
    gap = jnp.zeros((HALF - x.shape[0], x.shape[1]), F32)
    high = x.astype(BF16).astype(F32)
    return jnp.concatenate([high, gap, x - high, gap], axis=0).astype(BF16)


def rows_equal(targets, row):
    return jnp.where(targets == row, 1.0, 0.0).astype(BF16)


def whole(shape):
    return pl.BlockSpec(shape, lambda *_: (0,) * len(shape))


VMEM = pl.BlockSpec(memory_space=pltpu.VMEM)
SMEM = pl.BlockSpec(memory_space=pltpu.SMEM)


def params():
    return pltpu.CompilerParams(vmem_limit_bytes=LIMIT)


def rank_kernel(tiles, span, key_ref, rank_ref, table_ref):
    count = key_ref.shape[1]
    ids = lax.broadcasted_iota(jnp.int32, (tiles, TILE), 0).astype(F32)
    tile_of = lambda n: jnp.floor((key_ref[:, n * TILE : (n + 1) * TILE] + 0.5) * (1.0 / span))
    total = jnp.zeros((tiles, TILE), F32)
    for n in range(count // TILE):
        total = total + jnp.where(ids == tile_of(n), 1.0, 0.0)
    total = jnp.sum(total, axis=1, keepdims=True)
    total = jnp.broadcast_to(total, (tiles, LANES))
    big = jnp.floor(total * (1.0 / HALF))
    row = lax.broadcasted_iota(jnp.int32, (tiles, tiles), 0)
    below = rows_equal(jnp.where(lax.broadcasted_iota(jnp.int32, (tiles, tiles), 1) < row, 1, 0), 1)
    add = lambda part: lax.dot_general(below, part.astype(BF16), NN, preferred_element_type=F32)
    base = add(big) * HALF + add(total - big * HALF)
    order = lax.broadcasted_iota(jnp.int32, (tiles, LANES), 0).astype(F32)
    lane = lax.broadcasted_iota(jnp.int32, (tiles, LANES), 1).astype(F32)
    last = jnp.maximum(jnp.ceil((base + total) * (1.0 / LANES)) - 1.0, 0.0) + order
    passed = jnp.where((last < lane) & (order < tiles - 1), 1.0, 0.0)
    table_ref[...] = jnp.sum(passed, axis=0, keepdims=True)
    ahead = jnp.where(
        lax.broadcasted_iota(jnp.int32, (TILE, TILE), 0) < lax.broadcasted_iota(jnp.int32, (TILE, TILE), 1), 1.0, 0.0
    ).astype(BF16)
    carry = base[:, :1]
    for n in range(count // TILE):
        hot = jnp.where(ids == tile_of(n), 1.0, 0.0)
        before = lax.dot_general(hot.astype(BF16), ahead, NN, preferred_element_type=F32) + carry
        rank_ref[:, n * TILE : (n + 1) * TILE] = jnp.sum(hot * before, axis=0, keepdims=True)
        carry = carry + jnp.sum(hot, axis=1, keepdims=True)


def rank_call(key, tiles, span):
    count = key.shape[1]
    return pl.pallas_call(
        functools.partial(rank_kernel, tiles, span),
        out_shape=[jax.ShapeDtypeStruct((1, count), F32), jax.ShapeDtypeStruct((1, LANES), F32)],
        in_specs=[VMEM],
        out_specs=[VMEM] * 2,
        compiler_params=params(),
        cost_estimate=pl.CostEstimate(flops=2 * tiles * TILE * count, bytes_accessed=8 * count, transcendentals=0),
        name="rank",
    )(key)


def permute_kernel(back, x_ref, rank_ref, out_ref, parts):
    rows, count = x_ref.shape
    chunk = 2 * TILE

    @pl.when(pl.program_id(0) == 0)
    def _():
        x = x_ref[...]
        high = x.astype(BF16).astype(F32)
        parts[...] = jnp.concatenate([high, x - high], axis=0).astype(BF16)

    total = jnp.zeros((2 * rows, TILE), F32)
    here = pl.program_id(0) * TILE
    for n in range(count // chunk):
        piece = slice(n * chunk, (n + 1) * chunk)
        if back:
            ids = lax.broadcasted_iota(jnp.int32, (chunk, TILE), 0) + n * chunk
            hot = rows_equal(ids.astype(F32), rank_ref[:, pl.ds(pl.multiple_of(here, TILE), TILE)])
            total = total + lax.dot_general(parts[:, piece], hot, NN, preferred_element_type=F32)
        else:
            ids = lax.broadcasted_iota(jnp.int32, (TILE, chunk), 0) + here
            hot = rows_equal(ids.astype(F32), rank_ref[:, piece])
            total = total + lax.dot_general(parts[:, piece], hot, NT, preferred_element_type=F32)
    out_ref[...] = total[:rows] + total[rows:]


def permute_call(x, rank, back):
    rows, count = x.shape
    return pl.pallas_call(
        functools.partial(permute_kernel, back),
        grid=(count // TILE,),
        out_shape=jax.ShapeDtypeStruct((rows, count), F32),
        in_specs=[whole(x.shape), whole(rank.shape)],
        out_specs=pl.BlockSpec((rows, TILE), lambda i: (0, i)),
        scratch_shapes=[pltpu.VMEM((2 * rows, count), BF16)],
        compiler_params=params(),
        cost_estimate=pl.CostEstimate(flops=4 * rows * count * count, bytes_accessed=8 * rows * count, transcendentals=0),
        name="unsort" if back else "sort",
    )(x, rank)


def weights_of(key, table, bins, per_tile):
    nshape = table.shape[1]
    cell = jnp.floor((key + 0.5) * (1.0 / nshape))
    shape = key - cell * nshape
    tile = jnp.floor((cell + 0.5) * (1.0 / per_tile))
    within = cell - tile * per_tile
    ids = lax.broadcasted_iota(jnp.int32, (nshape, key.shape[1]), 0).astype(F32)
    picked = lax.dot_general(table, rows_equal(ids, shape), NN, preferred_element_type=F32)
    columns = []
    for part in (picked[:bins], picked[bins:]):
        columns.append(jnp.concatenate([jnp.where(within == m, part, 0.0) for m in range(per_tile)], axis=0))
    return jnp.concatenate(columns, axis=1).astype(BF16), tile


def split_table(table):
    high = table.astype(BF16).astype(F32)
    return jnp.concatenate([high, table - high], axis=0).astype(BF16)


def prepare_weights(source, index, key_row, table, bins, per_tile, weights, tiles):
    def step(n, _):
        key = source[key_row : key_row + 1, pl.ds(pl.multiple_of(n * LANES, LANES), LANES)]
        block, tile = weights_of(key, table, bins, per_tile)
        weights[index + n] = block
        tiles[index + n] = jnp.broadcast_to(tile, tiles.shape[1:])
        return 0

    lax.fori_loop(0, source.shape[1] // LANES, step, 0, unroll=2)


def collect_kernel(species, bins, per_tile, pairs, lists, first, *refs):
    sources, refs = refs[:lists], refs[lists:]
    table_ref, steps_ref, *refs = refs
    acc_ref = None if first else refs.pop(0)
    out_ref, weights, tiles, parts = refs
    rows, count = sources[0].shape
    blocks = count // LANES
    out_ref[...] = jnp.zeros_like(out_ref) if first else acc_ref[...]
    table = split_table(table_ref[...])
    line = lax.broadcasted_iota(jnp.int32, (rows, LANES), 0)
    for number, source in enumerate(sources):
        prepare_weights(source, number * blocks, species, table, bins, per_tile, weights, tiles)

        def split(n, _, source=source, number=number):
            x = source[:, pl.ds(pl.multiple_of(n * LANES, LANES), LANES)]
            x = jnp.where(line < species, x, jnp.where(line == species, 1.0, 0.0))
            parts[number * blocks + n] = padded_halves(x)
            return 0

        lax.fori_loop(0, blocks, split, 0, unroll=2)

    def step(n, _):
        for number in range(lists):
            for g in range(GROUP):
                k = n * GROUP + g
                tile = steps_ref[number, k]
                block = jnp.minimum(k - tile, blocks - 1) + number * blocks
                wanted = jnp.where(k < pairs, tile, -1).astype(F32)
                mask = jnp.where(tiles[block] == wanted, 1.0, 0.0).astype(BF16)
                mask = jnp.concatenate([mask] * (2 * HALF // mask.shape[0]), axis=0)
                x = parts[block] * mask
                both = jnp.concatenate([x, x], axis=1)
                got = lax.dot_general(both, weights[block], NT, preferred_element_type=F32)
                place = pl.ds(pl.multiple_of(tile * TILE, TILE), TILE)
                out_ref[:, place] += got[:rows] + got[HALF : HALF + rows]
        return 0

    lax.fori_loop(0, -(-pairs // GROUP), step, 0)


def collect_call(sources, table, steps, acc, species, bins, per_tile, ntiles):
    rows, count = sources[0].shape
    lists, blocks = len(sources), count // LANES
    pairs = blocks + ntiles - 1
    args = list(sources) + [table, steps]
    specs = [VMEM] * (lists + 1) + [SMEM]
    alias = {}
    if acc is not None:
        alias = {len(args): 0}
        args.append(acc)
        specs.append(VMEM)
    return pl.pallas_call(
        functools.partial(collect_kernel, species, bins, per_tile, pairs, lists, acc is None),
        out_shape=jax.ShapeDtypeStruct((rows, ntiles * TILE), F32),
        in_specs=specs,
        out_specs=VMEM,
        scratch_shapes=[
            pltpu.VMEM((lists * blocks, TILE, 2 * LANES), BF16),
            pltpu.VMEM((lists * blocks, 16, LANES), F32),
            pltpu.VMEM((lists * blocks, 2 * HALF, LANES), BF16),
        ],
        input_output_aliases=alias,
        compiler_params=params(),
        cost_estimate=pl.CostEstimate(flops=lists * pairs * 2 * LANES * TILE * TILE, bytes_accessed=0, transcendentals=0),
        name="collect",
    )(*args)


def project_kernel(bins, per_tile, pairs, lists, species, *refs):
    means, refs = refs[:3], refs[3:]
    keys_ref, table_ref, steps_ref, out_ref, weights, tiles, parts = refs
    rows = means[0].shape[0]
    count = keys_ref.shape[1]
    blocks = count // LANES
    per_mean = means[0].shape[1] // TILE
    for number, mean in enumerate(means):

        def split(n, _, number=number, mean=mean):
            parts[number * per_mean + n] = padded_halves(mean[:, pl.ds(pl.multiple_of(n * TILE, TILE), TILE)])
            return 0

        lax.fori_loop(0, per_mean, split, 0, unroll=2)
    table = split_table(table_ref[...])
    out_ref[...] = jnp.zeros_like(out_ref)
    for number in range(lists):
        prepare_weights(keys_ref.at[number : number + 1], number * blocks, 0, table, bins, per_tile, weights, tiles)

    def step(n, _):
        for number in range(lists):
            for g in range(GROUP):
                k = n * GROUP + g
                tile = steps_ref[number, k]
                local = jnp.minimum(k - tile, blocks - 1)
                block = local + number * blocks
                wanted = jnp.where(k < pairs, tile, -1).astype(F32)
                got = lax.dot_general(parts[tile], weights[block], NN, preferred_element_type=F32)
                got = got[:rows] + got[HALF : HALF + rows]
                got = got[:, :LANES] + got[:, LANES:]
                got = jnp.where(tiles[block][:1] == wanted, got, 0.0)
                place = pl.ds(pl.multiple_of(local * LANES, LANES), LANES)
                out_ref[number, :, place] += got
        return 0

    lax.fori_loop(0, -(-pairs // GROUP), step, 0)


def project_call(means, keys, table, steps, species, bins, per_tile, ntiles):
    rows = means[0].shape[0]
    lists, count = keys.shape
    blocks = count // LANES
    pairs = blocks + ntiles - 1
    return pl.pallas_call(
        functools.partial(project_kernel, bins, per_tile, pairs, lists, species),
        out_shape=jax.ShapeDtypeStruct((lists, rows, count), F32),
        in_specs=[VMEM] * 5 + [SMEM],
        out_specs=VMEM,
        scratch_shapes=[
            pltpu.VMEM((lists * blocks, TILE, 2 * LANES), BF16),
            pltpu.VMEM((lists * blocks, 16, LANES), F32),
            pltpu.VMEM((ntiles, 2 * HALF, TILE), BF16),
        ],
        compiler_params=params(),
        cost_estimate=pl.CostEstimate(flops=lists * pairs * 2 * LANES * TILE * TILE, bytes_accessed=0, transcendentals=0),
        name="project",
    )(*means, keys, table, steps)


def edge_rows(bins, chunk, cells, start):
    lane = lax.broadcasted_iota(jnp.int32, (cells, chunk), 1) + start
    cell = lax.broadcasted_iota(jnp.int32, (cells, chunk), 0)
    pick = lambda b: jnp.where(lane == cell * bins + b, 1.0, 0.0)
    return jnp.concatenate([pick(0), pick(bins - 1)], axis=0).astype(BF16)


def blend_kernel(species, bins, own_ref, got_ref, moved_ref, out_ref, edge_ref):
    rows, width = own_ref.shape
    cells = width // bins
    edge = jnp.zeros((2 * rows, 2 * cells), F32)
    for n in range(width // TILE):
        piece = slice(n * TILE, (n + 1) * TILE)
        total = own_ref[:, piece] + got_ref[:, piece]
        blended = (total + moved_ref[:, piece]) / (total[species : species + 1] + 1.0)
        out_ref[:, piece] = blended
        high = blended.astype(BF16).astype(F32)
        parts = jnp.concatenate([high, blended - high], axis=0).astype(BF16)
        edge = edge + lax.dot_general(parts, edge_rows(bins, TILE, cells, n * TILE), NT, preferred_element_type=F32)
    edge_ref[...] = edge[:rows] + edge[rows:]


def chem_kernel(species, bins, state_ref, edge_ref, diss_ref, rate_ref, count_ref, matrix_ref, out_ref):
    rows, width = state_ref.shape
    cells = width // bins
    third = matrix_ref.shape[1] // 3
    high, low = halves(matrix_ref[...])
    column = lax.broadcasted_iota(jnp.int32, matrix_ref.shape, 1)
    matrix = jnp.where(column < 2 * third, high.astype(F32), low.astype(F32)).astype(BF16)
    chunk = 2 * TILE
    line = lax.broadcasted_iota(jnp.int32, (rows, chunk), 0)
    slot = lax.broadcasted_iota(jnp.int32, (rows, chunk), 1) % bins
    gap = [jnp.zeros((third - rows, chunk), F32)] * (third > rows)
    edge = edge_ref[...]
    high = edge.astype(BF16).astype(F32)
    edges = jnp.concatenate([high, edge - high], axis=0).astype(BF16)
    for n in range(width // chunk):
        piece = slice(n * chunk, (n + 1) * chunk)
        here = state_ref[:, piece]
        outer = lax.dot_general(edges, edge_rows(bins, chunk, cells, n * chunk), NN, preferred_element_type=F32)
        outer = outer[:rows] + outer[rows:]
        before = jnp.where(slot == 0, outer, pltpu.roll(here, 1, 1))
        after = jnp.where(slot == bins - 1, outer, pltpu.roll(here, chunk - 1, 1))
        state = here + diss_ref[:, piece] * (after - 2.0 * here + before)
        half = 0.5 * rate_ref[:, piece]
        count = count_ref[:, piece]
        for k in range(KMAX):
            high, low = (part.astype(F32) for part in halves(state))
            stack = jnp.concatenate([high, *gap, low, *gap, high, *gap], axis=0).astype(BF16)
            rate = lax.dot_general(matrix, stack, NN, preferred_element_type=F32)
            state = jnp.where(k < count, state + half * jnp.tanh(rate), state)
        out_ref[:, piece] = jnp.where(line == species, 1.0, state)


def on_device(
    les_state, cmc_state, cmc_map, pdf_index, pdf_table, diffusion, chem_matrix, dissipation, reaction_rate, substeps
):
    species = les_state.shape[0]
    rows = -(-(species + 2) // 8) * 8
    bins, cells = cmc_state.shape[1:]
    nshape = pdf_table.shape[0]
    count = cmc_map.size
    ncross = lax.axis_size("cross")
    per_tile = TILE // bins
    ntiles = 3 * cells // per_tile
    width = cells * bins
    odd = lax.axis_index("slab") % 2 == 1

    below = shift(les_state[:, -1:], "slab", 1)
    above = shift(les_state[:, :1], "slab", -1)
    behind = shift(les_state[:, :, -1:], "cross", 1)
    ahead = shift(les_state[:, :, :1], "cross", -1)

    offset = cmc_map.reshape(1, count) - (lax.axis_index("slab") - 1) * cells
    block = offset // cells
    offset = jnp.where(odd, (2 - block) * cells + offset - block * cells, offset)
    key = (offset * nshape + pdf_index.reshape(1, count)).astype(F32)
    rank, steps = rank_call(key, ntiles, nshape * per_tile)

    xs = jnp.concatenate([below, les_state, above], axis=1)
    ys = jnp.concatenate([behind, les_state, ahead], axis=2)
    zs = jnp.pad(les_state, ((0, 0), (0, 0), (0, 0), (1, 1)))
    around = xs[:, 2:] + xs[:, :-2] + ys[:, :, 2:] + ys[:, :, :-2] + zs[..., 2:] + zs[..., :-2]
    transported = les_state + diffusion[:, None, None, None] * (around - 6.0 * les_state)
    flat = transported.reshape(species, count)
    fill = [jnp.zeros((rows - species - 1, count), F32)]
    mine = permute_call(jnp.concatenate([flat, key] + fill, axis=0), rank, False)
    mine = mine.at[rows - 1, :LANES].set(steps[0])

    table = lax.dynamic_slice_in_dim(pdf_table.T, lax.axis_index("cross") * bins, bins, axis=0)

    bits = [1 << k for k in range(ncross.bit_length() - 1)]
    sources = [mine]
    if bits:
        far_off = swap(mine, "cross", bits[-1])
        sources += [swap(mine, "cross", bit) for bit in bits[:-1]] + [far_off]
        sources += [swap(far_off, "cross", bit) for bit in bits[:-1]]
    steps_of = lambda group: jnp.stack([s[rows - 1, :LANES] for s in group]).astype(jnp.int32)

    spread = lambda a: a.transpose(0, 2, 1).reshape(a.shape[0], width)
    wide = lambda a: a.T.reshape(1, width)
    state = spread(cmc_state)
    left = jnp.concatenate([shift(state[:, -bins:], "slab", 1), state[:, :-bins]], axis=1)
    right = jnp.concatenate([state[:, bins:], shift(state[:, :bins], "slab", -1)], axis=1)
    moved = state - 0.4 * (state - left) + 0.1 * (right - 2.0 * state + left)
    moved = jnp.pad(moved, ((0, rows - species), (0, 0)))

    acc = None
    for source in sources:
        acc = collect_call([source], table, steps_of([source]), acc, species, bins, per_tile, ntiles)
    far, own, near = (acc[:, n * width : (n + 1) * width] for n in range(3))
    near = near + hop(far, "slab", True)
    got = swap(near, "slab", 1)

    blended, edge = pl.pallas_call(
        functools.partial(blend_kernel, species, bins),
        out_shape=[jax.ShapeDtypeStruct((rows, width), F32), jax.ShapeDtypeStruct((rows, 2 * cells), F32)],
        in_specs=[VMEM] * 3,
        out_specs=[VMEM] * 2,
        compiler_params=params(),
        name="blend",
    )(own, got, moved)
    edge = jnp.concatenate(
        [shift(edge[:, cells:], "cross", 1), shift(edge[:, :cells], "cross", -1)], axis=1
    )
    extra = rows - species
    fresh = pl.pallas_call(
        functools.partial(chem_kernel, species, bins),
        out_shape=jax.ShapeDtypeStruct((rows, width), F32),
        in_specs=[VMEM] * 6,
        out_specs=VMEM,
        compiler_params=params(),
        name="chem",
    )(
        blended, edge, wide(dissipation), wide(reaction_rate), jnp.repeat(substeps, bins)[None, :],
        jnp.tile(jnp.pad(chem_matrix, ((0, extra), (0, -(-rows // 16) * 16 - species))), (1, 3)),
    )
    cmc_out = fresh[:species].reshape(species, cells, bins).transpose(0, 2, 1)
    next_mean = swap(fresh, "slab", 1)
    far_mean = hop(next_mean, "slab", False)

    keys = jnp.concatenate([s[species : species + 1] for s in sources], axis=0)
    part = project_call(
        [far_mean, fresh, next_mean], keys, table, steps_of(sources), species, bins, per_tile, ntiles
    )
    part = [part[n] for n in range(len(sources))]
    if bits:
        half = len(part) // 2
        here, there = part[:half], part[half:]

        def gather(group):
            total = group[0]
            for bit, piece in zip(bits[:-1], group[1:]):
                total = total + swap(piece, "cross", bit)
            return total

        there = gather(there)
        part = [gather(here) + swap(there, "cross", bits[-1])]
    total = permute_call(part[0], rank, True)
    conditional = (total[:species] / total[species : species + 1]).reshape(transported.shape)
    les_out = transported + 0.5 * (conditional - transported)
    return (les_out, cmc_out)


def solution(mesh):
    return jax.shard_map(
        on_device,
        mesh=mesh,
        in_specs=(
            P(None, "slab", "cross", None),
            P(None, "cross", "slab"),
            P("slab", "cross", None),
            P("slab", "cross", None),
            P(),
            P(),
            P(),
            P("cross", "slab"),
            P("cross", "slab"),
            P("slab"),
        ),
        out_specs=(P(None, "slab", "cross", None), P(None, "cross", "slab")),
        check_vma=False,
    )
```

time: 255 us -> 307 us (1.20)
  waiting for transfers between devices: 12.7 us -> 112 us
  Pallas kernels: 167 us -> 108 us
  other arithmetic: 10.4 us -> 24.3 us
  starting transfers between devices: 39.8 us -> 30.7 us
  local copies, waits for them, and re-layouts: 22.4 us -> 28.7 us
    ppermute x5 -> x8, waiting for transfers between devices: 0.01 us -> 73.2 us  [swap(): return lax.ppermute(array, axis, [(i, i ^ bit) for i in range(count)])]
    pallas_call x15 -> x10, Pallas kernels: 167 us -> 108 us  [the longest x4 45.7 us: collect_call(): pl.pallas_call(functools.partial(collect_kernel, species, bins, per_tile,...]
    ppermute x0 -> x2, waiting for transfers between devices: none -> 39 us  [hop(): lax.ppermute(array, axis, [(i, i + step(i)) for i in range(count) if 0 <=...]
    ppermute x12 -> x8, waiting for transfers between devices: 12.7 us -> 0.04 us  [shift(): lax.ppermute(array, axis, [(i, i + by) for i in range(count) if 0 <= i +...]
    ppermute x12 -> x8, starting transfers between devices: 31.8 us -> 20.6 us  [shift(): lax.ppermute(array, axis, [(i, i + by) for i in range(count) if 0 <= i +...]
    ppermute x0 -> x2, starting transfers between devices: none -> 4.83 us  [hop(): lax.ppermute(array, axis, [(i, i + step(i)) for i in range(count) if 0 <=...]
    add x3 -> x4, other arithmetic: 3.08 us -> 6.59 us  [the longest x1 2.8 us: on_device(): part = [gather(here) + swap(there, 'cross', bits[-1])]]
    optimization_barrier x2 -> x0, local copies, waits for them, and re-layouts: 3.45 us -> none  [on_device(): cmc_state, t_own = lax.optimization_barrier((cmc_state, t_own))]
  transfers between devices with their start and end apart: 17 -> 18, of which waited for: 4 -> 7; matrix products, arithmetic and copies ran while one was open for 5% -> 9% of each run, Pallas kernels for 50% -> 16%
where the time goes in v1:
time: 307 us; the launch traced here: 305 us
  waiting for transfers between devices  112 us (36%)
  Pallas kernels  108 us (35%)
  starting transfers between devices  30.7 us (10%)
  local copies, waits for them, and re-layouts  28.7 us (9%)
  other arithmetic  24.3 us (8%)
    ppermute x8, waiting for transfers between devices, swap(): return lax.ppermute(array, axis, [(i, i ^ bit) for i in range(count)])  73.2 us
    pallas_call x4, Pallas kernels, collect_call(): pl.pallas_call(functools.partial(collect_kernel, species, bins, per_tile,...  45.7 us
    ppermute x2, waiting for transfers between devices, hop(): lax.ppermute(array, axis, [(i, i + step(i)) for i in range(count) if 0 <=...  39 us
    pallas_call x2, Pallas kernels, permute_call(): pl.pallas_call(functools.partial(permute_kernel, back), grid=(count // TI...  25.8 us
    pallas_call x1, Pallas kernels, project_call(): pl.pallas_call(functools.partial(project_kernel, bins, per_tile, pairs, l...  23.1 us
    ppermute x8, starting transfers between devices, shift(): lax.ppermute(array, axis, [(i, i + by) for i in range(count) if 0 <= i +...  20.6 us
    pallas_call x1, Pallas kernels, on_device(): pl.pallas_call(functools.partial(chem_kernel, species, bins), out_shape=j...  8.31 us
    unnamed x42, local copies, waits for them, and re-layouts  6.16 us
  transfers between devices with their start and end apart: 18, of which 7 were waited for; matrix products, arithmetic and copies ran while one was open for 9% of the time, Pallas kernels for 16%

profile of v1, /device:TPU:2, one launch (start us, length us, event | category | flops | bytes accessed | tf_op | source)
XLA Modules:
  0.0 304.9 jit_solution(10063480784054488604)
XLA Ops:
  0.6 1.9 fusion.23
  2.6 1.3 collective-permute-start.2
  3.9 3.0 collective-permute-start.3
  7.9 1.9 collective-permute-start
  9.8 4.8 %collective-permute-start.1 = (f32[54,1,4,128]{3,2,1,0:T(4,128)S(1)}, f32[54,1,4,128]{3,2,1,0:T(4,128)S(1)}, u32[]{:S(2)}, u32[]{:S(2)}) collective-permute-start(f32[54,1,4,128]{3,2,1,0:T(4,128)S(1)} %get-tuple-element.41), channel_id=1, source_target_pairs={{0,4},{4,8},{8,12},{12,16},{16,20},{20,24},{24,28},{1,5},{5,9},{9,... | collective-permute-start | bytes 331784 | tf_op jit(solution)/shard_map/ppermute | solution.py:24
  15.4 1.4 fusion.16.key_ref
  16.9 2.0 rank.1
  19.6 5.2 %fusion.10 = f32[54,8,4,128]{3,2,1,0:T(4,128)S(1)} fusion(f32[54,8,4,128]{3,2,1,0:T(4,128)} %param.12, f32[54,8,1,128]{3,2,1,0:T(1,128)S(1)} %bitcast.39, f32[54,8,1,128]{3,2,1,0:T(1,128)S(1)} %bitcast.37, f32[54,1,4,128]{3,2,1,0:T(4,128)S(1)} %collective-permute-done.1, f32[54,1,4,128]{3,2,1,0:T(4,128)S(1)} %collective-permute-done, f32[54]{0:T(128)} %param.17), kind=kLoop, calls=%fused_computation.21 | loop fusion | flops 2875392 | bytes 2433240 | tf_op jit(solution)/shard_map/add | solution.py:388
  25.2 1.1 maximum_maximum_fusion.x_ref
  26.3 14.9 %sort.1 = f32[56,4096]{1,0:T(8,128)} custom-call(f32[56,4096]{1,0:T(8,128)} %maximum_maximum_fusion.x_ref, f32[1,4096]{1,0:T(1,128)} %get-tuple-element.18.rank_ref), custom_call_target="tpu_custom_call" | custom-call | flops 3758096384 | bytes 1835008 | tf_op jit(solution)/shard_map/sort/pallas_call | solution.py:135
  41.2 1.3 scatter.4.refs_0_
  42.5 1.5 collective-permute-start.4
  44.0 1.9 copy.38
  46.7 1.9 collective-permute-start.10
  48.6 4.8 %collective-permute-start.9 = (f32[54,32]{1,0:T(8,128)S(1)}, f32[54,32]{1,0:T(8,128)S(1)}, u32[]{:S(2)}, u32[]{:S(2)}) collective-permute-start(f32[54,32]{1,0:T(8,128)S(1)} %get-tuple-element.36), channel_id=1, source_target_pairs={{0,4},{4,8},{8,12},{12,16},{16,20},{20,24},{24,28},{1,5},{5,9},{9,... | collective-permute-start | bytes 20744 | tf_op jit(solution)/shard_map/ppermute | solution.py:24
  54.0 11.7 %collective-permute-done.4.refs_0_ = f32[56,4096]{1,0:T(8,128)} collective-permute-done((f32[56,4096]{1,0:T(8,128)}, f32[56,4096]{1,0:T(8,128)}, u32[]{:S(2)}, u32[]{:S(2)}) %collective-permute-start.4) | collective-permute-done | bytes 917536 | tf_op jit(solution)/shard_map/ppermute | solution.py:29
  66.4 10.7 %collect.4.refs_3_ = f32[56,12288]{1,0:T(8,128)} custom-call(f32[56,4096]{1,0:T(8,128)} %scatter.4.refs_0_, f32[32,128]{1,0:T(8,128)} %bitcast.41, s32[1,128]{1,0:T(1,128)} %convert_element_type.28.refs_2_), custom_call_target="tpu_custom_call" | custom-call | flops 1325400064 | tf_op jit(solution)/shard_map/collect/pallas_call | solution.py:229
  77.1 1.2 fusion.17
  78.3 11.6 %collect.5.refs_3_ = f32[56,12288]{1,0:T(8,128)} custom-call(f32[56,4096]{1,0:T(8,128)} %collective-permute-done.6.refs_0_, f32[32,128]{1,0:T(8,128)} %bitcast.42, s32[1,128]{1,0:T(1,128)} %get-tuple-element.31.refs_2_, f32[56,12288]{1,0:T(8,128)} %collect.4.refs_3_), custom_call_target="tpu_custom_call", output_to_operand_aliasing={{}: (3, {})} | custom-call | flops 1325400064 | tf_op jit(solution)/shard_map/collect/pallas_call | solution.py:229
  90.0 1.2 fusion.18
  91.2 11.7 %collect.6.refs_3_ = f32[56,12288]{1,0:T(8,128)} custom-call(f32[56,4096]{1,0:T(8,128)} %collective-permute-done.4.refs_0_, f32[32,128]{1,0:T(8,128)} %bitcast.43, s32[1,128]{1,0:T(1,128)} %get-tuple-element.33.refs_2_, f32[56,12288]{1,0:T(8,128)} %collect.5.refs_3_), custom_call_target="tpu_custom_call", output_to_operand_aliasing={{}: (3, {})} | custom-call | flops 1325400064 | tf_op jit(solution)/shard_map/collect/pallas_call | solution.py:229
  103.8 11.6 %collect.7 = f32[56,12288]{1,0:T(8,128)} custom-call(f32[56,4096]{1,0:T(8,128)} %copy-done.4, f32[32,128]{1,0:T(8,128)} %bitcast.44, s32[1,128]{1,0:T(1,128)} %get-tuple-element.35.refs_2_, f32[56,12288]{1,0:T(8,128)} %collect.6.refs_3_), custom_call_target="tpu_custom_call", output_to_operand_aliasing={{}: (3, {})} | custom-call | flops 1325400064 | tf_op jit(solution)/shard_map/collect/pallas_call | solution.py:229
  115.5 1.4 slice.165
  116.8 3.5 %collective-permute-start.7 = (f32[56,4096]{1,0:T(8,128)S(1)}, f32[56,4096]{1,0:T(8,128)S(1)}, u32[]{:S(2)}, u32[]{:S(2)}) collective-permute-start(f32[56,4096]{1,0:T(8,128)S(1)} %slice.165), channel_id=1, source_target_pairs={{4,12},{8,0},{12,20},{16,8},{20,28},{24,16},{5,13},{9,1},{13,21},{... | collective-permute-start | bytes 2752520 | tf_op jit(solution)/shard_map/ppermute | solution.py:35
  120.7 19.9 %collective-permute-done.7 = f32[56,4096]{1,0:T(8,128)S(1)} collective-permute-done((f32[56,4096]{1,0:T(8,128)S(1)}, f32[56,4096]{1,0:T(8,128)S(1)}, u32[]{:S(2)}, u32[]{:S(2)}) %collective-permute-start.7) | collective-permute-done | bytes 917536 | tf_op jit(solution)/shard_map/ppermute | solution.py:35
  140.6 1.1 slice_add_fusion
  141.7 1.5 collective-permute-start.8
  143.7 1.0 pad.16.moved_ref
  144.7 19.0 %collective-permute-done.8.got_ref = f32[56,4096]{1,0:T(8,128)S(1)} collective-permute-done((f32[56,4096]{1,0:T(8,128)S(1)}, f32[56,4096]{1,0:T(8,128)S(1)}, u32[]{:S(2)}, u32[]{:S(2)}) %collective-permute-start.8) | collective-permute-done | bytes 917536 | tf_op jit(solution)/shard_map/ppermute | solution.py:29
  164.6 3.3 %blend.1 = (f32[56,4096]{1,0:T(8,128)}, f32[56,256]{1,0:T(8,128)}) custom-call(f32[56,4096]{1,0:T(8,128)} %get-tuple-element.29.own_ref, f32[56,4096]{1,0:T(8,128)} %copy-done.5, f32[56,4096]{1,0:T(8,128)} %pad.16.moved_ref), custom_call_target="tpu_custom_call" | custom-call | tf_op jit(solution)/shard_map/blend/pallas_call | solution.py:419
  168.7 1.3 collective-permute-start.11
  170.0 1.5 collective-permute-start.12
  175.3 8.3 %chem.1.refs_1_ = f32[56,4096]{1,0:T(8,128)} custom-call(f32[56,4096]{1,0:T(8,128)} %get-tuple-element.20.state_ref, f32[56,256]{1,0:T(8,128)} %pad_maximum_fusion.6.edge_ref, f32[1,4096]{1,0:T(1,128)} %reshape.184.diss_ref, f32[1,4096]{1,0:T(1,128)} %reshape.185.rate_ref, s32[1,4096]{1,0:T(1,128)} %broadcast_in_dim_reshape.3.count_ref, ...), custom_call_target="tpu_custom_call" | custom-call | tf_op jit(solution)/shard_map/chem/pallas_call | solution.py:431
  183.6 1.7 collective-permute-start.13
  185.3 21.0 %collective-permute-done.13.refs_2_ = f32[56,4096]{1,0:T(8,128)S(1)} collective-permute-done((f32[56,4096]{1,0:T(8,128)}, f32[56,4096]{1,0:T(8,128)S(1)}, u32[]{:S(2)}, u32[]{:S(2)}) %collective-permute-start.13) | collective-permute-done | bytes 917536 | tf_op jit(solution)/shard_map/ppermute | solution.py:29
  206.3 1.3 collective-permute-start.14
  212.6 19.1 %collective-permute-done.14.refs_0_ = f32[56,4096]{1,0:T(8,128)S(1)} collective-permute-done((f32[56,4096]{1,0:T(8,128)S(1)}, f32[56,4096]{1,0:T(8,128)S(1)}, u32[]{:S(2)}, u32[]{:S(2)}) %collective-permute-start.14) | collective-permute-done | bytes 917536 | tf_op jit(solution)/shard_map/ppermute | solution.py:35
  232.6 23.1 %project.1 = f32[4,56,4096]{2,1,0:T(8,128)} custom-call(f32[56,4096]{1,0:T(8,128)} %copy-done.19, f32[56,4096]{1,0:T(8,128)} %chem.1.refs_1_, f32[56,4096]{1,0:T(8,128)} %copy-done.18, f32[4,4096]{1,0:T(4,128)} %pad_maximum_fusion.5.refs_3_, f32[32,128]{1,0:T(8,128)} %bitcast.45, s32[4,128]{1,0:T(4,128)} %maximum_convert_fusion.refs_5_), custom_call_target="tpu_custom_call" | custom-call | flops 5301600256 | tf_op jit(solution)/shard_map/project/pallas_call | solution.py:289
  255.7 2.6 slice_bitcast_fusion.2
  258.8 2.0 collective-permute-done.16
  260.7 2.3 fusion
  263.7 2.5 copy.49
  266.2 19.6 %collective-permute-done.17 = f32[56,4096]{1,0:T(8,128)} collective-permute-done((f32[56,4096]{1,0:T(8,128)}, f32[56,4096]{1,0:T(8,128)}, u32[]{:S(2)}, u32[]{:S(2)}) %collective-permute-start.17) | collective-permute-done | bytes 917536 | tf_op jit(solution)/shard_map/ppermute | solution.py:29
  285.7 2.8 fusion.2.x_ref
  288.5 10.9 %unsort.1 = f32[56,4096]{1,0:T(8,128)} custom-call(f32[56,4096]{1,0:T(8,128)} %fusion.2.x_ref, f32[1,4096]{1,0:T(1,128)} %get-tuple-element.18.rank_ref), custom_call_target="tpu_custom_call" | custom-call | flops 3758096384 | bytes 1835008 | tf_op jit(solution)/shard_map/unsort/pallas_call | solution.py:135
  299.5 1.0 slice.179
  300.5 1.3 slice_divide_fusion
  302.4 2.6 multiply_add_fusion
  (87 shorter events, 19.8 us)
Async XLA Ops:
  0.6 65.0 %copy-start = (f32[128,128]{1,0:T(8,128)S(1)}, f32[128,128]{1,0:T(8,128)}, u32[]{:S(2)}) copy-start(f32[128,128]{1,0:T(8,128)} %param.16) | copy-start | bytes 196612
  2.6 16.4 %collective-permute-start.2 = (f32[54,8,1,128]{3,1,2,0:T(8,128)S(1)}, f32[54,8,1,128]{3,1,2,0:T(8,128)S(1)}, u32[]{:S(2)}, u32[]{:S(2)}) collective-permute-start(f32[54,8,1,128]{3,1,2,0:T(8,128)S(1)} %bitcast.47), channel_id=1, source_target_pairs={{1,0},{2,1},{3,2},{5,4},{6,5},{7,6},{9,8},{10,9},{11,10},{13,12},{... | collective-permute-start | bytes 663560 | tf_op jit(solution)/shard_map/ppermute | solution.py:24
  3.9 15.1 %collective-permute-start.3 = (f32[54,8,1,128]{3,1,2,0:T(8,128)S(1)}, f32[54,8,1,128]{3,1,2,0:T(8,128)S(1)}, u32[]{:S(2)}, u32[]{:S(2)}) collective-permute-start(f32[54,8,1,128]{3,1,2,0:T(8,128)S(1)} %bitcast.46), channel_id=1, source_target_pairs={{0,1},{1,2},{2,3},{4,5},{5,6},{6,7},{8,9},{9,10},{10,11},{12,13},{... | collective-permute-start | bytes 663560 | tf_op jit(solution)/shard_map/ppermute | solution.py:24
  7.9 11.0 %collective-permute-start = (f32[54,1,4,128]{3,2,1,0:T(4,128)S(1)}, f32[54,1,4,128]{3,2,1,0:T(4,128)S(1)}, u32[]{:S(2)}, u32[]{:S(2)}) collective-permute-start(f32[54,1,4,128]{3,2,1,0:T(4,128)S(1)} %get-tuple-element.40), channel_id=1, source_target_pairs={{4,0},{8,4},{12,8},{16,12},{20,16},{24,20},{28,24},{5,1},{9,5},{13... | collective-permute-start | bytes 331784 | tf_op jit(solution)/shard_map/ppermute | solution.py:24
  9.8 9.1 %collective-permute-start.1 = (f32[54,1,4,128]{3,2,1,0:T(4,128)S(1)}, f32[54,1,4,128]{3,2,1,0:T(4,128)S(1)}, u32[]{:S(2)}, u32[]{:S(2)}) collective-permute-start(f32[54,1,4,128]{3,2,1,0:T(4,128)S(1)} %get-tuple-element.41), channel_id=1, source_target_pairs={{0,4},{4,8},{8,12},{12,16},{16,20},{20,24},{24,28},{1,5},{5,9},{9,... | collective-permute-start | bytes 331784 | tf_op jit(solution)/shard_map/ppermute | solution.py:24
  16.8 8.4 %copy-start.11 = (f32[1,4096]{1,0:T(1,128)S(1)}, f32[1,4096]{1,0:T(1,128)}, u32[]{:S(2)}) copy-start(f32[1,4096]{1,0:T(1,128)} %fusion.16.key_ref) | copy-start | bytes 49156
  18.9 0.6 copy-start.7
  19.0 0.7 copy-start.9
  26.3 14.9 %copy-start.15 = (f32[1,128]{1,0:T(1,128)S(1)}, f32[1,128]{1,0:T(1,128)}, u32[]{:S(2)}) copy-start(f32[1,128]{1,0:T(1,128)} %get-tuple-element.19) | copy-start | bytes 1540
  26.3 17.7 %copy-start.6 = (f32[54,32,128]{2,1,0:T(8,128)S(1)}, f32[54,32,128]{2,1,0:T(8,128)}, u32[]{:S(2)}) copy-start(f32[54,32,128]{2,1,0:T(8,128)} %param.13) | copy-start | bytes 2654212
  42.5 23.1 %collective-permute-start.4 = (f32[56,4096]{1,0:T(8,128)}, f32[56,4096]{1,0:T(8,128)}, u32[]{:S(2)}, u32[]{:S(2)}) collective-permute-start(f32[56,4096]{1,0:T(8,128)} %scatter.4.refs_0_), channel_id=1, source_target_pairs={{0,2},{1,3},{2,0},{3,1},{4,6},{5,7},{6,4},{7,5},{8,10},{9,11},{10,... | collective-permute-start | bytes 2752520 | tf_op jit(solution)/shard_map/ppermute | solution.py:29
  44.0 33.1 %collective-permute-start.6 = (f32[56,4096]{1,0:T(8,128)}, f32[56,4096]{1,0:T(8,128)}, u32[]{:S(2)}, u32[]{:S(2)}) collective-permute-start(f32[56,4096]{1,0:T(8,128)} %scatter.4.refs_0_), channel_id=1, source_target_pairs={{0,1},{1,0},{2,3},{3,2},{4,5},{5,4},{6,7},{7,6},{8,9},{9,8},{10,11... | collective-permute-start | bytes 2752520 | tf_op jit(solution)/shard_map/ppermute | solution.py:29
  46.7 96.6 %collective-permute-start.10 = (f32[54,32]{1,0:T(8,128)S(1)}, f32[54,32]{1,0:T(8,128)S(1)}, u32[]{:S(2)}, u32[]{:S(2)}) collective-permute-start(f32[54,32]{1,0:T(8,128)S(1)} %get-tuple-element.37), channel_id=1, source_target_pairs={{4,0},{8,4},{12,8},{16,12},{20,16},{24,20},{28,24},{5,1},{9,5},{13... | collective-permute-start | bytes 20744 | tf_op jit(solution)/shard_map/ppermute | solution.py:24
  48.6 94.6 %collective-permute-start.9 = (f32[54,32]{1,0:T(8,128)S(1)}, f32[54,32]{1,0:T(8,128)S(1)}, u32[]{:S(2)}, u32[]{:S(2)}) collective-permute-start(f32[54,32]{1,0:T(8,128)S(1)} %get-tuple-element.36), channel_id=1, source_target_pairs={{0,4},{4,8},{8,12},{12,16},{16,20},{20,24},{24,28},{1,5},{5,9},{9,... | collective-permute-start | bytes 20744 | tf_op jit(solution)/shard_map/ppermute | solution.py:24
  65.6 37.2 %collective-permute-start.5 = (f32[56,4096]{1,0:T(8,128)}, f32[56,4096]{1,0:T(8,128)S(1)}, u32[]{:S(2)}, u32[]{:S(2)}) collective-permute-start(f32[56,4096]{1,0:T(8,128)} %collective-permute-done.4.refs_0_), channel_id=1, source_target_pairs={{0,1},{1,0},{2,3},{3,2},{4,5},{5,4},{6,7},{7,6},{8,9},{9,8},{10,11... | collective-permute-start | bytes 2752520 | tf_op jit(solution)/shard_map/ppermute | solution.py:29
  102.8 1.0 copy-start.4
  115.4 25.2 %copy-start.1 = (f32[56,12288]{1,0:T(8,128)S(1)}, f32[56,12288]{1,0:T(8,128)}, u32[]{:S(2)}) copy-start(f32[56,12288]{1,0:T(8,128)} %collect.7) | copy-start | bytes 8257540
  116.8 23.8 %collective-permute-start.7 = (f32[56,4096]{1,0:T(8,128)S(1)}, f32[56,4096]{1,0:T(8,128)S(1)}, u32[]{:S(2)}, u32[]{:S(2)}) collective-permute-start(f32[56,4096]{1,0:T(8,128)S(1)} %slice.165), channel_id=1, source_target_pairs={{4,12},{8,0},{12,20},{16,8},{20,28},{24,16},{5,13},{9,1},{13,21},{... | collective-permute-start | bytes 2752520 | tf_op jit(solution)/shard_map/ppermute | solution.py:35
  141.7 22.0 %collective-permute-start.8 = (f32[56,4096]{1,0:T(8,128)S(1)}, f32[56,4096]{1,0:T(8,128)S(1)}, u32[]{:S(2)}, u32[]{:S(2)}) collective-permute-start(f32[56,4096]{1,0:T(8,128)S(1)} %get-tuple-element.28), channel_id=1, source_target_pairs={{0,4},{4,0},{8,12},{12,8},{16,20},{20,16},{24,28},{28,24},{1,5},{5... | collective-permute-start | bytes 2752520 | tf_op jit(solution)/shard_map/ppermute | solution.py:29
  143.6 27.8 %copy-start.12 = (f32[54,54]{1,0:T(8,128)S(1)}, f32[54,54]{1,0:T(8,128)}, u32[]{:S(2)}) copy-start(f32[54,54]{1,0:T(8,128)} %param.18) | copy-start | bytes 34996
  143.7 28.6 %copy-start.17 = (s32[128]{0:T(128)S(1)}, s32[128]{0:T(128)}, u32[]{:S(2)}) copy-start(s32[128]{0:T(128)} %param.21) | copy-start | bytes 1540
  143.7 29.4 %copy-start.13 = (f32[32,128]{1,0:T(8,128)S(1)}, f32[32,128]{1,0:T(8,128)}, u32[]{:S(2)}) copy-start(f32[32,128]{1,0:T(8,128)} %param.19) | copy-start | bytes 49156
  143.7 30.2 %copy-start.14 = (f32[32,128]{1,0:T(8,128)S(1)}, f32[32,128]{1,0:T(8,128)}, u32[]{:S(2)}) copy-start(f32[32,128]{1,0:T(8,128)} %param.20) | copy-start | bytes 49156
  163.7 0.9 copy-start.5
  168.7 5.9 %collective-permute-start.11 = (f32[56,128]{1,0:T(8,128)S(1)}, f32[56,128]{1,0:T(8,128)S(1)}, u32[]{:S(2)}, u32[]{:S(2)}) collective-permute-start(f32[56,128]{1,0:T(8,128)S(1)} %get-tuple-element.44), channel_id=1, source_target_pairs={{0,1},{1,2},{2,3},{4,5},{5,6},{6,7},{8,9},{9,10},{10,11},{12,13},{... | collective-permute-start | bytes 86024 | tf_op jit(solution)/shard_map/ppermute | solution.py:24
  170.0 4.7 %collective-permute-start.12 = (f32[56,128]{1,0:T(8,128)S(1)}, f32[56,128]{1,0:T(8,128)S(1)}, u32[]{:S(2)}, u32[]{:S(2)}) collective-permute-start(f32[56,128]{1,0:T(8,128)S(1)} %get-tuple-element.45), channel_id=1, source_target_pairs={{1,0},{2,1},{3,2},{5,4},{6,5},{7,6},{9,8},{10,9},{11,10},{13,12},{... | collective-permute-start | bytes 86024 | tf_op jit(solution)/shard_map/ppermute | solution.py:24
  183.6 22.7 %collective-permute-start.13 = (f32[56,4096]{1,0:T(8,128)}, f32[56,4096]{1,0:T(8,128)S(1)}, u32[]{:S(2)}, u32[]{:S(2)}) collective-permute-start(f32[56,4096]{1,0:T(8,128)} %chem.1.refs_1_), channel_id=1, source_target_pairs={{0,4},{4,0},{8,12},{12,8},{16,20},{20,16},{24,28},{28,24},{1,5},{5... | collective-permute-start | bytes 2752520 | tf_op jit(solution)/shard_map/ppermute | solution.py:29
  206.3 25.4 %copy-start.18 = (f32[56,4096]{1,0:T(8,128)}, f32[56,4096]{1,0:T(8,128)S(1)}, u32[]{:S(2)}) copy-start(f32[56,4096]{1,0:T(8,128)S(1)} %collective-permute-done.13.refs_2_) | copy-start | bytes 2752516
  206.3 25.4 %collective-permute-start.14 = (f32[56,4096]{1,0:T(8,128)S(1)}, f32[56,4096]{1,0:T(8,128)S(1)}, u32[]{:S(2)}, u32[]{:S(2)}) collective-permute-start(f32[56,4096]{1,0:T(8,128)S(1)} %collective-permute-done.13.refs_2_), channel_id=1, source_target_pairs={{0,8},{8,16},{12,4},{16,24},{20,12},{28,20},{1,9},{9,17},{13,5},{1... | collective-permute-start | bytes 2752520 | tf_op jit(solution)/shard_map/ppermute | solution.py:35
  231.7 0.9 copy-start.19
  255.7 7.4 %copy-start.3 = (f32[56,4096]{1,0:T(8,128)S(1)}, f32[56,4096]{1,0:T(8,128)}, u32[]{:S(2)}) copy-start(f32[56,4096]{1,0:T(8,128)} %chem.1.refs_1_) | copy-start | bytes 2752516
  258.3 2.5 collective-permute-start.16
  258.3 7.9 %collective-permute-start.15 = (f32[56,4096]{1,0:T(8,128)}, f32[56,4096]{1,0:T(8,128)}, u32[]{:S(2)}, u32[]{:S(2)}) collective-permute-start(f32[56,4096]{1,0:T(8,128)} %get-tuple-element.26), channel_id=1, source_target_pairs={{0,1},{1,0},{2,3},{3,2},{4,5},{5,4},{6,7},{7,6},{8,9},{9,8},{10,11... | collective-permute-start | bytes 2752520 | tf_op jit(solution)/shard_map/ppermute | solution.py:29
  263.0 22.7 %collective-permute-start.17 = (f32[56,4096]{1,0:T(8,128)}, f32[56,4096]{1,0:T(8,128)}, u32[]{:S(2)}, u32[]{:S(2)}) collective-permute-start(f32[56,4096]{1,0:T(8,128)} %fusion), channel_id=1, source_target_pairs={{0,2},{1,3},{2,0},{3,1},{4,6},{5,7},{6,4},{7,5},{8,10},{9,11},{10,... | collective-permute-start | bytes 2752520 | tf_op jit(solution)/shard_map/ppermute | solution.py:29
  299.4 2.9 copy-start.2
  299.4 2.9 copy-start.8
  299.4 2.9 copy-start.10
  299.5 2.9 copy-start.16

commit v2 on v1

--- a/solution.py
+++ b/solution.py
@@ -17,6 +17,7 @@
 HALF = 64
 GROUP = 8
 LIMIT = 56 << 20
+LAG = (2, 4, 6)
 
 
 def shift(array, axis, by):
@@ -27,12 +28,6 @@
 def swap(array, axis, bit):
     count = lax.axis_size(axis)
     return lax.ppermute(array, axis, [(i, i ^ bit) for i in range(count)])
-
-
-def hop(array, axis, outward):
-    count = lax.axis_size(axis)
-    step = lambda i: 2 if (i % 2 == 1) == outward else -2
-    return lax.ppermute(array, axis, [(i, i + step(i)) for i in range(count) if 0 <= i + step(i) < count])
 
 
 def halves(x):
@@ -302,58 +297,182 @@
     )(*means, keys, table, steps)
 
 
-def edge_rows(bins, chunk, cells, start):
-    lane = lax.broadcasted_iota(jnp.int32, (cells, chunk), 1) + start
-    cell = lax.broadcasted_iota(jnp.int32, (cells, chunk), 0)
-    pick = lambda b: jnp.where(lane == cell * bins + b, 1.0, 0.0)
-    return jnp.concatenate([pick(0), pick(bins - 1)], axis=0).astype(BF16)
-
-
-def blend_kernel(species, bins, own_ref, got_ref, moved_ref, out_ref, edge_ref):
-    rows, width = own_ref.shape
-    cells = width // bins
-    edge = jnp.zeros((2 * rows, 2 * cells), F32)
-    for n in range(width // TILE):
-        piece = slice(n * TILE, (n + 1) * TILE)
-        total = own_ref[:, piece] + got_ref[:, piece]
-        blended = (total + moved_ref[:, piece]) / (total[species : species + 1] + 1.0)
-        out_ref[:, piece] = blended
-        high = blended.astype(BF16).astype(F32)
-        parts = jnp.concatenate([high, blended - high], axis=0).astype(BF16)
-        edge = edge + lax.dot_general(parts, edge_rows(bins, TILE, cells, n * TILE), NT, preferred_element_type=F32)
-    edge_ref[...] = edge[:rows] + edge[rows:]
-
-
-def chem_kernel(species, bins, state_ref, edge_ref, diss_ref, rate_ref, count_ref, matrix_ref, out_ref):
-    rows, width = state_ref.shape
-    cells = width // bins
+def middle_kernel(species, bins, chunk, refs_in, refs_out, scratch):
+    acc_ref, moved_ref, diss_ref, rate_ref, count_ref, matrix_ref = refs_in
+    fresh_ref, next_ref, far_ref = refs_out
+    hopped, summed, got, state_ref, edge_out, edge_in, pick_ref, third_ref, send, recv = scratch
+    rows, width = fresh_ref.shape
+    steps = width // chunk
+    per_chunk = chunk // bins
+    slab, nslab = lax.axis_index("slab"), lax.axis_size("slab")
+    cross, ncross = lax.axis_index("cross"), lax.axis_size("cross")
+    parity = lax.rem(slab, 2)
+    outer = slab + 4 * parity - 2
+    inner = slab - 4 * parity + 2
+    partner = slab + 1 - 2 * parity
+    has_outer = (outer >= 0) & (outer < nslab)
+    has_inner = (inner >= 0) & (inner < nslab)
+    has_before, has_after = cross > 0, cross < ncross - 1
+    mesh = pl.DeviceIdType.MESH
+
+    @pl.when(jnp.logical_not(has_inner))
+    def _():
+        hopped[...] = jnp.zeros_like(hopped)
+
+    @pl.when(jnp.logical_not(has_outer))
+    def _():
+        far_ref[...] = jnp.zeros_like(far_ref)
+
+    @pl.when(jnp.logical_not(has_before))
+    def _():
+        edge_in[:, :, :LANES] = jnp.zeros(edge_in.shape[:2] + (LANES,), F32)
+
+    @pl.when(jnp.logical_not(has_after))
+    def _():
+        edge_in[:, :, LANES:] = jnp.zeros(edge_in.shape[:2] + (LANES,), F32)
+
+    barrier = pltpu.get_barrier_semaphore()
+    greet = lambda where: pl.semaphore_signal(barrier, inc=1, device_id=where, device_id_type=mesh)
+    greet({"slab": partner})
+    pl.when(has_outer)(lambda: greet({"slab": outer}))
+    pl.when(has_inner)(lambda: greet({"slab": inner}))
+    pl.when(has_before)(lambda: greet({"cross": cross - 1}))
+    pl.when(has_after)(lambda: greet({"cross": cross + 1}))
+    number = lambda flag: jnp.where(flag, 1, 0)
+    pl.semaphore_wait(barrier, 1 + number(has_outer) + number(has_inner) + number(has_before) + number(has_after))
+
+    def lanes(c, base=0):
+        return pl.ds(pl.multiple_of(base + c * chunk, chunk), chunk)
+
+    def remote(kind, c, source, target, where):
+        return pltpu.make_async_remote_copy(
+            src_ref=source, dst_ref=target, send_sem=send.at[kind, c], recv_sem=recv.at[kind, c],
+            device_id=where, device_id_type=mesh,
+        )
+
+    to_outer = lambda c: remote(0, c, acc_ref.at[:, lanes(c)], hopped.at[:, lanes(c)], {"slab": outer})
+    to_partner = lambda c: remote(1, c, summed.at[:, lanes(c)], got.at[:, lanes(c)], {"slab": partner})
+    to_after = lambda c: remote(2, c, edge_out.at[c, :, LANES:], edge_in.at[c, :, :LANES], {"cross": cross + 1})
+    to_before = lambda c: remote(3, c, edge_out.at[c, :, :LANES], edge_in.at[c, :, LANES:], {"cross": cross - 1})
+    give = lambda c: remote(4, c, fresh_ref.at[:, lanes(c)], next_ref.at[:, lanes(c)], {"slab": partner})
+    pass_on = lambda c: remote(5, c, next_ref.at[:, lanes(c)], far_ref.at[:, lanes(c)], {"slab": inner})
+
+    @pl.when(has_outer)
+    def _():
+        for c in range(steps):
+            to_outer(c).start()
+
+    lane = lax.broadcasted_iota(jnp.int32, (2 * LANES, chunk), 1)
+    row = lax.broadcasted_iota(jnp.int32, (2 * LANES, chunk), 0)
+    target = jnp.where(row < LANES, row * bins, (row - LANES) * bins + bins - 1)
+    pick_ref[...] = rows_equal(target, lane)
     third = matrix_ref.shape[1] // 3
     high, low = halves(matrix_ref[...])
     column = lax.broadcasted_iota(jnp.int32, matrix_ref.shape, 1)
-    matrix = jnp.where(column < 2 * third, high.astype(F32), low.astype(F32)).astype(BF16)
-    chunk = 2 * TILE
+    third_ref[...] = jnp.where(column < 2 * third, high.astype(F32), low.astype(F32)).astype(BF16)
     line = lax.broadcasted_iota(jnp.int32, (rows, chunk), 0)
     slot = lax.broadcasted_iota(jnp.int32, (rows, chunk), 1) % bins
     gap = [jnp.zeros((third - rows, chunk), F32)] * (third > rows)
-    edge = edge_ref[...]
-    high = edge.astype(BF16).astype(F32)
-    edges = jnp.concatenate([high, edge - high], axis=0).astype(BF16)
-    for n in range(width // chunk):
-        piece = slice(n * chunk, (n + 1) * chunk)
-        here = state_ref[:, piece]
-        outer = lax.dot_general(edges, edge_rows(bins, chunk, cells, n * chunk), NN, preferred_element_type=F32)
-        outer = outer[:rows] + outer[rows:]
-        before = jnp.where(slot == 0, outer, pltpu.roll(here, 1, 1))
-        after = jnp.where(slot == bins - 1, outer, pltpu.roll(here, chunk - 1, 1))
-        state = here + diss_ref[:, piece] * (after - 2.0 * here + before)
-        half = 0.5 * rate_ref[:, piece]
-        count = count_ref[:, piece]
+
+    def stacked(x):
+        high = x.astype(BF16).astype(F32)
+        return jnp.concatenate([high, x - high], axis=0).astype(BF16)
+
+    def add_hop(c):
+        pl.when(has_inner)(lambda: to_outer(c).wait_recv())
+        summed[:, lanes(c)] = acc_ref[:, lanes(c, 2 * width)] + hopped[:, lanes(c)]
+
+    def blend(c):
+        total = acc_ref[:, lanes(c, width)] + got[:, lanes(c)]
+        blended = (total + moved_ref[:, lanes(c)]) / (total[species : species + 1] + 1.0)
+        state_ref[:, lanes(c)] = blended
+        edge = lax.dot_general(stacked(blended), pick_ref[...], NT, preferred_element_type=F32)
+        edge_out[c] = edge[:rows] + edge[rows:]
+
+    def send_edges(c):
+        pl.when(has_after)(lambda: to_after(c).start())
+        pl.when(has_before)(lambda: to_before(c).start())
+
+    def wait_edges(c):
+        pl.when(has_before)(lambda: to_after(c).wait_recv())
+        pl.when(has_after)(lambda: to_before(c).wait_recv())
+
+    def react(c):
+        here = state_ref[:, lanes(c)]
+        around = lax.dot_general(stacked(edge_in[c]), pick_ref[...], NN, preferred_element_type=F32)
+        around = around[:rows] + around[rows:]
+        before = jnp.where(slot == 0, around, pltpu.roll(here, 1, 1))
+        after = jnp.where(slot == bins - 1, around, pltpu.roll(here, chunk - 1, 1))
+        state = here + diss_ref[:, lanes(c)] * (after - 2.0 * here + before)
+        half = 0.5 * rate_ref[:, lanes(c)]
+        count = count_ref[:, lanes(c)]
         for k in range(KMAX):
             high, low = (part.astype(F32) for part in halves(state))
             stack = jnp.concatenate([high, *gap, low, *gap, high, *gap], axis=0).astype(BF16)
-            rate = lax.dot_general(matrix, stack, NN, preferred_element_type=F32)
+            rate = lax.dot_general(third_ref[...], stack, NN, preferred_element_type=F32)
             state = jnp.where(k < count, state + half * jnp.tanh(rate), state)
-        out_ref[:, piece] = jnp.where(line == species, 1.0, state)
+        fresh_ref[:, lanes(c)] = jnp.where(line == species, 1.0, state)
+
+    def step(t, _):
+        def when(lag, body):
+            c = t - lag
+            pl.when((c >= 0) & (c < steps))(lambda: body(c))
+
+        def second(c):
+            to_partner(c).wait_recv()
+            blend(c)
+
+        def third_stage(c):
+            wait_edges(c)
+            react(c)
+
+        def fourth(c):
+            give(c).wait_recv()
+            pl.when(has_inner)(lambda: pass_on(c).start())
+
+        when(0, add_hop)
+        when(LAG[0], second)
+        when(0, lambda c: to_partner(c).start())
+        when(LAG[1], third_stage)
+        when(LAG[0], send_edges)
+        when(LAG[2], fourth)
+        when(LAG[1], lambda c: give(c).start())
+        return 0
+
+    lax.fori_loop(0, steps + LAG[2], step, 0)
+
+    def finish(c, _):
+        pl.when(has_outer)(lambda: to_outer(c).wait_send())
+        to_partner(c).wait_send()
+        pl.when(has_after)(lambda: to_after(c).wait_send())
+        pl.when(has_before)(lambda: to_before(c).wait_send())
+        give(c).wait_send()
+        pl.when(has_inner)(lambda: pass_on(c).wait_send())
+        pl.when(has_outer)(lambda: pass_on(c).wait_recv())
+        return 0
+
+    lax.fori_loop(0, steps, finish, 0)
+
+
+def middle_call(acc, moved, diss, rate, count, matrix, species, bins, chunk=512):
+    rows, width = moved.shape
+    steps = width // chunk
+
+    def kernel(*refs):
+        middle_kernel(species, bins, chunk, refs[:6], refs[6:9], refs[9:])
+
+    return pl.pallas_call(
+        kernel,
+        out_shape=[jax.ShapeDtypeStruct((rows, width), F32)] * 3,
+        in_specs=[VMEM] * 6,
+        out_specs=[VMEM] * 3,
+        scratch_shapes=[pltpu.VMEM((rows, width), F32)] * 4
+        + [pltpu.VMEM((steps, rows, 2 * LANES), F32)] * 2
+        + [pltpu.VMEM((2 * LANES, chunk), BF16), pltpu.VMEM(matrix.shape, BF16)]
+        + [pltpu.SemaphoreType.DMA((6, steps))] * 2,
+        compiler_params=pltpu.CompilerParams(vmem_limit_bytes=LIMIT, collective_id=1, has_side_effects=True),
+        name="middle",
+    )(acc, moved, diss, rate, count, matrix)
 
 
 def on_device(
@@ -398,7 +517,7 @@
     if bits:
         far_off = swap(mine, "cross", bits[-1])
         sources += [swap(mine, "cross", bit) for bit in bits[:-1]] + [far_off]
-        sources += [swap(far_off, "cross", bit) for bit in bits[:-1]]
+        sources += [None] * (len(bits) - 1)
     steps_of = lambda group: jnp.stack([s[rows - 1, :LANES] for s in group]).astype(jnp.int32)
 
     spread = lambda a: a.transpose(0, 2, 1).reshape(a.shape[0], width)
@@ -410,38 +529,18 @@
     moved = jnp.pad(moved, ((0, rows - species), (0, 0)))
 
     acc = None
-    for source in sources:
-        acc = collect_call([source], table, steps_of([source]), acc, species, bins, per_tile, ntiles)
-    far, own, near = (acc[:, n * width : (n + 1) * width] for n in range(3))
-    near = near + hop(far, "slab", True)
-    got = swap(near, "slab", 1)
-
-    blended, edge = pl.pallas_call(
-        functools.partial(blend_kernel, species, bins),
-        out_shape=[jax.ShapeDtypeStruct((rows, width), F32), jax.ShapeDtypeStruct((rows, 2 * cells), F32)],
-        in_specs=[VMEM] * 3,
-        out_specs=[VMEM] * 2,
-        compiler_params=params(),
-        name="blend",
-    )(own, got, moved)
-    edge = jnp.concatenate(
-        [shift(edge[:, cells:], "cross", 1), shift(edge[:, :cells], "cross", -1)], axis=1
-    )
+    for number, source in enumerate(sources):
+        if number and number == len(sources) // 2:
+            acc, far_off, moved = lax.optimization_barrier((acc, far_off, moved))
+            sources[number] = source = far_off
+            sources[number + 1 :] = [swap(far_off, "cross", bit) for bit in bits[:-1]]
+        acc = collect_call([sources[number]], table, steps_of([sources[number]]), acc, species, bins, per_tile, ntiles)
     extra = rows - species
-    fresh = pl.pallas_call(
-        functools.partial(chem_kernel, species, bins),
-        out_shape=jax.ShapeDtypeStruct((rows, width), F32),
-        in_specs=[VMEM] * 6,
-        out_specs=VMEM,
-        compiler_params=params(),
-        name="chem",
-    )(
-        blended, edge, wide(dissipation), wide(reaction_rate), jnp.repeat(substeps, bins)[None, :],
-        jnp.tile(jnp.pad(chem_matrix, ((0, extra), (0, -(-rows // 16) * 16 - species))), (1, 3)),
+    matrix = jnp.tile(jnp.pad(chem_matrix, ((0, extra), (0, -(-rows // 16) * 16 - species))), (1, 3))
+    fresh, next_mean, far_mean = middle_call(
+        acc, moved, wide(dissipation), wide(reaction_rate), jnp.repeat(substeps, bins)[None, :], matrix, species, bins
     )
     cmc_out = fresh[:species].reshape(species, cells, bins).transpose(0, 2, 1)
-    next_mean = swap(fresh, "slab", 1)
-    far_mean = hop(next_mean, "slab", False)
 
     keys = jnp.concatenate([s[species : species + 1] for s in sources], axis=0)
     part = project_call(

time: 307 us -> 249 us (0.81)
  waiting for transfers between devices: 112 us -> 20.3 us
  Pallas kernels: 108 us -> 154 us
  starting transfers between devices: 30.7 us -> 20.9 us
    ppermute x8 -> x6, waiting for transfers between devices: 73.2 us -> 20.2 us  [swap(): return lax.ppermute(array, axis, [(i, i ^ bit) for i in range(count)])]
    pallas_call x2 -> x1, Pallas kernels: 11.6 us -> 57.6 us  [middle_call(): pl.pallas_call(kernel, out_shape=[jax.ShapeDtypeStruct((rows, width), F32...]
    ppermute x2 -> x0, waiting for transfers between devices: 39 us -> none  [hop(): lax.ppermute(array, axis, [(i, i + step(i)) for i in range(count) if 0 <=...]
    ppermute x8 -> x6, starting transfers between devices: 20.6 us -> 15.3 us  [shift(): lax.ppermute(array, axis, [(i, i + by) for i in range(count) if 0 <= i +...]
    ppermute x2 -> x0, starting transfers between devices: 4.83 us -> none  [hop(): lax.ppermute(array, axis, [(i, i + step(i)) for i in range(count) if 0 <=...]
    unnamed x42 -> x30, local copies, waits for them, and re-layouts: 6.16 us -> 3.64 us
  transfers between devices with their start and end apart: 18 -> 12, of which waited for: 7 -> 2; matrix products, arithmetic and copies ran while one was open for 9% -> 15% of each run, Pallas kernels for 16% -> 21%
where the time goes in v2:
time: 249 us; the launch traced here: 248 us
  Pallas kernels  154 us (62%)
  local copies, waits for them, and re-layouts  29.8 us (12%)
  other arithmetic  22.3 us (9%)
  starting transfers between devices  20.9 us (8%)
  waiting for transfers between devices  20.3 us (8%)
    pallas_call x1, Pallas kernels, middle_call(): pl.pallas_call(kernel, out_shape=[jax.ShapeDtypeStruct((rows, width), F32...  57.6 us
    pallas_call x4, Pallas kernels, collect_call(): pl.pallas_call(functools.partial(collect_kernel, species, bins, per_tile,...  45.7 us
    pallas_call x2, Pallas kernels, permute_call(): pl.pallas_call(functools.partial(permute_kernel, back), grid=(count // TI...  25.7 us
    pallas_call x1, Pallas kernels, project_call(): pl.pallas_call(functools.partial(project_kernel, bins, per_tile, pairs, l...  23.1 us
    ppermute x6, waiting for transfers between devices, swap(): return lax.ppermute(array, axis, [(i, i ^ bit) for i in range(count)])  20.2 us
    ppermute x6, starting transfers between devices, shift(): lax.ppermute(array, axis, [(i, i + by) for i in range(count) if 0 <= i +...  15.3 us
    ppermute x6, starting transfers between devices, swap(): return lax.ppermute(array, axis, [(i, i ^ bit) for i in range(count)])  5.65 us
  transfers between devices with their start and end apart: 12, of which 2 were waited for; matrix products, arithmetic and copies ran while one was open for 15% of the time, Pallas kernels for 21%

profile of v2, /device:TPU:2, one launch (start us, length us, event | category | flops | bytes accessed | tf_op | source)
XLA Modules:
  0.0 248.3 jit_solution(1119657456579605324)
XLA Ops:
  0.6 1.7 fusion.22
  2.3 1.9 collective-permute-start
  4.2 4.8 %collective-permute-start.1 = (f32[54,1,4,128]{3,2,1,0:T(4,128)}, f32[54,1,4,128]{3,2,1,0:T(4,128)}, u32[]{:S(2)}, u32[]{:S(2)}) collective-permute-start(f32[54,1,4,128]{3,2,1,0:T(4,128)} %get-tuple-element.47), channel_id=1, source_target_pairs={{0,4},{4,8},{8,12},{12,16},{16,20},{20,24},{24,28},{1,5},{5,9},{9,... | collective-permute-start | bytes 331784 | tf_op jit(solution)/shard_map/ppermute | solution.py:25
  9.1 2.7 %fusion.23 = (f32[54,8,1,128]{3,2,1,0:T(1,128)}, f32[54,8,1,128]{3,2,1,0:T(1,128)}) fusion(f32[54,8,4,128]{3,2,1,0:T(4,128)} %param.12), kind=kLoop, calls=%fused_computation.50 | loop fusion | bytes 884736 | tf_op jit(solution)/shard_map/slice | solution.py:495
  11.8 1.3 collective-permute-start.3
  13.1 1.3 collective-permute-start.2
  14.4 3.0 %copy.38 = f32[54,128,32]{0,2,1:T(8,128)S(1)} copy(f32[54,128,32]{1,2,0:T(8,128)} %bitcast.36) | data formatting | bytes 1769472 | tf_op jit(solution)/shard_map/transpose | solution.py:523
  18.2 2.7 %collective-permute-start.6 = (f32[54,32]{1,0:T(8,128)S(1)}, f32[54,32]{1,0:T(8,128)S(1)}, u32[]{:S(2)}, u32[]{:S(2)}) collective-permute-start(f32[54,32]{1,0:T(8,128)S(1)} %get-tuple-element.42), channel_id=1, source_target_pairs={{0,4},{4,8},{8,12},{12,16},{16,20},{20,24},{24,28},{1,5},{5,9},{9,... | collective-permute-start | bytes 20744 | tf_op jit(solution)/shard_map/ppermute | solution.py:25
  20.9 1.3 fusion.21
  22.2 0.7 fusion.16.key_ref
  22.9 2.1 rank.1
  25.0 1.2 convert_element_type.26.refs_2_
  26.3 0.7 copy.52
  27.0 3.3 %collective-permute-start.7 = (f32[54,32]{1,0:T(8,128)S(1)}, f32[54,32]{1,0:T(8,128)S(1)}, u32[]{:S(2)}, u32[]{:S(2)}) collective-permute-start(f32[54,32]{1,0:T(8,128)S(1)} %get-tuple-element.43), channel_id=1, source_target_pairs={{4,0},{8,4},{12,8},{16,12},{20,16},{24,20},{28,24},{5,1},{9,5},{13... | collective-permute-start | bytes 20744 | tf_op jit(solution)/shard_map/ppermute | solution.py:25
  30.4 3.2 %fusion.10 = f32[54,8,4,128]{3,2,1,0:T(4,128)} fusion(f32[54,8,4,128]{3,2,1,0:T(4,128)S(1)} %copy-done.1, f32[54,8,1,128]{3,2,1,0:T(1,128)S(1)} %bitcast.37, f32[54,8,1,128]{3,2,1,0:T(1,128)S(1)} %bitcast.39, f32[54,1,4,128]{3,2,1,0:T(4,128)} %collective-permute-done.1, f32[54,1,4,128]{3,2,1,0:T(4,128)} %collective-permute-done, f32[54]{0:T(128)S(1)} %copy-done.11), kind=kLoop, calls=%fused_computation.20 | loop fusion | flops 2875392 | bytes 2433240 | tf_op jit(solution)/shard_map/add | solution.py:507
  33.6 2.5 reshape.181
  36.1 2.2 maximum_maximum_fusion.x_ref
  38.3 14.8 %sort.1 = f32[56,4096]{1,0:T(8,128)} custom-call(f32[56,4096]{1,0:T(8,128)} %maximum_maximum_fusion.x_ref, f32[1,4096]{1,0:T(1,128)} %get-tuple-element.22.rank_ref), custom_call_target="tpu_custom_call" | custom-call | flops 3758096384 | bytes 1835008 | tf_op jit(solution)/shard_map/sort/pallas_call | solution.py:130
  53.1 1.3 scatter.4.refs_0_
  54.4 4.5 %collective-permute-start.5 = (f32[56,4096]{1,0:T(8,128)}, f32[56,4096]{1,0:T(8,128)}, u32[]{:S(2)}, u32[]{:S(2)}) collective-permute-start(f32[56,4096]{1,0:T(8,128)} %scatter.4.refs_0_), channel_id=1, source_target_pairs={{0,2},{1,3},{2,0},{3,1},{4,6},{5,7},{6,4},{7,5},{8,10},{9,11},{10,... | collective-permute-start | bytes 2752520 | tf_op jit(solution)/shard_map/ppermute | solution.py:30
  58.9 1.5 fusion.5
  60.5 1.0 pad.16.refs_1_
  61.5 10.7 %collect.4.refs_3_ = f32[56,12288]{1,0:T(8,128)} custom-call(f32[56,4096]{1,0:T(8,128)} %scatter.4.refs_0_, f32[32,128]{1,0:T(8,128)} %bitcast.41, s32[1,128]{1,0:T(1,128)} %convert_element_type.26.refs_2_), custom_call_target="tpu_custom_call" | custom-call | flops 1325400064 | tf_op jit(solution)/shard_map/collect/pallas_call | solution.py:224
  73.2 11.7 %collect.5.refs_3_ = f32[56,12288]{1,0:T(8,128)} custom-call(f32[56,4096]{1,0:T(8,128)} %copy-done.2, f32[32,128]{1,0:T(8,128)} %bitcast.42, s32[1,128]{1,0:T(1,128)} %get-tuple-element.37.refs_2_, f32[56,12288]{1,0:T(8,128)} %collect.4.refs_3_), custom_call_target="tpu_custom_call", output_to_operand_aliasing={{}: (3, {})} | custom-call | flops 1325400064 | tf_op jit(solution)/shard_map/collect/pallas_call | solution.py:224
  85.5 0.7 reshape.184.refs_2_
  86.3 0.7 reshape.185.refs_3_
  87.1 0.7 broadcast_in_dim_reshape.3.refs_4_
  87.8 0.7 tile.10.refs_5_
  88.6 0.9 slice.146
  89.5 0.9 slice.131
  90.4 0.9 slice.147
  91.3 1.2 fusion.18
  92.5 11.7 %collect.6.refs_3_ = f32[56,12288]{1,0:T(8,128)} custom-call(f32[56,4096]{1,0:T(8,128)} %collective-permute-done.5.refs_0_, f32[32,128]{1,0:T(8,128)} %bitcast.43, s32[1,128]{1,0:T(1,128)} %get-tuple-element.39.refs_2_, f32[56,12288]{1,0:T(8,128)} %collect.5.refs_3_), custom_call_target="tpu_custom_call", output_to_operand_aliasing={{}: (3, {})} | custom-call | flops 1325400064 | tf_op jit(solution)/shard_map/collect/pallas_call | solution.py:224
  105.4 0.7 pad_maximum_fusion.5.refs_3_
  106.1 11.7 %collect.7.refs_0_ = f32[56,12288]{1,0:T(8,128)} custom-call(f32[56,4096]{1,0:T(8,128)} %copy-done.3, f32[32,128]{1,0:T(8,128)} %bitcast.44, s32[1,128]{1,0:T(1,128)} %get-tuple-element.41.refs_2_, f32[56,12288]{1,0:T(8,128)} %collect.6.refs_3_), custom_call_target="tpu_custom_call", output_to_operand_aliasing={{}: (3, {})} | custom-call | flops 1325400064 | tf_op jit(solution)/shard_map/collect/pallas_call | solution.py:224
  117.7 57.6 %middle.1 = (f32[56,4096]{1,0:T(8,128)}, f32[56,4096]{1,0:T(8,128)}, f32[56,4096]{1,0:T(8,128)}) custom-call(f32[56,12288]{1,0:T(8,128)} %collect.7.refs_0_, f32[56,4096]{1,0:T(8,128)} %pad.16.refs_1_, f32[1,4096]{1,0:T(1,128)} %reshape.184.refs_2_, f32[1,4096]{1,0:T(1,128)} %reshape.185.refs_3_, s32[1,4096]{1,0:T(1,128)} %broadcast_in_dim_reshape.3.refs_4_, ...), custom_call_target="tpu_custom_call" | custom-call | tf_op jit(solution)/shard_map/middle/pallas_call | solution.py:464
  175.3 23.1 %project.1 = f32[4,56,4096]{2,1,0:T(8,128)} custom-call(f32[56,4096]{1,0:T(8,128)} %get-tuple-element.27.refs_0_, f32[56,4096]{1,0:T(8,128)} %get-tuple-element.28.refs_1_, f32[56,4096]{1,0:T(8,128)} %get-tuple-element.29.refs_2_, f32[4,4096]{1,0:T(4,128)} %pad_maximum_fusion.5.refs_3_, f32[32,128]{1,0:T(8,128)} %bitcast.45, ...), custom_call_target="tpu_custom_call" | custom-call | flops 5301600256 | tf_op jit(solution)/shard_map/project/pallas_call | solution.py:284
  198.4 2.5 %slice_bitcast_fusion.2 = (f32[56,4096]{1,0:T(8,128)}, f32[56,4096]{1,0:T(8,128)S(1)}) fusion(f32[4,56,4096]{2,1,0:T(8,128)} %project.1), kind=kLoop, calls=%fused_computation.6 | loop fusion | bytes 3670016 | tf_op jit(solution)/shard_map/squeeze | solution.py:549
  201.4 2.0 collective-permute-done.10
  203.4 2.3 fusion
  205.8 1.8 copy.48
  207.7 2.5 copy.49
  210.2 18.3 %collective-permute-done.11 = f32[56,4096]{1,0:T(8,128)} collective-permute-done((f32[56,4096]{1,0:T(8,128)}, f32[56,4096]{1,0:T(8,128)}, u32[]{:S(2)}, u32[]{:S(2)}) %collective-permute-start.11) | collective-permute-done | bytes 917536 | tf_op jit(solution)/shard_map/ppermute | solution.py:30
  228.4 2.8 %fusion.2.x_ref = f32[56,4096]{1,0:T(8,128)} fusion(f32[56,4096]{1,0:T(8,128)} %collective-permute-done.11, f32[56,4096]{1,0:T(8,128)} %collective-permute-done.9, f32[4,56,4096]{2,1,0:T(8,128)} %project.1), kind=kLoop, calls=%fused_computation.9 | loop fusion | flops 458752 | bytes 3670016 | tf_op jit(solution)/shard_map/add | solution.py:561
  231.2 10.9 %unsort.1 = f32[56,4096]{1,0:T(8,128)} custom-call(f32[56,4096]{1,0:T(8,128)} %fusion.2.x_ref, f32[1,4096]{1,0:T(1,128)} %get-tuple-element.22.rank_ref), custom_call_target="tpu_custom_call" | custom-call | flops 3758096384 | bytes 1835008 | tf_op jit(solution)/shard_map/unsort/pallas_call | solution.py:130
  242.1 0.9 slice.154
  243.0 1.3 slice_divide_fusion
  244.9 3.4 %multiply_add_fusion = f32[54,8,4,128]{3,2,1,0:T(4,128)} fusion(f32[54,8,4,128]{3,2,1,0:T(4,128)S(1)} %reshape.186, f32[54,8,4,128]{3,2,1,0:T(4,128)S(1)} %copy-done.1, f32[54,8,1,128]{3,2,1,0:T(1,128)S(1)} %bitcast.38, f32[54,8,1,128]{3,2,1,0:T(1,128)S(1)} %bitcast.40, f32[54,1,4,128]{3,2,1,0:T(4,128)} %collective-permute-done.1, ...), kind=kLoop, calls=%fused_computation.28 | loop fusion | flops 3538944 | bytes 3317976 | tf_op jit(solution)/shard_map/add | solution.py:564
  (58 shorter events, 5.2 us)
Async XLA Ops:
  0.6 25.6 %copy-start = (f32[128,128]{1,0:T(8,128)S(1)}, f32[128,128]{1,0:T(8,128)}, u32[]{:S(2)}) copy-start(f32[128,128]{1,0:T(8,128)} %param.16) | copy-start | bytes 196612
  2.3 24.7 %collective-permute-start = (f32[54,1,4,128]{3,2,1,0:T(4,128)}, f32[54,1,4,128]{3,2,1,0:T(4,128)}, u32[]{:S(2)}, u32[]{:S(2)}) collective-permute-start(f32[54,1,4,128]{3,2,1,0:T(4,128)} %get-tuple-element.46), channel_id=1, source_target_pairs={{4,0},{8,4},{12,8},{16,12},{20,16},{24,20},{28,24},{5,1},{9,5},{13... | collective-permute-start | bytes 331784 | tf_op jit(solution)/shard_map/ppermute | solution.py:25
  4.2 26.1 %collective-permute-start.1 = (f32[54,1,4,128]{3,2,1,0:T(4,128)}, f32[54,1,4,128]{3,2,1,0:T(4,128)}, u32[]{:S(2)}, u32[]{:S(2)}) collective-permute-start(f32[54,1,4,128]{3,2,1,0:T(4,128)} %get-tuple-element.47), channel_id=1, source_target_pairs={{0,4},{4,8},{8,12},{12,16},{16,20},{20,24},{24,28},{1,5},{5,9},{9,... | collective-permute-start | bytes 331784 | tf_op jit(solution)/shard_map/ppermute | solution.py:25
  11.8 18.5 %collective-permute-start.3 = (f32[54,8,1,128]{3,1,2,0:T(8,128)}, f32[54,8,1,128]{3,1,2,0:T(8,128)S(1)}, u32[]{:S(2)}, u32[]{:S(2)}) collective-permute-start(f32[54,8,1,128]{3,1,2,0:T(8,128)} %bitcast.18), channel_id=1, source_target_pairs={{0,1},{1,2},{2,3},{4,5},{5,6},{6,7},{8,9},{9,10},{10,11},{12,13},{... | collective-permute-start | bytes 663560 | tf_op jit(solution)/shard_map/ppermute | solution.py:25
  13.1 17.2 %collective-permute-start.2 = (f32[54,8,1,128]{3,1,2,0:T(8,128)}, f32[54,8,1,128]{3,1,2,0:T(8,128)S(1)}, u32[]{:S(2)}, u32[]{:S(2)}) collective-permute-start(f32[54,8,1,128]{3,1,2,0:T(8,128)} %bitcast.17), channel_id=1, source_target_pairs={{1,0},{2,1},{3,2},{5,4},{6,5},{7,6},{9,8},{10,9},{11,10},{13,12},{... | collective-permute-start | bytes 663560 | tf_op jit(solution)/shard_map/ppermute | solution.py:25
  17.4 4.7 %copy-start.9 = (s32[8,4,128]{2,1,0:T(4,128)S(1)}, s32[8,4,128]{2,1,0:T(4,128)}, u32[]{:S(2)}) copy-start(s32[8,4,128]{2,1,0:T(4,128)} %param.14) | copy-start | bytes 49156
  17.5 4.7 %copy-start.6 = (s32[8,4,128]{2,1,0:T(4,128)S(1)}, s32[8,4,128]{2,1,0:T(4,128)}, u32[]{:S(2)}) copy-start(s32[8,4,128]{2,1,0:T(4,128)} %param.15) | copy-start | bytes 49156
  18.1 12.2 %copy-start.1 = (f32[54,8,4,128]{3,2,1,0:T(4,128)S(1)}, f32[54,8,4,128]{3,2,1,0:T(4,128)}, u32[]{:S(2)}) copy-start(f32[54,8,4,128]{3,2,1,0:T(4,128)} %param.12) | copy-start | bytes 2654212
  18.1 12.2 %copy-start.11 = (f32[54]{0:T(128)S(1)}, f32[54]{0:T(128)}, u32[]{:S(2)}) copy-start(f32[54]{0:T(128)} %param.17) | copy-start | bytes 652
  18.2 40.7 %collective-permute-start.6 = (f32[54,32]{1,0:T(8,128)S(1)}, f32[54,32]{1,0:T(8,128)S(1)}, u32[]{:S(2)}, u32[]{:S(2)}) collective-permute-start(f32[54,32]{1,0:T(8,128)S(1)} %get-tuple-element.42), channel_id=1, source_target_pairs={{0,4},{4,8},{8,12},{12,16},{16,20},{20,24},{24,28},{1,5},{5,9},{9,... | collective-permute-start | bytes 20744 | tf_op jit(solution)/shard_map/ppermute | solution.py:25
  22.9 13.2 %copy-start.4 = (f32[1,4096]{1,0:T(1,128)S(1)}, f32[1,4096]{1,0:T(1,128)}, u32[]{:S(2)}) copy-start(f32[1,4096]{1,0:T(1,128)} %fusion.16.key_ref) | copy-start | bytes 49156
  27.0 31.9 %collective-permute-start.7 = (f32[54,32]{1,0:T(8,128)S(1)}, f32[54,32]{1,0:T(8,128)S(1)}, u32[]{:S(2)}, u32[]{:S(2)}) collective-permute-start(f32[54,32]{1,0:T(8,128)S(1)} %get-tuple-element.43), channel_id=1, source_target_pairs={{4,0},{8,4},{12,8},{16,12},{20,16},{24,20},{28,24},{5,1},{9,5},{13... | collective-permute-start | bytes 20744 | tf_op jit(solution)/shard_map/ppermute | solution.py:25
  38.3 14.8 %copy-start.10 = (f32[1,128]{1,0:T(1,128)S(1)}, f32[1,128]{1,0:T(1,128)}, u32[]{:S(2)}) copy-start(f32[1,128]{1,0:T(1,128)} %get-tuple-element.23) | copy-start | bytes 1540
  54.4 30.5 %collective-permute-start.5 = (f32[56,4096]{1,0:T(8,128)}, f32[56,4096]{1,0:T(8,128)}, u32[]{:S(2)}, u32[]{:S(2)}) collective-permute-start(f32[56,4096]{1,0:T(8,128)} %scatter.4.refs_0_), channel_id=1, source_target_pairs={{0,2},{1,3},{2,0},{3,1},{4,6},{5,7},{6,4},{7,5},{8,10},{9,11},{10,... | collective-permute-start | bytes 2752520 | tf_op jit(solution)/shard_map/ppermute | solution.py:30
  58.9 13.3 %collective-permute-start.4 = (f32[56,4096]{1,0:T(8,128)}, f32[56,4096]{1,0:T(8,128)S(1)}, u32[]{:S(2)}, u32[]{:S(2)}) collective-permute-start(f32[56,4096]{1,0:T(8,128)} %scatter.4.refs_0_), channel_id=1, source_target_pairs={{0,1},{1,0},{2,3},{3,2},{4,5},{5,4},{6,7},{7,6},{8,9},{9,8},{10,11... | collective-permute-start | bytes 2752520 | tf_op jit(solution)/shard_map/ppermute | solution.py:30
  72.2 1.0 copy-start.2
  73.2 12.2 %copy-start.5 = (f32[54,54]{1,0:T(8,128)S(1)}, f32[54,54]{1,0:T(8,128)}, u32[]{:S(2)}) copy-start(f32[54,54]{1,0:T(8,128)} %param.18) | copy-start | bytes 34996
  73.2 12.2 %copy-start.7 = (f32[32,128]{1,0:T(8,128)S(1)}, f32[32,128]{1,0:T(8,128)}, u32[]{:S(2)}) copy-start(f32[32,128]{1,0:T(8,128)} %param.19) | copy-start | bytes 49156
  73.2 13.0 %copy-start.8 = (f32[32,128]{1,0:T(8,128)S(1)}, f32[32,128]{1,0:T(8,128)}, u32[]{:S(2)}) copy-start(f32[32,128]{1,0:T(8,128)} %param.20) | copy-start | bytes 49156
  73.2 13.8 %copy-start.13 = (s32[128]{0:T(128)S(1)}, s32[128]{0:T(128)}, u32[]{:S(2)}) copy-start(s32[128]{0:T(128)} %param.21) | copy-start | bytes 1540
  84.9 19.3 %collective-permute-start.8 = (f32[56,4096]{1,0:T(8,128)}, f32[56,4096]{1,0:T(8,128)S(1)}, u32[]{:S(2)}, u32[]{:S(2)}) collective-permute-start(f32[56,4096]{1,0:T(8,128)} %collective-permute-done.5.refs_0_), channel_id=1, source_target_pairs={{0,1},{1,0},{2,3},{3,2},{4,5},{5,4},{6,7},{7,6},{8,9},{9,8},{10,11... | collective-permute-start | bytes 2752520 | tf_op jit(solution)/shard_map/ppermute | solution.py:30
  104.2 1.9 copy-start.3
  200.9 2.5 collective-permute-start.10
  200.9 9.2 %collective-permute-start.9 = (f32[56,4096]{1,0:T(8,128)}, f32[56,4096]{1,0:T(8,128)}, u32[]{:S(2)}, u32[]{:S(2)}) collective-permute-start(f32[56,4096]{1,0:T(8,128)} %get-tuple-element.34), channel_id=1, source_target_pairs={{0,1},{1,0},{2,3},{3,2},{4,5},{5,4},{6,7},{7,6},{8,9},{9,8},{10,11... | collective-permute-start | bytes 2752520 | tf_op jit(solution)/shard_map/ppermute | solution.py:30
  205.7 22.7 %collective-permute-start.11 = (f32[56,4096]{1,0:T(8,128)}, f32[56,4096]{1,0:T(8,128)}, u32[]{:S(2)}, u32[]{:S(2)}) collective-permute-start(f32[56,4096]{1,0:T(8,128)} %fusion), channel_id=1, source_target_pairs={{0,2},{1,3},{2,0},{3,1},{4,6},{5,7},{6,4},{7,5},{8,10},{9,11},{10,... | collective-permute-start | bytes 2752520 | tf_op jit(solution)/shard_map/ppermute | solution.py:30
  242.1 2.8 %copy-start.12 = (f32[54]{0:T(128)S(1)}, f32[54]{0:T(128)}, u32[]{:S(2)}) copy-start(f32[54]{0:T(128)} %param.17) | copy-start | bytes 652

commit v3 on v2

--- a/solution.py
+++ b/solution.py
@@ -15,8 +15,7 @@
 LANES = 128
 TILE = 256
 HALF = 64
-GROUP = 8
-LIMIT = 56 << 20
+GROUP = 16
 LAG = (2, 4, 6)
 
 
@@ -53,8 +52,21 @@
 SMEM = pl.BlockSpec(memory_space=pltpu.SMEM)
 
 
-def params():
-    return pltpu.CompilerParams(vmem_limit_bytes=LIMIT)
+def params(mib):
+    return pltpu.CompilerParams(vmem_limit_bytes=mib << 20)
+
+
+def fetch_rows(sources, steps, sems, keys=None):
+    rows = sources[0].shape[0]
+    copies = []
+    for number, source in enumerate(sources):
+        last = source.at[rows - 8 : rows]
+        copies.append(pltpu.make_async_copy(last.at[:, :LANES], steps.at[number], sems.at[0, number]))
+        if keys is not None:
+            copies.append(pltpu.make_async_copy(last, keys.at[number], sems.at[1, number]))
+    for copy in copies:
+        copy.start()
+    return copies
 
 
 def rank_kernel(tiles, span, key_ref, rank_ref, table_ref):
@@ -94,19 +106,25 @@
         out_shape=[jax.ShapeDtypeStruct((1, count), F32), jax.ShapeDtypeStruct((1, LANES), F32)],
         in_specs=[VMEM],
         out_specs=[VMEM] * 2,
-        compiler_params=params(),
+        compiler_params=params(8),
         cost_estimate=pl.CostEstimate(flops=2 * tiles * TILE * count, bytes_accessed=8 * count, transcendentals=0),
         name="rank",
     )(key)
 
 
-def permute_kernel(back, x_ref, rank_ref, out_ref, parts):
-    rows, count = x_ref.shape
+def permute_kernel(back, count, rank_ref, *refs):
+    xs, (out_ref, parts) = refs[:count], refs[count:]
+    steps_ref = None
+    if not back:
+        xs, steps_ref = xs[:-1], xs[-1]
+    rows, count = xs[0].shape
     chunk = 2 * TILE
 
     @pl.when(pl.program_id(0) == 0)
     def _():
-        x = x_ref[...]
+        x = xs[0][...]
+        for more in xs[1:]:
+            x = x + more[...]
         high = x.astype(BF16).astype(F32)
         parts[...] = jnp.concatenate([high, x - high], axis=0).astype(BF16)
 
@@ -122,22 +140,29 @@
             ids = lax.broadcasted_iota(jnp.int32, (TILE, chunk), 0) + here
             hot = rows_equal(ids.astype(F32), rank_ref[:, piece])
             total = total + lax.dot_general(parts[:, piece], hot, NT, preferred_element_type=F32)
-    out_ref[...] = total[:rows] + total[rows:]
-
-
-def permute_call(x, rank, back):
-    rows, count = x.shape
+    total = total[:rows] + total[rows:]
+    if back:
+        out_ref[...] = total / total[rows - 2 : rows - 1]
+    else:
+        line = lax.broadcasted_iota(jnp.int32, (rows, TILE), 0)
+        steps = jnp.concatenate([steps_ref[...]] * (TILE // LANES), axis=1)
+        out_ref[...] = jnp.where(line == rows - 1, steps, total)
+
+
+def permute_call(xs, rank, steps, back):
+    rows, count = xs[0].shape
+    args = list(xs) + ([] if back else [steps])
     return pl.pallas_call(
-        functools.partial(permute_kernel, back),
+        functools.partial(permute_kernel, back, len(args)),
         grid=(count // TILE,),
         out_shape=jax.ShapeDtypeStruct((rows, count), F32),
-        in_specs=[whole(x.shape), whole(rank.shape)],
+        in_specs=[whole(rank.shape)] + [whole(x.shape) for x in args],
         out_specs=pl.BlockSpec((rows, TILE), lambda i: (0, i)),
         scratch_shapes=[pltpu.VMEM((2 * rows, count), BF16)],
-        compiler_params=params(),
+        compiler_params=params(12),
         cost_estimate=pl.CostEstimate(flops=4 * rows * count * count, bytes_accessed=8 * rows * count, transcendentals=0),
         name="unsort" if back else "sort",
-    )(x, rank)
+    )(rank, *args)
 
 
 def weights_of(key, table, bins, per_tile):
@@ -147,11 +172,12 @@
     tile = jnp.floor((cell + 0.5) * (1.0 / per_tile))
     within = cell - tile * per_tile
     ids = lax.broadcasted_iota(jnp.int32, (nshape, key.shape[1]), 0).astype(F32)
-    picked = lax.dot_general(table, rows_equal(ids, shape), NN, preferred_element_type=F32)
+    picked = lax.dot_general(table, rows_equal(ids, shape), NN, preferred_element_type=F32).astype(BF16)
+    masks = [jnp.where(within == m, 1.0, 0.0).astype(BF16) for m in range(per_tile)]
     columns = []
     for part in (picked[:bins], picked[bins:]):
-        columns.append(jnp.concatenate([jnp.where(within == m, part, 0.0) for m in range(per_tile)], axis=0))
-    return jnp.concatenate(columns, axis=1).astype(BF16), tile
+        columns.append(jnp.concatenate([part * mask for mask in masks], axis=0))
+    return jnp.concatenate(columns, axis=1), tile
 
 
 def split_table(table):
@@ -167,14 +193,15 @@
         tiles[index + n] = jnp.broadcast_to(tile, tiles.shape[1:])
         return 0
 
-    lax.fori_loop(0, source.shape[1] // LANES, step, 0, unroll=2)
+    lax.fori_loop(0, source.shape[1] // LANES, step, 0, unroll=4)
 
 
 def collect_kernel(species, bins, per_tile, pairs, lists, first, *refs):
     sources, refs = refs[:lists], refs[lists:]
-    table_ref, steps_ref, *refs = refs
+    table_ref, *refs = refs
     acc_ref = None if first else refs.pop(0)
-    out_ref, weights, tiles, parts = refs
+    out_ref, weights, tiles, parts, steps, sems = refs
+    copies = fetch_rows(sources, steps, sems)
     rows, count = sources[0].shape
     blocks = count // LANES
     out_ref[...] = jnp.zeros_like(out_ref) if first else acc_ref[...]
@@ -191,11 +218,14 @@
 
         lax.fori_loop(0, blocks, split, 0, unroll=2)
 
+    for copy in copies:
+        copy.wait()
+
     def step(n, _):
         for number in range(lists):
             for g in range(GROUP):
                 k = n * GROUP + g
-                tile = steps_ref[number, k]
+                tile = steps[number, 7, k].astype(jnp.int32)
                 block = jnp.minimum(k - tile, blocks - 1) + number * blocks
                 wanted = jnp.where(k < pairs, tile, -1).astype(F32)
                 mask = jnp.where(tiles[block] == wanted, 1.0, 0.0).astype(BF16)
@@ -210,12 +240,12 @@
     lax.fori_loop(0, -(-pairs // GROUP), step, 0)
 
 
-def collect_call(sources, table, steps, acc, species, bins, per_tile, ntiles):
+def collect_call(sources, table, acc, species, bins, per_tile, ntiles):
     rows, count = sources[0].shape
     lists, blocks = len(sources), count // LANES
     pairs = blocks + ntiles - 1
-    args = list(sources) + [table, steps]
-    specs = [VMEM] * (lists + 1) + [SMEM]
+    args = list(sources) + [table]
+    specs = [VMEM] * (lists + 1)
     alias = {}
     if acc is not None:
         alias = {len(args): 0}
@@ -230,19 +260,23 @@
             pltpu.VMEM((lists * blocks, TILE, 2 * LANES), BF16),
             pltpu.VMEM((lists * blocks, 16, LANES), F32),
             pltpu.VMEM((lists * blocks, 2 * HALF, LANES), BF16),
+            pltpu.SMEM((lists, 8, LANES), F32),
+            pltpu.SemaphoreType.DMA((2, lists)),
         ],
         input_output_aliases=alias,
-        compiler_params=params(),
+        compiler_params=params(24),
         cost_estimate=pl.CostEstimate(flops=lists * pairs * 2 * LANES * TILE * TILE, bytes_accessed=0, transcendentals=0),
         name="collect",
     )(*args)
 
 
-def project_kernel(bins, per_tile, pairs, lists, species, *refs):
+def project_kernel(bins, per_tile, pairs, lists, *refs):
     means, refs = refs[:3], refs[3:]
-    keys_ref, table_ref, steps_ref, out_ref, weights, tiles, parts = refs
-    rows = means[0].shape[0]
-    count = keys_ref.shape[1]
+    sources, refs = refs[:lists], refs[lists:]
+    table_ref, *refs = refs
+    outs, (weights, tiles, parts, keys, steps, sems) = refs[:lists], refs[lists:]
+    copies = fetch_rows(sources, steps, sems, keys)
+    rows, count = outs[0].shape
     blocks = count // LANES
     per_mean = means[0].shape[1] // TILE
     for number, mean in enumerate(means):
@@ -253,15 +287,17 @@
 
         lax.fori_loop(0, per_mean, split, 0, unroll=2)
     table = split_table(table_ref[...])
-    out_ref[...] = jnp.zeros_like(out_ref)
+    for copy in copies:
+        copy.wait()
     for number in range(lists):
-        prepare_weights(keys_ref.at[number : number + 1], number * blocks, 0, table, bins, per_tile, weights, tiles)
+        outs[number][...] = jnp.zeros_like(outs[number])
+        prepare_weights(keys.at[number], number * blocks, 6, table, bins, per_tile, weights, tiles)
 
     def step(n, _):
         for number in range(lists):
             for g in range(GROUP):
                 k = n * GROUP + g
-                tile = steps_ref[number, k]
+                tile = steps[number, 7, k].astype(jnp.int32)
                 local = jnp.minimum(k - tile, blocks - 1)
                 block = local + number * blocks
                 wanted = jnp.where(k < pairs, tile, -1).astype(F32)
@@ -270,31 +306,34 @@
                 got = got[:, :LANES] + got[:, LANES:]
                 got = jnp.where(tiles[block][:1] == wanted, got, 0.0)
                 place = pl.ds(pl.multiple_of(local * LANES, LANES), LANES)
-                out_ref[number, :, place] += got
+                outs[number][:, place] += got
         return 0
 
     lax.fori_loop(0, -(-pairs // GROUP), step, 0)
 
 
-def project_call(means, keys, table, steps, species, bins, per_tile, ntiles):
-    rows = means[0].shape[0]
-    lists, count = keys.shape
+def project_call(means, sources, table, bins, per_tile, ntiles):
+    rows, count = sources[0].shape
+    lists = len(sources)
     blocks = count // LANES
     pairs = blocks + ntiles - 1
     return pl.pallas_call(
-        functools.partial(project_kernel, bins, per_tile, pairs, lists, species),
-        out_shape=jax.ShapeDtypeStruct((lists, rows, count), F32),
-        in_specs=[VMEM] * 5 + [SMEM],
-        out_specs=VMEM,
+        functools.partial(project_kernel, bins, per_tile, pairs, lists),
+        out_shape=[jax.ShapeDtypeStruct((rows, count), F32)] * lists,
+        in_specs=[VMEM] * 3 + [pl.BlockSpec(memory_space=pl.ANY)] * lists + [VMEM],
+        out_specs=[VMEM] * lists,
         scratch_shapes=[
             pltpu.VMEM((lists * blocks, TILE, 2 * LANES), BF16),
             pltpu.VMEM((lists * blocks, 16, LANES), F32),
             pltpu.VMEM((ntiles, 2 * HALF, TILE), BF16),
+            pltpu.VMEM((lists, 8, count), F32),
+            pltpu.SMEM((lists, 8, LANES), F32),
+            pltpu.SemaphoreType.DMA((2, lists)),
         ],
-        compiler_params=params(),
+        compiler_params=params(24),
         cost_estimate=pl.CostEstimate(flops=lists * pairs * 2 * LANES * TILE * TILE, bytes_accessed=0, transcendentals=0),
         name="project",
-    )(*means, keys, table, steps)
+    )(*means, *sources, table)
 
 
 def middle_kernel(species, bins, chunk, refs_in, refs_out, scratch):
@@ -470,7 +509,7 @@
         + [pltpu.VMEM((steps, rows, 2 * LANES), F32)] * 2
         + [pltpu.VMEM((2 * LANES, chunk), BF16), pltpu.VMEM(matrix.shape, BF16)]
         + [pltpu.SemaphoreType.DMA((6, steps))] * 2,
-        compiler_params=pltpu.CompilerParams(vmem_limit_bytes=LIMIT, collective_id=1, has_side_effects=True),
+        compiler_params=pltpu.CompilerParams(vmem_limit_bytes=24 << 20, collective_id=1, has_side_effects=True),
         name="middle",
     )(acc, moved, diss, rate, count, matrix)
 
@@ -507,18 +546,18 @@
     transported = les_state + diffusion[:, None, None, None] * (around - 6.0 * les_state)
     flat = transported.reshape(species, count)
     fill = [jnp.zeros((rows - species - 1, count), F32)]
-    mine = permute_call(jnp.concatenate([flat, key] + fill, axis=0), rank, False)
-    mine = mine.at[rows - 1, :LANES].set(steps[0])
+    mine = permute_call([jnp.concatenate([flat, key] + fill, axis=0)], rank, steps, False)
 
     table = lax.dynamic_slice_in_dim(pdf_table.T, lax.axis_index("cross") * bins, bins, axis=0)
 
+    mine, cmc_state, dissipation, reaction_rate, substeps, chem_matrix = lax.optimization_barrier(
+        (mine, cmc_state, dissipation, reaction_rate, substeps, chem_matrix)
+    )
     bits = [1 << k for k in range(ncross.bit_length() - 1)]
-    sources = [mine]
+    near_lists, far_lists = [mine], []
     if bits:
-        far_off = swap(mine, "cross", bits[-1])
-        sources += [swap(mine, "cross", bit) for bit in bits[:-1]] + [far_off]
-        sources += [None] * (len(bits) - 1)
-    steps_of = lambda group: jnp.stack([s[rows - 1, :LANES] for s in group]).astype(jnp.int32)
+        far_lists = [swap(mine, "cross", bits[-1])]
+        near_lists += [swap(mine, "cross", bit) for bit in bits[:-1]]
 
     spread = lambda a: a.transpose(0, 2, 1).reshape(a.shape[0], width)
     wide = lambda a: a.T.reshape(1, width)
@@ -528,39 +567,34 @@
     moved = state - 0.4 * (state - left) + 0.1 * (right - 2.0 * state + left)
     moved = jnp.pad(moved, ((0, rows - species), (0, 0)))
 
-    acc = None
-    for number, source in enumerate(sources):
-        if number and number == len(sources) // 2:
-            acc, far_off, moved = lax.optimization_barrier((acc, far_off, moved))
-            sources[number] = source = far_off
-            sources[number + 1 :] = [swap(far_off, "cross", bit) for bit in bits[:-1]]
-        acc = collect_call([sources[number]], table, steps_of([sources[number]]), acc, species, bins, per_tile, ntiles)
     extra = rows - species
     matrix = jnp.tile(jnp.pad(chem_matrix, ((0, extra), (0, -(-rows // 16) * 16 - species))), (1, 3))
-    fresh, next_mean, far_mean = middle_call(
-        acc, moved, wide(dissipation), wide(reaction_rate), jnp.repeat(substeps, bins)[None, :], matrix, species, bins
-    )
+    terms = (moved, wide(dissipation), wide(reaction_rate), jnp.repeat(substeps, bins)[None, :], matrix)
+    acc = collect_call(near_lists, table, None, species, bins, per_tile, ntiles)
+    if bits:
+        acc, far_lists, terms = lax.optimization_barrier((acc, far_lists, terms))
+        far_lists = list(far_lists) + [swap(far_lists[0], "cross", bit) for bit in bits[:-1]]
+        acc = collect_call(far_lists, table, acc, species, bins, per_tile, ntiles)
+    means = middle_call(acc, *terms, species, bins)
+    fresh = means[0]
+    means = [means[2], means[0], means[1]]
     cmc_out = fresh[:species].reshape(species, cells, bins).transpose(0, 2, 1)
 
-    keys = jnp.concatenate([s[species : species + 1] for s in sources], axis=0)
-    part = project_call(
-        [far_mean, fresh, next_mean], keys, table, steps_of(sources), species, bins, per_tile, ntiles
-    )
-    part = [part[n] for n in range(len(sources))]
+
+    def gather(group):
+        total = group[0]
+        for bit, piece in zip(bits[:-1], group[1:]):
+            total = total + swap(piece, "cross", bit)
+        return total
+
     if bits:
-        half = len(part) // 2
-        here, there = part[:half], part[half:]
-
-        def gather(group):
-            total = group[0]
-            for bit, piece in zip(bits[:-1], group[1:]):
-                total = total + swap(piece, "cross", bit)
-            return total
-
-        there = gather(there)
-        part = [gather(here) + swap(there, "cross", bits[-1])]
-    total = permute_call(part[0], rank, True)
-    conditional = (total[:species] / total[species : species + 1]).reshape(transported.shape)
+        there = gather(project_call(means, far_lists, table, bins, per_tile, ntiles))
+        there, means = lax.optimization_barrier((there, means))
+        there = swap(there, "cross", bits[-1])
+    here = project_call(means, near_lists, table, bins, per_tile, ntiles)
+    total = [here[0]] + [swap(piece, "cross", bit) for bit, piece in zip(bits[:-1], here[1:])]
+    conditional = permute_call(total + [there] * bool(bits), rank, None, True)
+    conditional = conditional[:species].reshape(transported.shape)
     les_out = transported + 0.5 * (conditional - transported)
     return (les_out, cmc_out)
 

time: 249 us -> 199 us (0.80)
  Pallas kernels: 154 us -> 116 us
  other arithmetic: 22.3 us -> 9.69 us
    pallas_call x4 -> x2, Pallas kernels: 45.7 us -> 23.2 us  [collect_call(): pl.pallas_call(functools.partial(collect_kernel, species, bins, per_tile,...]
    pallas_call x1 -> x2, Pallas kernels: 23.1 us -> 17 us  [project_call(): pl.pallas_call(functools.partial(project_kernel, bins, per_tile, pairs, l...]
    unnamed x30 -> x34, local copies, waits for them, and re-layouts: 3.64 us -> 8.69 us
    pallas_call x1, Pallas kernels: 57.6 us -> 53.5 us  [middle_call(): pl.pallas_call(kernel, out_shape=[jax.ShapeDtypeStruct((rows, width), F32...]
    pallas_call x2, Pallas kernels: 25.7 us -> 21.7 us  [permute_call(): pl.pallas_call(functools.partial(permute_kernel, back, len(args)), grid=(...]
    slice x5 -> x0, local copies, waits for them, and re-layouts: 3.71 us -> none  [the longest x4 2.78 us: on_device(): keys = jnp.concatenate([s[species:species + 1] for s in sources], axis=0)]
    add x1 -> x0, other arithmetic: 2.77 us -> none  [on_device(): part = [gather(here) + swap(there, 'cross', bits[-1])]]
    squeeze x1 -> x0, local copies, waits for them, and re-layouts: 2.53 us -> none  [on_device(): part = [part[n] for n in range(len(sources))]]
  transfers between devices with their start and end apart: 12 -> 12, of which waited for: 2 -> 4; matrix products, arithmetic and copies ran while one was open for 15% -> 12% of each run, Pallas kernels for 21% -> 6%
where the time goes in v3:
time: 199 us; the launch traced here: 198 us
  Pallas kernels  116 us (58%)
  local copies, waits for them, and re-layouts  27.4 us (14%)
  waiting for transfers between devices  22.1 us (11%)
  starting transfers between devices  21.6 us (11%)
  other arithmetic  9.69 us (5%)
    pallas_call x1, Pallas kernels, middle_call(): pl.pallas_call(kernel, out_shape=[jax.ShapeDtypeStruct((rows, width), F32...  53.5 us
    pallas_call x2, Pallas kernels, collect_call(): pl.pallas_call(functools.partial(collect_kernel, species, bins, per_tile,...  23.2 us
    pallas_call x2, Pallas kernels, permute_call(): pl.pallas_call(functools.partial(permute_kernel, back, len(args)), grid=(...  21.7 us
    ppermute x6, waiting for transfers between devices, swap(): return lax.ppermute(array, axis, [(i, i ^ bit) for i in range(count)])  20.9 us
    pallas_call x2, Pallas kernels, project_call(): pl.pallas_call(functools.partial(project_kernel, bins, per_tile, pairs, l...  17 us
    ppermute x6, starting transfers between devices, shift(): lax.ppermute(array, axis, [(i, i + by) for i in range(count) if 0 <= i +...  15.7 us
    unnamed x34, local copies, waits for them, and re-layouts  8.69 us
    ppermute x6, starting transfers between devices, swap(): return lax.ppermute(array, axis, [(i, i ^ bit) for i in range(count)])  5.86 us
  transfers between devices with their start and end apart: 12, of which 4 were waited for; matrix products, arithmetic and copies ran while one was open for 12% of the time, Pallas kernels for 6%

profile of v3, /device:TPU:2, one launch (start us, length us, event | category | flops | bytes accessed | tf_op | source)
XLA Modules:
  0.0 197.8 jit_solution(13150045396215771503)
XLA Ops:
  0.7 1.1 fusion.16
  1.7 1.9 collective-permute-start
  3.6 4.8 %collective-permute-start.1 = (f32[54,1,4,128]{3,2,1,0:T(4,128)S(1)}, f32[54,1,4,128]{3,2,1,0:T(4,128)S(1)}, u32[]{:S(2)}, u32[]{:S(2)}) collective-permute-start(f32[54,1,4,128]{3,2,1,0:T(4,128)S(1)} %get-tuple-element.63), channel_id=1, source_target_pairs={{0,4},{4,8},{8,12},{12,16},{16,20},{20,24},{24,28},{1,5},{5,9},{9,... | collective-permute-start | bytes 331784 | tf_op jit(solution)/shard_map/ppermute | solution.py:24
  8.5 1.9 fusion.17
  10.4 1.3 collective-permute-start.3
  11.7 1.3 collective-permute-start.2
  13.0 0.7 broadcast_subtract_fusion
  13.8 0.8 fusion.13.key_ref
  14.9 0.7 rank.1
  15.6 1.2 collective-permute-done.2
  16.9 2.3 %fusion.7 = f32[54,8,4,128]{3,2,1,0:T(4,128)S(1)} fusion(f32[54,8,4,128]{3,2,1,0:T(4,128)S(1)} %copy-done.5, f32[54,8,1,128]{3,2,1,0:T(1,128)S(1)} %bitcast.28, f32[54,8,1,128]{3,2,1,0:T(1,128)S(1)} %bitcast.30, f32[54,1,4,128]{3,2,1,0:T(4,128)S(1)} %collective-permute-done.1, f32[54,1,4,128]{3,2,1,0:T(4,128)S(1)} %collective-permute-done, f32[54]{0:T(128)} %param.15), kind=kLoop, calls=%fused_computation.12 | loop fusion | flops 2875392 | bytes 2433240 | tf_op jit(solution)/shard_map/add | solution.py:546
  19.2 0.4 reshape.153
  19.6 0.1 maximum_maximum_fusion.refs_0_
  19.7 13.0 %sort.1.refs_0_.refs_3_ = f32[56,4096]{1,0:T(8,128)S(1)} custom-call(f32[1,4096]{1,0:T(1,128)S(1)} %get-tuple-element.28.rank_ref, f32[56,4096]{1,0:T(8,128)S(1)} %maximum_maximum_fusion.refs_0_, f32[1,128]{1,0:T(1,128)S(1)} %get-tuple-element.29.refs_1_), custom_call_target="tpu_custom_call" | custom-call | flops 3758096384 | bytes 1835008 | tf_op jit(solution)/shard_map/sort/pallas_call | solution.py:155
  32.7 4.2 %collective-permute-start.5 = (f32[56,4096]{1,0:T(8,128)S(1)}, f32[56,4096]{1,0:T(8,128)S(1)}, u32[]{:S(2)}, u32[]{:S(2)}) collective-permute-start(f32[56,4096]{1,0:T(8,128)S(1)} %sort.1.refs_0_.refs_3_), channel_id=1, source_target_pairs={{0,2},{1,3},{2,0},{3,1},{4,6},{5,7},{6,4},{7,5},{8,10},{9,11},{10,... | collective-permute-start | bytes 2752520 | tf_op jit(solution)/shard_map/ppermute | solution.py:29
  36.9 0.4 collective-permute-start.4
  37.2 4.1 %copy.36 = f32[54,128,32]{0,2,1:T(8,128)} copy(f32[54,128,32]{1,2,0:T(8,128)} %bitcast.27) | data formatting | bytes 1769472 | tf_op jit(solution)/shard_map/transpose | solution.py:562
  41.3 3.2 %copy.40 = f32[54,4096]{1,0:T(8,128)} copy(f32[54,4096]{0,1:T(8,128)} %bitcast.26) | data formatting | bytes 1769472 | tf_op jit(solution)/shard_map/reshape | solution.py:562
  44.5 1.5 fusion.14
  46.0 2.5 %collective-permute-start.6 = (f32[54,32]{1,0:T(8,128)}, f32[54,32]{1,0:T(8,128)}, u32[]{:S(2)}, u32[]{:S(2)}) collective-permute-start(f32[54,32]{1,0:T(8,128)} %get-tuple-element.58), channel_id=1, source_target_pairs={{0,4},{4,8},{8,12},{12,16},{16,20},{20,24},{24,28},{1,5},{5,9},{9,... | collective-permute-start | bytes 20744 | tf_op jit(solution)/shard_map/ppermute | solution.py:24
  48.6 3.9 %collective-permute-start.7 = (f32[54,32]{1,0:T(8,128)}, f32[54,32]{1,0:T(8,128)}, u32[]{:S(2)}, u32[]{:S(2)}) collective-permute-start(f32[54,32]{1,0:T(8,128)} %get-tuple-element.59), channel_id=1, source_target_pairs={{4,0},{8,4},{12,8},{16,12},{20,16},{24,20},{28,24},{5,1},{9,5},{13... | collective-permute-start | bytes 20744 | tf_op jit(solution)/shard_map/ppermute | solution.py:24
  52.4 3.0 %fusion.15 = (f32[54,4064]{1,0:T(8,128)}, f32[54,4064]{1,0:T(8,128)}) fusion(f32[54,4096]{1,0:T(8,128)} %copy.40), kind=kLoop, calls=%fused_computation.32 | loop fusion | bytes 3511296 | tf_op jit(solution)/shard_map/slice | solution.py:565
  55.6 0.1 reshape.155.refs_2_
  55.8 0.1 reshape.156.refs_3_
  56.0 0.1 broadcast_in_dim_reshape.3.refs_4_
  56.1 0.1 tile.10.refs_5_
  56.2 2.1 %fusion.2 = f32[54,4096]{1,0:T(8,128)S(1)} fusion(f32[54,32]{1,0:T(8,128)} %collective-permute-done.7, f32[54,4064]{1,0:T(8,128)} %get-tuple-element.61, f32[54,4096]{1,0:T(8,128)} %copy.40, f32[54,4064]{1,0:T(8,128)} %get-tuple-element.60, f32[54,32]{1,0:T(8,128)} %collective-permute-done.6), kind=kLoop, calls=%fused_computation.7 | loop fusion | flops 2211840 | bytes 3538944 | tf_op jit(solution)/shard_map/add | solution.py:567
  58.4 11.5 %collect.2.refs_3_ = f32[56,12288]{1,0:T(8,128)S(1)} custom-call(f32[56,4096]{1,0:T(8,128)S(1)} %sort.1.refs_0_.refs_3_, f32[56,4096]{1,0:T(8,128)S(1)} %collective-permute-done.4.refs_1_.refs_4_, f32[32,128]{1,0:T(8,128)S(1)} %bitcast.21), custom_call_target="tpu_custom_call" | custom-call | flops 2650800128 | tf_op jit(solution)/shard_map/collect/pallas_call | solution.py:254
  70.0 2.5 %collective-permute-done.8.refs_1_.refs_4_ = f32[56,4096]{1,0:T(8,128)S(1)} collective-permute-done((f32[56,4096]{1,0:T(8,128)S(1)}, f32[56,4096]{1,0:T(8,128)S(1)}, u32[]{:S(2)}, u32[]{:S(2)}) %collective-permute-start.8) | collective-permute-done | bytes 917536 | tf_op jit(solution)/shard_map/ppermute | solution.py:29
  72.5 11.7 %collect.3.refs_0_ = f32[56,12288]{1,0:T(8,128)S(1)} custom-call(f32[56,4096]{1,0:T(8,128)S(1)} %collective-permute-done.5.refs_0_.refs_3_, f32[56,4096]{1,0:T(8,128)S(1)} %collective-permute-done.8.refs_1_.refs_4_, f32[32,128]{1,0:T(8,128)S(1)} %bitcast.22, f32[56,12288]{1,0:T(8,128)S(1)} %collect.2.refs_3_), custom_call_target="tpu_custom_call", output_to_operand_aliasing={{}: (3, {})} | custom-call | flops 2650800128 | tf_op jit(solution)/shard_map/collect/pallas_call | solution.py:254
  84.2 0.9 copy-done.1
  85.1 53.5 %middle.1 = (f32[56,4096]{1,0:T(8,128)S(1)}, f32[56,4096]{1,0:T(8,128)S(1)}, f32[56,4096]{1,0:T(8,128)S(1)}) custom-call(f32[56,12288]{1,0:T(8,128)S(1)} %collect.3.refs_0_, f32[56,4096]{1,0:T(8,128)S(1)} %pad.13.refs_1_, f32[1,4096]{1,0:T(1,128)S(1)} %reshape.155.refs_2_, f32[1,4096]{1,0:T(1,128)S(1)} %reshape.156.refs_3_, ...), custom_call_target="tpu_custom_call" | custom-call | tf_op jit(solution)/shard_map/middle/pallas_call | solution.py:503
  138.6 1.2 copy-done.2
  139.8 8.0 %project.2 = (f32[56,4096]{1,0:T(8,128)S(1)}, f32[56,4096]{1,0:T(8,128)S(1)}) custom-call(f32[56,4096]{1,0:T(8,128)S(1)} %get-tuple-element.48.refs_0_, f32[56,4096]{1,0:T(8,128)S(1)} %get-tuple-element.49.refs_1_, f32[56,4096]{1,0:T(8,128)S(1)} %get-tuple-element.50.refs_2_, f32[56,4096]{1,0:T(8,128)S(1)} %copy-done.2, ...), custom_call_target="tpu_custom_call" | custom-call | flops 2650800128 | tf_op jit(solution)/shard_map/project/pallas_call | solution.py:320
  147.9 2.5 %collective-permute-done.9 = f32[56,4096]{1,0:T(8,128)S(1)} collective-permute-done((f32[56,4096]{1,0:T(8,128)S(1)}, f32[56,4096]{1,0:T(8,128)S(1)}, u32[]{:S(2)}, u32[]{:S(2)}) %collective-permute-start.9) | collective-permute-done | bytes 917536 | tf_op jit(solution)/shard_map/ppermute | solution.py:29
  150.4 1.0 add.87
  151.4 9.0 %project.3 = (f32[56,4096]{1,0:T(8,128)S(1)}, f32[56,4096]{1,0:T(8,128)}) custom-call(f32[56,4096]{1,0:T(8,128)S(1)} %get-tuple-element.48.refs_0_, f32[56,4096]{1,0:T(8,128)S(1)} %get-tuple-element.49.refs_1_, f32[56,4096]{1,0:T(8,128)S(1)} %get-tuple-element.50.refs_2_, f32[56,4096]{1,0:T(8,128)S(1)} %sort.1.refs_0_.refs_3_, ...), custom_call_target="tpu_custom_call" | custom-call | flops 2650800128 | tf_op jit(solution)/shard_map/project/pallas_call | solution.py:320
  160.4 0.9 copy-done.3
  161.3 0.1 collective-permute-start.10
  161.5 1.1 collective-permute-start.11
  162.5 2.0 %copy.46 = f32[54,4096]{0,1:T(8,128)} copy(f32[54,4096]{1,0:T(8,128)S(1)} %bitcast.20) | data formatting | bytes 1769472 | tf_op jit(solution)/shard_map/slice | solution.py:581
  164.5 3.8 %copy.47 = f32[54,32,128]{2,1,0:T(8,128)} copy(f32[54,32,128]{0,1,2:T(8,128)} %bitcast.25) | data formatting | bytes 1769472
  168.4 15.9 %collective-permute-done.11.refs_2_ = f32[56,4096]{1,0:T(8,128)S(1)} collective-permute-done((f32[56,4096]{1,0:T(8,128)}, f32[56,4096]{1,0:T(8,128)S(1)}, u32[]{:S(2)}, u32[]{:S(2)}) %collective-permute-start.11) | collective-permute-done | bytes 917536 | tf_op jit(solution)/shard_map/ppermute | solution.py:29
  184.3 1.2 copy-done.4
  185.5 8.6 %unsort.1 = f32[56,4096]{1,0:T(8,128)S(1)} custom-call(f32[1,4096]{1,0:T(1,128)S(1)} %get-tuple-element.28.rank_ref, f32[56,4096]{1,0:T(8,128)S(1)} %copy-done.4, f32[56,4096]{1,0:T(8,128)S(1)} %collective-permute-done.10.refs_1_, f32[56,4096]{1,0:T(8,128)S(1)} %collective-permute-done.11.refs_2_), custom_call_target="tpu_custom_call" | custom-call | flops 3758096384 | bytes 1835008 | tf_op jit(solution)/shard_map/unsort/pallas_call | solution.py:155
  194.1 0.6 reshape.157
  194.8 0.5 copy-done.6
  195.3 2.5 %multiply_add_fusion = f32[54,8,4,128]{3,2,1,0:T(4,128)} fusion(f32[54,8,4,128]{3,2,1,0:T(4,128)S(1)} %reshape.157, f32[54,8,4,128]{3,2,1,0:T(4,128)S(1)} %copy-done.6, f32[54,8,1,128]{3,2,1,0:T(1,128)S(1)} %bitcast.29, f32[54,8,1,128]{3,2,1,0:T(1,128)S(1)} %bitcast.31, f32[54,1,4,128]{3,2,1,0:T(4,128)S(1)} %copy-done.10, ...), kind=kLoop, calls=%fused_computation.20 | loop fusion | flops 3538944 | bytes 3317976 | tf_op jit(solution)/shard_map/add | solution.py:598
  (46 shorter events, 0.8 us)
Async XLA Ops:
  0.6 14.0 %copy-start = (f32[128,128]{1,0:T(8,128)S(1)}, f32[128,128]{1,0:T(8,128)}, u32[]{:S(2)}) copy-start(f32[128,128]{1,0:T(8,128)} %param.14) | copy-start | bytes 196612
  0.6 16.2 %copy-start.5 = (f32[54,8,4,128]{3,2,1,0:T(4,128)S(1)}, f32[54,8,4,128]{3,2,1,0:T(4,128)}, u32[]{:S(2)}) copy-start(f32[54,8,4,128]{3,2,1,0:T(4,128)} %param.10) | copy-start | bytes 2654212
  1.7 13.9 %collective-permute-start = (f32[54,1,4,128]{3,2,1,0:T(4,128)S(1)}, f32[54,1,4,128]{3,2,1,0:T(4,128)S(1)}, u32[]{:S(2)}, u32[]{:S(2)}) collective-permute-start(f32[54,1,4,128]{3,2,1,0:T(4,128)S(1)} %get-tuple-element.62), channel_id=1, source_target_pairs={{4,0},{8,4},{12,8},{16,12},{20,16},{24,20},{28,24},{5,1},{9,5},{13... | collective-permute-start | bytes 331784 | tf_op jit(solution)/shard_map/ppermute | solution.py:24
  3.6 12.0 %collective-permute-start.1 = (f32[54,1,4,128]{3,2,1,0:T(4,128)S(1)}, f32[54,1,4,128]{3,2,1,0:T(4,128)S(1)}, u32[]{:S(2)}, u32[]{:S(2)}) collective-permute-start(f32[54,1,4,128]{3,2,1,0:T(4,128)S(1)} %get-tuple-element.63), channel_id=1, source_target_pairs={{0,4},{4,8},{8,12},{12,16},{16,20},{20,24},{24,28},{1,5},{5,9},{9,... | collective-permute-start | bytes 331784 | tf_op jit(solution)/shard_map/ppermute | solution.py:24
  10.4 5.2 %collective-permute-start.3 = (f32[54,8,1,128]{3,1,2,0:T(8,128)S(1)}, f32[54,8,1,128]{3,1,2,0:T(8,128)S(1)}, u32[]{:S(2)}, u32[]{:S(2)}) collective-permute-start(f32[54,8,1,128]{3,1,2,0:T(8,128)S(1)} %bitcast.33), channel_id=1, source_target_pairs={{0,1},{1,2},{2,3},{4,5},{5,6},{6,7},{8,9},{9,10},{10,11},{12,13},{... | collective-permute-start | bytes 663560 | tf_op jit(solution)/shard_map/ppermute | solution.py:24
  11.7 5.1 %collective-permute-start.2 = (f32[54,8,1,128]{3,1,2,0:T(8,128)S(1)}, f32[54,8,1,128]{3,1,2,0:T(8,128)S(1)}, u32[]{:S(2)}, u32[]{:S(2)}) collective-permute-start(f32[54,8,1,128]{3,1,2,0:T(8,128)S(1)} %bitcast.32), channel_id=1, source_target_pairs={{1,0},{2,1},{3,2},{5,4},{6,5},{7,6},{9,8},{10,9},{11,10},{13,12},{... | collective-permute-start | bytes 663560 | tf_op jit(solution)/shard_map/ppermute | solution.py:24
  15.6 4.0 %copy-start.7 = (f32[54,1,4,128]{3,2,1,0:T(4,128)}, f32[54,1,4,128]{3,2,1,0:T(4,128)S(1)}, u32[]{:S(2)}) copy-start(f32[54,1,4,128]{3,2,1,0:T(4,128)S(1)} %collective-permute-done) | copy-start | bytes 331780
  15.6 1.2 copy-start.9
  32.7 37.2 %collective-permute-start.5 = (f32[56,4096]{1,0:T(8,128)S(1)}, f32[56,4096]{1,0:T(8,128)S(1)}, u32[]{:S(2)}, u32[]{:S(2)}) collective-permute-start(f32[56,4096]{1,0:T(8,128)S(1)} %sort.1.refs_0_.refs_3_), channel_id=1, source_target_pairs={{0,2},{1,3},{2,0},{3,1},{4,6},{5,7},{6,4},{7,5},{8,10},{9,11},{10,... | collective-permute-start | bytes 2752520 | tf_op jit(solution)/shard_map/ppermute | solution.py:29
  36.9 21.5 %collective-permute-start.4 = (f32[56,4096]{1,0:T(8,128)S(1)}, f32[56,4096]{1,0:T(8,128)S(1)}, u32[]{:S(2)}, u32[]{:S(2)}) collective-permute-start(f32[56,4096]{1,0:T(8,128)S(1)} %sort.1.refs_0_.refs_3_), channel_id=1, source_target_pairs={{0,1},{1,0},{2,3},{3,2},{4,5},{5,4},{6,7},{7,6},{8,9},{9,8},{10,11... | collective-permute-start | bytes 2752520 | tf_op jit(solution)/shard_map/ppermute | solution.py:29
  44.5 11.0 %copy-start.11 = (f32[54,54]{1,0:T(8,128)S(1)}, f32[54,54]{1,0:T(8,128)}, u32[]{:S(2)}) copy-start(f32[54,54]{1,0:T(8,128)} %param.16) | copy-start | bytes 34996
  44.5 11.0 %copy-start.12 = (f32[32,128]{1,0:T(8,128)S(1)}, f32[32,128]{1,0:T(8,128)}, u32[]{:S(2)}) copy-start(f32[32,128]{1,0:T(8,128)} %param.17) | copy-start | bytes 49156
  44.5 11.2 %copy-start.13 = (f32[32,128]{1,0:T(8,128)S(1)}, f32[32,128]{1,0:T(8,128)}, u32[]{:S(2)}) copy-start(f32[32,128]{1,0:T(8,128)} %param.18) | copy-start | bytes 49156
  44.5 11.4 %copy-start.15 = (s32[128]{0:T(128)S(1)}, s32[128]{0:T(128)}, u32[]{:S(2)}) copy-start(s32[128]{0:T(128)} %param.19) | copy-start | bytes 1540
  46.0 10.2 %collective-permute-start.6 = (f32[54,32]{1,0:T(8,128)}, f32[54,32]{1,0:T(8,128)}, u32[]{:S(2)}, u32[]{:S(2)}) collective-permute-start(f32[54,32]{1,0:T(8,128)} %get-tuple-element.58), channel_id=1, source_target_pairs={{0,4},{4,8},{8,12},{12,16},{16,20},{20,24},{24,28},{1,5},{5,9},{9,... | collective-permute-start | bytes 20744 | tf_op jit(solution)/shard_map/ppermute | solution.py:24
  48.6 7.7 %collective-permute-start.7 = (f32[54,32]{1,0:T(8,128)}, f32[54,32]{1,0:T(8,128)}, u32[]{:S(2)}, u32[]{:S(2)}) collective-permute-start(f32[54,32]{1,0:T(8,128)} %get-tuple-element.59), channel_id=1, source_target_pairs={{4,0},{8,4},{12,8},{16,12},{20,16},{24,20},{28,24},{5,1},{9,5},{13... | collective-permute-start | bytes 20744 | tf_op jit(solution)/shard_map/ppermute | solution.py:24
  69.9 2.5 %collective-permute-start.8 = (f32[56,4096]{1,0:T(8,128)S(1)}, f32[56,4096]{1,0:T(8,128)S(1)}, u32[]{:S(2)}, u32[]{:S(2)}) collective-permute-start(f32[56,4096]{1,0:T(8,128)S(1)} %collective-permute-done.5.refs_0_.refs_3_), channel_id=1, source_target_pairs={{0,1},{1,0},{2,3},{3,2},{4,5},{5,4},{6,7},{7,6},{8,9},{9,8},{10,11... | collective-permute-start | bytes 2752520 | tf_op jit(solution)/shard_map/ppermute | solution.py:29
  84.2 0.9 copy-start.1
  138.6 1.2 copy-start.2
  147.8 2.5 %collective-permute-start.9 = (f32[56,4096]{1,0:T(8,128)S(1)}, f32[56,4096]{1,0:T(8,128)S(1)}, u32[]{:S(2)}, u32[]{:S(2)}) collective-permute-start(f32[56,4096]{1,0:T(8,128)S(1)} %get-tuple-element.47), channel_id=1, source_target_pairs={{0,1},{1,0},{2,3},{3,2},{4,5},{5,4},{6,7},{7,6},{8,9},{9,8},{10,11... | collective-permute-start | bytes 2752520 | tf_op jit(solution)/shard_map/ppermute | solution.py:29
  160.4 0.9 copy-start.3
  161.3 7.0 %collective-permute-start.10 = (f32[56,4096]{1,0:T(8,128)}, f32[56,4096]{1,0:T(8,128)S(1)}, u32[]{:S(2)}, u32[]{:S(2)}) collective-permute-start(f32[56,4096]{1,0:T(8,128)} %get-tuple-element.52), channel_id=1, source_target_pairs={{0,1},{1,0},{2,3},{3,2},{4,5},{5,4},{6,7},{7,6},{8,9},{9,8},{10,11... | collective-permute-start | bytes 2752520 | tf_op jit(solution)/shard_map/ppermute | solution.py:29
  161.5 22.8 %collective-permute-start.11 = (f32[56,4096]{1,0:T(8,128)}, f32[56,4096]{1,0:T(8,128)S(1)}, u32[]{:S(2)}, u32[]{:S(2)}) collective-permute-start(f32[56,4096]{1,0:T(8,128)} %add.87), channel_id=1, source_target_pairs={{0,2},{1,3},{2,0},{3,1},{4,6},{5,7},{6,4},{7,5},{8,10},{9,11},{10,... | collective-permute-start | bytes 2752520 | tf_op jit(solution)/shard_map/ppermute | solution.py:29
  184.3 1.2 copy-start.4
  185.5 9.3 %copy-start.8 = (f32[54,1,4,128]{3,2,1,0:T(4,128)S(1)}, f32[54,1,4,128]{3,2,1,0:T(4,128)}, u32[]{:S(2)}) copy-start(f32[54,1,4,128]{3,2,1,0:T(4,128)} %copy-done.7) | copy-start | bytes 331780
  185.5 9.3 %copy-start.10 = (f32[54,1,4,128]{3,2,1,0:T(4,128)S(1)}, f32[54,1,4,128]{3,2,1,0:T(4,128)}, u32[]{:S(2)}) copy-start(f32[54,1,4,128]{3,2,1,0:T(4,128)} %copy-done.9) | copy-start | bytes 331780
  185.5 9.3 %copy-start.14 = (f32[54]{0:T(128)S(1)}, f32[54]{0:T(128)}, u32[]{:S(2)}) copy-start(f32[54]{0:T(128)} %param.15) | copy-start | bytes 652
  194.1 1.2 copy-start.6

commit v4 on v3

--- a/solution.py
+++ b/solution.py
@@ -1,4 +1,5 @@
 import functools
+
 
 import jax
 import jax.numpy as jnp
@@ -19,11 +20,6 @@
 LAG = (2, 4, 6)
 
 
-def shift(array, axis, by):
-    count = lax.axis_size(axis)
-    return lax.ppermute(array, axis, [(i, i + by) for i in range(count) if 0 <= i + by < count])
-
-
 def swap(array, axis, bit):
     count = lax.axis_size(axis)
     return lax.ppermute(array, axis, [(i, i ^ bit) for i in range(count)])
@@ -56,23 +52,19 @@
     return pltpu.CompilerParams(vmem_limit_bytes=mib << 20)
 
 
-def fetch_rows(sources, steps, sems, keys=None):
-    rows = sources[0].shape[0]
+def fetch_rows(sources, steps, sems):
     copies = []
     for number, source in enumerate(sources):
-        last = source.at[rows - 8 : rows]
-        copies.append(pltpu.make_async_copy(last.at[:, :LANES], steps.at[number], sems.at[0, number]))
-        if keys is not None:
-            copies.append(pltpu.make_async_copy(last, keys.at[number], sems.at[1, number]))
-    for copy in copies:
-        copy.start()
+        last = source.at[source.shape[0] - 8 : source.shape[0], :LANES]
+        copies.append(pltpu.make_async_copy(last, steps.at[number], sems.at[number]))
+        copies[-1].start()
     return copies
 
 
-def rank_kernel(tiles, span, key_ref, rank_ref, table_ref):
-    count = key_ref.shape[1]
+def ranks(tiles, span, key_ref, rank_ref, table_ref):
+    count = rank_ref.shape[1]
     ids = lax.broadcasted_iota(jnp.int32, (tiles, TILE), 0).astype(F32)
-    tile_of = lambda n: jnp.floor((key_ref[:, n * TILE : (n + 1) * TILE] + 0.5) * (1.0 / span))
+    tile_of = lambda n: jnp.floor((key_ref[:1, n * TILE : (n + 1) * TILE] + 0.5) * (1.0 / span))
     total = jnp.zeros((tiles, TILE), F32)
     for n in range(count // TILE):
         total = total + jnp.where(ids == tile_of(n), 1.0, 0.0)
@@ -99,24 +91,102 @@
         carry = carry + jnp.sum(hot, axis=1, keepdims=True)
 
 
-def rank_call(key, tiles, span):
-    count = key.shape[1]
+def head_kernel(grid_shape, cells, nshape, tiles, span, *refs):
+    les_ref, map_ref, shape_ref, diff_ref, t_ref, rank_ref, table_ref, key_ref, *refs = refs
+    faces, halos, (send, recv) = refs[:4], refs[4:8], refs[8:]
+    species, nx, ny = grid_shape
+    count = rank_ref.shape[1]
+    slab, nslab = lax.axis_index("slab"), lax.axis_size("slab")
+    cross, ncross = lax.axis_index("cross"), lax.axis_size("cross")
+    mesh = pl.DeviceIdType.MESH
+    sides = [
+        (slab > 0, {"slab": slab - 1}),
+        (slab < nslab - 1, {"slab": slab + 1}),
+        (cross > 0, {"cross": cross - 1}),
+        (cross < ncross - 1, {"cross": cross + 1}),
+    ]
+    barrier = pltpu.get_barrier_semaphore()
+    for n, (there, where) in enumerate(sides):
+
+        @pl.when(jnp.logical_not(there))
+        def _(n=n):
+            halos[n][...] = jnp.zeros_like(halos[n])
+
+    line = lambda x, y: les_ref[pl.ds(x * ny + y, species, stride=nx * ny), :]
+    for n, x in enumerate((0, nx - 1)):
+        for y in range(ny):
+            faces[n][y, :species] = line(x, y)
+    for n, y in enumerate((0, ny - 1)):
+        for x in range(nx):
+            faces[2 + n][x, :species] = line(x, y)
+    for there, where in sides:
+
+        @pl.when(there)
+        def _(where=where):
+            pl.semaphore_signal(barrier, inc=1, device_id=where, device_id_type=mesh)
+
+    pl.semaphore_wait(barrier, sum(jnp.where(there, 1, 0) for there, _ in sides))
+    copies = []
+    for n, (there, where) in enumerate(sides):
+        copy = pltpu.make_async_remote_copy(
+            src_ref=faces[n], dst_ref=halos[n ^ 1], send_sem=send.at[n], recv_sem=recv.at[n ^ 1],
+            device_id=where, device_id_type=mesh,
+        )
+        pl.when(there)(copy.start)
+        copies.append(copy)
+    offset = map_ref[...] - (slab - 1) * cells
+    block = jnp.where(offset >= cells, 1, 0) + jnp.where(offset >= 2 * cells, 1, 0)
+    offset = jnp.where(lax.rem(slab, 2) == 1, (2 - block) * cells + offset - block * cells, offset)
+    key = (offset * nshape + shape_ref[...]).astype(F32)
+    key_ref[:1, :] = key
+    t_ref[species:, :] = jnp.concatenate([key] + [jnp.zeros((t_ref.shape[0] - species - 1, count), F32)], axis=0)
+    ranks(tiles, span, key_ref, rank_ref, table_ref)
+    row = lax.broadcasted_iota(jnp.int32, (species, species), 0)
+    number = jnp.where(row == lax.broadcasted_iota(jnp.int32, (species, species), 1), diff_ref[...], 0.0)
+    number = jnp.sum(number, axis=1, keepdims=True)
+    lane = lax.broadcasted_iota(jnp.int32, (species, LANES), 1)
+    for n, (there, _) in enumerate(sides):
+        pl.when(sides[n ^ 1][0])(copies[n].wait_recv)
+    for x in range(nx):
+        for y in range(ny):
+            here = line(x, y)
+            around = line(x + 1, y) if x < nx - 1 else halos[1][y, :species]
+            around = around + (line(x - 1, y) if x else halos[0][y, :species])
+            around = around + (line(x, y + 1) if y < ny - 1 else halos[3][x, :species])
+            around = around + (line(x, y - 1) if y else halos[2][x, :species])
+            around = around + jnp.where(lane < LANES - 1, pltpu.roll(here, LANES - 1, 1), 0.0)
+            around = around + jnp.where(lane > 0, pltpu.roll(here, 1, 1), 0.0)
+            place = (x * ny + y) * LANES
+            t_ref[:species, place : place + LANES] = here + number * (around - 6.0 * here)
+    for n, (there, _) in enumerate(sides):
+        pl.when(there)(copies[n].wait_send)
+
+
+def head_call(les_state, cmc_map, pdf_index, diffusion, rows, cells, nshape, tiles, span):
+    species, nx, ny, nz = les_state.shape
+    count = nx * ny * nz
+    halo = [pltpu.VMEM((n, rows, LANES), F32) for n in (ny, ny, nx, nx)]
     return pl.pallas_call(
-        functools.partial(rank_kernel, tiles, span),
-        out_shape=[jax.ShapeDtypeStruct((1, count), F32), jax.ShapeDtypeStruct((1, LANES), F32)],
-        in_specs=[VMEM],
-        out_specs=[VMEM] * 2,
-        compiler_params=params(8),
-        cost_estimate=pl.CostEstimate(flops=2 * tiles * TILE * count, bytes_accessed=8 * count, transcendentals=0),
-        name="rank",
-    )(key)
+        functools.partial(head_kernel, (species, nx, ny), cells, nshape, tiles, span),
+        out_shape=[
+            jax.ShapeDtypeStruct((rows, count), F32),
+            jax.ShapeDtypeStruct((1, count), F32),
+            jax.ShapeDtypeStruct((1, LANES), F32),
+        ],
+        in_specs=[VMEM] * 4,
+        out_specs=[VMEM] * 3,
+        scratch_shapes=[pltpu.VMEM((8, count), F32)] + halo * 2 + [pltpu.SemaphoreType.DMA((4,))] * 2,
+        compiler_params=pltpu.CompilerParams(vmem_limit_bytes=12 << 20, collective_id=2, has_side_effects=True),
+        name="head",
+    )(
+        les_state.reshape(species * nx * ny, nz), cmc_map.reshape(1, count), pdf_index.reshape(1, count),
+        diffusion.reshape(1, species),
+    )
 
 
 def permute_kernel(back, count, rank_ref, *refs):
     xs, (out_ref, parts) = refs[:count], refs[count:]
-    steps_ref = None
-    if not back:
-        xs, steps_ref = xs[:-1], xs[-1]
+    xs, extra_ref = xs[:-1], xs[-1]
     rows, count = xs[0].shape
     chunk = 2 * TILE
 
@@ -142,22 +212,33 @@
             total = total + lax.dot_general(parts[:, piece], hot, NT, preferred_element_type=F32)
     total = total[:rows] + total[rows:]
     if back:
-        out_ref[...] = total / total[rows - 2 : rows - 1]
+        species = rows - 2
+        lines = count // LANES
+        for n in range(TILE // LANES):
+            piece = total[:, n * LANES : (n + 1) * LANES]
+            moved = extra_ref[:species, pl.ds(pl.multiple_of(here + n * LANES, LANES), LANES)]
+            piece = piece[:species] / piece[species : species + 1]
+            line = pl.program_id(0) * (TILE // LANES) + n
+            out_ref[pl.ds(line, species, stride=lines), :] = moved + 0.5 * (piece - moved)
     else:
         line = lax.broadcasted_iota(jnp.int32, (rows, TILE), 0)
-        steps = jnp.concatenate([steps_ref[...]] * (TILE // LANES), axis=1)
+        steps = jnp.concatenate([extra_ref[...]] * (TILE // LANES), axis=1)
         out_ref[...] = jnp.where(line == rows - 1, steps, total)
 
 
-def permute_call(xs, rank, steps, back):
+def permute_call(xs, rank, extra, back):
     rows, count = xs[0].shape
-    args = list(xs) + ([] if back else [steps])
+    args = list(xs) + [extra]
+    lines = (rows - 2) * count // LANES
+    out_shape, out_spec = (rows, count), pl.BlockSpec((rows, TILE), lambda i: (0, i))
+    if back:
+        out_shape, out_spec = (lines, LANES), whole((lines, LANES))
     return pl.pallas_call(
         functools.partial(permute_kernel, back, len(args)),
         grid=(count // TILE,),
-        out_shape=jax.ShapeDtypeStruct((rows, count), F32),
+        out_shape=jax.ShapeDtypeStruct(out_shape, F32),
         in_specs=[whole(rank.shape)] + [whole(x.shape) for x in args],
-        out_specs=pl.BlockSpec((rows, TILE), lambda i: (0, i)),
+        out_specs=out_spec,
         scratch_shapes=[pltpu.VMEM((2 * rows, count), BF16)],
         compiler_params=params(12),
         cost_estimate=pl.CostEstimate(flops=4 * rows * count * count, bytes_accessed=8 * rows * count, transcendentals=0),
@@ -200,8 +281,11 @@
     sources, refs = refs[:lists], refs[lists:]
     table_ref, *refs = refs
     acc_ref = None if first else refs.pop(0)
-    out_ref, weights, tiles, parts, steps, sems = refs
+    out_ref, *refs = refs
+    keys, (weights, tiles, parts, steps, sems) = refs[:lists], refs[lists:]
     copies = fetch_rows(sources, steps, sems)
+    for key, source in zip(keys, sources):
+        key[...] = source[source.shape[0] - 8 :, :]
     rows, count = sources[0].shape
     blocks = count // LANES
     out_ref[...] = jnp.zeros_like(out_ref) if first else acc_ref[...]
@@ -253,18 +337,18 @@
         specs.append(VMEM)
     return pl.pallas_call(
         functools.partial(collect_kernel, species, bins, per_tile, pairs, lists, acc is None),
-        out_shape=jax.ShapeDtypeStruct((rows, ntiles * TILE), F32),
+        out_shape=[jax.ShapeDtypeStruct((rows, ntiles * TILE), F32)] + [jax.ShapeDtypeStruct((8, count), F32)] * lists,
         in_specs=specs,
-        out_specs=VMEM,
+        out_specs=[VMEM] * (lists + 1),
         scratch_shapes=[
             pltpu.VMEM((lists * blocks, TILE, 2 * LANES), BF16),
             pltpu.VMEM((lists * blocks, 16, LANES), F32),
             pltpu.VMEM((lists * blocks, 2 * HALF, LANES), BF16),
             pltpu.SMEM((lists, 8, LANES), F32),
-            pltpu.SemaphoreType.DMA((2, lists)),
+            pltpu.SemaphoreType.DMA((lists,)),
         ],
         input_output_aliases=alias,
-        compiler_params=params(24),
+        compiler_params=params(19),
         cost_estimate=pl.CostEstimate(flops=lists * pairs * 2 * LANES * TILE * TILE, bytes_accessed=0, transcendentals=0),
         name="collect",
     )(*args)
@@ -274,8 +358,8 @@
     means, refs = refs[:3], refs[3:]
     sources, refs = refs[:lists], refs[lists:]
     table_ref, *refs = refs
-    outs, (weights, tiles, parts, keys, steps, sems) = refs[:lists], refs[lists:]
-    copies = fetch_rows(sources, steps, sems, keys)
+    outs, (weights, tiles, parts, steps, sems) = refs[:lists], refs[lists:]
+    copies = fetch_rows(sources, steps, sems)
     rows, count = outs[0].shape
     blocks = count // LANES
     per_mean = means[0].shape[1] // TILE
@@ -291,7 +375,7 @@
         copy.wait()
     for number in range(lists):
         outs[number][...] = jnp.zeros_like(outs[number])
-        prepare_weights(keys.at[number], number * blocks, 6, table, bins, per_tile, weights, tiles)
+        prepare_weights(sources[number], number * blocks, 6, table, bins, per_tile, weights, tiles)
 
     def step(n, _):
         for number in range(lists):
@@ -313,36 +397,34 @@
 
 
 def project_call(means, sources, table, bins, per_tile, ntiles):
-    rows, count = sources[0].shape
+    rows, count = means[0].shape[0], sources[0].shape[1]
     lists = len(sources)
     blocks = count // LANES
     pairs = blocks + ntiles - 1
     return pl.pallas_call(
         functools.partial(project_kernel, bins, per_tile, pairs, lists),
         out_shape=[jax.ShapeDtypeStruct((rows, count), F32)] * lists,
-        in_specs=[VMEM] * 3 + [pl.BlockSpec(memory_space=pl.ANY)] * lists + [VMEM],
+        in_specs=[VMEM] * (lists + 4),
         out_specs=[VMEM] * lists,
         scratch_shapes=[
             pltpu.VMEM((lists * blocks, TILE, 2 * LANES), BF16),
             pltpu.VMEM((lists * blocks, 16, LANES), F32),
             pltpu.VMEM((ntiles, 2 * HALF, TILE), BF16),
-            pltpu.VMEM((lists, 8, count), F32),
             pltpu.SMEM((lists, 8, LANES), F32),
-            pltpu.SemaphoreType.DMA((2, lists)),
+            pltpu.SemaphoreType.DMA((lists,)),
         ],
-        compiler_params=params(24),
+        compiler_params=params(19),
         cost_estimate=pl.CostEstimate(flops=lists * pairs * 2 * LANES * TILE * TILE, bytes_accessed=0, transcendentals=0),
         name="project",
     )(*means, *sources, table)
 
 
 def middle_kernel(species, bins, chunk, refs_in, refs_out, scratch):
-    acc_ref, moved_ref, diss_ref, rate_ref, count_ref, matrix_ref = refs_in
+    acc_ref, old_ref, diss_ref, rate_ref, count_ref, matrix_ref = refs_in
     fresh_ref, next_ref, far_ref = refs_out
-    hopped, summed, got, state_ref, edge_out, edge_in, pick_ref, third_ref, send, recv = scratch
+    hopped, summed, got, state_ref, edge_out, edge_in, side_in, pick_ref, third_ref, send, recv, side_send, side_recv = scratch
     rows, width = fresh_ref.shape
     steps = width // chunk
-    per_chunk = chunk // bins
     slab, nslab = lax.axis_index("slab"), lax.axis_size("slab")
     cross, ncross = lax.axis_index("cross"), lax.axis_size("cross")
     parity = lax.rem(slab, 2)
@@ -352,6 +434,7 @@
     has_outer = (outer >= 0) & (outer < nslab)
     has_inner = (inner >= 0) & (inner < nslab)
     has_before, has_after = cross > 0, cross < ncross - 1
+    has_down, has_up = slab > 0, slab < nslab - 1
     mesh = pl.DeviceIdType.MESH
 
     @pl.when(jnp.logical_not(has_inner))
@@ -370,15 +453,25 @@
     def _():
         edge_in[:, :, LANES:] = jnp.zeros(edge_in.shape[:2] + (LANES,), F32)
 
+    @pl.when(jnp.logical_not(has_down))
+    def _():
+        side_in[0] = jnp.zeros(side_in.shape[1:], F32)
+
+    @pl.when(jnp.logical_not(has_up))
+    def _():
+        side_in[1] = jnp.zeros(side_in.shape[1:], F32)
+
     barrier = pltpu.get_barrier_semaphore()
     greet = lambda where: pl.semaphore_signal(barrier, inc=1, device_id=where, device_id_type=mesh)
-    greet({"slab": partner})
+    pl.when(has_down)(lambda: greet({"slab": slab - 1}))
+    pl.when(has_up)(lambda: greet({"slab": slab + 1}))
     pl.when(has_outer)(lambda: greet({"slab": outer}))
     pl.when(has_inner)(lambda: greet({"slab": inner}))
     pl.when(has_before)(lambda: greet({"cross": cross - 1}))
     pl.when(has_after)(lambda: greet({"cross": cross + 1}))
     number = lambda flag: jnp.where(flag, 1, 0)
-    pl.semaphore_wait(barrier, 1 + number(has_outer) + number(has_inner) + number(has_before) + number(has_after))
+    flags = (has_down, has_up, has_outer, has_inner, has_before, has_after)
+    pl.semaphore_wait(barrier, sum(number(flag) for flag in flags))
 
     def lanes(c, base=0):
         return pl.ds(pl.multiple_of(base + c * chunk, chunk), chunk)
@@ -396,10 +489,22 @@
     give = lambda c: remote(4, c, fresh_ref.at[:, lanes(c)], next_ref.at[:, lanes(c)], {"slab": partner})
     pass_on = lambda c: remote(5, c, next_ref.at[:, lanes(c)], far_ref.at[:, lanes(c)], {"slab": inner})
 
+    def side(n, source, where):
+        return pltpu.make_async_remote_copy(
+            src_ref=source, dst_ref=side_in.at[n], send_sem=side_send.at[n], recv_sem=side_recv.at[n],
+            device_id=where, device_id_type=mesh,
+        )
+
+    to_up = side(0, old_ref.at[:, width - LANES : width], {"slab": slab + 1})
+    to_down = side(1, old_ref.at[:, :LANES], {"slab": slab - 1})
+
     @pl.when(has_outer)
     def _():
         for c in range(steps):
             to_outer(c).start()
+
+    pl.when(has_up)(to_up.start)
+    pl.when(has_down)(to_down.start)
 
     lane = lax.broadcasted_iota(jnp.int32, (2 * LANES, chunk), 1)
     row = lax.broadcasted_iota(jnp.int32, (2 * LANES, chunk), 0)
@@ -421,9 +526,21 @@
         pl.when(has_inner)(lambda: to_outer(c).wait_recv())
         summed[:, lanes(c)] = acc_ref[:, lanes(c, 2 * width)] + hopped[:, lanes(c)]
 
+    def advect(c):
+        here = old_ref[:, lanes(c)]
+        start = jnp.maximum(c * chunk - LANES, 0)
+        stop = jnp.minimum((c + 1) * chunk, width - LANES)
+        low = old_ref[:, pl.ds(pl.multiple_of(start, LANES), LANES)]
+        high = old_ref[:, pl.ds(pl.multiple_of(stop, LANES), LANES)]
+        low = jnp.where(c == 0, side_in[0], low)
+        high = jnp.where(c == steps - 1, side_in[1], high)
+        left = pltpu.roll(jnp.concatenate([low, here], axis=1), bins, 1)[:, LANES:]
+        right = pltpu.roll(jnp.concatenate([here, high], axis=1), chunk + LANES - bins, 1)[:, :chunk]
+        return here - 0.4 * (here - left) + 0.1 * (right - 2.0 * here + left)
+
     def blend(c):
         total = acc_ref[:, lanes(c, width)] + got[:, lanes(c)]
-        blended = (total + moved_ref[:, lanes(c)]) / (total[species : species + 1] + 1.0)
+        blended = (total + advect(c)) / (total[species : species + 1] + 1.0)
         state_ref[:, lanes(c)] = blended
         edge = lax.dot_general(stacked(blended), pick_ref[...], NT, preferred_element_type=F32)
         edge_out[c] = edge[:rows] + edge[rows:]
@@ -458,6 +575,8 @@
             pl.when((c >= 0) & (c < steps))(lambda: body(c))
 
         def second(c):
+            pl.when((c == 0) & has_down)(to_up.wait_recv)
+            pl.when((c == 0) & has_up)(to_down.wait_recv)
             to_partner(c).wait_recv()
             blend(c)
 
@@ -491,10 +610,12 @@
         return 0
 
     lax.fori_loop(0, steps, finish, 0)
-
-
-def middle_call(acc, moved, diss, rate, count, matrix, species, bins, chunk=512):
-    rows, width = moved.shape
+    pl.when(has_up)(to_up.wait_send)
+    pl.when(has_down)(to_down.wait_send)
+
+
+def middle_call(acc, old, diss, rate, count, matrix, species, bins, chunk=512):
+    rows, width = old.shape
     steps = width // chunk
 
     def kernel(*refs):
@@ -507,11 +628,12 @@
         out_specs=[VMEM] * 3,
         scratch_shapes=[pltpu.VMEM((rows, width), F32)] * 4
         + [pltpu.VMEM((steps, rows, 2 * LANES), F32)] * 2
-        + [pltpu.VMEM((2 * LANES, chunk), BF16), pltpu.VMEM(matrix.shape, BF16)]
-        + [pltpu.SemaphoreType.DMA((6, steps))] * 2,
-        compiler_params=pltpu.CompilerParams(vmem_limit_bytes=24 << 20, collective_id=1, has_side_effects=True),
+        + [pltpu.VMEM((2, rows, LANES), F32), pltpu.VMEM((2 * LANES, chunk), BF16), pltpu.VMEM(matrix.shape, BF16)]
+        + [pltpu.SemaphoreType.DMA((6, steps))] * 2
+        + [pltpu.SemaphoreType.DMA((2,))] * 2,
+        compiler_params=pltpu.CompilerParams(vmem_limit_bytes=16 << 20, collective_id=1, has_side_effects=True),
         name="middle",
-    )(acc, moved, diss, rate, count, matrix)
+    )(acc, old, diss, rate, count, matrix)
 
 
 def on_device(
@@ -521,32 +643,14 @@
     rows = -(-(species + 2) // 8) * 8
     bins, cells = cmc_state.shape[1:]
     nshape = pdf_table.shape[0]
-    count = cmc_map.size
     ncross = lax.axis_size("cross")
     per_tile = TILE // bins
     ntiles = 3 * cells // per_tile
     width = cells * bins
-    odd = lax.axis_index("slab") % 2 == 1
-
-    below = shift(les_state[:, -1:], "slab", 1)
-    above = shift(les_state[:, :1], "slab", -1)
-    behind = shift(les_state[:, :, -1:], "cross", 1)
-    ahead = shift(les_state[:, :, :1], "cross", -1)
-
-    offset = cmc_map.reshape(1, count) - (lax.axis_index("slab") - 1) * cells
-    block = offset // cells
-    offset = jnp.where(odd, (2 - block) * cells + offset - block * cells, offset)
-    key = (offset * nshape + pdf_index.reshape(1, count)).astype(F32)
-    rank, steps = rank_call(key, ntiles, nshape * per_tile)
-
-    xs = jnp.concatenate([below, les_state, above], axis=1)
-    ys = jnp.concatenate([behind, les_state, ahead], axis=2)
-    zs = jnp.pad(les_state, ((0, 0), (0, 0), (0, 0), (1, 1)))
-    around = xs[:, 2:] + xs[:, :-2] + ys[:, :, 2:] + ys[:, :, :-2] + zs[..., 2:] + zs[..., :-2]
-    transported = les_state + diffusion[:, None, None, None] * (around - 6.0 * les_state)
-    flat = transported.reshape(species, count)
-    fill = [jnp.zeros((rows - species - 1, count), F32)]
-    mine = permute_call([jnp.concatenate([flat, key] + fill, axis=0)], rank, steps, False)
+    flat, rank, steps = head_call(
+        les_state, cmc_map, pdf_index, diffusion, rows, cells, nshape, ntiles, nshape * per_tile
+    )
+    mine = permute_call([flat], rank, steps, False)
 
     table = lax.dynamic_slice_in_dim(pdf_table.T, lax.axis_index("cross") * bins, bins, axis=0)
 
@@ -561,20 +665,15 @@
 
     spread = lambda a: a.transpose(0, 2, 1).reshape(a.shape[0], width)
     wide = lambda a: a.T.reshape(1, width)
-    state = spread(cmc_state)
-    left = jnp.concatenate([shift(state[:, -bins:], "slab", 1), state[:, :-bins]], axis=1)
-    right = jnp.concatenate([state[:, bins:], shift(state[:, :bins], "slab", -1)], axis=1)
-    moved = state - 0.4 * (state - left) + 0.1 * (right - 2.0 * state + left)
-    moved = jnp.pad(moved, ((0, rows - species), (0, 0)))
-
+    state = spread(jnp.pad(cmc_state, ((0, rows - species), (0, 0), (0, 0))))
     extra = rows - species
     matrix = jnp.tile(jnp.pad(chem_matrix, ((0, extra), (0, -(-rows // 16) * 16 - species))), (1, 3))
-    terms = (moved, wide(dissipation), wide(reaction_rate), jnp.repeat(substeps, bins)[None, :], matrix)
-    acc = collect_call(near_lists, table, None, species, bins, per_tile, ntiles)
+    terms = (state, wide(dissipation), wide(reaction_rate), jnp.repeat(substeps, bins)[None, :], matrix)
+    acc, *near_keys = collect_call(near_lists, table, None, species, bins, per_tile, ntiles)
     if bits:
         acc, far_lists, terms = lax.optimization_barrier((acc, far_lists, terms))
         far_lists = list(far_lists) + [swap(far_lists[0], "cross", bit) for bit in bits[:-1]]
-        acc = collect_call(far_lists, table, acc, species, bins, per_tile, ntiles)
+        acc, *far_keys = collect_call(far_lists, table, acc, species, bins, per_tile, ntiles)
     means = middle_call(acc, *terms, species, bins)
     fresh = means[0]
     means = [means[2], means[0], means[1]]
@@ -588,15 +687,13 @@
         return total
 
     if bits:
-        there = gather(project_call(means, far_lists, table, bins, per_tile, ntiles))
+        there = gather(project_call(means, far_keys, table, bins, per_tile, ntiles))
         there, means = lax.optimization_barrier((there, means))
         there = swap(there, "cross", bits[-1])
-    here = project_call(means, near_lists, table, bins, per_tile, ntiles)
+    here = project_call(means, near_keys, table, bins, per_tile, ntiles)
     total = [here[0]] + [swap(piece, "cross", bit) for bit, piece in zip(bits[:-1], here[1:])]
-    conditional = permute_call(total + [there] * bool(bits), rank, None, True)
-    conditional = conditional[:species].reshape(transported.shape)
-    les_out = transported + 0.5 * (conditional - transported)
-    return (les_out, cmc_out)
+    les_out = permute_call(total + [there] * bool(bits), rank, flat, True)
+    return (les_out.reshape(les_state.shape), cmc_out)
 
 
 def solution(mesh):

time: 199 us -> 194 us (0.975)
  Pallas kernels: 116 us -> 143 us
  starting transfers between devices: 21.6 us -> 1.99 us
  other arithmetic: 9.69 us -> 1.03 us
  waiting for transfers between devices: 22.1 us -> 19.5 us
    ppermute x6 -> x0, starting transfers between devices: 15.7 us -> none  [shift(): lax.ppermute(array, axis, [(i, i + by) for i in range(count) if 0 <= i +...]
    pallas_call x1, Pallas kernels: 53.5 us -> 66.2 us  [middle_call(): pl.pallas_call(kernel, out_shape=[jax.ShapeDtypeStruct((rows, width), F32...]
    pallas_call x1, Pallas kernels: 0.72 us -> 10.3 us  [head_call(): pl.pallas_call(functools.partial(head_kernel, (species, nx, ny), cells, n...]
    slice x4 -> x0, local copies, waits for them, and re-layouts: 7.51 us -> none  [the longest x1 3.01 us: on_device(): state[:, :-bins]]
    add x3 -> x0, other arithmetic: 6.96 us -> none  [the longest x1 2.53 us: on_device(): les_out = transported + 0.5 * (conditional - transported)]
    unnamed x34 -> x32, local copies, waits for them, and re-layouts: 8.69 us -> 14.8 us
    reshape x3 -> x0, local copies, waits for them, and re-layouts: 4.14 us -> none  [the longest x1 3.18 us: on_device(): spread = lambda a: a.transpose(0, 2, 1).reshape(a.shape[0], width)]
    ppermute x6, starting transfers between devices: 5.86 us -> 1.99 us  [swap(): return lax.ppermute(array, axis, [(i, i ^ bit) for i in range(count)])]
  transfers between devices with their start and end apart: 12 -> 6, of which waited for: 4 -> 4; matrix products, arithmetic and copies ran while one was open for 12% -> 8% of each run, Pallas kernels for 6% -> 7%
where the time goes in v4:
time: 194 us; the launch traced here: 193 us
  Pallas kernels  143 us (74%)
  local copies, waits for them, and re-layouts  26 us (13%)
  waiting for transfers between devices  19.5 us (10%)
  starting transfers between devices  1.99 us (1%)
    pallas_call x1, Pallas kernels, middle_call(): pl.pallas_call(kernel, out_shape=[jax.ShapeDtypeStruct((rows, width), F32...  66.2 us
    pallas_call x2, Pallas kernels, collect_call(): pl.pallas_call(functools.partial(collect_kernel, species, bins, per_tile,...  25.5 us
    pallas_call x2, Pallas kernels, permute_call(): pl.pallas_call(functools.partial(permute_kernel, back, len(args)), grid=(...  24.4 us
    ppermute x6, waiting for transfers between devices, swap(): return lax.ppermute(array, axis, [(i, i ^ bit) for i in range(count)])  19.5 us
    pallas_call x2, Pallas kernels, project_call(): pl.pallas_call(functools.partial(project_kernel, bins, per_tile, pairs, l...  16.6 us
    unnamed x32, local copies, waits for them, and re-layouts  14.8 us
    pallas_call x1, Pallas kernels, head_call(): pl.pallas_call(functools.partial(head_kernel, (species, nx, ny), cells, n...  10.3 us
    transpose x2, local copies, waits for them, and re-layouts, on_device(): spread = lambda a: a.transpose(0, 2, 1).reshape(a.shape[0], width)  6.23 us
  transfers between devices with their start and end apart: 6, of which 4 were waited for; matrix products, arithmetic and copies ran while one was open for 8% of the time, Pallas kernels for 7%

profile of v4, /device:TPU:2, one launch (start us, length us, event | category | flops | bytes accessed | tf_op | source)
XLA Modules:
  0.0 192.6 jit_solution(4239087013150552747)
XLA Ops:
  0.6 0.0 copy-start
  0.7 1.2 copy-done.5
  1.8 0.7 copy-done.6
  2.6 0.7 copy-done.7
  3.3 0.7 copy-done.8
  3.9 10.3 %head.1 = (f32[56,4096]{1,0:T(8,128)S(1)}, f32[1,4096]{1,0:T(1,128)S(1)}, f32[1,128]{1,0:T(1,128)S(1)}) custom-call(f32[1728,128]{1,0:T(8,128)S(1)} %bitcast.16, s32[1,4096]{1,0:T(1,128)S(1)} %bitcast.17, s32[1,4096]{1,0:T(1,128)S(1)} %bitcast.18, f32[1,54]{1,0:T(1,128)S(1)} %bitcast.23), custom_call_target="tpu_custom_call" | custom-call | tf_op jit(solution)/shard_map/head/pallas_call | solution.py:169
  14.3 0.0 copy-start.12
  14.3 0.0 copy-start.13
  14.3 0.0 copy-start.14
  14.3 0.0 copy-start.11
  14.3 13.0 %sort.1.refs_0_ = f32[56,4096]{1,0:T(8,128)S(1)} custom-call(f32[1,4096]{1,0:T(1,128)S(1)} %get-tuple-element.35.rank_ref, f32[56,4096]{1,0:T(8,128)S(1)} %get-tuple-element.36.refs_0_.refs_3_, f32[1,128]{1,0:T(1,128)S(1)} %get-tuple-element.37.refs_1_), custom_call_target="tpu_custom_call" | custom-call | flops 3758096384 | bytes 1835008 | tf_op jit(solution)/shard_map/sort/pallas_call | solution.py:236
  27.4 0.1 collective-permute-start
  27.5 1.0 collective-permute-start.1
  28.5 0.1 constant_dynamic-slice_fusion
  28.5 0.1 copy.25
  28.6 0.1 copy.20
  28.7 0.1 reshape.40.refs_2_
  28.8 0.1 copy.21
  28.9 0.1 reshape.41.refs_3_
  29.0 0.1 broadcast_in_dim.3
  29.1 0.1 broadcast_in_dim_reshape.3.refs_4_
  29.3 0.1 tile.10.refs_5_
  29.4 2.2 %pad_bitcast_fusion = f32[56,128,32]{1,2,0:T(8,128)} fusion(f32[54,32,128]{2,1,0:T(8,128)} %param.11), kind=kLoop, calls=%fused_computation | loop fusion | bytes 1802240 | tf_op jit(solution)/shard_map/transpose | solution.py:666
  31.6 4.0 %copy.19 = f32[56,128,32]{0,2,1:T(8,128)} copy(f32[56,128,32]{1,2,0:T(8,128)} %pad_bitcast_fusion) | data formatting | bytes 1835008 | tf_op jit(solution)/shard_map/transpose | solution.py:666
  35.6 0.0 collective-permute-done.refs_1_
  35.6 12.7 %collect.2 = (f32[56,12288]{1,0:T(8,128)S(1)}, f32[8,4096]{1,0:T(8,128)S(1)}, f32[8,4096]{1,0:T(8,128)S(1)}) custom-call(f32[56,4096]{1,0:T(8,128)S(1)} %sort.1.refs_0_, f32[56,4096]{1,0:T(8,128)} %collective-permute-done.refs_1_, f32[32,128]{1,0:T(8,128)S(1)} %bitcast.19), custom_call_target="tpu_custom_call" | custom-call | flops 2650800128 | tf_op jit(solution)/shard_map/collect/pallas_call | solution.py:338
  48.3 1.5 copy-done.1
  49.9 0.4 collective-permute-done.1.refs_0_
  50.2 0.0 collective-permute-start.2
  50.2 2.2 %copy.22.refs_1_ = f32[56,4096]{1,0:T(8,128)S(1)} copy(f32[56,4096]{0,1:T(8,128)} %bitcast.24) | data formatting | bytes 1835008 | tf_op jit(solution)/shard_map/optimization_barrier | solution.py:674
  52.4 0.4 collective-permute-done.2.refs_1_
  52.8 1.8 copy-done.2
  54.6 12.8 %collect.3 = (f32[56,12288]{1,0:T(8,128)S(1)}, f32[8,4096]{1,0:T(8,128)S(1)}, f32[8,4096]{1,0:T(8,128)S(1)}) custom-call(f32[56,4096]{1,0:T(8,128)S(1)} %collective-permute-done.1.refs_0_, f32[56,4096]{1,0:T(8,128)} %collective-permute-done.2.refs_1_, f32[32,128]{1,0:T(8,128)S(1)} %bitcast.20, f32[56,12288]{1,0:T(8,128)S(1)} %copy-done.2), custom_call_target="tpu_custom_call", output_to_operand_aliasing={{0}: (3, {})} | custom-call | flops 2650800128 | tf_op jit(solution)/shard_map/collect/pallas_call | solution.py:338
  67.5 1.5 copy-done.3
  69.0 1.8 copy-done.4
  70.8 66.2 %middle.1 = (f32[56,4096]{1,0:T(8,128)S(1)}, f32[56,4096]{1,0:T(8,128)S(1)}, f32[56,4096]{1,0:T(8,128)S(1)}) custom-call(f32[56,12288]{1,0:T(8,128)S(1)} %copy-done.4, f32[56,4096]{1,0:T(8,128)S(1)} %copy.22.refs_1_, f32[1,4096]{1,0:T(1,128)S(1)} %reshape.40.refs_2_, f32[1,4096]{1,0:T(1,128)S(1)} %reshape.41.refs_3_, ...), custom_call_target="tpu_custom_call" | custom-call | tf_op jit(solution)/shard_map/middle/pallas_call | solution.py:624
  137.0 7.9 %project.2 = (f32[56,4096]{1,0:T(8,128)S(1)}, f32[56,4096]{1,0:T(8,128)S(1)}) custom-call(f32[56,4096]{1,0:T(8,128)S(1)} %get-tuple-element.60.refs_0_, f32[56,4096]{1,0:T(8,128)S(1)} %get-tuple-element.61.refs_1_, f32[56,4096]{1,0:T(8,128)S(1)} %get-tuple-element.62.refs_2_, f32[8,4096]{1,0:T(8,128)S(1)} %get-tuple-element.56.refs_3_, ...), custom_call_target="tpu_custom_call" | custom-call | flops 2650800128 | tf_op jit(solution)/shard_map/project/pallas_call | solution.py:404
  144.8 0.1 collective-permute-start.3
  144.9 2.5 %collective-permute-done.3 = f32[56,4096]{1,0:T(8,128)S(1)} collective-permute-done((f32[56,4096]{1,0:T(8,128)S(1)}, f32[56,4096]{1,0:T(8,128)S(1)}, u32[]{:S(2)}, u32[]{:S(2)}) %collective-permute-start.3) | collective-permute-done | bytes 917536 | tf_op jit(solution)/shard_map/ppermute | solution.py:25
  147.4 1.0 add.11
  148.4 8.8 %project.3 = (f32[56,4096]{1,0:T(8,128)S(1)}, f32[56,4096]{1,0:T(8,128)}) custom-call(f32[56,4096]{1,0:T(8,128)S(1)} %get-tuple-element.60.refs_0_, f32[56,4096]{1,0:T(8,128)S(1)} %get-tuple-element.61.refs_1_, f32[56,4096]{1,0:T(8,128)S(1)} %get-tuple-element.62.refs_2_, f32[8,4096]{1,0:T(8,128)S(1)} %get-tuple-element.63.refs_3_, ...), custom_call_target="tpu_custom_call" | custom-call | flops 2650800128 | tf_op jit(solution)/shard_map/project/pallas_call | solution.py:404
  157.2 0.9 copy-done.9
  158.1 0.1 collective-permute-start.4
  158.3 0.7 collective-permute-start.5
  159.0 2.0 %copy.23 = f32[54,4096]{0,1:T(8,128)} copy(f32[54,4096]{1,0:T(8,128)S(1)} %bitcast.15) | data formatting | bytes 1769472 | tf_op jit(solution)/shard_map/slice | solution.py:680
  161.0 3.9 %copy.24 = f32[54,32,128]{2,1,0:T(8,128)} copy(f32[54,32,128]{0,1,2:T(8,128)} %bitcast.25) | data formatting | bytes 1769472
  164.9 16.3 %collective-permute-done.5.refs_2_ = f32[56,4096]{1,0:T(8,128)} collective-permute-done((f32[56,4096]{1,0:T(8,128)}, f32[56,4096]{1,0:T(8,128)}, u32[]{:S(2)}, u32[]{:S(2)}) %collective-permute-start.5) | collective-permute-done | bytes 917536 | tf_op jit(solution)/shard_map/ppermute | solution.py:25
  181.2 11.4 %unsort.1 = f32[1728,128]{1,0:T(8,128)} custom-call(f32[1,4096]{1,0:T(1,128)S(1)} %get-tuple-element.35.rank_ref, f32[56,4096]{1,0:T(8,128)S(1)} %copy-done.10, f32[56,4096]{1,0:T(8,128)S(1)} %collective-permute-done.4.refs_1_, f32[56,4096]{1,0:T(8,128)} %collective-permute-done.5.refs_2_, f32[56,4096]{1,0:T(8,128)S(1)} %get-tuple-element.36.refs_0_.refs_3_), custom_call_target="tpu_custom_call" | custom-call | flops 3758096384 | bytes 1835008 | tf_op jit(solution)/shard_map/unsort/pallas_call | solution.py:236
  (19 shorter events, 0.1 us)
Async XLA Ops:
  0.6 27.8 %copy-start = (f32[128,128]{1,0:T(8,128)S(1)}, f32[128,128]{1,0:T(8,128)}, u32[]{:S(2)}) copy-start(f32[128,128]{1,0:T(8,128)} %param.14) | copy-start | bytes 196612
  0.6 1.2 copy-start.5
  1.8 0.7 copy-start.6
  2.6 0.7 copy-start.7
  3.3 0.7 copy-start.8
  14.3 14.3 %copy-start.12 = (f32[32,128]{1,0:T(8,128)S(1)}, f32[32,128]{1,0:T(8,128)}, u32[]{:S(2)}) copy-start(f32[32,128]{1,0:T(8,128)} %param.17) | copy-start | bytes 49156
  14.3 14.5 %copy-start.13 = (f32[32,128]{1,0:T(8,128)S(1)}, f32[32,128]{1,0:T(8,128)}, u32[]{:S(2)}) copy-start(f32[32,128]{1,0:T(8,128)} %param.18) | copy-start | bytes 49156
  14.3 14.7 %copy-start.14 = (s32[128]{0:T(128)S(1)}, s32[128]{0:T(128)}, u32[]{:S(2)}) copy-start(s32[128]{0:T(128)} %param.19) | copy-start | bytes 1540
  14.3 14.9 %copy-start.11 = (f32[54,54]{1,0:T(8,128)S(1)}, f32[54,54]{1,0:T(8,128)}, u32[]{:S(2)}) copy-start(f32[54,54]{1,0:T(8,128)} %param.16) | copy-start | bytes 34996
  27.4 8.3 %collective-permute-start = (f32[56,4096]{1,0:T(8,128)S(1)}, f32[56,4096]{1,0:T(8,128)}, u32[]{:S(2)}, u32[]{:S(2)}) collective-permute-start(f32[56,4096]{1,0:T(8,128)S(1)} %sort.1.refs_0_), channel_id=1, source_target_pairs={{0,1},{1,0},{2,3},{3,2},{4,5},{5,4},{6,7},{7,6},{8,9},{9,8},{10,11... | collective-permute-start | bytes 2752520 | tf_op jit(solution)/shard_map/ppermute | solution.py:25
  27.5 22.8 %collective-permute-start.1 = (f32[56,4096]{1,0:T(8,128)S(1)}, f32[56,4096]{1,0:T(8,128)S(1)}, u32[]{:S(2)}, u32[]{:S(2)}) collective-permute-start(f32[56,4096]{1,0:T(8,128)S(1)} %sort.1.refs_0_), channel_id=1, source_target_pairs={{0,2},{1,3},{2,0},{3,1},{4,6},{5,7},{6,4},{7,5},{8,10},{9,11},{10,... | collective-permute-start | bytes 2752520 | tf_op jit(solution)/shard_map/ppermute | solution.py:25
  48.3 1.5 copy-start.1
  50.2 2.6 %collective-permute-start.2 = (f32[56,4096]{1,0:T(8,128)S(1)}, f32[56,4096]{1,0:T(8,128)}, u32[]{:S(2)}, u32[]{:S(2)}) collective-permute-start(f32[56,4096]{1,0:T(8,128)S(1)} %collective-permute-done.1.refs_0_), channel_id=1, source_target_pairs={{0,1},{1,0},{2,3},{3,2},{4,5},{5,4},{6,7},{7,6},{8,9},{9,8},{10,11... | collective-permute-start | bytes 2752520 | tf_op jit(solution)/shard_map/ppermute | solution.py:25
  52.8 1.8 copy-start.2
  67.5 1.5 copy-start.3
  69.0 1.8 copy-start.4
  144.8 2.5 %collective-permute-start.3 = (f32[56,4096]{1,0:T(8,128)S(1)}, f32[56,4096]{1,0:T(8,128)S(1)}, u32[]{:S(2)}, u32[]{:S(2)}) collective-permute-start(f32[56,4096]{1,0:T(8,128)S(1)} %get-tuple-element.59), channel_id=1, source_target_pairs={{0,1},{1,0},{2,3},{3,2},{4,5},{5,4},{6,7},{7,6},{8,9},{9,8},{10,11... | collective-permute-start | bytes 2752520 | tf_op jit(solution)/shard_map/ppermute | solution.py:25
  157.2 0.9 copy-start.9
  158.1 6.8 %collective-permute-start.4 = (f32[56,4096]{1,0:T(8,128)}, f32[56,4096]{1,0:T(8,128)S(1)}, u32[]{:S(2)}, u32[]{:S(2)}) collective-permute-start(f32[56,4096]{1,0:T(8,128)} %get-tuple-element.66), channel_id=1, source_target_pairs={{0,1},{1,0},{2,3},{3,2},{4,5},{5,4},{6,7},{7,6},{8,9},{9,8},{10,11... | collective-permute-start | bytes 2752520 | tf_op jit(solution)/shard_map/ppermute | solution.py:25
  158.3 22.9 %collective-permute-start.5 = (f32[56,4096]{1,0:T(8,128)}, f32[56,4096]{1,0:T(8,128)}, u32[]{:S(2)}, u32[]{:S(2)}) collective-permute-start(f32[56,4096]{1,0:T(8,128)} %add.11), channel_id=1, source_target_pairs={{0,2},{1,3},{2,0},{3,1},{4,6},{5,7},{6,4},{7,5},{8,10},{9,11},{10,... | collective-permute-start | bytes 2752520 | tf_op jit(solution)/shard_map/ppermute | solution.py:25
  161.0 20.2 %copy-start.10 = (f32[56,4096]{1,0:T(8,128)S(1)}, f32[56,4096]{1,0:T(8,128)}, u32[]{:S(2)}) copy-start(f32[56,4096]{1,0:T(8,128)} %copy-done.9) | copy-start | bytes 2752516

commit v5 on v4

--- a/solution.py
+++ b/solution.py
@@ -92,8 +92,15 @@
 
 
 def head_kernel(grid_shape, cells, nshape, tiles, span, *refs):
-    les_ref, map_ref, shape_ref, diff_ref, t_ref, rank_ref, table_ref, key_ref, *refs = refs
-    faces, halos, (send, recv) = refs[:4], refs[4:8], refs[8:]
+    given, (t_ref, rank_ref, table_ref), refs = refs[:4], refs[4:7], refs[7:]
+    les_ref, map_ref, shape_ref, diff_ref, key_ref, *refs = refs
+    faces, halos, (send, recv, load) = refs[:4], refs[4:8], refs[8:]
+    loads = [
+        pltpu.make_async_copy(source, target, load.at[n])
+        for n, (source, target) in enumerate(zip(given, (les_ref, map_ref, shape_ref, diff_ref)))
+    ]
+    for copy in loads:
+        copy.start()
     species, nx, ny = grid_shape
     count = rank_ref.shape[1]
     slab, nslab = lax.axis_index("slab"), lax.axis_size("slab")
@@ -112,6 +119,8 @@
         def _(n=n):
             halos[n][...] = jnp.zeros_like(halos[n])
 
+    for copy in loads:
+        copy.wait()
     line = lambda x, y: les_ref[pl.ds(x * ny + y, species, stride=nx * ny), :]
     for n, x in enumerate((0, nx - 1)):
         for y in range(ny):
@@ -173,10 +182,16 @@
             jax.ShapeDtypeStruct((1, count), F32),
             jax.ShapeDtypeStruct((1, LANES), F32),
         ],
-        in_specs=[VMEM] * 4,
+        in_specs=[pl.BlockSpec(memory_space=pltpu.HBM)] * 4,
         out_specs=[VMEM] * 3,
-        scratch_shapes=[pltpu.VMEM((8, count), F32)] + halo * 2 + [pltpu.SemaphoreType.DMA((4,))] * 2,
-        compiler_params=pltpu.CompilerParams(vmem_limit_bytes=12 << 20, collective_id=2, has_side_effects=True),
+        scratch_shapes=[
+            pltpu.VMEM((species * nx * ny, nz), F32),
+            pltpu.VMEM((1, count), jnp.int32),
+            pltpu.VMEM((1, count), jnp.int32),
+            pltpu.VMEM((1, species), F32),
+            pltpu.VMEM((8, count), F32),
+        ] + halo * 2 + [pltpu.SemaphoreType.DMA((4,))] * 3,
+        compiler_params=pltpu.CompilerParams(vmem_limit_bytes=60 << 20, collective_id=2, has_side_effects=True),
         name="head",
     )(
         les_state.reshape(species * nx * ny, nz), cmc_map.reshape(1, count), pdf_index.reshape(1, count),
@@ -277,18 +292,16 @@
     lax.fori_loop(0, source.shape[1] // LANES, step, 0, unroll=4)
 
 
-def collect_kernel(species, bins, per_tile, pairs, lists, first, *refs):
+def collect_kernel(species, bins, per_tile, pairs, lists, *refs):
     sources, refs = refs[:lists], refs[lists:]
-    table_ref, *refs = refs
-    acc_ref = None if first else refs.pop(0)
-    out_ref, *refs = refs
+    table_ref, out_ref, *refs = refs
     keys, (weights, tiles, parts, steps, sems) = refs[:lists], refs[lists:]
     copies = fetch_rows(sources, steps, sems)
     for key, source in zip(keys, sources):
         key[...] = source[source.shape[0] - 8 :, :]
     rows, count = sources[0].shape
     blocks = count // LANES
-    out_ref[...] = jnp.zeros_like(out_ref) if first else acc_ref[...]
+    out_ref[...] = jnp.zeros_like(out_ref)
     table = split_table(table_ref[...])
     line = lax.broadcasted_iota(jnp.int32, (rows, LANES), 0)
     for number, source in enumerate(sources):
@@ -324,19 +337,14 @@
     lax.fori_loop(0, -(-pairs // GROUP), step, 0)
 
 
-def collect_call(sources, table, acc, species, bins, per_tile, ntiles):
+def collect_call(sources, table, species, bins, per_tile, ntiles):
     rows, count = sources[0].shape
     lists, blocks = len(sources), count // LANES
     pairs = blocks + ntiles - 1
     args = list(sources) + [table]
     specs = [VMEM] * (lists + 1)
-    alias = {}
-    if acc is not None:
-        alias = {len(args): 0}
-        args.append(acc)
-        specs.append(VMEM)
     return pl.pallas_call(
-        functools.partial(collect_kernel, species, bins, per_tile, pairs, lists, acc is None),
+        functools.partial(collect_kernel, species, bins, per_tile, pairs, lists),
         out_shape=[jax.ShapeDtypeStruct((rows, ntiles * TILE), F32)] + [jax.ShapeDtypeStruct((8, count), F32)] * lists,
         in_specs=specs,
         out_specs=[VMEM] * (lists + 1),
@@ -347,7 +355,6 @@
             pltpu.SMEM((lists, 8, LANES), F32),
             pltpu.SemaphoreType.DMA((lists,)),
         ],
-        input_output_aliases=alias,
         compiler_params=params(19),
         cost_estimate=pl.CostEstimate(flops=lists * pairs * 2 * LANES * TILE * TILE, bytes_accessed=0, transcendentals=0),
         name="collect",
@@ -420,9 +427,9 @@
 
 
 def middle_kernel(species, bins, chunk, refs_in, refs_out, scratch):
-    acc_ref, old_ref, diss_ref, rate_ref, count_ref, matrix_ref = refs_in
+    *accs, old_ref, diss_ref, rate_ref, count_ref, matrix_ref = refs_in
     fresh_ref, next_ref, far_ref = refs_out
-    hopped, summed, got, state_ref, edge_out, edge_in, side_in, pick_ref, third_ref, send, recv, side_send, side_recv = scratch
+    outward, hopped, summed, got, state_ref, edge_out, edge_in, side_in, pick_ref, third_ref, send, recv, side_send, side_recv = scratch
     rows, width = fresh_ref.shape
     steps = width // chunk
     slab, nslab = lax.axis_index("slab"), lax.axis_size("slab")
@@ -437,6 +444,14 @@
     has_down, has_up = slab > 0, slab < nslab - 1
     mesh = pl.DeviceIdType.MESH
 
+    def partial_sum(piece):
+        total = accs[0][:, piece]
+        for more in accs[1:]:
+            total = total + more[:, piece]
+        return total
+
+    outward[...] = partial_sum(slice(0, width))
+
     @pl.when(jnp.logical_not(has_inner))
     def _():
         hopped[...] = jnp.zeros_like(hopped)
@@ -482,7 +497,7 @@
             device_id=where, device_id_type=mesh,
         )
 
-    to_outer = lambda c: remote(0, c, acc_ref.at[:, lanes(c)], hopped.at[:, lanes(c)], {"slab": outer})
+    to_outer = lambda c: remote(0, c, outward.at[:, lanes(c)], hopped.at[:, lanes(c)], {"slab": outer})
     to_partner = lambda c: remote(1, c, summed.at[:, lanes(c)], got.at[:, lanes(c)], {"slab": partner})
     to_after = lambda c: remote(2, c, edge_out.at[c, :, LANES:], edge_in.at[c, :, :LANES], {"cross": cross + 1})
     to_before = lambda c: remote(3, c, edge_out.at[c, :, :LANES], edge_in.at[c, :, LANES:], {"cross": cross - 1})
@@ -498,13 +513,13 @@
     to_up = side(0, old_ref.at[:, width - LANES : width], {"slab": slab + 1})
     to_down = side(1, old_ref.at[:, :LANES], {"slab": slab - 1})
 
+    pl.when(has_up)(to_up.start)
+    pl.when(has_down)(to_down.start)
+
     @pl.when(has_outer)
     def _():
         for c in range(steps):
             to_outer(c).start()
-
-    pl.when(has_up)(to_up.start)
-    pl.when(has_down)(to_down.start)
 
     lane = lax.broadcasted_iota(jnp.int32, (2 * LANES, chunk), 1)
     row = lax.broadcasted_iota(jnp.int32, (2 * LANES, chunk), 0)
@@ -524,7 +539,7 @@
 
     def add_hop(c):
         pl.when(has_inner)(lambda: to_outer(c).wait_recv())
-        summed[:, lanes(c)] = acc_ref[:, lanes(c, 2 * width)] + hopped[:, lanes(c)]
+        summed[:, lanes(c)] = partial_sum(lanes(c, 2 * width)) + hopped[:, lanes(c)]
 
     def advect(c):
         here = old_ref[:, lanes(c)]
@@ -539,7 +554,7 @@
         return here - 0.4 * (here - left) + 0.1 * (right - 2.0 * here + left)
 
     def blend(c):
-        total = acc_ref[:, lanes(c, width)] + got[:, lanes(c)]
+        total = partial_sum(lanes(c, width)) + got[:, lanes(c)]
         blended = (total + advect(c)) / (total[species : species + 1] + 1.0)
         state_ref[:, lanes(c)] = blended
         edge = lax.dot_general(stacked(blended), pick_ref[...], NT, preferred_element_type=F32)
@@ -614,26 +629,27 @@
     pl.when(has_down)(to_down.wait_send)
 
 
-def middle_call(acc, old, diss, rate, count, matrix, species, bins, chunk=512):
+def middle_call(accs, old, diss, rate, count, matrix, species, bins, chunk=512):
     rows, width = old.shape
     steps = width // chunk
+    given = len(accs) + 5
 
     def kernel(*refs):
-        middle_kernel(species, bins, chunk, refs[:6], refs[6:9], refs[9:])
+        middle_kernel(species, bins, chunk, refs[:given], refs[given : given + 3], refs[given + 3 :])
 
     return pl.pallas_call(
         kernel,
         out_shape=[jax.ShapeDtypeStruct((rows, width), F32)] * 3,
-        in_specs=[VMEM] * 6,
+        in_specs=[VMEM] * given,
         out_specs=[VMEM] * 3,
-        scratch_shapes=[pltpu.VMEM((rows, width), F32)] * 4
+        scratch_shapes=[pltpu.VMEM((rows, width), F32)] * 5
         + [pltpu.VMEM((steps, rows, 2 * LANES), F32)] * 2
         + [pltpu.VMEM((2, rows, LANES), F32), pltpu.VMEM((2 * LANES, chunk), BF16), pltpu.VMEM(matrix.shape, BF16)]
         + [pltpu.SemaphoreType.DMA((6, steps))] * 2
         + [pltpu.SemaphoreType.DMA((2,))] * 2,
-        compiler_params=pltpu.CompilerParams(vmem_limit_bytes=16 << 20, collective_id=1, has_side_effects=True),
+        compiler_params=pltpu.CompilerParams(vmem_limit_bytes=20 << 20, collective_id=1, has_side_effects=True),
         name="middle",
-    )(acc, old, diss, rate, count, matrix)
+    )(*accs, old, diss, rate, count, matrix)
 
 
 def on_device(
@@ -669,12 +685,14 @@
     extra = rows - species
     matrix = jnp.tile(jnp.pad(chem_matrix, ((0, extra), (0, -(-rows // 16) * 16 - species))), (1, 3))
     terms = (state, wide(dissipation), wide(reaction_rate), jnp.repeat(substeps, bins)[None, :], matrix)
-    acc, *near_keys = collect_call(near_lists, table, None, species, bins, per_tile, ntiles)
+    acc, *near_keys = collect_call(near_lists, table, species, bins, per_tile, ntiles)
+    accs = [acc]
     if bits:
-        acc, far_lists, terms = lax.optimization_barrier((acc, far_lists, terms))
+        accs, far_lists, terms = lax.optimization_barrier((accs, far_lists, terms))
         far_lists = list(far_lists) + [swap(far_lists[0], "cross", bit) for bit in bits[:-1]]
-        acc, *far_keys = collect_call(far_lists, table, acc, species, bins, per_tile, ntiles)
-    means = middle_call(acc, *terms, species, bins)
+        acc, *far_keys = collect_call(far_lists, table, species, bins, per_tile, ntiles)
+        accs = list(accs) + [acc]
+    means = middle_call(accs, *terms, species, bins)
     fresh = means[0]
     means = [means[2], means[0], means[1]]
     cmc_out = fresh[:species].reshape(species, cells, bins).transpose(0, 2, 1)

time: 194 us -> 176 us (0.907)
  Pallas kernels: 143 us -> 131 us
  local copies, waits for them, and re-layouts: 26 us -> 20.1 us
    pallas_call x1, Pallas kernels: 66.2 us -> 54.7 us  [middle_call(): pl.pallas_call(kernel, out_shape=[jax.ShapeDtypeStruct((rows, width), F32...]
    unnamed x32 -> x30, local copies, waits for them, and re-layouts: 14.8 us -> 8.92 us
    pallas_call x2, Pallas kernels: 25.5 us -> 23 us  [collect_call(): pl.pallas_call(functools.partial(collect_kernel, species, bins, per_tile,...]
    pallas_call x1, Pallas kernels: 10.3 us -> 12.5 us  [head_call(): pl.pallas_call(functools.partial(head_kernel, (species, nx, ny), cells, n...]
  transfers between devices with their start and end apart: 6 -> 6, of which waited for: 4 -> 4; matrix products, arithmetic and copies ran while one was open for 8% -> 9% of each run, Pallas kernels for 7% -> 7%
where the time goes in v5:
time: 176 us
  Pallas kernels  131 us (74%)
  waiting for transfers between devices  20.3 us (12%)
  local copies, waits for them, and re-layouts  20.1 us (11%)
  starting transfers between devices  2.23 us (1%)
    pallas_call x1, Pallas kernels, middle_call(): pl.pallas_call(kernel, out_shape=[jax.ShapeDtypeStruct((rows, width), F32...  54.7 us
    pallas_call x2, Pallas kernels, permute_call(): pl.pallas_call(functools.partial(permute_kernel, back, len(args)), grid=(...  24.4 us
    pallas_call x2, Pallas kernels, collect_call(): pl.pallas_call(functools.partial(collect_kernel, species, bins, per_tile,...  23 us
    ppermute x6, waiting for transfers between devices, swap(): return lax.ppermute(array, axis, [(i, i ^ bit) for i in range(count)])  20.3 us
    pallas_call x2, Pallas kernels, project_call(): pl.pallas_call(functools.partial(project_kernel, bins, per_tile, pairs, l...  16.6 us
    pallas_call x1, Pallas kernels, head_call(): pl.pallas_call(functools.partial(head_kernel, (species, nx, ny), cells, n...  12.5 us
    unnamed x30, local copies, waits for them, and re-layouts  8.92 us
    transpose x2, local copies, waits for them, and re-layouts, on_device(): spread = lambda a: a.transpose(0, 2, 1).reshape(a.shape[0], width)  6.22 us
  transfers between devices with their start and end apart: 6, of which 4 were waited for; matrix products, arithmetic and copies ran while one was open for 9% of the time, Pallas kernels for 7%

profile of v5, /device:TPU:2, one launch (start us, length us, event | category | flops | bytes accessed | tf_op | source)
XLA Modules:
  0.0 175.9 jit_solution(13949669105517301238)
XLA Ops:
  0.6 0.0 copy-start
  0.6 12.5 %head.1 = (f32[56,4096]{1,0:T(8,128)}, f32[1,4096]{1,0:T(1,128)}, f32[1,128]{1,0:T(1,128)}) custom-call(f32[1728,128]{1,0:T(8,128)} %bitcast.22, s32[1,4096]{1,0:T(1,128)} %bitcast.23, s32[1,4096]{1,0:T(1,128)} %bitcast.24, f32[1,54]{1,0:T(1,128)} %bitcast.27), custom_call_target="tpu_custom_call" | custom-call | tf_op jit(solution)/shard_map/head/pallas_call | solution.py:178
  13.2 0.0 copy-start.3
  13.2 1.2 copy-done.3
  14.4 0.7 copy-done.5
  15.1 0.6 copy-done.7
  15.7 13.0 %sort.1.refs_0_ = f32[56,4096]{1,0:T(8,128)S(1)} custom-call(f32[1,4096]{1,0:T(1,128)S(1)} %copy-done.5, f32[56,4096]{1,0:T(8,128)S(1)} %copy-done.3, f32[1,128]{1,0:T(1,128)S(1)} %copy-done.7), custom_call_target="tpu_custom_call" | custom-call | flops 3758096384 | bytes 1835008 | tf_op jit(solution)/shard_map/sort/pallas_call | solution.py:251
  28.7 0.1 collective-permute-start
  28.8 1.0 collective-permute-start.1
  29.8 0.0 copy-done
  29.8 0.1 constant_dynamic-slice_fusion
  29.8 0.1 copy.24
  29.9 0.0 copy-done.11
  29.9 0.1 copy.19
  30.0 0.1 reshape.40.refs_3_
  30.1 0.0 copy-done.12
  30.1 0.1 copy.20
  30.2 0.1 reshape.41.refs_4_
  30.4 0.1 broadcast_in_dim.3
  30.4 0.1 broadcast_in_dim_reshape.3.refs_5_
  30.6 0.1 tile.10.refs_6_
  30.7 2.2 %pad_bitcast_fusion = f32[56,128,32]{1,2,0:T(8,128)} fusion(f32[54,32,128]{2,1,0:T(8,128)} %param.11), kind=kLoop, calls=%fused_computation | loop fusion | bytes 1802240 | tf_op jit(solution)/shard_map/transpose | solution.py:682
  32.9 4.0 %copy.18 = f32[56,128,32]{0,2,1:T(8,128)} copy(f32[56,128,32]{1,2,0:T(8,128)} %pad_bitcast_fusion) | data formatting | bytes 1835008 | tf_op jit(solution)/shard_map/transpose | solution.py:682
  36.9 0.0 collective-permute-done.refs_1_
  36.9 11.5 %collect.2 = (f32[56,12288]{1,0:T(8,128)S(1)}, f32[8,4096]{1,0:T(8,128)S(1)}, f32[8,4096]{1,0:T(8,128)S(1)}) custom-call(f32[56,4096]{1,0:T(8,128)S(1)} %sort.1.refs_0_, f32[56,4096]{1,0:T(8,128)S(1)} %collective-permute-done.refs_1_, f32[32,128]{1,0:T(8,128)S(1)} %bitcast.16), custom_call_target="tpu_custom_call" | custom-call | flops 2650800128 | tf_op jit(solution)/shard_map/collect/pallas_call | solution.py:346
  48.5 0.0 copy-start.1
  48.5 1.5 copy-done.1
  50.0 1.5 collective-permute-done.1.refs_0_
  51.5 0.0 collective-permute-start.2
  51.5 2.2 %copy.21.refs_2_ = f32[56,4096]{1,0:T(8,128)S(1)} copy(f32[56,4096]{0,1:T(8,128)} %bitcast.20) | data formatting | bytes 1835008 | tf_op jit(solution)/shard_map/optimization_barrier | solution.py:691
  53.7 0.3 collective-permute-done.2.refs_1_
  54.0 11.5 %collect.3 = (f32[56,12288]{1,0:T(8,128)S(1)}, f32[8,4096]{1,0:T(8,128)S(1)}, f32[8,4096]{1,0:T(8,128)S(1)}) custom-call(f32[56,4096]{1,0:T(8,128)S(1)} %collective-permute-done.1.refs_0_, f32[56,4096]{1,0:T(8,128)S(1)} %collective-permute-done.2.refs_1_, f32[32,128]{1,0:T(8,128)S(1)} %bitcast.17), custom_call_target="tpu_custom_call" | custom-call | flops 2650800128 | tf_op jit(solution)/shard_map/collect/pallas_call | solution.py:346
  65.5 54.7 %middle.1 = (f32[56,4096]{1,0:T(8,128)S(1)}, f32[56,4096]{1,0:T(8,128)S(1)}, f32[56,4096]{1,0:T(8,128)S(1)}) custom-call(f32[56,12288]{1,0:T(8,128)S(1)} %copy-done.2, f32[56,12288]{1,0:T(8,128)S(1)} %get-tuple-element.47.refs_1_, f32[56,4096]{1,0:T(8,128)S(1)} %copy.21.refs_2_, f32[1,4096]{1,0:T(1,128)S(1)} %reshape.40.refs_3_, ...), custom_call_target="tpu_custom_call" | custom-call | tf_op jit(solution)/shard_map/middle/pallas_call | solution.py:640
  120.3 7.9 %project.2 = (f32[56,4096]{1,0:T(8,128)S(1)}, f32[56,4096]{1,0:T(8,128)S(1)}) custom-call(f32[56,4096]{1,0:T(8,128)S(1)} %get-tuple-element.60.refs_0_, f32[56,4096]{1,0:T(8,128)S(1)} %get-tuple-element.61.refs_1_, f32[56,4096]{1,0:T(8,128)S(1)} %get-tuple-element.62.refs_2_, f32[8,4096]{1,0:T(8,128)S(1)} %get-tuple-element.56.refs_3_, ...), custom_call_target="tpu_custom_call" | custom-call | flops 2650800128 | tf_op jit(solution)/shard_map/project/pallas_call | solution.py:411
  128.1 0.1 collective-permute-start.3
  128.2 2.5 %collective-permute-done.3 = f32[56,4096]{1,0:T(8,128)S(1)} collective-permute-done((f32[56,4096]{1,0:T(8,128)S(1)}, f32[56,4096]{1,0:T(8,128)S(1)}, u32[]{:S(2)}, u32[]{:S(2)}) %collective-permute-start.3) | collective-permute-done | bytes 917536 | tf_op jit(solution)/shard_map/ppermute | solution.py:25
  130.7 1.0 add.11
  131.7 8.8 %project.3 = (f32[56,4096]{1,0:T(8,128)S(1)}, f32[56,4096]{1,0:T(8,128)}) custom-call(f32[56,4096]{1,0:T(8,128)S(1)} %get-tuple-element.60.refs_0_, f32[56,4096]{1,0:T(8,128)S(1)} %get-tuple-element.61.refs_1_, f32[56,4096]{1,0:T(8,128)S(1)} %get-tuple-element.62.refs_2_, f32[8,4096]{1,0:T(8,128)S(1)} %get-tuple-element.63.refs_3_, ...), custom_call_target="tpu_custom_call" | custom-call | flops 2650800128 | tf_op jit(solution)/shard_map/project/pallas_call | solution.py:411
  140.5 0.0 copy-start.8
  140.5 0.9 copy-done.8
  141.4 0.1 collective-permute-start.4
  141.5 1.0 collective-permute-start.5
  142.5 2.0 %copy.22 = f32[54,4096]{0,1:T(8,128)} copy(f32[54,4096]{1,0:T(8,128)S(1)} %bitcast.15) | data formatting | bytes 1769472 | tf_op jit(solution)/shard_map/slice | solution.py:698
  144.5 3.9 %copy.23 = f32[54,32,128]{2,1,0:T(8,128)} copy(f32[54,32,128]{0,1,2:T(8,128)} %bitcast.21) | data formatting | bytes 1769472
  148.4 0.0 collective-permute-done.4.refs_1_
  148.4 16.1 %collective-permute-done.5.refs_2_ = f32[56,4096]{1,0:T(8,128)} collective-permute-done((f32[56,4096]{1,0:T(8,128)}, f32[56,4096]{1,0:T(8,128)}, u32[]{:S(2)}, u32[]{:S(2)}) %collective-permute-start.5) | collective-permute-done | bytes 917536 | tf_op jit(solution)/shard_map/ppermute | solution.py:25
  164.5 0.0 copy-done.4
  164.5 11.4 %unsort.1 = f32[1728,128]{1,0:T(8,128)} custom-call(f32[1,4096]{1,0:T(1,128)S(1)} %copy-done.6, f32[56,4096]{1,0:T(8,128)S(1)} %copy-done.9, f32[56,4096]{1,0:T(8,128)S(1)} %collective-permute-done.4.refs_1_, f32[56,4096]{1,0:T(8,128)} %collective-permute-done.5.refs_2_, f32[56,4096]{1,0:T(8,128)S(1)} %copy-done.4), custom_call_target="tpu_custom_call" | custom-call | flops 3758096384 | bytes 1835008 | tf_op jit(solution)/shard_map/unsort/pallas_call | solution.py:251
  (17 shorter events, 0.1 us)
Async XLA Ops:
  0.6 29.1 %copy-start = (f32[128,128]{1,0:T(8,128)S(1)}, f32[128,128]{1,0:T(8,128)}, u32[]{:S(2)}) copy-start(f32[128,128]{1,0:T(8,128)} %param.14) | copy-start | bytes 196612
  13.2 1.2 copy-start.3
  14.4 0.7 copy-start.5
  15.1 0.6 copy-start.7
  15.6 14.2 %copy-start.11 = (f32[32,128]{1,0:T(8,128)S(1)}, f32[32,128]{1,0:T(8,128)}, u32[]{:S(2)}) copy-start(f32[32,128]{1,0:T(8,128)} %param.17) | copy-start | bytes 49156
  15.7 14.5 %copy-start.12 = (f32[32,128]{1,0:T(8,128)S(1)}, f32[32,128]{1,0:T(8,128)}, u32[]{:S(2)}) copy-start(f32[32,128]{1,0:T(8,128)} %param.18) | copy-start | bytes 49156
  15.7 14.7 %copy-start.13 = (s32[128]{0:T(128)S(1)}, s32[128]{0:T(128)}, u32[]{:S(2)}) copy-start(s32[128]{0:T(128)} %param.19) | copy-start | bytes 1540
  15.7 14.9 %copy-start.10 = (f32[54,54]{1,0:T(8,128)S(1)}, f32[54,54]{1,0:T(8,128)}, u32[]{:S(2)}) copy-start(f32[54,54]{1,0:T(8,128)} %param.16) | copy-start | bytes 34996
  28.7 8.2 %collective-permute-start = (f32[56,4096]{1,0:T(8,128)S(1)}, f32[56,4096]{1,0:T(8,128)S(1)}, u32[]{:S(2)}, u32[]{:S(2)}) collective-permute-start(f32[56,4096]{1,0:T(8,128)S(1)} %sort.1.refs_0_), channel_id=1, source_target_pairs={{0,1},{1,0},{2,3},{3,2},{4,5},{5,4},{6,7},{7,6},{8,9},{9,8},{10,11... | collective-permute-start | bytes 2752520 | tf_op jit(solution)/shard_map/ppermute | solution.py:25
  28.8 22.8 %collective-permute-start.1 = (f32[56,4096]{1,0:T(8,128)S(1)}, f32[56,4096]{1,0:T(8,128)S(1)}, u32[]{:S(2)}, u32[]{:S(2)}) collective-permute-start(f32[56,4096]{1,0:T(8,128)S(1)} %sort.1.refs_0_), channel_id=1, source_target_pairs={{0,2},{1,3},{2,0},{3,1},{4,6},{5,7},{6,4},{7,5},{8,10},{9,11},{10,... | collective-permute-start | bytes 2752520 | tf_op jit(solution)/shard_map/ppermute | solution.py:25
  48.5 1.5 copy-start.1
  51.5 2.5 %collective-permute-start.2 = (f32[56,4096]{1,0:T(8,128)S(1)}, f32[56,4096]{1,0:T(8,128)S(1)}, u32[]{:S(2)}, u32[]{:S(2)}) collective-permute-start(f32[56,4096]{1,0:T(8,128)S(1)} %collective-permute-done.1.refs_0_), channel_id=1, source_target_pairs={{0,1},{1,0},{2,3},{3,2},{4,5},{5,4},{6,7},{7,6},{8,9},{9,8},{10,11... | collective-permute-start | bytes 2752520 | tf_op jit(solution)/shard_map/ppermute | solution.py:25
  53.7 11.8 %copy-start.2 = (f32[56,12288]{1,0:T(8,128)S(1)}, f32[56,12288]{1,0:T(8,128)}, u32[]{:S(2)}) copy-start(f32[56,12288]{1,0:T(8,128)} %copy-done.1) | copy-start | bytes 8257540
  128.1 2.5 %collective-permute-start.3 = (f32[56,4096]{1,0:T(8,128)S(1)}, f32[56,4096]{1,0:T(8,128)S(1)}, u32[]{:S(2)}, u32[]{:S(2)}) collective-permute-start(f32[56,4096]{1,0:T(8,128)S(1)} %get-tuple-element.59), channel_id=1, source_target_pairs={{0,1},{1,0},{2,3},{3,2},{4,5},{5,4},{6,7},{7,6},{8,9},{9,8},{10,11... | collective-permute-start | bytes 2752520 | tf_op jit(solution)/shard_map/ppermute | solution.py:25
  140.5 0.9 copy-start.8
  141.4 7.0 %collective-permute-start.4 = (f32[56,4096]{1,0:T(8,128)}, f32[56,4096]{1,0:T(8,128)S(1)}, u32[]{:S(2)}, u32[]{:S(2)}) collective-permute-start(f32[56,4096]{1,0:T(8,128)} %get-tuple-element.66), channel_id=1, source_target_pairs={{0,1},{1,0},{2,3},{3,2},{4,5},{5,4},{6,7},{7,6},{8,9},{9,8},{10,11... | collective-permute-start | bytes 2752520 | tf_op jit(solution)/shard_map/ppermute | solution.py:25
  141.5 22.9 %collective-permute-start.5 = (f32[56,4096]{1,0:T(8,128)}, f32[56,4096]{1,0:T(8,128)}, u32[]{:S(2)}, u32[]{:S(2)}) collective-permute-start(f32[56,4096]{1,0:T(8,128)} %add.11), channel_id=1, source_target_pairs={{0,2},{1,3},{2,0},{3,1},{4,6},{5,7},{6,4},{7,5},{8,10},{9,11},{10,... | collective-permute-start | bytes 2752520 | tf_op jit(solution)/shard_map/ppermute | solution.py:25
  142.5 22.0 %copy-start.4 = (f32[56,4096]{1,0:T(8,128)S(1)}, f32[56,4096]{1,0:T(8,128)}, u32[]{:S(2)}) copy-start(f32[56,4096]{1,0:T(8,128)} %get-tuple-element.36.refs_0_.refs_3_) | copy-start | bytes 2752516
  142.5 22.0 %copy-start.6 = (f32[1,4096]{1,0:T(1,128)S(1)}, f32[1,4096]{1,0:T(1,128)}, u32[]{:S(2)}) copy-start(f32[1,4096]{1,0:T(1,128)} %get-tuple-element.35.rank_ref) | copy-start | bytes 49156
  144.5 20.0 %copy-start.9 = (f32[56,4096]{1,0:T(8,128)S(1)}, f32[56,4096]{1,0:T(8,128)}, u32[]{:S(2)}) copy-start(f32[56,4096]{1,0:T(8,128)} %copy-done.8) | copy-start | bytes 2752516

commit v6 on v5

--- a/solution.py
+++ b/solution.py
@@ -361,11 +361,42 @@
     )(*args)
 
 
-def project_kernel(bins, per_tile, pairs, lists, *refs):
+def turn_back(mean, out_ref, bins, quads, turned):
+    rows, width = mean.shape
+    lines = width // LANES
+    fold = LANES // bins
+    for q in range(lines):
+        quads[pl.ds(q, rows, stride=lines), :] = mean[:, q * LANES : (q + 1) * LANES]
+    blocked = lax.broadcasted_iota(jnp.int32, (lines, LANES), 1) // bins
+
+    def turn(g):
+        source = [quads[pl.ds(pl.multiple_of(g * LANES + k * lines, lines), lines), :] for k in range(fold)]
+        for r in range(fold):
+            out = source[r]
+            for k in range(fold):
+                if k != r:
+                    out = jnp.where(blocked == k, pltpu.roll(source[k], (k - r) * bins % LANES, 1), out)
+            turned[pl.ds(r, lines, stride=fold), :] = out
+        return turned[...].T
+
+    full, rest = out_ref.shape[0] // LANES, out_ref.shape[0] % LANES
+
+    def step(g, _):
+        out_ref[pl.ds(pl.multiple_of(g * LANES, LANES), LANES), :] = turn(g)
+        return 0
+
+    lax.fori_loop(0, full, step, 0)
+    if rest:
+        out_ref[full * LANES :, :] = turn(full)[:rest]
+
+
+def project_kernel(bins, per_tile, pairs, lists, state_rows, *refs):
     means, refs = refs[:3], refs[3:]
     sources, refs = refs[:lists], refs[lists:]
     table_ref, *refs = refs
-    outs, (weights, tiles, parts, steps, sems) = refs[:lists], refs[lists:]
+    outs, refs = refs[:lists], refs[lists:]
+    state_ref = refs.pop(0) if state_rows else None
+    weights, tiles, parts, steps, sems, *turning = refs
     copies = fetch_rows(sources, steps, sems)
     rows, count = outs[0].shape
     blocks = count // LANES
@@ -377,6 +408,8 @@
             return 0
 
         lax.fori_loop(0, per_mean, split, 0, unroll=2)
+    if state_rows:
+        turn_back(means[1], state_ref, bins, *turning)
     table = split_table(table_ref[...])
     for copy in copies:
         copy.wait()
@@ -403,23 +436,24 @@
     lax.fori_loop(0, -(-pairs // GROUP), step, 0)
 
 
-def project_call(means, sources, table, bins, per_tile, ntiles):
+def project_call(means, sources, table, bins, per_tile, ntiles, state_rows=0):
     rows, count = means[0].shape[0], sources[0].shape[1]
     lists = len(sources)
     blocks = count // LANES
     pairs = blocks + ntiles - 1
     return pl.pallas_call(
-        functools.partial(project_kernel, bins, per_tile, pairs, lists),
-        out_shape=[jax.ShapeDtypeStruct((rows, count), F32)] * lists,
+        functools.partial(project_kernel, bins, per_tile, pairs, lists, state_rows),
+        out_shape=[jax.ShapeDtypeStruct((rows, count), F32)] * lists
+        + [jax.ShapeDtypeStruct((state_rows, LANES), F32)] * bool(state_rows),
         in_specs=[VMEM] * (lists + 4),
-        out_specs=[VMEM] * lists,
+        out_specs=[VMEM] * (lists + bool(state_rows)),
         scratch_shapes=[
             pltpu.VMEM((lists * blocks, TILE, 2 * LANES), BF16),
             pltpu.VMEM((lists * blocks, 16, LANES), F32),
             pltpu.VMEM((ntiles, 2 * HALF, TILE), BF16),
             pltpu.SMEM((lists, 8, LANES), F32),
             pltpu.SemaphoreType.DMA((lists,)),
-        ],
+        ] + [pltpu.VMEM((rows * means[0].shape[1] // LANES, LANES), F32), pltpu.VMEM((LANES, LANES), F32)] * bool(state_rows),
         compiler_params=params(19),
         cost_estimate=pl.CostEstimate(flops=lists * pairs * 2 * LANES * TILE * TILE, bytes_accessed=0, transcendentals=0),
         name="project",
@@ -427,9 +461,9 @@
 
 
 def middle_kernel(species, bins, chunk, refs_in, refs_out, scratch):
-    *accs, old_ref, diss_ref, rate_ref, count_ref, matrix_ref = refs_in
+    *accs, cmc_ref, diss_ref, rate_ref, count_ref, matrix_ref = refs_in
     fresh_ref, next_ref, far_ref = refs_out
-    outward, hopped, summed, got, state_ref, edge_out, edge_in, side_in, pick_ref, third_ref, send, recv, side_send, side_recv = scratch
+    nat, quads, turned, side_out, load, outward, hopped, summed, got, state_ref, edge_out, edge_in, side_in, pick_ref, third_ref, send, recv, side_send, side_recv = scratch
     rows, width = fresh_ref.shape
     steps = width // chunk
     slab, nslab = lax.axis_index("slab"), lax.axis_size("slab")
@@ -450,6 +484,14 @@
             total = total + more[:, piece]
         return total
 
+    loads, start = [], 0
+    for n, source in enumerate((cmc_ref, diss_ref, rate_ref)):
+        target = nat.at[start : start + source.shape[0]]
+        loads.append(pltpu.make_async_copy(source, target, load.at[n]))
+        loads[-1].start()
+        start += source.shape[0]
+    if start < nat.shape[0]:
+        nat[start:, :] = jnp.zeros((nat.shape[0] - start, LANES), F32)
     outward[...] = partial_sum(slice(0, width))
 
     @pl.when(jnp.logical_not(has_inner))
@@ -510,16 +552,38 @@
             device_id=where, device_id_type=mesh,
         )
 
-    to_up = side(0, old_ref.at[:, width - LANES : width], {"slab": slab + 1})
-    to_down = side(1, old_ref.at[:, :LANES], {"slab": slab - 1})
-
-    pl.when(has_up)(to_up.start)
-    pl.when(has_down)(to_down.start)
-
-    @pl.when(has_outer)
-    def _():
-        for c in range(steps):
-            to_outer(c).start()
+    to_up = side(0, side_out.at[0], {"slab": slab + 1})
+    to_down = side(1, side_out.at[1], {"slab": slab - 1})
+
+    def start_hops(chunks):
+        @pl.when(has_outer)
+        def _():
+            for c in chunks:
+                to_outer(c).start()
+
+    start_hops(range(2))
+    for copy in loads:
+        copy.wait()
+    lines = width // LANES
+    fold = LANES // bins
+    blocked = lax.broadcasted_iota(jnp.int32, (LANES // fold, LANES), 1) // bins
+
+    def turn(g, _):
+        turned[...] = nat[pl.ds(pl.multiple_of(g * LANES, LANES), LANES), :].T
+        parts = [turned[pl.ds(r, LANES // fold, stride=fold), :] for r in range(fold)]
+        for k in range(fold):
+            out = parts[k]
+            for r in range(fold):
+                if r != k:
+                    out = jnp.where(blocked == r, pltpu.roll(parts[r], (r - k) * bins % LANES, 1), out)
+            place = pl.multiple_of(g * LANES + k * lines, lines)
+            quads[pl.ds(place, lines), :] = out
+        return 0
+
+    lax.fori_loop(0, nat.shape[0] // LANES, turn, 0)
+    tile = lambda q: quads[pl.ds(q, rows, stride=lines), :]
+    side_out[0] = tile(lines - 1)
+    side_out[1] = tile(0)
 
     lane = lax.broadcasted_iota(jnp.int32, (2 * LANES, chunk), 1)
     row = lax.broadcasted_iota(jnp.int32, (2 * LANES, chunk), 0)
@@ -533,6 +597,10 @@
     slot = lax.broadcasted_iota(jnp.int32, (rows, chunk), 1) % bins
     gap = [jnp.zeros((third - rows, chunk), F32)] * (third > rows)
 
+    pl.when(has_up)(to_up.start)
+    pl.when(has_down)(to_down.start)
+    start_hops(range(2, steps))
+
     def stacked(x):
         high = x.astype(BF16).astype(F32)
         return jnp.concatenate([high, x - high], axis=0).astype(BF16)
@@ -541,17 +609,19 @@
         pl.when(has_inner)(lambda: to_outer(c).wait_recv())
         summed[:, lanes(c)] = partial_sum(lanes(c, 2 * width)) + hopped[:, lanes(c)]
 
+    per = chunk // LANES
+
     def advect(c):
-        here = old_ref[:, lanes(c)]
-        start = jnp.maximum(c * chunk - LANES, 0)
-        stop = jnp.minimum((c + 1) * chunk, width - LANES)
-        low = old_ref[:, pl.ds(pl.multiple_of(start, LANES), LANES)]
-        high = old_ref[:, pl.ds(pl.multiple_of(stop, LANES), LANES)]
-        low = jnp.where(c == 0, side_in[0], low)
-        high = jnp.where(c == steps - 1, side_in[1], high)
+        here = jnp.concatenate([tile(c * per + n) for n in range(per)], axis=1)
+        low = jnp.where(c == 0, side_in[0], tile(jnp.maximum(c * per - 1, 0)))
+        high = jnp.where(c == steps - 1, side_in[1], tile(jnp.minimum((c + 1) * per, lines - 1)))
         left = pltpu.roll(jnp.concatenate([low, here], axis=1), bins, 1)[:, LANES:]
         right = pltpu.roll(jnp.concatenate([here, high], axis=1), chunk + LANES - bins, 1)[:, :chunk]
         return here - 0.4 * (here - left) + 0.1 * (right - 2.0 * here + left)
+
+    def cell_row(n, c):
+        start = (species + n) * lines + c * per
+        return jnp.concatenate([quads[pl.ds(start + k, 1), :] for k in range(per)], axis=1)
 
     def blend(c):
         total = partial_sum(lanes(c, width)) + got[:, lanes(c)]
@@ -574,8 +644,8 @@
         around = around[:rows] + around[rows:]
         before = jnp.where(slot == 0, around, pltpu.roll(here, 1, 1))
         after = jnp.where(slot == bins - 1, around, pltpu.roll(here, chunk - 1, 1))
-        state = here + diss_ref[:, lanes(c)] * (after - 2.0 * here + before)
-        half = 0.5 * rate_ref[:, lanes(c)]
+        state = here + cell_row(0, c) * (after - 2.0 * here + before)
+        half = 0.5 * cell_row(1, c)
         count = count_ref[:, lanes(c)]
         for k in range(KMAX):
             high, low = (part.astype(F32) for part in halves(state))
@@ -629,8 +699,8 @@
     pl.when(has_down)(to_down.wait_send)
 
 
-def middle_call(accs, old, diss, rate, count, matrix, species, bins, chunk=512):
-    rows, width = old.shape
+def middle_call(accs, cmc, diss, rate, count, matrix, species, bins, chunk=512):
+    rows, width = accs[0].shape[0], count.shape[1]
     steps = width // chunk
     given = len(accs) + 5
 
@@ -640,16 +710,18 @@
     return pl.pallas_call(
         kernel,
         out_shape=[jax.ShapeDtypeStruct((rows, width), F32)] * 3,
-        in_specs=[VMEM] * given,
+        in_specs=[VMEM] * len(accs) + [pl.BlockSpec(memory_space=pl.ANY)] * 3 + [VMEM] * 2,
         out_specs=[VMEM] * 3,
-        scratch_shapes=[pltpu.VMEM((rows, width), F32)] * 5
+        scratch_shapes=[pltpu.VMEM((rows * bins, LANES), F32), pltpu.VMEM((rows * width // LANES, LANES), F32)]
+        + [pltpu.VMEM((LANES, LANES), F32), pltpu.VMEM((2, rows, LANES), F32), pltpu.SemaphoreType.DMA((3,))]
+        + [pltpu.VMEM((rows, width), F32)] * 5
         + [pltpu.VMEM((steps, rows, 2 * LANES), F32)] * 2
         + [pltpu.VMEM((2, rows, LANES), F32), pltpu.VMEM((2 * LANES, chunk), BF16), pltpu.VMEM(matrix.shape, BF16)]
         + [pltpu.SemaphoreType.DMA((6, steps))] * 2
         + [pltpu.SemaphoreType.DMA((2,))] * 2,
         compiler_params=pltpu.CompilerParams(vmem_limit_bytes=20 << 20, collective_id=1, has_side_effects=True),
         name="middle",
-    )(*accs, old, diss, rate, count, matrix)
+    )(*accs, cmc, diss, rate, count, matrix)
 
 
 def on_device(
@@ -662,7 +734,6 @@
     ncross = lax.axis_size("cross")
     per_tile = TILE // bins
     ntiles = 3 * cells // per_tile
-    width = cells * bins
     flat, rank, steps = head_call(
         les_state, cmc_map, pdf_index, diffusion, rows, cells, nshape, ntiles, nshape * per_tile
     )
@@ -679,12 +750,9 @@
         far_lists = [swap(mine, "cross", bits[-1])]
         near_lists += [swap(mine, "cross", bit) for bit in bits[:-1]]
 
-    spread = lambda a: a.transpose(0, 2, 1).reshape(a.shape[0], width)
-    wide = lambda a: a.T.reshape(1, width)
-    state = spread(jnp.pad(cmc_state, ((0, rows - species), (0, 0), (0, 0))))
     extra = rows - species
     matrix = jnp.tile(jnp.pad(chem_matrix, ((0, extra), (0, -(-rows // 16) * 16 - species))), (1, 3))
-    terms = (state, wide(dissipation), wide(reaction_rate), jnp.repeat(substeps, bins)[None, :], matrix)
+    terms = (cmc_state.reshape(species * bins, cells), dissipation, reaction_rate, jnp.repeat(substeps, bins)[None, :], matrix)
     acc, *near_keys = collect_call(near_lists, table, species, bins, per_tile, ntiles)
     accs = [acc]
     if bits:
@@ -693,10 +761,7 @@
         acc, *far_keys = collect_call(far_lists, table, species, bins, per_tile, ntiles)
         accs = list(accs) + [acc]
     means = middle_call(accs, *terms, species, bins)
-    fresh = means[0]
     means = [means[2], means[0], means[1]]
-    cmc_out = fresh[:species].reshape(species, cells, bins).transpose(0, 2, 1)
-
 
     def gather(group):
         total = group[0]
@@ -708,10 +773,10 @@
         there = gather(project_call(means, far_keys, table, bins, per_tile, ntiles))
         there, means = lax.optimization_barrier((there, means))
         there = swap(there, "cross", bits[-1])
-    here = project_call(means, near_keys, table, bins, per_tile, ntiles)
+    *here, cmc_out = project_call(means, near_keys, table, bins, per_tile, ntiles, species * bins)
     total = [here[0]] + [swap(piece, "cross", bit) for bit, piece in zip(bits[:-1], here[1:])]
     les_out = permute_call(total + [there] * bool(bits), rank, flat, True)
-    return (les_out.reshape(les_state.shape), cmc_out)
+    return (les_out.reshape(les_state.shape), cmc_out.reshape(species, bins, cells))
 
 
 def solution(mesh):

time: 176 us -> 177 us (level)
  local copies, waits for them, and re-layouts: 20.1 us -> 3.06 us
  waiting for transfers between devices: 20.3 us -> 36.4 us
  Pallas kernels: 131 us -> 134 us
    ppermute x6, waiting for transfers between devices: 20.3 us -> 36.4 us  [swap(): return lax.ppermute(array, axis, [(i, i ^ bit) for i in range(count)])]
    transpose x4 -> x0, local copies, waits for them, and re-layouts: 6.43 us -> none  [the longest x2 6.22 us: on_device(): spread = lambda a: a.transpose(0, 2, 1).reshape(a.shape[0], width)]
    unnamed x30 -> x23, local copies, waits for them, and re-layouts: 8.92 us -> 2.62 us
    pallas_call x2, Pallas kernels: 16.6 us -> 20.2 us  [project_call(): pl.pallas_call(functools.partial(project_kernel, bins, per_tile, pairs, l...]
    optimization_barrier x1 -> x0, local copies, waits for them, and re-layouts: 2.17 us -> none  [on_device(): accs, far_lists, terms = lax.optimization_barrier((accs, far_lists, terms))]
    slice x1 -> x0, local copies, waits for them, and re-layouts: 1.99 us -> none  [on_device(): cmc_out = fresh[:species].reshape(species, cells, bins).transpose(0, 2, 1)]
  transfers between devices with their start and end apart: 6 -> 6, of which waited for: 4 -> 6; matrix products, arithmetic and copies ran while one was open for 9% -> 0% of each run, Pallas kernels for 7% -> 7%
where the time goes in v6:
time: 177 us
  Pallas kernels  134 us (76%)
  waiting for transfers between devices  36.4 us (21%)
  local copies, waits for them, and re-layouts  3.06 us (2%)
  starting transfers between devices  2.22 us (1%)
    pallas_call x1, Pallas kernels, middle_call(): pl.pallas_call(kernel, out_shape=[jax.ShapeDtypeStruct((rows, width), F32...  55.2 us
    ppermute x6, waiting for transfers between devices, swap(): return lax.ppermute(array, axis, [(i, i ^ bit) for i in range(count)])  36.4 us
    pallas_call x2, Pallas kernels, permute_call(): pl.pallas_call(functools.partial(permute_kernel, back, len(args)), grid=(...  23.2 us
    pallas_call x2, Pallas kernels, collect_call(): pl.pallas_call(functools.partial(collect_kernel, species, bins, per_tile,...  23 us
    pallas_call x2, Pallas kernels, project_call(): pl.pallas_call(functools.partial(project_kernel, bins, per_tile, pairs, l...  20.2 us
    pallas_call x1, Pallas kernels, head_call(): pl.pallas_call(functools.partial(head_kernel, (species, nx, ny), cells, n...  12.5 us
  transfers between devices with their start and end apart: 6, of which 6 were waited for; matrix products, arithmetic and copies ran while one was open for 0% of the time, Pallas kernels for 7%

profile of v6, /device:TPU:2, one launch (start us, length us, event | category | flops | bytes accessed | tf_op | source)
XLA Modules:
  0.0 176.6 jit_solution(18097216860530091873)
XLA Ops:
  0.6 0.0 copy-start
  0.6 12.5 %head.1 = (f32[56,4096]{1,0:T(8,128)}, f32[1,4096]{1,0:T(1,128)}, f32[1,128]{1,0:T(1,128)}) custom-call(f32[1728,128]{1,0:T(8,128)} %bitcast.13, s32[1,4096]{1,0:T(1,128)} %bitcast.14, s32[1,4096]{1,0:T(1,128)} %bitcast.15, f32[1,54]{1,0:T(1,128)} %bitcast.16), custom_call_target="tpu_custom_call" | custom-call | tf_op jit(solution)/shard_map/head/pallas_call | solution.py:178
  13.2 0.0 copy-start.4
  13.2 1.2 copy-done.4
  14.4 0.0 copy-start.6
  14.4 0.7 copy-done.6
  15.1 0.0 copy-start.8
  15.1 0.6 copy-done.8
  15.7 0.0 copy-start.10
  15.7 0.0 copy-start.9
  15.7 13.0 %sort.1.refs_0_ = f32[56,4096]{1,0:T(8,128)S(1)} custom-call(f32[1,4096]{1,0:T(1,128)S(1)} %copy-done.6, f32[56,4096]{1,0:T(8,128)S(1)} %copy-done.4, f32[1,128]{1,0:T(1,128)S(1)} %copy-done.8), custom_call_target="tpu_custom_call" | custom-call | flops 3758096384 | bytes 1835008 | tf_op jit(solution)/shard_map/sort/pallas_call | solution.py:251
  28.7 0.1 collective-permute-start
  28.8 1.0 collective-permute-start.1
  29.8 0.0 copy-done
  29.8 0.1 constant_dynamic-slice_fusion
  29.9 0.1 copy.14
  29.9 0.0 copy-done.10
  29.9 0.1 broadcast_in_dim.3
  30.0 0.1 broadcast_in_dim_reshape.3.refs_5_
  30.1 0.0 copy-done.9
  30.2 0.1 tile.10.refs_6_
  30.3 0.9 collective-permute-done.refs_1_
  31.3 11.5 %collect.2 = (f32[56,12288]{1,0:T(8,128)S(1)}, f32[8,4096]{1,0:T(8,128)S(1)}, f32[8,4096]{1,0:T(8,128)S(1)}) custom-call(f32[56,4096]{1,0:T(8,128)S(1)} %sort.1.refs_0_, f32[56,4096]{1,0:T(8,128)S(1)} %collective-permute-done.refs_1_, f32[32,128]{1,0:T(8,128)S(1)} %bitcast.9), custom_call_target="tpu_custom_call" | custom-call | flops 2650800128 | tf_op jit(solution)/shard_map/collect/pallas_call | solution.py:346
  42.8 8.8 %collective-permute-done.1.refs_0_ = f32[56,4096]{1,0:T(8,128)S(1)} collective-permute-done((f32[56,4096]{1,0:T(8,128)S(1)}, f32[56,4096]{1,0:T(8,128)S(1)}, u32[]{:S(2)}, u32[]{:S(2)}) %collective-permute-start.1) | collective-permute-done | bytes 917536 | tf_op jit(solution)/shard_map/ppermute | solution.py:25
  51.6 0.0 copy-start.1
  51.6 0.0 copy-start.2
  51.6 0.0 copy-start.3
  51.6 0.0 collective-permute-start.2
  51.6 2.5 %collective-permute-done.2.refs_1_ = f32[56,4096]{1,0:T(8,128)S(1)} collective-permute-done((f32[56,4096]{1,0:T(8,128)S(1)}, f32[56,4096]{1,0:T(8,128)S(1)}, u32[]{:S(2)}, u32[]{:S(2)}) %collective-permute-start.2) | collective-permute-done | bytes 917536 | tf_op jit(solution)/shard_map/ppermute | solution.py:25
  54.0 11.5 %collect.3 = (f32[56,12288]{1,0:T(8,128)S(1)}, f32[8,4096]{1,0:T(8,128)S(1)}, f32[8,4096]{1,0:T(8,128)S(1)}) custom-call(f32[56,4096]{1,0:T(8,128)S(1)} %collective-permute-done.1.refs_0_, f32[56,4096]{1,0:T(8,128)S(1)} %collective-permute-done.2.refs_1_, f32[32,128]{1,0:T(8,128)S(1)} %bitcast.10), custom_call_target="tpu_custom_call" | custom-call | flops 2650800128 | tf_op jit(solution)/shard_map/collect/pallas_call | solution.py:346
  65.5 0.0 copy-done.1
  65.5 0.0 copy-done.2
  65.6 0.0 copy-done.3
  65.6 55.2 %middle.1 = (f32[56,4096]{1,0:T(8,128)S(1)}, f32[56,4096]{1,0:T(8,128)S(1)}, f32[56,4096]{1,0:T(8,128)S(1)}) custom-call(f32[56,12288]{1,0:T(8,128)S(1)} %get-tuple-element.46.refs_0_, f32[56,12288]{1,0:T(8,128)S(1)} %get-tuple-element.48.refs_1_, f32[1728,128]{1,0:T(8,128)S(1)} %bitcast.8, f32[32,128]{1,0:T(8,128)S(1)} %copy-done.2, ...), custom_call_target="tpu_custom_call" | custom-call | tf_op jit(solution)/shard_map/middle/pallas_call | solution.py:710
  120.7 7.9 %project.2 = (f32[56,4096]{1,0:T(8,128)S(1)}, f32[56,4096]{1,0:T(8,128)S(1)}) custom-call(f32[56,4096]{1,0:T(8,128)S(1)} %get-tuple-element.61.refs_0_, f32[56,4096]{1,0:T(8,128)S(1)} %get-tuple-element.62.refs_1_, f32[56,4096]{1,0:T(8,128)S(1)} %get-tuple-element.63.refs_2_, f32[8,4096]{1,0:T(8,128)S(1)} %get-tuple-element.57.refs_3_, ...), custom_call_target="tpu_custom_call" | custom-call | flops 2650800128 | tf_op jit(solution)/shard_map/project/pallas_call | solution.py:444
  128.6 0.1 collective-permute-start.3
  128.7 2.5 %collective-permute-done.3 = f32[56,4096]{1,0:T(8,128)S(1)} collective-permute-done((f32[56,4096]{1,0:T(8,128)S(1)}, f32[56,4096]{1,0:T(8,128)S(1)}, u32[]{:S(2)}, u32[]{:S(2)}) %collective-permute-start.3) | collective-permute-done | bytes 917536 | tf_op jit(solution)/shard_map/ppermute | solution.py:25
  131.1 0.1 add.9
  131.2 0.0 copy-start.5
  131.2 0.0 copy-start.7
  131.2 12.3 %project.3 = (f32[56,4096]{1,0:T(8,128)S(1)}, f32[56,4096]{1,0:T(8,128)S(1)}, f32[1728,128]{1,0:T(8,128)}) custom-call(f32[56,4096]{1,0:T(8,128)S(1)} %get-tuple-element.61.refs_0_, f32[56,4096]{1,0:T(8,128)S(1)} %get-tuple-element.62.refs_1_, f32[56,4096]{1,0:T(8,128)S(1)} %get-tuple-element.63.refs_2_, f32[8,4096]{1,0:T(8,128)S(1)} %get-tuple-element.64.refs_3_, ...), custom_call_target="tpu_custom_call" | custom-call | flops 2650800128 | tf_op jit(solution)/shard_map/project/pallas_call | solution.py:444
  143.6 0.2 collective-permute-start.4
  143.8 0.9 collective-permute-start.5
  144.6 1.4 collective-permute-done.4.refs_1_
  146.1 20.3 %collective-permute-done.5.refs_2_ = f32[56,4096]{1,0:T(8,128)S(1)} collective-permute-done((f32[56,4096]{1,0:T(8,128)S(1)}, f32[56,4096]{1,0:T(8,128)S(1)}, u32[]{:S(2)}, u32[]{:S(2)}) %collective-permute-start.5) | collective-permute-done | bytes 917536 | tf_op jit(solution)/shard_map/ppermute | solution.py:25
  166.4 0.0 copy-done.5
  166.4 0.0 copy-done.7
  166.4 10.2 %unsort.1 = f32[1728,128]{1,0:T(8,128)} custom-call(f32[1,4096]{1,0:T(1,128)S(1)} %copy-done.7, f32[56,4096]{1,0:T(8,128)S(1)} %get-tuple-element.66.refs_0_, f32[56,4096]{1,0:T(8,128)S(1)} %collective-permute-done.4.refs_1_, f32[56,4096]{1,0:T(8,128)S(1)} %collective-permute-done.5.refs_2_, f32[56,4096]{1,0:T(8,128)S(1)} %copy-done.5), custom_call_target="tpu_custom_call" | custom-call | flops 3758096384 | bytes 1835008 | tf_op jit(solution)/shard_map/unsort/pallas_call | solution.py:251
  (2 shorter events, 0.0 us)
Async XLA Ops:
  0.6 29.2 %copy-start = (f32[128,128]{1,0:T(8,128)S(1)}, f32[128,128]{1,0:T(8,128)}, u32[]{:S(2)}) copy-start(f32[128,128]{1,0:T(8,128)} %param.14) | copy-start | bytes 196612
  13.2 1.2 copy-start.4
  14.4 0.7 copy-start.6
  15.1 0.6 copy-start.8
  15.7 14.2 %copy-start.10 = (s32[128]{0:T(128)S(1)}, s32[128]{0:T(128)}, u32[]{:S(2)}) copy-start(s32[128]{0:T(128)} %param.19) | copy-start | bytes 1540
  15.7 14.4 %copy-start.9 = (f32[54,54]{1,0:T(8,128)S(1)}, f32[54,54]{1,0:T(8,128)}, u32[]{:S(2)}) copy-start(f32[54,54]{1,0:T(8,128)} %param.16) | copy-start | bytes 34996
  28.7 2.5 %collective-permute-start = (f32[56,4096]{1,0:T(8,128)S(1)}, f32[56,4096]{1,0:T(8,128)S(1)}, u32[]{:S(2)}, u32[]{:S(2)}) collective-permute-start(f32[56,4096]{1,0:T(8,128)S(1)} %sort.1.refs_0_), channel_id=1, source_target_pairs={{0,1},{1,0},{2,3},{3,2},{4,5},{5,4},{6,7},{7,6},{8,9},{9,8},{10,11... | collective-permute-start | bytes 2752520 | tf_op jit(solution)/shard_map/ppermute | solution.py:25
  28.8 22.8 %collective-permute-start.1 = (f32[56,4096]{1,0:T(8,128)S(1)}, f32[56,4096]{1,0:T(8,128)S(1)}, u32[]{:S(2)}, u32[]{:S(2)}) collective-permute-start(f32[56,4096]{1,0:T(8,128)S(1)} %sort.1.refs_0_), channel_id=1, source_target_pairs={{0,2},{1,3},{2,0},{3,1},{4,6},{5,7},{6,4},{7,5},{8,10},{9,11},{10,... | collective-permute-start | bytes 2752520 | tf_op jit(solution)/shard_map/ppermute | solution.py:25
  51.6 14.0 %copy-start.1 = (f32[54,32,128]{2,1,0:T(8,128)S(1)}, f32[54,32,128]{2,1,0:T(8,128)}, u32[]{:S(2)}) copy-start(f32[54,32,128]{2,1,0:T(8,128)} %param.11) | copy-start | bytes 2654212
  51.6 14.0 %copy-start.2 = (f32[32,128]{1,0:T(8,128)S(1)}, f32[32,128]{1,0:T(8,128)}, u32[]{:S(2)}) copy-start(f32[32,128]{1,0:T(8,128)} %refs_3_) | copy-start | bytes 49156
  51.6 14.0 %copy-start.3 = (f32[32,128]{1,0:T(8,128)S(1)}, f32[32,128]{1,0:T(8,128)}, u32[]{:S(2)}) copy-start(f32[32,128]{1,0:T(8,128)} %refs_4_) | copy-start | bytes 49156
  51.6 2.5 %collective-permute-start.2 = (f32[56,4096]{1,0:T(8,128)S(1)}, f32[56,4096]{1,0:T(8,128)S(1)}, u32[]{:S(2)}, u32[]{:S(2)}) collective-permute-start(f32[56,4096]{1,0:T(8,128)S(1)} %collective-permute-done.1.refs_0_), channel_id=1, source_target_pairs={{0,1},{1,0},{2,3},{3,2},{4,5},{5,4},{6,7},{7,6},{8,9},{9,8},{10,11... | collective-permute-start | bytes 2752520 | tf_op jit(solution)/shard_map/ppermute | solution.py:25
  128.6 2.5 %collective-permute-start.3 = (f32[56,4096]{1,0:T(8,128)S(1)}, f32[56,4096]{1,0:T(8,128)S(1)}, u32[]{:S(2)}, u32[]{:S(2)}) collective-permute-start(f32[56,4096]{1,0:T(8,128)S(1)} %get-tuple-element.60), channel_id=1, source_target_pairs={{0,1},{1,0},{2,3},{3,2},{4,5},{5,4},{6,7},{7,6},{8,9},{9,8},{10,11... | collective-permute-start | bytes 2752520 | tf_op jit(solution)/shard_map/ppermute | solution.py:25
  131.2 35.2 %copy-start.5 = (f32[56,4096]{1,0:T(8,128)S(1)}, f32[56,4096]{1,0:T(8,128)}, u32[]{:S(2)}) copy-start(f32[56,4096]{1,0:T(8,128)} %get-tuple-element.37.refs_0_.refs_3_) | copy-start | bytes 2752516
  131.2 35.2 %copy-start.7 = (f32[1,4096]{1,0:T(1,128)S(1)}, f32[1,4096]{1,0:T(1,128)}, u32[]{:S(2)}) copy-start(f32[1,4096]{1,0:T(1,128)} %get-tuple-element.36.rank_ref) | copy-start | bytes 49156
  143.6 2.5 %collective-permute-start.4 = (f32[56,4096]{1,0:T(8,128)S(1)}, f32[56,4096]{1,0:T(8,128)S(1)}, u32[]{:S(2)}, u32[]{:S(2)}) collective-permute-start(f32[56,4096]{1,0:T(8,128)S(1)} %get-tuple-element.67), channel_id=1, source_target_pairs={{0,1},{1,0},{2,3},{3,2},{4,5},{5,4},{6,7},{7,6},{8,9},{9,8},{10,11... | collective-permute-start | bytes 2752520 | tf_op jit(solution)/shard_map/ppermute | solution.py:25
  143.8 22.6 %collective-permute-start.5 = (f32[56,4096]{1,0:T(8,128)S(1)}, f32[56,4096]{1,0:T(8,128)S(1)}, u32[]{:S(2)}, u32[]{:S(2)}) collective-permute-start(f32[56,4096]{1,0:T(8,128)S(1)} %add.9), channel_id=1, source_target_pairs={{0,2},{1,3},{2,0},{3,1},{4,6},{5,7},{6,4},{7,5},{8,10},{9,11},{10,... | collective-permute-start | bytes 2752520 | tf_op jit(solution)/shard_map/ppermute | solution.py:25

commit v7 on v6

--- a/solution.py
+++ b/solution.py
@@ -92,8 +92,8 @@
 
 
 def head_kernel(grid_shape, cells, nshape, tiles, span, *refs):
-    given, (t_ref, rank_ref, table_ref), refs = refs[:4], refs[4:7], refs[7:]
-    les_ref, map_ref, shape_ref, diff_ref, key_ref, *refs = refs
+    given, (t_ref, rank_ref, parts_ref, half_ref), refs = refs[:4], refs[4:8], refs[8:]
+    les_ref, map_ref, shape_ref, diff_ref, key_ref, table_ref, *refs = refs
     faces, halos, (send, recv, load) = refs[:4], refs[4:8], refs[8:]
     loads = [
         pltpu.make_async_copy(source, target, load.at[n])
@@ -167,6 +167,10 @@
             around = around + jnp.where(lane > 0, pltpu.roll(here, 1, 1), 0.0)
             place = (x * ny + y) * LANES
             t_ref[:species, place : place + LANES] = here + number * (around - 6.0 * here)
+    x = t_ref[...]
+    high = x.astype(BF16).astype(F32)
+    parts_ref[...] = jnp.concatenate([high, x - high], axis=0).astype(BF16)
+    sort_tiles(parts_ref, rank_ref, table_ref[...], half_ref, 0)
     for n, (there, _) in enumerate(sides):
         pl.when(there)(copies[n].wait_send)
 
@@ -180,16 +184,18 @@
         out_shape=[
             jax.ShapeDtypeStruct((rows, count), F32),
             jax.ShapeDtypeStruct((1, count), F32),
-            jax.ShapeDtypeStruct((1, LANES), F32),
+            jax.ShapeDtypeStruct((2 * rows, count), BF16),
+            jax.ShapeDtypeStruct((rows, count // 2), F32),
         ],
         in_specs=[pl.BlockSpec(memory_space=pltpu.HBM)] * 4,
-        out_specs=[VMEM] * 3,
+        out_specs=[VMEM] * 4,
         scratch_shapes=[
             pltpu.VMEM((species * nx * ny, nz), F32),
             pltpu.VMEM((1, count), jnp.int32),
             pltpu.VMEM((1, count), jnp.int32),
             pltpu.VMEM((1, species), F32),
             pltpu.VMEM((8, count), F32),
+            pltpu.VMEM((1, LANES), F32),
         ] + halo * 2 + [pltpu.SemaphoreType.DMA((4,))] * 3,
         compiler_params=pltpu.CompilerParams(vmem_limit_bytes=60 << 20, collective_id=2, has_side_effects=True),
         name="head",
@@ -199,11 +205,54 @@
     )
 
 
-def permute_kernel(back, count, rank_ref, *refs):
-    xs, (out_ref, parts) = refs[:count], refs[count:]
-    xs, extra_ref = xs[:-1], xs[-1]
-    rows, count = xs[0].shape
-    chunk = 2 * TILE
+CHUNK = 2 * TILE
+
+
+def sort_tiles(parts, rank_ref, steps, out_ref, first):
+    rows = out_ref.shape[0]
+    count = rank_ref.shape[1]
+
+    def step(n, _):
+        here = (first + n) * TILE
+        total = jnp.zeros((2 * rows, TILE), F32)
+        for k in range(count // CHUNK):
+            piece = slice(k * CHUNK, (k + 1) * CHUNK)
+            ids = lax.broadcasted_iota(jnp.int32, (TILE, CHUNK), 0) + here
+            hot = rows_equal(ids.astype(F32), rank_ref[:, piece])
+            total = total + lax.dot_general(parts[:, piece], hot, NT, preferred_element_type=F32)
+        total = total[:rows] + total[rows:]
+        if steps is not None:
+            line = lax.broadcasted_iota(jnp.int32, (rows, TILE), 0)
+            total = jnp.where(line == rows - 1, jnp.concatenate([steps] * (TILE // LANES), axis=1), total)
+        out_ref[:, pl.ds(pl.multiple_of(n * TILE, TILE), TILE)] = total
+        return 0
+
+    lax.fori_loop(0, out_ref.shape[1] // TILE, step, 0)
+
+
+def sort_kernel(parts_ref, rank_ref, out_ref):
+    sort_tiles(parts_ref, rank_ref, None, out_ref, out_ref.shape[1] // TILE)
+
+
+def sort_call(parts, rank):
+    rows, count = parts.shape[0] // 2, parts.shape[1]
+    return pl.pallas_call(
+        sort_kernel,
+        out_shape=jax.ShapeDtypeStruct((rows, count // 2), F32),
+        in_specs=[VMEM] * 2,
+        out_specs=VMEM,
+        compiler_params=params(8),
+        cost_estimate=pl.CostEstimate(flops=2 * rows * count * count, bytes_accessed=4 * rows * count, transcendentals=0),
+        name="sort",
+    )(parts, rank)
+
+
+def unsort_kernel(half, given, rank_ref, *refs):
+    xs, refs = refs[:given], refs[given:]
+    before, (flat_ref,) = (refs[:1], refs[1:2]) if half else ((), (None,))
+    out_ref, parts = refs[-2:]
+    rows, count = xs[0].shape[0], rank_ref.shape[1]
+    width = xs[0].shape[1]
 
     @pl.when(pl.program_id(0) == 0)
     def _():
@@ -214,51 +263,49 @@
         parts[...] = jnp.concatenate([high, x - high], axis=0).astype(BF16)
 
     total = jnp.zeros((2 * rows, TILE), F32)
-    here = pl.program_id(0) * TILE
-    for n in range(count // chunk):
-        piece = slice(n * chunk, (n + 1) * chunk)
-        if back:
-            ids = lax.broadcasted_iota(jnp.int32, (chunk, TILE), 0) + n * chunk
-            hot = rows_equal(ids.astype(F32), rank_ref[:, pl.ds(pl.multiple_of(here, TILE), TILE)])
-            total = total + lax.dot_general(parts[:, piece], hot, NN, preferred_element_type=F32)
-        else:
-            ids = lax.broadcasted_iota(jnp.int32, (TILE, chunk), 0) + here
-            hot = rows_equal(ids.astype(F32), rank_ref[:, piece])
-            total = total + lax.dot_general(parts[:, piece], hot, NT, preferred_element_type=F32)
+    for k in range(width // CHUNK):
+        ids = lax.broadcasted_iota(jnp.int32, (CHUNK, TILE), 0) + (half * width + k * CHUNK)
+        hot = rows_equal(ids.astype(F32), rank_ref[:, pl.ds(pl.multiple_of(pl.program_id(0) * TILE, TILE), TILE)])
+        piece = parts[:, k * CHUNK : (k + 1) * CHUNK]
+        total = total + lax.dot_general(piece, hot, NN, preferred_element_type=F32)
     total = total[:rows] + total[rows:]
-    if back:
-        species = rows - 2
-        lines = count // LANES
-        for n in range(TILE // LANES):
-            piece = total[:, n * LANES : (n + 1) * LANES]
-            moved = extra_ref[:species, pl.ds(pl.multiple_of(here + n * LANES, LANES), LANES)]
-            piece = piece[:species] / piece[species : species + 1]
-            line = pl.program_id(0) * (TILE // LANES) + n
-            out_ref[pl.ds(line, species, stride=lines), :] = moved + 0.5 * (piece - moved)
-    else:
-        line = lax.broadcasted_iota(jnp.int32, (rows, TILE), 0)
-        steps = jnp.concatenate([extra_ref[...]] * (TILE // LANES), axis=1)
-        out_ref[...] = jnp.where(line == rows - 1, steps, total)
-
-
-def permute_call(xs, rank, extra, back):
-    rows, count = xs[0].shape
-    args = list(xs) + [extra]
-    lines = (rows - 2) * count // LANES
-    out_shape, out_spec = (rows, count), pl.BlockSpec((rows, TILE), lambda i: (0, i))
-    if back:
+    if not half:
+        out_ref[...] = total
+        return
+    total = total + before[0][...]
+    species = rows - 2
+    ratio = 0.5 / total[species : species + 1]
+    for n in range(TILE // LANES):
+        piece = slice(n * LANES, (n + 1) * LANES)
+        line = pl.program_id(0) * (TILE // LANES) + n
+        value = 0.5 * flat_ref[:species, piece] + total[:species, piece] * ratio[:, piece]
+        out_ref[pl.ds(line, species, stride=count // LANES), :] = value
+
+
+def unsort_call(wholes, piece, rank, before, flat):
+    half = int(before is not None)
+    rows, count = wholes[0].shape
+    part = pl.BlockSpec((rows, count // 2), lambda i: (0, half))
+    column = pl.BlockSpec((rows, TILE), lambda i: (0, i))
+    args = [rank, *wholes, piece]
+    specs = [whole(rank.shape)] + [part] * len(wholes) + [whole(piece.shape)]
+    out_shape, out_spec = (rows, count), column
+    if half:
+        args += [before, flat]
+        specs += [column, column]
+        lines = (rows - 2) * count // LANES
         out_shape, out_spec = (lines, LANES), whole((lines, LANES))
     return pl.pallas_call(
-        functools.partial(permute_kernel, back, len(args)),
+        functools.partial(unsort_kernel, half, len(wholes) + 1),
         grid=(count // TILE,),
         out_shape=jax.ShapeDtypeStruct(out_shape, F32),
-        in_specs=[whole(rank.shape)] + [whole(x.shape) for x in args],
+        in_specs=specs,
         out_specs=out_spec,
-        scratch_shapes=[pltpu.VMEM((2 * rows, count), BF16)],
+        scratch_shapes=[pltpu.VMEM((2 * rows, count // 2), BF16)],
         compiler_params=params(12),
-        cost_estimate=pl.CostEstimate(flops=4 * rows * count * count, bytes_accessed=8 * rows * count, transcendentals=0),
-        name="unsort" if back else "sort",
-    )(rank, *args)
+        cost_estimate=pl.CostEstimate(flops=2 * rows * count * count, bytes_accessed=4 * rows * count, transcendentals=0),
+        name="unsort",
+    )(*args)
 
 
 def weights_of(key, table, bins, per_tile):
@@ -293,27 +340,31 @@
 
 
 def collect_kernel(species, bins, per_tile, pairs, lists, *refs):
-    sources, refs = refs[:lists], refs[lists:]
+    sources, refs = [refs[2 * n : 2 * n + 2] for n in range(lists)], refs[2 * lists :]
     table_ref, out_ref, *refs = refs
     keys, (weights, tiles, parts, steps, sems) = refs[:lists], refs[lists:]
-    copies = fetch_rows(sources, steps, sems)
+    copies = fetch_rows([source[0] for source in sources], steps, sems)
+    rows, part = sources[0][0].shape
+    count = 2 * part
     for key, source in zip(keys, sources):
-        key[...] = source[source.shape[0] - 8 :, :]
-    rows, count = sources[0].shape
+        key[:, :part] = source[0][rows - 8 :, :]
+        key[:, part:] = source[1][rows - 8 :, :]
     blocks = count // LANES
     out_ref[...] = jnp.zeros_like(out_ref)
     table = split_table(table_ref[...])
     line = lax.broadcasted_iota(jnp.int32, (rows, LANES), 0)
-    for number, source in enumerate(sources):
-        prepare_weights(source, number * blocks, species, table, bins, per_tile, weights, tiles)
-
-        def split(n, _, source=source, number=number):
+    for number in range(2 * lists):
+        source = sources[number // 2][number % 2]
+        start = number * blocks // 2
+        prepare_weights(source, start, species, table, bins, per_tile, weights, tiles)
+
+        def split(n, _, source=source, start=start):
             x = source[:, pl.ds(pl.multiple_of(n * LANES, LANES), LANES)]
             x = jnp.where(line < species, x, jnp.where(line == species, 1.0, 0.0))
-            parts[number * blocks + n] = padded_halves(x)
+            parts[start + n] = padded_halves(x)
             return 0
 
-        lax.fori_loop(0, blocks, split, 0, unroll=2)
+        lax.fori_loop(0, blocks // 2, split, 0, unroll=4)
 
     for copy in copies:
         copy.wait()
@@ -338,11 +389,11 @@
 
 
 def collect_call(sources, table, species, bins, per_tile, ntiles):
-    rows, count = sources[0].shape
+    rows, count = sources[0][0].shape[0], 2 * sources[0][0].shape[1]
     lists, blocks = len(sources), count // LANES
     pairs = blocks + ntiles - 1
-    args = list(sources) + [table]
-    specs = [VMEM] * (lists + 1)
+    args = [half for source in sources for half in source] + [table]
+    specs = [VMEM] * (2 * lists + 1)
     return pl.pallas_call(
         functools.partial(collect_kernel, species, bins, per_tile, pairs, lists),
         out_shape=[jax.ShapeDtypeStruct((rows, ntiles * TILE), F32)] + [jax.ShapeDtypeStruct((8, count), F32)] * lists,
@@ -731,51 +782,45 @@
     rows = -(-(species + 2) // 8) * 8
     bins, cells = cmc_state.shape[1:]
     nshape = pdf_table.shape[0]
+    count = cmc_map.size
     ncross = lax.axis_size("cross")
     per_tile = TILE // bins
     ntiles = 3 * cells // per_tile
-    flat, rank, steps = head_call(
+    flat, rank, parts, low = head_call(
         les_state, cmc_map, pdf_index, diffusion, rows, cells, nshape, ntiles, nshape * per_tile
     )
-    mine = permute_call([flat], rank, steps, False)
+    bits = [1 << k for k in range(ncross.bit_length() - 1)]
+    low_there = swap(low, "cross", bits[-1])
+    high = sort_call(parts, rank)
+    high_there = swap(high, "cross", bits[-1])
+    near_lists = [(low, high)] + [(swap(low, "cross", bit), swap(high, "cross", bit)) for bit in bits[:-1]]
+    low_far = [low_there] + [swap(low_there, "cross", bit) for bit in bits[:-1]]
 
     table = lax.dynamic_slice_in_dim(pdf_table.T, lax.axis_index("cross") * bins, bins, axis=0)
-
-    mine, cmc_state, dissipation, reaction_rate, substeps, chem_matrix = lax.optimization_barrier(
-        (mine, cmc_state, dissipation, reaction_rate, substeps, chem_matrix)
-    )
-    bits = [1 << k for k in range(ncross.bit_length() - 1)]
-    near_lists, far_lists = [mine], []
-    if bits:
-        far_lists = [swap(mine, "cross", bits[-1])]
-        near_lists += [swap(mine, "cross", bit) for bit in bits[:-1]]
 
     extra = rows - species
     matrix = jnp.tile(jnp.pad(chem_matrix, ((0, extra), (0, -(-rows // 16) * 16 - species))), (1, 3))
     terms = (cmc_state.reshape(species * bins, cells), dissipation, reaction_rate, jnp.repeat(substeps, bins)[None, :], matrix)
     acc, *near_keys = collect_call(near_lists, table, species, bins, per_tile, ntiles)
-    accs = [acc]
-    if bits:
-        accs, far_lists, terms = lax.optimization_barrier((accs, far_lists, terms))
-        far_lists = list(far_lists) + [swap(far_lists[0], "cross", bit) for bit in bits[:-1]]
-        acc, *far_keys = collect_call(far_lists, table, species, bins, per_tile, ntiles)
-        accs = list(accs) + [acc]
+    acc, high_there, terms = lax.optimization_barrier((acc, high_there, terms))
+    high_far = [high_there] + [swap(high_there, "cross", bit) for bit in bits[:-1]]
+    more, *far_keys = collect_call(list(zip(low_far, high_far)), table, species, bins, per_tile, ntiles)
+    accs = [acc, more]
     means = middle_call(accs, *terms, species, bins)
     means = [means[2], means[0], means[1]]
-
-    def gather(group):
-        total = group[0]
-        for bit, piece in zip(bits[:-1], group[1:]):
-            total = total + swap(piece, "cross", bit)
-        return total
-
-    if bits:
-        there = gather(project_call(means, far_keys, table, bins, per_tile, ntiles))
-        there, means = lax.optimization_barrier((there, means))
-        there = swap(there, "cross", bits[-1])
+    there, *pieces = project_call(means, far_keys, table, bins, per_tile, ntiles)
+    pieces = [swap(piece, "cross", bit) for bit, piece in zip(bits[:-1], pieces)]
+    part = count // 2
+    low, high = there[:, :part], there[:, part:]
+    for piece in pieces:
+        low, high = low + piece[:, :part], high + piece[:, part:]
+    low, means = lax.optimization_barrier((low, means))
+    low = swap(low, "cross", bits[-1])
+    high = swap(high, "cross", bits[-1])
     *here, cmc_out = project_call(means, near_keys, table, bins, per_tile, ntiles, species * bins)
     total = [here[0]] + [swap(piece, "cross", bit) for bit, piece in zip(bits[:-1], here[1:])]
-    les_out = permute_call(total + [there] * bool(bits), rank, flat, True)
+    before = unsort_call(total, low, rank, None, None)
+    les_out = unsort_call(total, high, rank, before, flat)
     return (les_out.reshape(les_state.shape), cmc_out.reshape(species, bins, cells))
 
 

time: 177 us -> 174 us (0.983)
  waiting for transfers between devices: 36.4 us -> 27.5 us
  starting transfers between devices: 2.22 us -> 5.4 us
  Pallas kernels: 134 us -> 137 us
    ppermute x6 -> x10, waiting for transfers between devices: 36.4 us -> 27.5 us  [swap(): return lax.ppermute(array, axis, [(i, i ^ bit) for i in range(count)])]
    pallas_call x1, Pallas kernels: 12.5 us -> 19.4 us  [head_call(): pl.pallas_call(functools.partial(head_kernel, (species, nx, ny), cells, n...]
    ppermute x6 -> x10, starting transfers between devices: 2.22 us -> 5.4 us  [swap(): return lax.ppermute(array, axis, [(i, i ^ bit) for i in range(count)])]
    pallas_call x2 -> x3, Pallas kernels: 23.2 us -> 20 us  [the longest x2 13.6 us: unsort_call(): pl.pallas_call(functools.partial(unsort_kernel, half, len(wholes) + 1), g...]
  transfers between devices with their start and end apart: 6 -> 10, of which waited for: 6 -> 6; matrix products, arithmetic and copies ran while one was open for 0% -> 0% of each run, Pallas kernels for 7% -> 10%
where the time goes in v7:
time: 174 us
  Pallas kernels  137 us (79%)
  waiting for transfers between devices  27.5 us (16%)
  starting transfers between devices  5.4 us (3%)
  local copies, waits for them, and re-layouts  2.43 us (1%)
    pallas_call x1, Pallas kernels, middle_call(): pl.pallas_call(kernel, out_shape=[jax.ShapeDtypeStruct((rows, width), F32...  55.2 us
    ppermute x10, waiting for transfers between devices, swap(): return lax.ppermute(array, axis, [(i, i ^ bit) for i in range(count)])  27.5 us
    pallas_call x2, Pallas kernels, collect_call(): pl.pallas_call(functools.partial(collect_kernel, species, bins, per_tile,...  22.7 us
    pallas_call x2, Pallas kernels, project_call(): pl.pallas_call(functools.partial(project_kernel, bins, per_tile, pairs, l...  20.2 us
    pallas_call x1, Pallas kernels, head_call(): pl.pallas_call(functools.partial(head_kernel, (species, nx, ny), cells, n...  19.4 us
    pallas_call x2, Pallas kernels, unsort_call(): pl.pallas_call(functools.partial(unsort_kernel, half, len(wholes) + 1), g...  13.6 us
    pallas_call x1, Pallas kernels, sort_call(): pl.pallas_call(sort_kernel, out_shape=jax.ShapeDtypeStruct((rows, count /...  6.36 us
    ppermute x10, starting transfers between devices, swap(): return lax.ppermute(array, axis, [(i, i ^ bit) for i in range(count)])  5.4 us
  transfers between devices with their start and end apart: 10, of which 6 were waited for; matrix products, arithmetic and copies ran while one was open for 0% of the time, Pallas kernels for 10%

profile of v7, /device:TPU:2, one launch (start us, length us, event | category | flops | bytes accessed | tf_op | source)
XLA Modules:
  0.0 173.8 jit_solution(10969241759720171171)
XLA Ops:
  0.6 0.0 copy-start
  0.6 19.4 %head.1 = (f32[56,4096]{1,0:T(8,128)}, f32[1,4096]{1,0:T(1,128)}, bf16[112,4096]{1,0:T(8,128)(2,1)}, f32[56,2048]{1,0:T(8,128)}) custom-call(f32[1728,128]{1,0:T(8,128)} %bitcast.13, s32[1,4096]{1,0:T(1,128)} %bitcast.14, s32[1,4096]{1,0:T(1,128)} %bitcast.15, f32[1,54]{1,0:T(1,128)} %bitcast.16), custom_call_target="tpu_custom_call" | custom-call | tf_op jit(solution)/shard_map/head/pallas_call | solution.py:182
  20.0 0.0 copy-start.5
  20.1 1.2 copy-done.5
  21.2 0.7 copy-done.7
  21.9 6.4 %sort.1.refs_1_ = f32[56,2048]{1,0:T(8,128)S(1)} custom-call(bf16[112,4096]{1,0:T(8,128)(2,1)S(1)} %copy-done.5, f32[1,4096]{1,0:T(1,128)S(1)} %copy-done.7), custom_call_target="tpu_custom_call" | custom-call | flops 1879048192 | bytes 917504 | tf_op jit(solution)/shard_map/sort/pallas_call | solution.py:239
  28.3 0.1 collective-permute-start.1
  28.4 0.0 copy-done.6
  28.4 0.5 collective-permute-start
  28.9 0.9 collective-permute-start.2
  29.8 1.1 collective-permute-start.3
  30.9 0.0 copy-done
  30.9 0.1 constant_dynamic-slice_fusion
  31.0 0.1 copy.14
  31.1 0.0 copy-done.10
  31.1 0.1 broadcast_in_dim.3
  31.2 0.1 broadcast_in_dim_reshape.3.refs_5_
  31.3 0.0 copy-done.9
  31.3 0.1 tile.10.refs_6_
  31.5 0.0 collective-permute-done.1.refs_3_
  31.5 0.0 collective-permute-done.refs_2_
  31.5 11.4 %collect.2 = (f32[56,12288]{1,0:T(8,128)S(1)}, f32[8,4096]{1,0:T(8,128)S(1)}, f32[8,4096]{1,0:T(8,128)S(1)}) custom-call(f32[56,2048]{1,0:T(8,128)S(1)} %copy-done.6, f32[56,2048]{1,0:T(8,128)S(1)} %sort.1.refs_1_, f32[56,2048]{1,0:T(8,128)S(1)} %collective-permute-done.refs_2_, f32[56,2048]{1,0:T(8,128)S(1)} %collective-permute-done.1.refs_3_, ...), custom_call_target="tpu_custom_call" | custom-call | flops 2650800128 | tf_op jit(solution)/shard_map/collect/pallas_call | solution.py:397
  42.9 0.0 collective-permute-done.2.refs_1_
  42.9 0.0 copy-start.1
  42.9 0.0 copy-start.2
  42.9 0.0 copy-start.3
  42.9 8.3 %collective-permute-done.3.refs_0_ = f32[56,2048]{1,0:T(8,128)S(1)} collective-permute-done((f32[56,2048]{1,0:T(8,128)S(1)}, f32[56,2048]{1,0:T(8,128)S(1)}, u32[]{:S(2)}, u32[]{:S(2)}) %collective-permute-start.3) | collective-permute-done | bytes 458784 | tf_op jit(solution)/shard_map/ppermute | solution.py:25
  51.2 0.0 collective-permute-start.4
  51.2 0.5 collective-permute-start.5
  51.8 1.3 collective-permute-done.4.refs_2_
  53.1 0.7 collective-permute-done.5.refs_3_
  53.7 11.4 %collect.3 = (f32[56,12288]{1,0:T(8,128)S(1)}, f32[8,4096]{1,0:T(8,128)S(1)}, f32[8,4096]{1,0:T(8,128)S(1)}) custom-call(f32[56,2048]{1,0:T(8,128)S(1)} %collective-permute-done.3.refs_0_, f32[56,2048]{1,0:T(8,128)S(1)} %collective-permute-done.2.refs_1_, f32[56,2048]{1,0:T(8,128)S(1)} %collective-permute-done.4.refs_2_, ...), custom_call_target="tpu_custom_call" | custom-call | flops 2650800128 | tf_op jit(solution)/shard_map/collect/pallas_call | solution.py:397
  65.1 55.2 %middle.1 = (f32[56,4096]{1,0:T(8,128)S(1)}, f32[56,4096]{1,0:T(8,128)S(1)}, f32[56,4096]{1,0:T(8,128)S(1)}) custom-call(f32[56,12288]{1,0:T(8,128)S(1)} %get-tuple-element.35.refs_0_, f32[56,12288]{1,0:T(8,128)S(1)} %get-tuple-element.37.refs_1_, f32[1728,128]{1,0:T(8,128)S(1)} %bitcast.8, f32[32,128]{1,0:T(8,128)S(1)} %copy-done.2, ...), custom_call_target="tpu_custom_call" | custom-call | tf_op jit(solution)/shard_map/middle/pallas_call | solution.py:761
  120.3 7.9 %project.2 = (f32[56,4096]{1,0:T(8,128)S(1)}, f32[56,4096]{1,0:T(8,128)S(1)}) custom-call(f32[56,4096]{1,0:T(8,128)S(1)} %get-tuple-element.50.refs_0_, f32[56,4096]{1,0:T(8,128)S(1)} %get-tuple-element.51.refs_1_, f32[56,4096]{1,0:T(8,128)S(1)} %get-tuple-element.52.refs_2_, f32[8,4096]{1,0:T(8,128)S(1)} %get-tuple-element.46.refs_3_, ...), custom_call_target="tpu_custom_call" | custom-call | flops 2650800128 | tf_op jit(solution)/shard_map/project/pallas_call | solution.py:495
  128.1 0.1 collective-permute-start.6
  128.2 2.5 %collective-permute-done.6 = f32[56,4096]{1,0:T(8,128)S(1)} collective-permute-done((f32[56,4096]{1,0:T(8,128)S(1)}, f32[56,4096]{1,0:T(8,128)S(1)}, u32[]{:S(2)}, u32[]{:S(2)}) %collective-permute-start.6) | collective-permute-done | bytes 917536 | tf_op jit(solution)/shard_map/ppermute | solution.py:25
  130.7 0.1 slice_add_fusion
  130.8 12.3 %project.3 = (f32[56,4096]{1,0:T(8,128)S(1)}, f32[56,4096]{1,0:T(8,128)S(1)}, f32[1728,128]{1,0:T(8,128)}) custom-call(f32[56,4096]{1,0:T(8,128)S(1)} %get-tuple-element.50.refs_0_, f32[56,4096]{1,0:T(8,128)S(1)} %get-tuple-element.51.refs_1_, f32[56,4096]{1,0:T(8,128)S(1)} %get-tuple-element.52.refs_2_, f32[8,4096]{1,0:T(8,128)S(1)} %get-tuple-element.53.refs_3_, ...), custom_call_target="tpu_custom_call" | custom-call | flops 2650800128 | tf_op jit(solution)/shard_map/project/pallas_call | solution.py:495
  143.1 0.2 collective-permute-start.7
  143.3 0.9 collective-permute-start.9
  144.2 1.1 collective-permute-start.8
  145.3 11.4 %collective-permute-done.9.refs_2_ = f32[56,2048]{1,0:T(8,128)S(1)} collective-permute-done((f32[56,2048]{1,0:T(8,128)S(1)}, f32[56,2048]{1,0:T(8,128)S(1)}, u32[]{:S(2)}, u32[]{:S(2)}) %collective-permute-start.9) | collective-permute-done | bytes 458784 | tf_op jit(solution)/shard_map/ppermute | solution.py:25
  156.7 0.0 collective-permute-done.7.refs_1_
  156.7 0.0 copy-done.8
  156.7 5.8 %unsort.2.refs_3_ = f32[56,4096]{1,0:T(8,128)S(1)} custom-call(f32[1,4096]{1,0:T(1,128)S(1)} %copy-done.8, f32[56,4096]{1,0:T(8,128)S(1)} %get-tuple-element.55.refs_0_, f32[56,4096]{1,0:T(8,128)S(1)} %collective-permute-done.7.refs_1_, f32[56,2048]{1,0:T(8,128)S(1)} %collective-permute-done.9.refs_2_), custom_call_target="tpu_custom_call" | custom-call | flops 1879048192 | bytes 917504 | tf_op jit(solution)/shard_map/unsort/pallas_call | solution.py:298
  162.5 3.4 %collective-permute-done.8.refs_2_ = f32[56,2048]{1,0:T(8,128)S(1)} collective-permute-done((f32[56,2048]{1,0:T(8,128)S(1)}, f32[56,2048]{1,0:T(8,128)S(1)}, u32[]{:S(2)}, u32[]{:S(2)}) %collective-permute-start.8) | collective-permute-done | bytes 458784 | tf_op jit(solution)/shard_map/ppermute | solution.py:25
  165.9 0.0 copy-done.4
  165.9 7.8 %unsort.3 = f32[1728,128]{1,0:T(8,128)} custom-call(f32[1,4096]{1,0:T(1,128)S(1)} %copy-done.8, f32[56,4096]{1,0:T(8,128)S(1)} %get-tuple-element.55.refs_0_, f32[56,4096]{1,0:T(8,128)S(1)} %collective-permute-done.7.refs_1_, f32[56,2048]{1,0:T(8,128)S(1)} %collective-permute-done.8.refs_2_, f32[56,4096]{1,0:T(8,128)S(1)} %unsort.2.refs_3_, ...), custom_call_target="tpu_custom_call" | custom-call | flops 1879048192 | bytes 917504 | tf_op jit(solution)/shard_map/unsort/pallas_call | solution.py:298
  (11 shorter events, 0.0 us)
Async XLA Ops:
  0.6 30.3 %copy-start = (f32[128,128]{1,0:T(8,128)S(1)}, f32[128,128]{1,0:T(8,128)}, u32[]{:S(2)}) copy-start(f32[128,128]{1,0:T(8,128)} %param.14) | copy-start | bytes 196612
  20.0 1.2 copy-start.5
  21.2 0.7 copy-start.7
  21.9 6.5 %copy-start.6 = (f32[56,2048]{1,0:T(8,128)S(1)}, f32[56,2048]{1,0:T(8,128)}, u32[]{:S(2)}) copy-start(f32[56,2048]{1,0:T(8,128)} %get-tuple-element.32.refs_0_) | copy-start | bytes 1376260
  21.9 9.1 %copy-start.10 = (s32[128]{0:T(128)S(1)}, s32[128]{0:T(128)}, u32[]{:S(2)}) copy-start(s32[128]{0:T(128)} %param.19) | copy-start | bytes 1540
  21.9 9.3 %copy-start.9 = (f32[54,54]{1,0:T(8,128)S(1)}, f32[54,54]{1,0:T(8,128)}, u32[]{:S(2)}) copy-start(f32[54,54]{1,0:T(8,128)} %param.16) | copy-start | bytes 34996
  28.3 3.1 %collective-permute-start.1 = (f32[56,2048]{1,0:T(8,128)S(1)}, f32[56,2048]{1,0:T(8,128)S(1)}, u32[]{:S(2)}, u32[]{:S(2)}) collective-permute-start(f32[56,2048]{1,0:T(8,128)S(1)} %sort.1.refs_1_), channel_id=1, source_target_pairs={{0,1},{1,0},{2,3},{3,2},{4,5},{5,4},{6,7},{7,6},{8,9},{9,8},{10,11... | collective-permute-start | bytes 1376264 | tf_op jit(solution)/shard_map/ppermute | solution.py:25
  28.4 3.1 %collective-permute-start = (f32[56,2048]{1,0:T(8,128)S(1)}, f32[56,2048]{1,0:T(8,128)S(1)}, u32[]{:S(2)}, u32[]{:S(2)}) collective-permute-start(f32[56,2048]{1,0:T(8,128)S(1)} %copy-done.6), channel_id=1, source_target_pairs={{0,1},{1,0},{2,3},{3,2},{4,5},{5,4},{6,7},{7,6},{8,9},{9,8},{10,11... | collective-permute-start | bytes 1376264 | tf_op jit(solution)/shard_map/ppermute | solution.py:25
  28.9 14.0 %collective-permute-start.2 = (f32[56,2048]{1,0:T(8,128)S(1)}, f32[56,2048]{1,0:T(8,128)S(1)}, u32[]{:S(2)}, u32[]{:S(2)}) collective-permute-start(f32[56,2048]{1,0:T(8,128)S(1)} %sort.1.refs_1_), channel_id=1, source_target_pairs={{0,2},{1,3},{2,0},{3,1},{4,6},{5,7},{6,4},{7,5},{8,10},{9,11},{10,... | collective-permute-start | bytes 1376264 | tf_op jit(solution)/shard_map/ppermute | solution.py:25
  29.8 21.4 %collective-permute-start.3 = (f32[56,2048]{1,0:T(8,128)S(1)}, f32[56,2048]{1,0:T(8,128)S(1)}, u32[]{:S(2)}, u32[]{:S(2)}) collective-permute-start(f32[56,2048]{1,0:T(8,128)S(1)} %copy-done.6), channel_id=1, source_target_pairs={{0,2},{1,3},{2,0},{3,1},{4,6},{5,7},{6,4},{7,5},{8,10},{9,11},{10,... | collective-permute-start | bytes 1376264 | tf_op jit(solution)/shard_map/ppermute | solution.py:25
  42.9 22.2 %copy-start.1 = (f32[54,32,128]{2,1,0:T(8,128)S(1)}, f32[54,32,128]{2,1,0:T(8,128)}, u32[]{:S(2)}) copy-start(f32[54,32,128]{2,1,0:T(8,128)} %param.11) | copy-start | bytes 2654212
  42.9 22.2 %copy-start.2 = (f32[32,128]{1,0:T(8,128)S(1)}, f32[32,128]{1,0:T(8,128)}, u32[]{:S(2)}) copy-start(f32[32,128]{1,0:T(8,128)} %refs_3_) | copy-start | bytes 49156
  42.9 22.2 %copy-start.3 = (f32[32,128]{1,0:T(8,128)S(1)}, f32[32,128]{1,0:T(8,128)}, u32[]{:S(2)}) copy-start(f32[32,128]{1,0:T(8,128)} %refs_4_) | copy-start | bytes 49156
  51.2 1.8 %collective-permute-start.4 = (f32[56,2048]{1,0:T(8,128)S(1)}, f32[56,2048]{1,0:T(8,128)S(1)}, u32[]{:S(2)}, u32[]{:S(2)}) collective-permute-start(f32[56,2048]{1,0:T(8,128)S(1)} %collective-permute-done.3.refs_0_), channel_id=1, source_target_pairs={{0,1},{1,0},{2,3},{3,2},{4,5},{5,4},{6,7},{7,6},{8,9},{9,8},{10,11... | collective-permute-start | bytes 1376264 | tf_op jit(solution)/shard_map/ppermute | solution.py:25
  51.2 2.5 %collective-permute-start.5 = (f32[56,2048]{1,0:T(8,128)S(1)}, f32[56,2048]{1,0:T(8,128)S(1)}, u32[]{:S(2)}, u32[]{:S(2)}) collective-permute-start(f32[56,2048]{1,0:T(8,128)S(1)} %collective-permute-done.2.refs_1_), channel_id=1, source_target_pairs={{0,1},{1,0},{2,3},{3,2},{4,5},{5,4},{6,7},{7,6},{8,9},{9,8},{10,11... | collective-permute-start | bytes 1376264 | tf_op jit(solution)/shard_map/ppermute | solution.py:25
  128.1 2.5 %collective-permute-start.6 = (f32[56,4096]{1,0:T(8,128)S(1)}, f32[56,4096]{1,0:T(8,128)S(1)}, u32[]{:S(2)}, u32[]{:S(2)}) collective-permute-start(f32[56,4096]{1,0:T(8,128)S(1)} %get-tuple-element.49), channel_id=1, source_target_pairs={{0,1},{1,0},{2,3},{3,2},{4,5},{5,4},{6,7},{7,6},{8,9},{9,8},{10,11... | collective-permute-start | bytes 2752520 | tf_op jit(solution)/shard_map/ppermute | solution.py:25
  130.8 25.9 %copy-start.8 = (f32[1,4096]{1,0:T(1,128)S(1)}, f32[1,4096]{1,0:T(1,128)}, u32[]{:S(2)}) copy-start(f32[1,4096]{1,0:T(1,128)} %get-tuple-element.31.rank_ref) | copy-start | bytes 49156
  143.1 13.6 %collective-permute-start.7 = (f32[56,4096]{1,0:T(8,128)S(1)}, f32[56,4096]{1,0:T(8,128)S(1)}, u32[]{:S(2)}, u32[]{:S(2)}) collective-permute-start(f32[56,4096]{1,0:T(8,128)S(1)} %get-tuple-element.56), channel_id=1, source_target_pairs={{0,1},{1,0},{2,3},{3,2},{4,5},{5,4},{6,7},{7,6},{8,9},{9,8},{10,11... | collective-permute-start | bytes 2752520 | tf_op jit(solution)/shard_map/ppermute | solution.py:25
  143.3 13.4 %collective-permute-start.9 = (f32[56,2048]{1,0:T(8,128)S(1)}, f32[56,2048]{1,0:T(8,128)S(1)}, u32[]{:S(2)}, u32[]{:S(2)}) collective-permute-start(f32[56,2048]{1,0:T(8,128)S(1)} %get-tuple-element.57), channel_id=1, source_target_pairs={{0,2},{1,3},{2,0},{3,1},{4,6},{5,7},{6,4},{7,5},{8,10},{9,11},{10,... | collective-permute-start | bytes 1376264 | tf_op jit(solution)/shard_map/ppermute | solution.py:25
  144.2 21.7 %collective-permute-start.8 = (f32[56,2048]{1,0:T(8,128)S(1)}, f32[56,2048]{1,0:T(8,128)S(1)}, u32[]{:S(2)}, u32[]{:S(2)}) collective-permute-start(f32[56,2048]{1,0:T(8,128)S(1)} %get-tuple-element.60), channel_id=1, source_target_pairs={{0,2},{1,3},{2,0},{3,1},{4,6},{5,7},{6,4},{7,5},{8,10},{9,11},{10,... | collective-permute-start | bytes 1376264 | tf_op jit(solution)/shard_map/ppermute | solution.py:25
  156.7 9.2 %copy-start.4 = (f32[56,4096]{1,0:T(8,128)S(1)}, f32[56,4096]{1,0:T(8,128)}, u32[]{:S(2)}) copy-start(f32[56,4096]{1,0:T(8,128)} %get-tuple-element.58.refs_4_) | copy-start | bytes 2752516

commit v8 on v7

--- a/solution.py
+++ b/solution.py
@@ -91,6 +91,9 @@
         carry = carry + jnp.sum(hot, axis=1, keepdims=True)
 
 
+HALO_ORDER = {2: lambda n: (), 3: lambda n: range(1, n - 1), 0: lambda n: (), 1: lambda n: sorted({0, n - 1})}
+
+
 def head_kernel(grid_shape, cells, nshape, tiles, span, *refs):
     given, (t_ref, rank_ref, parts_ref, half_ref), refs = refs[:4], refs[4:8], refs[8:]
     les_ref, map_ref, shape_ref, diff_ref, key_ref, table_ref, *refs = refs
@@ -154,10 +157,9 @@
     number = jnp.where(row == lax.broadcasted_iota(jnp.int32, (species, species), 1), diff_ref[...], 0.0)
     number = jnp.sum(number, axis=1, keepdims=True)
     lane = lax.broadcasted_iota(jnp.int32, (species, LANES), 1)
-    for n, (there, _) in enumerate(sides):
+    for n in (2, 3, 0, 1):
         pl.when(sides[n ^ 1][0])(copies[n].wait_recv)
-    for x in range(nx):
-        for y in range(ny):
+        for x, y in [(x, y) for x in HALO_ORDER[n](nx) for y in range(ny)]:
             here = line(x, y)
             around = line(x + 1, y) if x < nx - 1 else halos[1][y, :species]
             around = around + (line(x - 1, y) if x else halos[0][y, :species])
@@ -314,8 +316,9 @@
     shape = key - cell * nshape
     tile = jnp.floor((cell + 0.5) * (1.0 / per_tile))
     within = cell - tile * per_tile
-    ids = lax.broadcasted_iota(jnp.int32, (nshape, key.shape[1]), 0).astype(F32)
-    picked = lax.dot_general(table, rows_equal(ids, shape), NN, preferred_element_type=F32).astype(BF16)
+    ids = lax.broadcasted_iota(jnp.int32, (nshape, key.shape[1]), 0).astype(F32).astype(BF16)
+    hot = jnp.where(ids == shape.astype(BF16), jnp.ones((), BF16), jnp.zeros((), BF16))
+    picked = lax.dot_general(table, hot, NN, preferred_element_type=F32).astype(BF16)
     masks = [jnp.where(within == m, 1.0, 0.0).astype(BF16) for m in range(per_tile)]
     columns = []
     for part in (picked[:bins], picked[bins:]):
@@ -342,13 +345,13 @@
 def collect_kernel(species, bins, per_tile, pairs, lists, *refs):
     sources, refs = [refs[2 * n : 2 * n + 2] for n in range(lists)], refs[2 * lists :]
     table_ref, out_ref, *refs = refs
-    keys, (weights, tiles, parts, steps, sems) = refs[:lists], refs[lists:]
+    weights, tiles, *refs = refs
+    keys, (parts, steps, sems) = refs[:lists], refs[lists:]
     copies = fetch_rows([source[0] for source in sources], steps, sems)
     rows, part = sources[0][0].shape
     count = 2 * part
     for key, source in zip(keys, sources):
-        key[:, :part] = source[0][rows - 8 :, :]
-        key[:, part:] = source[1][rows - 8 :, :]
+        key[...] = source[0][rows - 8 :, :LANES]
     blocks = count // LANES
     out_ref[...] = jnp.zeros_like(out_ref)
     table = split_table(table_ref[...])
@@ -396,12 +399,15 @@
     specs = [VMEM] * (2 * lists + 1)
     return pl.pallas_call(
         functools.partial(collect_kernel, species, bins, per_tile, pairs, lists),
-        out_shape=[jax.ShapeDtypeStruct((rows, ntiles * TILE), F32)] + [jax.ShapeDtypeStruct((8, count), F32)] * lists,
+        out_shape=[
+            jax.ShapeDtypeStruct((rows, ntiles * TILE), F32),
+            jax.ShapeDtypeStruct((lists * blocks, TILE, 2 * LANES), BF16),
+            jax.ShapeDtypeStruct((lists * blocks, 16, LANES), F32),
+        ]
+        + [jax.ShapeDtypeStruct((8, LANES), F32)] * lists,
         in_specs=specs,
-        out_specs=[VMEM] * (lists + 1),
+        out_specs=[VMEM] * (lists + 3),
         scratch_shapes=[
-            pltpu.VMEM((lists * blocks, TILE, 2 * LANES), BF16),
-            pltpu.VMEM((lists * blocks, 16, LANES), F32),
             pltpu.VMEM((lists * blocks, 2 * HALF, LANES), BF16),
             pltpu.SMEM((lists, 8, LANES), F32),
             pltpu.SemaphoreType.DMA((lists,)),
@@ -441,32 +447,22 @@
         out_ref[full * LANES :, :] = turn(full)[:rest]
 
 
-def project_kernel(bins, per_tile, pairs, lists, state_rows, *refs):
-    means, refs = refs[:3], refs[3:]
+def project_kernel(bins, pairs, lists, state_rows, *refs):
+    parts, weights, tiles, *refs = refs
     sources, refs = refs[:lists], refs[lists:]
-    table_ref, *refs = refs
+    mean = refs.pop(0) if state_rows else None
     outs, refs = refs[:lists], refs[lists:]
     state_ref = refs.pop(0) if state_rows else None
-    weights, tiles, parts, steps, sems, *turning = refs
+    steps, sems, *turning = refs
     copies = fetch_rows(sources, steps, sems)
     rows, count = outs[0].shape
     blocks = count // LANES
-    per_mean = means[0].shape[1] // TILE
-    for number, mean in enumerate(means):
-
-        def split(n, _, number=number, mean=mean):
-            parts[number * per_mean + n] = padded_halves(mean[:, pl.ds(pl.multiple_of(n * TILE, TILE), TILE)])
-            return 0
-
-        lax.fori_loop(0, per_mean, split, 0, unroll=2)
+    for out in outs:
+        out[...] = jnp.zeros_like(out)
     if state_rows:
-        turn_back(means[1], state_ref, bins, *turning)
-    table = split_table(table_ref[...])
+        turn_back(mean, state_ref, bins, *turning)
     for copy in copies:
         copy.wait()
-    for number in range(lists):
-        outs[number][...] = jnp.zeros_like(outs[number])
-        prepare_weights(sources[number], number * blocks, 6, table, bins, per_tile, weights, tiles)
 
     def step(n, _):
         for number in range(lists):
@@ -487,34 +483,31 @@
     lax.fori_loop(0, -(-pairs // GROUP), step, 0)
 
 
-def project_call(means, sources, table, bins, per_tile, ntiles, state_rows=0):
-    rows, count = means[0].shape[0], sources[0].shape[1]
+def project_call(parts, collected, rows, count, bins, ntiles, mean=None, state_rows=0):
+    weights, tiles, *sources = collected
     lists = len(sources)
-    blocks = count // LANES
-    pairs = blocks + ntiles - 1
+    pairs = count // LANES + ntiles - 1
+    extra = [] if mean is None else [mean]
+    scratch = [pltpu.SMEM((lists, 8, LANES), F32), pltpu.SemaphoreType.DMA((lists,))]
+    if extra:
+        scratch += [pltpu.VMEM((mean.size // LANES, LANES), F32), pltpu.VMEM((LANES, LANES), F32)]
     return pl.pallas_call(
-        functools.partial(project_kernel, bins, per_tile, pairs, lists, state_rows),
+        functools.partial(project_kernel, bins, pairs, lists, state_rows),
         out_shape=[jax.ShapeDtypeStruct((rows, count), F32)] * lists
-        + [jax.ShapeDtypeStruct((state_rows, LANES), F32)] * bool(state_rows),
-        in_specs=[VMEM] * (lists + 4),
-        out_specs=[VMEM] * (lists + bool(state_rows)),
-        scratch_shapes=[
-            pltpu.VMEM((lists * blocks, TILE, 2 * LANES), BF16),
-            pltpu.VMEM((lists * blocks, 16, LANES), F32),
-            pltpu.VMEM((ntiles, 2 * HALF, TILE), BF16),
-            pltpu.SMEM((lists, 8, LANES), F32),
-            pltpu.SemaphoreType.DMA((lists,)),
-        ] + [pltpu.VMEM((rows * means[0].shape[1] // LANES, LANES), F32), pltpu.VMEM((LANES, LANES), F32)] * bool(state_rows),
-        compiler_params=params(19),
+        + [jax.ShapeDtypeStruct((state_rows, LANES), F32)] * len(extra),
+        in_specs=[VMEM] * (3 + lists + len(extra)),
+        out_specs=[VMEM] * (lists + len(extra)),
+        scratch_shapes=scratch,
+        compiler_params=params(20),
         cost_estimate=pl.CostEstimate(flops=lists * pairs * 2 * LANES * TILE * TILE, bytes_accessed=0, transcendentals=0),
         name="project",
-    )(*means, *sources, table)
+    )(parts, weights, tiles, *sources, *extra)
 
 
 def middle_kernel(species, bins, chunk, refs_in, refs_out, scratch):
     *accs, cmc_ref, diss_ref, rate_ref, count_ref, matrix_ref = refs_in
-    fresh_ref, next_ref, far_ref = refs_out
-    nat, quads, turned, side_out, load, outward, hopped, summed, got, state_ref, edge_out, edge_in, side_in, pick_ref, third_ref, send, recv, side_send, side_recv = scratch
+    fresh_ref, parts_ref = refs_out
+    next_ref, far_ref, nat, quads, turned, side_out, load, outward, hopped, summed, got, state_ref, edge_out, edge_in, side_in, pick_ref, third_ref, send, recv, side_send, side_recv = scratch
     rows, width = fresh_ref.shape
     steps = width // chunk
     slab, nslab = lax.axis_index("slab"), lax.axis_size("slab")
@@ -703,7 +696,14 @@
             stack = jnp.concatenate([high, *gap, low, *gap, high, *gap], axis=0).astype(BF16)
             rate = lax.dot_general(third_ref[...], stack, NN, preferred_element_type=F32)
             state = jnp.where(k < count, state + half * jnp.tanh(rate), state)
-        fresh_ref[:, lanes(c)] = jnp.where(line == species, 1.0, state)
+        state = jnp.where(line == species, 1.0, state)
+        fresh_ref[:, lanes(c)] = state
+        keep(1, c, state)
+
+    def keep(which, c, mean):
+        for n in range(chunk // TILE):
+            index = which * (width // TILE) + c * (chunk // TILE) + n
+            parts_ref[index] = padded_halves(mean[:, n * TILE : (n + 1) * TILE])
 
     def step(t, _):
         def when(lag, body):
@@ -723,6 +723,7 @@
         def fourth(c):
             give(c).wait_recv()
             pl.when(has_inner)(lambda: pass_on(c).start())
+            keep(2, c, next_ref[:, lanes(c)])
 
         when(0, add_hop)
         when(LAG[0], second)
@@ -743,6 +744,7 @@
         give(c).wait_send()
         pl.when(has_inner)(lambda: pass_on(c).wait_send())
         pl.when(has_outer)(lambda: pass_on(c).wait_recv())
+        keep(0, c, far_ref[:, lanes(c)])
         return 0
 
     lax.fori_loop(0, steps, finish, 0)
@@ -750,27 +752,31 @@
     pl.when(has_down)(to_down.wait_send)
 
 
-def middle_call(accs, cmc, diss, rate, count, matrix, species, bins, chunk=512):
+def middle_call(accs, cmc, diss, rate, count, matrix, species, bins, chunk=256):
     rows, width = accs[0].shape[0], count.shape[1]
     steps = width // chunk
     given = len(accs) + 5
 
     def kernel(*refs):
-        middle_kernel(species, bins, chunk, refs[:given], refs[given : given + 3], refs[given + 3 :])
+        middle_kernel(species, bins, chunk, refs[:given], refs[given : given + 2], refs[given + 2 :])
 
     return pl.pallas_call(
         kernel,
-        out_shape=[jax.ShapeDtypeStruct((rows, width), F32)] * 3,
+        out_shape=[
+            jax.ShapeDtypeStruct((rows, width), F32),
+            jax.ShapeDtypeStruct((3 * width // TILE, 2 * HALF, TILE), BF16),
+        ],
         in_specs=[VMEM] * len(accs) + [pl.BlockSpec(memory_space=pl.ANY)] * 3 + [VMEM] * 2,
-        out_specs=[VMEM] * 3,
-        scratch_shapes=[pltpu.VMEM((rows * bins, LANES), F32), pltpu.VMEM((rows * width // LANES, LANES), F32)]
+        out_specs=[VMEM] * 2,
+        scratch_shapes=[pltpu.VMEM((rows, width), F32)] * 2
+        + [pltpu.VMEM((rows * bins, LANES), F32), pltpu.VMEM((rows * width // LANES, LANES), F32)]
         + [pltpu.VMEM((LANES, LANES), F32), pltpu.VMEM((2, rows, LANES), F32), pltpu.SemaphoreType.DMA((3,))]
         + [pltpu.VMEM((rows, width), F32)] * 5
         + [pltpu.VMEM((steps, rows, 2 * LANES), F32)] * 2
         + [pltpu.VMEM((2, rows, LANES), F32), pltpu.VMEM((2 * LANES, chunk), BF16), pltpu.VMEM(matrix.shape, BF16)]
         + [pltpu.SemaphoreType.DMA((6, steps))] * 2
         + [pltpu.SemaphoreType.DMA((2,))] * 2,
-        compiler_params=pltpu.CompilerParams(vmem_limit_bytes=20 << 20, collective_id=1, has_side_effects=True),
+        compiler_params=pltpu.CompilerParams(vmem_limit_bytes=22 << 20, collective_id=1, has_side_effects=True),
         name="middle",
     )(*accs, cmc, diss, rate, count, matrix)
 
@@ -801,23 +807,30 @@
     extra = rows - species
     matrix = jnp.tile(jnp.pad(chem_matrix, ((0, extra), (0, -(-rows // 16) * 16 - species))), (1, 3))
     terms = (cmc_state.reshape(species * bins, cells), dissipation, reaction_rate, jnp.repeat(substeps, bins)[None, :], matrix)
-    acc, *near_keys = collect_call(near_lists, table, species, bins, per_tile, ntiles)
+    acc, *near = collect_call(near_lists, table, species, bins, per_tile, ntiles)
     acc, high_there, terms = lax.optimization_barrier((acc, high_there, terms))
     high_far = [high_there] + [swap(high_there, "cross", bit) for bit in bits[:-1]]
-    more, *far_keys = collect_call(list(zip(low_far, high_far)), table, species, bins, per_tile, ntiles)
-    accs = [acc, more]
-    means = middle_call(accs, *terms, species, bins)
-    means = [means[2], means[0], means[1]]
-    there, *pieces = project_call(means, far_keys, table, bins, per_tile, ntiles)
-    pieces = [swap(piece, "cross", bit) for bit, piece in zip(bits[:-1], pieces)]
+    accs, far = [acc], []
+    for pair in zip(low_far, high_far):
+        acc, *collected = collect_call([pair], table, species, bins, per_tile, ntiles)
+        accs.append(acc)
+        far.append(collected)
+    fresh, parts = middle_call(accs, *terms, species, bins)
+
+    pieces = []
+    for bit, collected in zip(bits[:-1], far[1:]):
+        (piece,) = project_call(parts, collected, rows, count, bins, ntiles)
+        piece, parts = lax.optimization_barrier((piece, parts))
+        pieces.append(swap(piece, "cross", bit))
+    (there,) = project_call(parts, far[0], rows, count, bins, ntiles)
     part = count // 2
     low, high = there[:, :part], there[:, part:]
     for piece in pieces:
         low, high = low + piece[:, :part], high + piece[:, part:]
-    low, means = lax.optimization_barrier((low, means))
+    low, parts = lax.optimization_barrier((low, parts))
     low = swap(low, "cross", bits[-1])
     high = swap(high, "cross", bits[-1])
-    *here, cmc_out = project_call(means, near_keys, table, bins, per_tile, ntiles, species * bins)
+    *here, cmc_out = project_call(parts, near, rows, count, bins, ntiles, fresh, species * bins)
     total = [here[0]] + [swap(piece, "cross", bit) for bit, piece in zip(bits[:-1], here[1:])]
     before = unsort_call(total, low, rank, None, None)
     les_out = unsort_call(total, high, rank, before, flat)

time: 174 us -> 167 us (0.960)
  waiting for transfers between devices: 27.5 us -> 23 us
  Pallas kernels: 137 us -> 134 us
    pallas_call x2 -> x3, Pallas kernels: 20.2 us -> 14.4 us  [project_call(): pl.pallas_call(functools.partial(project_kernel, bins, pairs, lists, stat...]
    ppermute x10, waiting for transfers between devices: 27.5 us -> 23 us  [swap(): return lax.ppermute(array, axis, [(i, i ^ bit) for i in range(count)])]
    pallas_call x1, Pallas kernels: 55.2 us -> 57.4 us  [middle_call(): pl.pallas_call(kernel, out_shape=[jax.ShapeDtypeStruct((rows, width), F32...]
    pallas_call x2 -> x3, Pallas kernels: 22.7 us -> 24 us  [collect_call(): pl.pallas_call(functools.partial(collect_kernel, species, bins, per_tile,...]
  transfers between devices with their start and end apart: 10 -> 10, of which waited for: 6 -> 3; matrix products, arithmetic and copies ran while one was open for 0% -> 0% of each run, Pallas kernels for 10% -> 16%
where the time goes in v8:
time: 167 us; the launch traced here: 166 us
  Pallas kernels  134 us (80%)
  waiting for transfers between devices  23 us (14%)
  starting transfers between devices  6.12 us (4%)
  local copies, waits for them, and re-layouts  2.43 us (1%)
    pallas_call x1, Pallas kernels, middle_call(): pl.pallas_call(kernel, out_shape=[jax.ShapeDtypeStruct((rows, width), F32...  57.4 us
    pallas_call x3, Pallas kernels, collect_call(): pl.pallas_call(functools.partial(collect_kernel, species, bins, per_tile,...  24 us
    ppermute x10, waiting for transfers between devices, swap(): return lax.ppermute(array, axis, [(i, i ^ bit) for i in range(count)])  23 us
    pallas_call x1, Pallas kernels, head_call(): pl.pallas_call(functools.partial(head_kernel, (species, nx, ny), cells, n...  18 us
    pallas_call x3, Pallas kernels, project_call(): pl.pallas_call(functools.partial(project_kernel, bins, pairs, lists, stat...  14.4 us
    pallas_call x2, Pallas kernels, unsort_call(): pl.pallas_call(functools.partial(unsort_kernel, half, len(wholes) + 1), g...  13.6 us
    pallas_call x1, Pallas kernels, sort_call(): pl.pallas_call(sort_kernel, out_shape=jax.ShapeDtypeStruct((rows, count /...  6.36 us
    ppermute x10, starting transfers between devices, swap(): return lax.ppermute(array, axis, [(i, i ^ bit) for i in range(count)])  6.12 us
  transfers between devices with their start and end apart: 10, of which 3 were waited for; matrix products, arithmetic and copies ran while one was open for 0% of the time, Pallas kernels for 16%

profile of v8, /device:TPU:2, one launch (start us, length us, event | category | flops | bytes accessed | tf_op | source)
XLA Modules:
  0.0 166.4 jit_solution(74960134365628999)
XLA Ops:
  0.6 0.0 copy-start
  0.6 18.0 %head.1 = (f32[56,4096]{1,0:T(8,128)}, f32[1,4096]{1,0:T(1,128)}, bf16[112,4096]{1,0:T(8,128)(2,1)}, f32[56,2048]{1,0:T(8,128)}) custom-call(f32[1728,128]{1,0:T(8,128)} %bitcast.12, s32[1,4096]{1,0:T(1,128)} %bitcast.13, s32[1,4096]{1,0:T(1,128)} %bitcast.14, f32[1,54]{1,0:T(1,128)} %bitcast.15), custom_call_target="tpu_custom_call" | custom-call | tf_op jit(solution)/shard_map/head/pallas_call | solution.py:184
  18.7 0.0 copy-start.5
  18.7 1.2 copy-done.5
  19.9 0.7 copy-done.7
  20.6 6.4 %sort.1.refs_1_ = f32[56,2048]{1,0:T(8,128)S(1)} custom-call(bf16[112,4096]{1,0:T(8,128)(2,1)S(1)} %copy-done.5, f32[1,4096]{1,0:T(1,128)S(1)} %copy-done.7), custom_call_target="tpu_custom_call" | custom-call | flops 1879048192 | bytes 917504 | tf_op jit(solution)/shard_map/sort/pallas_call | solution.py:241
  27.0 0.8 collective-permute-start.1
  27.8 0.0 copy-done.6
  27.8 0.1 collective-permute-start
  27.9 0.6 collective-permute-start.2
  28.5 1.5 collective-permute-start.3
  29.9 0.0 copy-done
  29.9 0.1 constant_dynamic-slice_fusion
  30.0 0.1 copy.14
  30.1 0.1 broadcast_in_dim.3
  30.2 0.1 broadcast_in_dim_reshape.3.refs_6_
  30.3 0.1 tile.10.refs_7_
  30.5 0.0 collective-permute-done.1.refs_3_
  30.5 0.0 collective-permute-done.refs_2_
  30.5 11.6 %collect.3 = (f32[56,12288]{1,0:T(8,128)S(1)}, bf16[64,256,256]{2,1,0:T(8,128)(2,1)S(1)}, f32[64,16,128]{2,1,0:T(8,128)S(1)}, f32[8,128]{1,0:T(8,128)S(1)}, f32[8,128]{1,0:T(8,128)S(1)}) custom-call(f32[56,2048]{1,0:T(8,128)S(1)} %copy-done.6, f32[56,2048]{1,0:T(8,128)S(1)} %sort.1.refs_1_, f32[56,2048]{1,0:T(8,128)S(1)} %collective-permute-done.refs_2_, ...), custom_call_target="tpu_custom_call" | custom-call | flops 2650800128 | tf_op jit(solution)/shard_map/collect/pallas_call | solution.py:400
  42.1 0.0 collective-permute-done.2.refs_1_
  42.1 8.5 %collective-permute-done.3.refs_0_ = f32[56,2048]{1,0:T(8,128)S(1)} collective-permute-done((f32[56,2048]{1,0:T(8,128)S(1)}, f32[56,2048]{1,0:T(8,128)S(1)}, u32[]{:S(2)}, u32[]{:S(2)}) %collective-permute-start.3) | collective-permute-done | bytes 458784 | tf_op jit(solution)/shard_map/ppermute | solution.py:25
  50.6 0.0 collective-permute-start.4
  50.6 0.5 collective-permute-start.5
  51.1 6.2 %collect.4 = (f32[56,12288]{1,0:T(8,128)S(1)}, bf16[32,256,256]{2,1,0:T(8,128)(2,1)S(1)}, f32[32,16,128]{2,1,0:T(8,128)S(1)}, f32[8,128]{1,0:T(8,128)S(1)}) custom-call(f32[56,2048]{1,0:T(8,128)S(1)} %collective-permute-done.3.refs_0_, f32[56,2048]{1,0:T(8,128)S(1)} %collective-permute-done.2.refs_1_, f32[32,128]{1,0:T(8,128)S(1)} %bitcast.10), custom_call_target="tpu_custom_call" | custom-call | flops 1325400064 | tf_op jit(solution)/shard_map/collect/pallas_call | solution.py:400
  57.3 0.0 copy-start.1
  57.3 0.0 copy-start.2
  57.3 0.0 copy-start.3
  57.3 0.0 collective-permute-done.4.refs_0_
  57.3 0.0 collective-permute-done.5.refs_1_
  57.4 6.2 %collect.5 = (f32[56,12288]{1,0:T(8,128)S(1)}, bf16[32,256,256]{2,1,0:T(8,128)(2,1)S(1)}, f32[32,16,128]{2,1,0:T(8,128)S(1)}, f32[8,128]{1,0:T(8,128)S(1)}) custom-call(f32[56,2048]{1,0:T(8,128)S(1)} %collective-permute-done.4.refs_0_, f32[56,2048]{1,0:T(8,128)S(1)} %collective-permute-done.5.refs_1_, f32[32,128]{1,0:T(8,128)S(1)} %bitcast.11), custom_call_target="tpu_custom_call" | custom-call | flops 1325400064 | tf_op jit(solution)/shard_map/collect/pallas_call | solution.py:400
  63.6 57.4 %middle.1 = (f32[56,4096]{1,0:T(8,128)S(1)}, bf16[48,128,256]{2,1,0:T(8,128)(2,1)S(1)}) custom-call(f32[56,12288]{1,0:T(8,128)S(1)} %get-tuple-element.39.refs_0_, f32[56,12288]{1,0:T(8,128)S(1)} %get-tuple-element.41.refs_1_, f32[56,12288]{1,0:T(8,128)S(1)} %get-tuple-element.42.refs_2_, f32[1728,128]{1,0:T(8,128)S(1)} %bitcast.8, f32[32,128]{1,0:T(8,128)S(1)} %copy-done.2, ...), custom_call_target="tpu_custom_call" | custom-call | tf_op jit(solution)/shard_map/middle/pallas_call | solution.py:763
  121.0 3.0 %project.3 = f32[56,4096]{1,0:T(8,128)S(1)} custom-call(bf16[48,128,256]{2,1,0:T(8,128)(2,1)S(1)} %get-tuple-element.57.refs_0_, bf16[32,256,256]{2,1,0:T(8,128)(2,1)S(1)} %get-tuple-element.49.refs_1_, f32[32,16,128]{2,1,0:T(8,128)S(1)} %get-tuple-element.50.refs_2_, f32[8,128]{1,0:T(8,128)S(1)} %get-tuple-element.51.refs_3_), custom_call_target="tpu_custom_call" | custom-call | flops 1325400064 | tf_op jit(solution)/shard_map/project/pallas_call | solution.py:494
  124.0 0.1 collective-permute-start.6
  124.1 3.0 %project.4 = f32[56,4096]{1,0:T(8,128)S(1)} custom-call(bf16[48,128,256]{2,1,0:T(8,128)(2,1)S(1)} %get-tuple-element.57.refs_0_, bf16[32,256,256]{2,1,0:T(8,128)(2,1)S(1)} %get-tuple-element.53.refs_1_, f32[32,16,128]{2,1,0:T(8,128)S(1)} %get-tuple-element.54.refs_2_, f32[8,128]{1,0:T(8,128)S(1)} %get-tuple-element.55.refs_3_), custom_call_target="tpu_custom_call" | custom-call | flops 1325400064 | tf_op jit(solution)/shard_map/project/pallas_call | solution.py:494
  127.1 0.0 collective-permute-done.6
  127.1 0.1 slice_add_fusion
  127.2 0.0 copy-start.8
  127.2 8.5 %project.5 = (f32[56,4096]{1,0:T(8,128)S(1)}, f32[56,4096]{1,0:T(8,128)S(1)}, f32[1728,128]{1,0:T(8,128)}) custom-call(bf16[48,128,256]{2,1,0:T(8,128)(2,1)S(1)} %get-tuple-element.57.refs_0_, bf16[64,256,256]{2,1,0:T(8,128)(2,1)S(1)} %get-tuple-element.58.refs_1_, f32[64,16,128]{2,1,0:T(8,128)S(1)} %get-tuple-element.59.refs_2_, ...), custom_call_target="tpu_custom_call" | custom-call | flops 2650800128 | tf_op jit(solution)/shard_map/project/pallas_call | solution.py:494
  135.7 0.6 collective-permute-start.7
  136.3 0.3 collective-permute-start.9
  136.6 1.7 %collective-permute-start.8 = (f32[56,2048]{1,0:T(8,128)S(1)}, f32[56,2048]{1,0:T(8,128)S(1)}, u32[]{:S(2)}, u32[]{:S(2)}) collective-permute-start(f32[56,2048]{1,0:T(8,128)S(1)} %get-tuple-element.68), channel_id=1, source_target_pairs={{0,2},{1,3},{2,0},{3,1},{4,6},{5,7},{6,4},{7,5},{8,10},{9,11},{10,... | collective-permute-start | bytes 1376264 | tf_op jit(solution)/shard_map/ppermute | solution.py:25
  138.3 11.4 %collective-permute-done.9.refs_2_ = f32[56,2048]{1,0:T(8,128)S(1)} collective-permute-done((f32[56,2048]{1,0:T(8,128)S(1)}, f32[56,2048]{1,0:T(8,128)S(1)}, u32[]{:S(2)}, u32[]{:S(2)}) %collective-permute-start.9) | collective-permute-done | bytes 458784 | tf_op jit(solution)/shard_map/ppermute | solution.py:25
  149.7 0.0 collective-permute-done.7.refs_1_
  149.7 5.8 %unsort.2.refs_3_ = f32[56,4096]{1,0:T(8,128)S(1)} custom-call(f32[1,4096]{1,0:T(1,128)S(1)} %copy-done.8, f32[56,4096]{1,0:T(8,128)S(1)} %get-tuple-element.63.refs_0_, f32[56,4096]{1,0:T(8,128)S(1)} %collective-permute-done.7.refs_1_, f32[56,2048]{1,0:T(8,128)S(1)} %collective-permute-done.9.refs_2_), custom_call_target="tpu_custom_call" | custom-call | flops 1879048192 | bytes 917504 | tf_op jit(solution)/shard_map/unsort/pallas_call | solution.py:300
  155.5 3.1 %collective-permute-done.8.refs_2_ = f32[56,2048]{1,0:T(8,128)S(1)} collective-permute-done((f32[56,2048]{1,0:T(8,128)S(1)}, f32[56,2048]{1,0:T(8,128)S(1)}, u32[]{:S(2)}, u32[]{:S(2)}) %collective-permute-start.8) | collective-permute-done | bytes 458784 | tf_op jit(solution)/shard_map/ppermute | solution.py:25
  158.6 0.0 copy-done.4
  158.6 7.8 %unsort.3 = f32[1728,128]{1,0:T(8,128)} custom-call(f32[1,4096]{1,0:T(1,128)S(1)} %copy-done.8, f32[56,4096]{1,0:T(8,128)S(1)} %get-tuple-element.63.refs_0_, f32[56,4096]{1,0:T(8,128)S(1)} %collective-permute-done.7.refs_1_, f32[56,2048]{1,0:T(8,128)S(1)} %collective-permute-done.8.refs_2_, f32[56,4096]{1,0:T(8,128)S(1)} %unsort.2.refs_3_, ...), custom_call_target="tpu_custom_call" | custom-call | flops 1879048192 | bytes 917504 | tf_op jit(solution)/shard_map/unsort/pallas_call | solution.py:300
  (13 shorter events, 0.0 us)
Async XLA Ops:
  0.6 29.3 %copy-start = (f32[128,128]{1,0:T(8,128)S(1)}, f32[128,128]{1,0:T(8,128)}, u32[]{:S(2)}) copy-start(f32[128,128]{1,0:T(8,128)} %param.14) | copy-start | bytes 196612
  18.7 1.2 copy-start.5
  19.9 0.7 copy-start.7
  20.6 7.2 %copy-start.6 = (f32[56,2048]{1,0:T(8,128)S(1)}, f32[56,2048]{1,0:T(8,128)}, u32[]{:S(2)}) copy-start(f32[56,2048]{1,0:T(8,128)} %get-tuple-element.36.refs_0_) | copy-start | bytes 1376260
  20.6 9.5 %copy-start.10 = (s32[128]{0:T(128)S(1)}, s32[128]{0:T(128)}, u32[]{:S(2)}) copy-start(s32[128]{0:T(128)} %param.19) | copy-start | bytes 1540
  20.6 9.7 %copy-start.9 = (f32[54,54]{1,0:T(8,128)S(1)}, f32[54,54]{1,0:T(8,128)}, u32[]{:S(2)}) copy-start(f32[54,54]{1,0:T(8,128)} %param.16) | copy-start | bytes 34996
  27.0 3.5 %collective-permute-start.1 = (f32[56,2048]{1,0:T(8,128)S(1)}, f32[56,2048]{1,0:T(8,128)S(1)}, u32[]{:S(2)}, u32[]{:S(2)}) collective-permute-start(f32[56,2048]{1,0:T(8,128)S(1)} %sort.1.refs_1_), channel_id=1, source_target_pairs={{0,1},{1,0},{2,3},{3,2},{4,5},{5,4},{6,7},{7,6},{8,9},{9,8},{10,11... | collective-permute-start | bytes 1376264 | tf_op jit(solution)/shard_map/ppermute | solution.py:25
  27.8 2.7 %collective-permute-start = (f32[56,2048]{1,0:T(8,128)S(1)}, f32[56,2048]{1,0:T(8,128)S(1)}, u32[]{:S(2)}, u32[]{:S(2)}) collective-permute-start(f32[56,2048]{1,0:T(8,128)S(1)} %copy-done.6), channel_id=1, source_target_pairs={{0,1},{1,0},{2,3},{3,2},{4,5},{5,4},{6,7},{7,6},{8,9},{9,8},{10,11... | collective-permute-start | bytes 1376264 | tf_op jit(solution)/shard_map/ppermute | solution.py:25
  27.9 14.2 %collective-permute-start.2 = (f32[56,2048]{1,0:T(8,128)S(1)}, f32[56,2048]{1,0:T(8,128)S(1)}, u32[]{:S(2)}, u32[]{:S(2)}) collective-permute-start(f32[56,2048]{1,0:T(8,128)S(1)} %sort.1.refs_1_), channel_id=1, source_target_pairs={{0,2},{1,3},{2,0},{3,1},{4,6},{5,7},{6,4},{7,5},{8,10},{9,11},{10,... | collective-permute-start | bytes 1376264 | tf_op jit(solution)/shard_map/ppermute | solution.py:25
  28.5 22.1 %collective-permute-start.3 = (f32[56,2048]{1,0:T(8,128)S(1)}, f32[56,2048]{1,0:T(8,128)S(1)}, u32[]{:S(2)}, u32[]{:S(2)}) collective-permute-start(f32[56,2048]{1,0:T(8,128)S(1)} %copy-done.6), channel_id=1, source_target_pairs={{0,2},{1,3},{2,0},{3,1},{4,6},{5,7},{6,4},{7,5},{8,10},{9,11},{10,... | collective-permute-start | bytes 1376264 | tf_op jit(solution)/shard_map/ppermute | solution.py:25
  50.6 6.8 %collective-permute-start.4 = (f32[56,2048]{1,0:T(8,128)S(1)}, f32[56,2048]{1,0:T(8,128)S(1)}, u32[]{:S(2)}, u32[]{:S(2)}) collective-permute-start(f32[56,2048]{1,0:T(8,128)S(1)} %collective-permute-done.3.refs_0_), channel_id=1, source_target_pairs={{0,1},{1,0},{2,3},{3,2},{4,5},{5,4},{6,7},{7,6},{8,9},{9,8},{10,11... | collective-permute-start | bytes 1376264 | tf_op jit(solution)/shard_map/ppermute | solution.py:25
  50.6 6.8 %collective-permute-start.5 = (f32[56,2048]{1,0:T(8,128)S(1)}, f32[56,2048]{1,0:T(8,128)S(1)}, u32[]{:S(2)}, u32[]{:S(2)}) collective-permute-start(f32[56,2048]{1,0:T(8,128)S(1)} %collective-permute-done.2.refs_1_), channel_id=1, source_target_pairs={{0,1},{1,0},{2,3},{3,2},{4,5},{5,4},{6,7},{7,6},{8,9},{9,8},{10,11... | collective-permute-start | bytes 1376264 | tf_op jit(solution)/shard_map/ppermute | solution.py:25
  57.3 6.3 %copy-start.1 = (f32[54,32,128]{2,1,0:T(8,128)S(1)}, f32[54,32,128]{2,1,0:T(8,128)}, u32[]{:S(2)}) copy-start(f32[54,32,128]{2,1,0:T(8,128)} %param.11) | copy-start | bytes 2654212
  57.3 6.3 %copy-start.2 = (f32[32,128]{1,0:T(8,128)S(1)}, f32[32,128]{1,0:T(8,128)}, u32[]{:S(2)}) copy-start(f32[32,128]{1,0:T(8,128)} %refs_4_) | copy-start | bytes 49156
  57.3 6.3 %copy-start.3 = (f32[32,128]{1,0:T(8,128)S(1)}, f32[32,128]{1,0:T(8,128)}, u32[]{:S(2)}) copy-start(f32[32,128]{1,0:T(8,128)} %refs_5_) | copy-start | bytes 49156
  124.0 3.0 %collective-permute-start.6 = (f32[56,4096]{1,0:T(8,128)S(1)}, f32[56,4096]{1,0:T(8,128)S(1)}, u32[]{:S(2)}, u32[]{:S(2)}) collective-permute-start(f32[56,4096]{1,0:T(8,128)S(1)} %project.3), channel_id=1, source_target_pairs={{0,1},{1,0},{2,3},{3,2},{4,5},{5,4},{6,7},{7,6},{8,9},{9,8},{10,11... | collective-permute-start | bytes 2752520 | tf_op jit(solution)/shard_map/ppermute | solution.py:25
  127.2 22.5 %copy-start.8 = (f32[1,4096]{1,0:T(1,128)S(1)}, f32[1,4096]{1,0:T(1,128)}, u32[]{:S(2)}) copy-start(f32[1,4096]{1,0:T(1,128)} %get-tuple-element.35.rank_ref) | copy-start | bytes 49156
  135.7 14.0 %collective-permute-start.7 = (f32[56,4096]{1,0:T(8,128)S(1)}, f32[56,4096]{1,0:T(8,128)S(1)}, u32[]{:S(2)}, u32[]{:S(2)}) collective-permute-start(f32[56,4096]{1,0:T(8,128)S(1)} %get-tuple-element.64), channel_id=1, source_target_pairs={{0,1},{1,0},{2,3},{3,2},{4,5},{5,4},{6,7},{7,6},{8,9},{9,8},{10,11... | collective-permute-start | bytes 2752520 | tf_op jit(solution)/shard_map/ppermute | solution.py:25
  136.3 13.4 %collective-permute-start.9 = (f32[56,2048]{1,0:T(8,128)S(1)}, f32[56,2048]{1,0:T(8,128)S(1)}, u32[]{:S(2)}, u32[]{:S(2)}) collective-permute-start(f32[56,2048]{1,0:T(8,128)S(1)} %get-tuple-element.65), channel_id=1, source_target_pairs={{0,2},{1,3},{2,0},{3,1},{4,6},{5,7},{6,4},{7,5},{8,10},{9,11},{10,... | collective-permute-start | bytes 1376264 | tf_op jit(solution)/shard_map/ppermute | solution.py:25
  136.6 22.0 %collective-permute-start.8 = (f32[56,2048]{1,0:T(8,128)S(1)}, f32[56,2048]{1,0:T(8,128)S(1)}, u32[]{:S(2)}, u32[]{:S(2)}) collective-permute-start(f32[56,2048]{1,0:T(8,128)S(1)} %get-tuple-element.68), channel_id=1, source_target_pairs={{0,2},{1,3},{2,0},{3,1},{4,6},{5,7},{6,4},{7,5},{8,10},{9,11},{10,... | collective-permute-start | bytes 1376264 | tf_op jit(solution)/shard_map/ppermute | solution.py:25
  149.7 8.9 %copy-start.4 = (f32[56,4096]{1,0:T(8,128)S(1)}, f32[56,4096]{1,0:T(8,128)}, u32[]{:S(2)}) copy-start(f32[56,4096]{1,0:T(8,128)} %get-tuple-element.66.refs_4_) | copy-start | bytes 2752516

commit v9 on v8

--- a/solution.py
+++ b/solution.py
@@ -17,7 +17,7 @@
 TILE = 256
 HALF = 64
 GROUP = 16
-LAG = (2, 4, 6)
+LAG = (3, 6, 9)
 
 
 def swap(array, axis, bit):
@@ -169,10 +169,17 @@
             around = around + jnp.where(lane > 0, pltpu.roll(here, 1, 1), 0.0)
             place = (x * ny + y) * LANES
             t_ref[:species, place : place + LANES] = here + number * (around - 6.0 * here)
-    x = t_ref[...]
-    high = x.astype(BF16).astype(F32)
-    parts_ref[...] = jnp.concatenate([high, x - high], axis=0).astype(BF16)
-    sort_tiles(parts_ref, rank_ref, table_ref[...], half_ref, 0)
+        planes = list(HALO_ORDER[n](nx))
+        for x in planes:
+            piece = slice(x * ny * LANES, (x + 1) * ny * LANES)
+            value = t_ref[:, piece]
+            high = value.astype(BF16).astype(F32)
+            parts_ref[:, piece] = jnp.concatenate([high, value - high], axis=0).astype(BF16)
+        if planes and ny * LANES == CHUNK:
+            last = n == 1
+            sort_tiles(parts_ref, rank_ref, table_ref[...] if last else None, half_ref, 0, planes, last and nx > 2)
+    if ny * LANES != CHUNK:
+        sort_tiles(parts_ref, rank_ref, table_ref[...], half_ref, 0)
     for n, (there, _) in enumerate(sides):
         pl.when(there)(copies[n].wait_send)
 
@@ -210,23 +217,26 @@
 CHUNK = 2 * TILE
 
 
-def sort_tiles(parts, rank_ref, steps, out_ref, first):
+def sort_tiles(parts, rank_ref, steps, out_ref, first, pieces=None, more=False):
     rows = out_ref.shape[0]
     count = rank_ref.shape[1]
 
     def step(n, _):
         here = (first + n) * TILE
         total = jnp.zeros((2 * rows, TILE), F32)
-        for k in range(count // CHUNK):
+        for k in range(count // CHUNK) if pieces is None else pieces:
             piece = slice(k * CHUNK, (k + 1) * CHUNK)
             ids = lax.broadcasted_iota(jnp.int32, (TILE, CHUNK), 0) + here
             hot = rows_equal(ids.astype(F32), rank_ref[:, piece])
             total = total + lax.dot_general(parts[:, piece], hot, NT, preferred_element_type=F32)
         total = total[:rows] + total[rows:]
+        place = pl.ds(pl.multiple_of(n * TILE, TILE), TILE)
+        if more:
+            total = total + out_ref[:, place]
         if steps is not None:
             line = lax.broadcasted_iota(jnp.int32, (rows, TILE), 0)
             total = jnp.where(line == rows - 1, jnp.concatenate([steps] * (TILE // LANES), axis=1), total)
-        out_ref[:, pl.ds(pl.multiple_of(n * TILE, TILE), TILE)] = total
+        out_ref[:, place] = total
         return 0
 
     lax.fori_loop(0, out_ref.shape[1] // TILE, step, 0)
@@ -752,7 +762,7 @@
     pl.when(has_down)(to_down.wait_send)
 
 
-def middle_call(accs, cmc, diss, rate, count, matrix, species, bins, chunk=256):
+def middle_call(accs, cmc, diss, rate, count, matrix, species, bins, chunk=512):
     rows, width = accs[0].shape[0], count.shape[1]
     steps = width // chunk
     given = len(accs) + 5

time: 167 us -> 165 us (0.988)
  Pallas kernels: 134 us -> 129 us
  starting transfers between devices: 6.12 us -> 9.91 us
    ppermute x10, starting transfers between devices: 6.12 us -> 9.91 us  [swap(): return lax.ppermute(array, axis, [(i, i ^ bit) for i in range(count)])]
    pallas_call x1, Pallas kernels: 57.4 us -> 54.6 us  [middle_call(): pl.pallas_call(kernel, out_shape=[jax.ShapeDtypeStruct((rows, width), F32...]
    pallas_call x1, Pallas kernels: 18 us -> 15.5 us  [head_call(): pl.pallas_call(functools.partial(head_kernel, (species, nx, ny), cells, n...]
where the time goes in v9:
time: 165 us
  Pallas kernels  129 us (78%)
  waiting for transfers between devices  23 us (14%)
  starting transfers between devices  9.91 us (6%)
  local copies, waits for them, and re-layouts  2.43 us (1%)
    pallas_call x1, Pallas kernels, middle_call(): pl.pallas_call(kernel, out_shape=[jax.ShapeDtypeStruct((rows, width), F32...  54.6 us
    pallas_call x3, Pallas kernels, collect_call(): pl.pallas_call(functools.partial(collect_kernel, species, bins, per_tile,...  24 us
    ppermute x10, waiting for transfers between devices, swap(): return lax.ppermute(array, axis, [(i, i ^ bit) for i in range(count)])  23 us
    pallas_call x1, Pallas kernels, head_call(): pl.pallas_call(functools.partial(head_kernel, (species, nx, ny), cells, n...  15.5 us
    pallas_call x3, Pallas kernels, project_call(): pl.pallas_call(functools.partial(project_kernel, bins, pairs, lists, stat...  14.4 us
    pallas_call x2, Pallas kernels, unsort_call(): pl.pallas_call(functools.partial(unsort_kernel, half, len(wholes) + 1), g...  13.6 us
    ppermute x10, starting transfers between devices, swap(): return lax.ppermute(array, axis, [(i, i ^ bit) for i in range(count)])  9.91 us
    pallas_call x1, Pallas kernels, sort_call(): pl.pallas_call(sort_kernel, out_shape=jax.ShapeDtypeStruct((rows, count /...  6.36 us
  transfers between devices with their start and end apart: 10, of which 3 were waited for; matrix products, arithmetic and copies ran while one was open for 0% of the time, Pallas kernels for 16%

profile of v9, /device:TPU:2, one launch (start us, length us, event | category | flops | bytes accessed | tf_op | source)
XLA Modules:
  0.0 164.8 jit_solution(3033970424637398635)
XLA Ops:
  0.6 0.0 copy-start
  0.6 15.5 %head.1 = (f32[56,4096]{1,0:T(8,128)}, f32[1,4096]{1,0:T(1,128)}, bf16[112,4096]{1,0:T(8,128)(2,1)}, f32[56,2048]{1,0:T(8,128)}) custom-call(f32[1728,128]{1,0:T(8,128)} %bitcast.12, s32[1,4096]{1,0:T(1,128)} %bitcast.13, s32[1,4096]{1,0:T(1,128)} %bitcast.14, f32[1,54]{1,0:T(1,128)} %bitcast.15), custom_call_target="tpu_custom_call" | custom-call | tf_op jit(solution)/shard_map/head/pallas_call | solution.py:191
  16.2 0.0 copy-start.5
  16.2 1.2 copy-done.5
  17.4 0.7 copy-done.7
  18.1 6.4 %sort.1.refs_1_ = f32[56,2048]{1,0:T(8,128)S(1)} custom-call(bf16[112,4096]{1,0:T(8,128)(2,1)S(1)} %copy-done.5, f32[1,4096]{1,0:T(1,128)S(1)} %copy-done.7), custom_call_target="tpu_custom_call" | custom-call | flops 1879048192 | bytes 917504 | tf_op jit(solution)/shard_map/sort/pallas_call | solution.py:251
  24.5 4.6 %collective-permute-start.1 = (f32[56,2048]{1,0:T(8,128)S(1)}, f32[56,2048]{1,0:T(8,128)S(1)}, u32[]{:S(2)}, u32[]{:S(2)}) collective-permute-start(f32[56,2048]{1,0:T(8,128)S(1)} %sort.1.refs_1_), channel_id=1, source_target_pairs={{0,1},{1,0},{2,3},{3,2},{4,5},{5,4},{6,7},{7,6},{8,9},{9,8},{10,11... | collective-permute-start | bytes 1376264 | tf_op jit(solution)/shard_map/ppermute | solution.py:25
  29.1 0.0 copy-done.6
  29.1 0.1 collective-permute-start
  29.2 0.2 collective-permute-start.2
  29.4 1.8 %collective-permute-start.3 = (f32[56,2048]{1,0:T(8,128)S(1)}, f32[56,2048]{1,0:T(8,128)S(1)}, u32[]{:S(2)}, u32[]{:S(2)}) collective-permute-start(f32[56,2048]{1,0:T(8,128)S(1)} %copy-done.6), channel_id=1, source_target_pairs={{0,2},{1,3},{2,0},{3,1},{4,6},{5,7},{6,4},{7,5},{8,10},{9,11},{10,... | collective-permute-start | bytes 1376264 | tf_op jit(solution)/shard_map/ppermute | solution.py:25
  31.2 0.0 copy-done
  31.2 0.1 constant_dynamic-slice_fusion
  31.3 0.1 copy.14
  31.3 0.0 copy-done.10
  31.3 0.1 broadcast_in_dim.3
  31.4 0.1 broadcast_in_dim_reshape.3.refs_6_
  31.6 0.1 tile.10.refs_7_
  31.7 0.0 collective-permute-done.1.refs_3_
  31.7 0.0 collective-permute-done.refs_2_
  31.7 11.6 %collect.3 = (f32[56,12288]{1,0:T(8,128)S(1)}, bf16[64,256,256]{2,1,0:T(8,128)(2,1)S(1)}, f32[64,16,128]{2,1,0:T(8,128)S(1)}, f32[8,128]{1,0:T(8,128)S(1)}, f32[8,128]{1,0:T(8,128)S(1)}) custom-call(f32[56,2048]{1,0:T(8,128)S(1)} %copy-done.6, f32[56,2048]{1,0:T(8,128)S(1)} %sort.1.refs_1_, f32[56,2048]{1,0:T(8,128)S(1)} %collective-permute-done.refs_2_, ...), custom_call_target="tpu_custom_call" | custom-call | flops 2650800128 | tf_op jit(solution)/shard_map/collect/pallas_call | solution.py:410
  43.3 0.0 collective-permute-done.2.refs_1_
  43.3 8.5 %collective-permute-done.3.refs_0_ = f32[56,2048]{1,0:T(8,128)S(1)} collective-permute-done((f32[56,2048]{1,0:T(8,128)S(1)}, f32[56,2048]{1,0:T(8,128)S(1)}, u32[]{:S(2)}, u32[]{:S(2)}) %collective-permute-start.3) | collective-permute-done | bytes 458784 | tf_op jit(solution)/shard_map/ppermute | solution.py:25
  51.8 0.0 collective-permute-start.4
  51.8 0.5 collective-permute-start.5
  52.3 6.2 %collect.4 = (f32[56,12288]{1,0:T(8,128)S(1)}, bf16[32,256,256]{2,1,0:T(8,128)(2,1)S(1)}, f32[32,16,128]{2,1,0:T(8,128)S(1)}, f32[8,128]{1,0:T(8,128)S(1)}) custom-call(f32[56,2048]{1,0:T(8,128)S(1)} %collective-permute-done.3.refs_0_, f32[56,2048]{1,0:T(8,128)S(1)} %collective-permute-done.2.refs_1_, f32[32,128]{1,0:T(8,128)S(1)} %bitcast.10), custom_call_target="tpu_custom_call" | custom-call | flops 1325400064 | tf_op jit(solution)/shard_map/collect/pallas_call | solution.py:410
  58.6 0.0 copy-start.1
  58.6 0.0 copy-start.2
  58.6 0.0 copy-start.3
  58.6 0.0 collective-permute-done.4.refs_0_
  58.6 0.0 collective-permute-done.5.refs_1_
  58.6 6.2 %collect.5 = (f32[56,12288]{1,0:T(8,128)S(1)}, bf16[32,256,256]{2,1,0:T(8,128)(2,1)S(1)}, f32[32,16,128]{2,1,0:T(8,128)S(1)}, f32[8,128]{1,0:T(8,128)S(1)}) custom-call(f32[56,2048]{1,0:T(8,128)S(1)} %collective-permute-done.4.refs_0_, f32[56,2048]{1,0:T(8,128)S(1)} %collective-permute-done.5.refs_1_, f32[32,128]{1,0:T(8,128)S(1)} %bitcast.11), custom_call_target="tpu_custom_call" | custom-call | flops 1325400064 | tf_op jit(solution)/shard_map/collect/pallas_call | solution.py:410
  64.9 54.6 %middle.1 = (f32[56,4096]{1,0:T(8,128)S(1)}, bf16[48,128,256]{2,1,0:T(8,128)(2,1)S(1)}) custom-call(f32[56,12288]{1,0:T(8,128)S(1)} %get-tuple-element.39.refs_0_, f32[56,12288]{1,0:T(8,128)S(1)} %get-tuple-element.41.refs_1_, f32[56,12288]{1,0:T(8,128)S(1)} %get-tuple-element.42.refs_2_, f32[1728,128]{1,0:T(8,128)S(1)} %bitcast.8, f32[32,128]{1,0:T(8,128)S(1)} %copy-done.2, ...), custom_call_target="tpu_custom_call" | custom-call | tf_op jit(solution)/shard_map/middle/pallas_call | solution.py:773
  119.4 3.0 %project.3 = f32[56,4096]{1,0:T(8,128)S(1)} custom-call(bf16[48,128,256]{2,1,0:T(8,128)(2,1)S(1)} %get-tuple-element.57.refs_0_, bf16[32,256,256]{2,1,0:T(8,128)(2,1)S(1)} %get-tuple-element.49.refs_1_, f32[32,16,128]{2,1,0:T(8,128)S(1)} %get-tuple-element.50.refs_2_, f32[8,128]{1,0:T(8,128)S(1)} %get-tuple-element.51.refs_3_), custom_call_target="tpu_custom_call" | custom-call | flops 1325400064 | tf_op jit(solution)/shard_map/project/pallas_call | solution.py:504
  122.4 0.1 collective-permute-start.6
  122.5 3.0 %project.4 = f32[56,4096]{1,0:T(8,128)S(1)} custom-call(bf16[48,128,256]{2,1,0:T(8,128)(2,1)S(1)} %get-tuple-element.57.refs_0_, bf16[32,256,256]{2,1,0:T(8,128)(2,1)S(1)} %get-tuple-element.53.refs_1_, f32[32,16,128]{2,1,0:T(8,128)S(1)} %get-tuple-element.54.refs_2_, f32[8,128]{1,0:T(8,128)S(1)} %get-tuple-element.55.refs_3_), custom_call_target="tpu_custom_call" | custom-call | flops 1325400064 | tf_op jit(solution)/shard_map/project/pallas_call | solution.py:504
  125.4 0.0 collective-permute-done.6
  125.5 0.1 slice_add_fusion
  125.6 8.5 %project.5 = (f32[56,4096]{1,0:T(8,128)S(1)}, f32[56,4096]{1,0:T(8,128)S(1)}, f32[1728,128]{1,0:T(8,128)}) custom-call(bf16[48,128,256]{2,1,0:T(8,128)(2,1)S(1)} %get-tuple-element.57.refs_0_, bf16[64,256,256]{2,1,0:T(8,128)(2,1)S(1)} %get-tuple-element.58.refs_1_, f32[64,16,128]{2,1,0:T(8,128)S(1)} %get-tuple-element.59.refs_2_, ...), custom_call_target="tpu_custom_call" | custom-call | flops 2650800128 | tf_op jit(solution)/shard_map/project/pallas_call | solution.py:504
  134.1 0.6 collective-permute-start.7
  134.7 0.4 collective-permute-start.9
  135.1 1.6 collective-permute-start.8
  136.7 11.4 %collective-permute-done.9.refs_2_ = f32[56,2048]{1,0:T(8,128)S(1)} collective-permute-done((f32[56,2048]{1,0:T(8,128)S(1)}, f32[56,2048]{1,0:T(8,128)S(1)}, u32[]{:S(2)}, u32[]{:S(2)}) %collective-permute-start.9) | collective-permute-done | bytes 458784 | tf_op jit(solution)/shard_map/ppermute | solution.py:25
  148.1 0.0 collective-permute-done.7.refs_1_
  148.1 5.8 %unsort.2.refs_3_ = f32[56,4096]{1,0:T(8,128)S(1)} custom-call(f32[1,4096]{1,0:T(1,128)S(1)} %copy-done.8, f32[56,4096]{1,0:T(8,128)S(1)} %get-tuple-element.63.refs_0_, f32[56,4096]{1,0:T(8,128)S(1)} %collective-permute-done.7.refs_1_, f32[56,2048]{1,0:T(8,128)S(1)} %collective-permute-done.9.refs_2_), custom_call_target="tpu_custom_call" | custom-call | flops 1879048192 | bytes 917504 | tf_op jit(solution)/shard_map/unsort/pallas_call | solution.py:310
  153.9 3.1 %collective-permute-done.8.refs_2_ = f32[56,2048]{1,0:T(8,128)S(1)} collective-permute-done((f32[56,2048]{1,0:T(8,128)S(1)}, f32[56,2048]{1,0:T(8,128)S(1)}, u32[]{:S(2)}, u32[]{:S(2)}) %collective-permute-start.8) | collective-permute-done | bytes 458784 | tf_op jit(solution)/shard_map/ppermute | solution.py:25
  157.0 0.0 copy-done.4
  157.0 7.8 %unsort.3 = f32[1728,128]{1,0:T(8,128)} custom-call(f32[1,4096]{1,0:T(1,128)S(1)} %copy-done.8, f32[56,4096]{1,0:T(8,128)S(1)} %get-tuple-element.63.refs_0_, f32[56,4096]{1,0:T(8,128)S(1)} %collective-permute-done.7.refs_1_, f32[56,2048]{1,0:T(8,128)S(1)} %collective-permute-done.8.refs_2_, f32[56,4096]{1,0:T(8,128)S(1)} %unsort.2.refs_3_, ...), custom_call_target="tpu_custom_call" | custom-call | flops 1879048192 | bytes 917504 | tf_op jit(solution)/shard_map/unsort/pallas_call | solution.py:310
  (13 shorter events, 0.0 us)
Async XLA Ops:
  0.6 30.6 %copy-start = (f32[128,128]{1,0:T(8,128)S(1)}, f32[128,128]{1,0:T(8,128)}, u32[]{:S(2)}) copy-start(f32[128,128]{1,0:T(8,128)} %param.14) | copy-start | bytes 196612
  16.2 1.2 copy-start.5
  17.4 0.7 copy-start.7
  18.1 11.0 %copy-start.6 = (f32[56,2048]{1,0:T(8,128)S(1)}, f32[56,2048]{1,0:T(8,128)}, u32[]{:S(2)}) copy-start(f32[56,2048]{1,0:T(8,128)} %get-tuple-element.36.refs_0_) | copy-start | bytes 1376260
  18.1 13.3 %copy-start.10 = (s32[128]{0:T(128)S(1)}, s32[128]{0:T(128)}, u32[]{:S(2)}) copy-start(s32[128]{0:T(128)} %param.19) | copy-start | bytes 1540
  18.1 13.5 %copy-start.9 = (f32[54,54]{1,0:T(8,128)S(1)}, f32[54,54]{1,0:T(8,128)}, u32[]{:S(2)}) copy-start(f32[54,54]{1,0:T(8,128)} %param.16) | copy-start | bytes 34996
  24.5 7.3 %collective-permute-start.1 = (f32[56,2048]{1,0:T(8,128)S(1)}, f32[56,2048]{1,0:T(8,128)S(1)}, u32[]{:S(2)}, u32[]{:S(2)}) collective-permute-start(f32[56,2048]{1,0:T(8,128)S(1)} %sort.1.refs_1_), channel_id=1, source_target_pairs={{0,1},{1,0},{2,3},{3,2},{4,5},{5,4},{6,7},{7,6},{8,9},{9,8},{10,11... | collective-permute-start | bytes 1376264 | tf_op jit(solution)/shard_map/ppermute | solution.py:25
  29.1 2.7 %collective-permute-start = (f32[56,2048]{1,0:T(8,128)S(1)}, f32[56,2048]{1,0:T(8,128)S(1)}, u32[]{:S(2)}, u32[]{:S(2)}) collective-permute-start(f32[56,2048]{1,0:T(8,128)S(1)} %copy-done.6), channel_id=1, source_target_pairs={{0,1},{1,0},{2,3},{3,2},{4,5},{5,4},{6,7},{7,6},{8,9},{9,8},{10,11... | collective-permute-start | bytes 1376264 | tf_op jit(solution)/shard_map/ppermute | solution.py:25
  29.2 14.2 %collective-permute-start.2 = (f32[56,2048]{1,0:T(8,128)S(1)}, f32[56,2048]{1,0:T(8,128)S(1)}, u32[]{:S(2)}, u32[]{:S(2)}) collective-permute-start(f32[56,2048]{1,0:T(8,128)S(1)} %sort.1.refs_1_), channel_id=1, source_target_pairs={{0,2},{1,3},{2,0},{3,1},{4,6},{5,7},{6,4},{7,5},{8,10},{9,11},{10,... | collective-permute-start | bytes 1376264 | tf_op jit(solution)/shard_map/ppermute | solution.py:25
  29.4 22.5 %collective-permute-start.3 = (f32[56,2048]{1,0:T(8,128)S(1)}, f32[56,2048]{1,0:T(8,128)S(1)}, u32[]{:S(2)}, u32[]{:S(2)}) collective-permute-start(f32[56,2048]{1,0:T(8,128)S(1)} %copy-done.6), channel_id=1, source_target_pairs={{0,2},{1,3},{2,0},{3,1},{4,6},{5,7},{6,4},{7,5},{8,10},{9,11},{10,... | collective-permute-start | bytes 1376264 | tf_op jit(solution)/shard_map/ppermute | solution.py:25
  51.8 6.8 %collective-permute-start.4 = (f32[56,2048]{1,0:T(8,128)S(1)}, f32[56,2048]{1,0:T(8,128)S(1)}, u32[]{:S(2)}, u32[]{:S(2)}) collective-permute-start(f32[56,2048]{1,0:T(8,128)S(1)} %collective-permute-done.3.refs_0_), channel_id=1, source_target_pairs={{0,1},{1,0},{2,3},{3,2},{4,5},{5,4},{6,7},{7,6},{8,9},{9,8},{10,11... | collective-permute-start | bytes 1376264 | tf_op jit(solution)/shard_map/ppermute | solution.py:25
  51.8 6.8 %collective-permute-start.5 = (f32[56,2048]{1,0:T(8,128)S(1)}, f32[56,2048]{1,0:T(8,128)S(1)}, u32[]{:S(2)}, u32[]{:S(2)}) collective-permute-start(f32[56,2048]{1,0:T(8,128)S(1)} %collective-permute-done.2.refs_1_), channel_id=1, source_target_pairs={{0,1},{1,0},{2,3},{3,2},{4,5},{5,4},{6,7},{7,6},{8,9},{9,8},{10,11... | collective-permute-start | bytes 1376264 | tf_op jit(solution)/shard_map/ppermute | solution.py:25
  58.6 6.3 %copy-start.1 = (f32[54,32,128]{2,1,0:T(8,128)S(1)}, f32[54,32,128]{2,1,0:T(8,128)}, u32[]{:S(2)}) copy-start(f32[54,32,128]{2,1,0:T(8,128)} %param.11) | copy-start | bytes 2654212
  58.6 6.3 %copy-start.2 = (f32[32,128]{1,0:T(8,128)S(1)}, f32[32,128]{1,0:T(8,128)}, u32[]{:S(2)}) copy-start(f32[32,128]{1,0:T(8,128)} %refs_4_) | copy-start | bytes 49156
  58.6 6.3 %copy-start.3 = (f32[32,128]{1,0:T(8,128)S(1)}, f32[32,128]{1,0:T(8,128)}, u32[]{:S(2)}) copy-start(f32[32,128]{1,0:T(8,128)} %refs_5_) | copy-start | bytes 49156
  122.4 3.0 %collective-permute-start.6 = (f32[56,4096]{1,0:T(8,128)S(1)}, f32[56,4096]{1,0:T(8,128)S(1)}, u32[]{:S(2)}, u32[]{:S(2)}) collective-permute-start(f32[56,4096]{1,0:T(8,128)S(1)} %project.3), channel_id=1, source_target_pairs={{0,1},{1,0},{2,3},{3,2},{4,5},{5,4},{6,7},{7,6},{8,9},{9,8},{10,11... | collective-permute-start | bytes 2752520 | tf_op jit(solution)/shard_map/ppermute | solution.py:25
  125.6 22.5 %copy-start.8 = (f32[1,4096]{1,0:T(1,128)S(1)}, f32[1,4096]{1,0:T(1,128)}, u32[]{:S(2)}) copy-start(f32[1,4096]{1,0:T(1,128)} %get-tuple-element.35.rank_ref) | copy-start | bytes 49156
  134.1 14.0 %collective-permute-start.7 = (f32[56,4096]{1,0:T(8,128)S(1)}, f32[56,4096]{1,0:T(8,128)S(1)}, u32[]{:S(2)}, u32[]{:S(2)}) collective-permute-start(f32[56,4096]{1,0:T(8,128)S(1)} %get-tuple-element.64), channel_id=1, source_target_pairs={{0,1},{1,0},{2,3},{3,2},{4,5},{5,4},{6,7},{7,6},{8,9},{9,8},{10,11... | collective-permute-start | bytes 2752520 | tf_op jit(solution)/shard_map/ppermute | solution.py:25
  134.7 13.4 %collective-permute-start.9 = (f32[56,2048]{1,0:T(8,128)S(1)}, f32[56,2048]{1,0:T(8,128)S(1)}, u32[]{:S(2)}, u32[]{:S(2)}) collective-permute-start(f32[56,2048]{1,0:T(8,128)S(1)} %get-tuple-element.65), channel_id=1, source_target_pairs={{0,2},{1,3},{2,0},{3,1},{4,6},{5,7},{6,4},{7,5},{8,10},{9,11},{10,... | collective-permute-start | bytes 1376264 | tf_op jit(solution)/shard_map/ppermute | solution.py:25
  135.1 21.9 %collective-permute-start.8 = (f32[56,2048]{1,0:T(8,128)S(1)}, f32[56,2048]{1,0:T(8,128)S(1)}, u32[]{:S(2)}, u32[]{:S(2)}) collective-permute-start(f32[56,2048]{1,0:T(8,128)S(1)} %get-tuple-element.68), channel_id=1, source_target_pairs={{0,2},{1,3},{2,0},{3,1},{4,6},{5,7},{6,4},{7,5},{8,10},{9,11},{10,... | collective-permute-start | bytes 1376264 | tf_op jit(solution)/shard_map/ppermute | solution.py:25
  148.1 8.9 %copy-start.4 = (f32[56,4096]{1,0:T(8,128)S(1)}, f32[56,4096]{1,0:T(8,128)}, u32[]{:S(2)}) copy-start(f32[56,4096]{1,0:T(8,128)} %get-tuple-element.66.refs_4_) | copy-start | bytes 2752516

commit v10 on v9

--- a/solution.py
+++ b/solution.py
@@ -79,7 +79,11 @@
     lane = lax.broadcasted_iota(jnp.int32, (tiles, LANES), 1).astype(F32)
     last = jnp.maximum(jnp.ceil((base + total) * (1.0 / LANES)) - 1.0, 0.0) + order
     passed = jnp.where((last < lane) & (order < tiles - 1), 1.0, 0.0)
-    table_ref[...] = jnp.sum(passed, axis=0, keepdims=True)
+    table = jnp.sum(passed, axis=0, keepdims=True)
+    number = lane[:1]
+    blocks = count // LANES
+    early = jnp.where((number - table < blocks // 2) & (number < blocks + tiles - 1), 1.0, 0.0)
+    table_ref[...] = jnp.where(number == LANES - 1, jnp.sum(early, axis=1, keepdims=True), table)
     ahead = jnp.where(
         lax.broadcasted_iota(jnp.int32, (TILE, TILE), 0) < lax.broadcasted_iota(jnp.int32, (TILE, TILE), 1), 1.0, 0.0
     ).astype(BF16)
@@ -138,14 +142,15 @@
             pl.semaphore_signal(barrier, inc=1, device_id=where, device_id_type=mesh)
 
     pl.semaphore_wait(barrier, sum(jnp.where(there, 1, 0) for there, _ in sides))
-    copies = []
-    for n, (there, where) in enumerate(sides):
+    copies = {}
+    for n in (2, 3, 0, 1):
+        there, where = sides[n]
         copy = pltpu.make_async_remote_copy(
             src_ref=faces[n], dst_ref=halos[n ^ 1], send_sem=send.at[n], recv_sem=recv.at[n ^ 1],
             device_id=where, device_id_type=mesh,
         )
         pl.when(there)(copy.start)
-        copies.append(copy)
+        copies[n] = copy
     offset = map_ref[...] - (slab - 1) * cells
     block = jnp.where(offset >= cells, 1, 0) + jnp.where(offset >= 2 * cells, 1, 0)
     offset = jnp.where(lax.rem(slab, 2) == 1, (2 - block) * cells + offset - block * cells, offset)
@@ -457,7 +462,7 @@
         out_ref[full * LANES :, :] = turn(full)[:rest]
 
 
-def project_kernel(bins, pairs, lists, state_rows, *refs):
+def project_kernel(bins, pairs, lists, state_rows, part, *refs):
     parts, weights, tiles, *refs = refs
     sources, refs = refs[:lists], refs[lists:]
     mean = refs.pop(0) if state_rows else None
@@ -467,6 +472,9 @@
     copies = fetch_rows(sources, steps, sems)
     rows, count = outs[0].shape
     blocks = count // LANES
+    whole_blocks = blocks if part is None else 2 * blocks
+    base = blocks * (part or 0)
+    group = GROUP if part is None else GROUP // 2
     for out in outs:
         out[...] = jnp.zeros_like(out)
     if state_rows:
@@ -476,12 +484,16 @@
 
     def step(n, _):
         for number in range(lists):
-            for g in range(GROUP):
-                k = n * GROUP + g
+            for g in range(group):
+                k = n * group + g
                 tile = steps[number, 7, k].astype(jnp.int32)
-                local = jnp.minimum(k - tile, blocks - 1)
-                block = local + number * blocks
-                wanted = jnp.where(k < pairs, tile, -1).astype(F32)
+                block = jnp.minimum(k - tile, whole_blocks - 1)
+                local = jnp.clip(block - base, 0, blocks - 1)
+                block = block + number * whole_blocks
+                valid = k < pairs
+                if part is not None:
+                    valid = valid & ((k < middle) == (part == 0))
+                wanted = jnp.where(valid, tile, -1).astype(F32)
                 got = lax.dot_general(parts[tile], weights[block], NN, preferred_element_type=F32)
                 got = got[:rows] + got[HALF : HALF + rows]
                 got = got[:, :LANES] + got[:, LANES:]
@@ -490,10 +502,14 @@
                 outs[number][:, place] += got
         return 0
 
-    lax.fori_loop(0, -(-pairs // GROUP), step, 0)
-
-
-def project_call(parts, collected, rows, count, bins, ntiles, mean=None, state_rows=0):
+    start, stop = 0, -(-pairs // group)
+    if part is not None:
+        middle = steps[0, 7, LANES - 1].astype(jnp.int32)
+        start, stop = (0, (middle + group - 1) // group) if part == 0 else (middle // group, stop)
+    lax.fori_loop(start, stop, step, 0)
+
+
+def project_call(parts, collected, rows, count, bins, ntiles, mean=None, state_rows=0, part=None):
     weights, tiles, *sources = collected
     lists = len(sources)
     pairs = count // LANES + ntiles - 1
@@ -502,8 +518,8 @@
     if extra:
         scratch += [pltpu.VMEM((mean.size // LANES, LANES), F32), pltpu.VMEM((LANES, LANES), F32)]
     return pl.pallas_call(
-        functools.partial(project_kernel, bins, pairs, lists, state_rows),
-        out_shape=[jax.ShapeDtypeStruct((rows, count), F32)] * lists
+        functools.partial(project_kernel, bins, pairs, lists, state_rows, part),
+        out_shape=[jax.ShapeDtypeStruct((rows, count if part is None else count // 2), F32)] * lists
         + [jax.ShapeDtypeStruct((state_rows, LANES), F32)] * len(extra),
         in_specs=[VMEM] * (3 + lists + len(extra)),
         out_specs=[VMEM] * (lists + len(extra)),
@@ -827,19 +843,18 @@
         far.append(collected)
     fresh, parts = middle_call(accs, *terms, species, bins)
 
-    pieces = []
-    for bit, collected in zip(bits[:-1], far[1:]):
-        (piece,) = project_call(parts, collected, rows, count, bins, ntiles)
-        piece, parts = lax.optimization_barrier((piece, parts))
-        pieces.append(swap(piece, "cross", bit))
-    (there,) = project_call(parts, far[0], rows, count, bins, ntiles)
-    part = count // 2
-    low, high = there[:, :part], there[:, part:]
-    for piece in pieces:
-        low, high = low + piece[:, :part], high + piece[:, part:]
-    low, parts = lax.optimization_barrier((low, parts))
-    low = swap(low, "cross", bits[-1])
-    high = swap(high, "cross", bits[-1])
+    ends = []
+    for part in range(2):
+        pieces = []
+        for bit, collected in zip(bits[:-1], far[1:]):
+            (piece,) = project_call(parts, collected, rows, count, bins, ntiles, part=part)
+            piece, parts = lax.optimization_barrier((piece, parts))
+            pieces.append(swap(piece, "cross", bit))
+        (there,) = project_call(parts, far[0], rows, count, bins, ntiles, part=part)
+        there = sum(pieces, there)
+        there, parts = lax.optimization_barrier((there, parts))
+        ends.append(swap(there, "cross", bits[-1]))
+    low, high = ends
     *here, cmc_out = project_call(parts, near, rows, count, bins, ntiles, fresh, species * bins)
     total = [here[0]] + [swap(piece, "cross", bit) for bit, piece in zip(bits[:-1], here[1:])]
     before = unsort_call(total, low, rank, None, None)

time: 165 us -> 170 us (1.030)
  Pallas kernels: 129 us -> 132 us
    pallas_call x3 -> x5, Pallas kernels: 14.4 us -> 18.1 us  [project_call(): pl.pallas_call(functools.partial(project_kernel, bins, pairs, lists, stat...]
    ppermute x10 -> x11, starting transfers between devices: 9.91 us -> 10.3 us  [swap(): return lax.ppermute(array, axis, [(i, i ^ bit) for i in range(count)])]
    ppermute x10 -> x11, waiting for transfers between devices: 23 us -> 23.3 us  [swap(): return lax.ppermute(array, axis, [(i, i ^ bit) for i in range(count)])]
  transfers between devices with their start and end apart: 10 -> 11, of which waited for: 3 -> 3; matrix products, arithmetic and copies ran while one was open for 0% -> 0% of each run, Pallas kernels for 16% -> 17%
where the time goes in v10:
time: 170 us; the launch traced here: 169 us
  Pallas kernels  132 us (78%)
  waiting for transfers between devices  23.3 us (14%)
  starting transfers between devices  10.3 us (6%)
  local copies, waits for them, and re-layouts  2.43 us (1%)
    pallas_call x1, Pallas kernels, middle_call(): pl.pallas_call(kernel, out_shape=[jax.ShapeDtypeStruct((rows, width), F32...  54.6 us
    pallas_call x3, Pallas kernels, collect_call(): pl.pallas_call(functools.partial(collect_kernel, species, bins, per_tile,...  24 us
    ppermute x11, waiting for transfers between devices, swap(): return lax.ppermute(array, axis, [(i, i ^ bit) for i in range(count)])  23.3 us
    pallas_call x5, Pallas kernels, project_call(): pl.pallas_call(functools.partial(project_kernel, bins, pairs, lists, stat...  18.1 us
    pallas_call x1, Pallas kernels, head_call(): pl.pallas_call(functools.partial(head_kernel, (species, nx, ny), cells, n...  15.5 us
    pallas_call x2, Pallas kernels, unsort_call(): pl.pallas_call(functools.partial(unsort_kernel, half, len(wholes) + 1), g...  13.6 us
    ppermute x11, starting transfers between devices, swap(): return lax.ppermute(array, axis, [(i, i ^ bit) for i in range(count)])  10.3 us
    pallas_call x1, Pallas kernels, sort_call(): pl.pallas_call(sort_kernel, out_shape=jax.ShapeDtypeStruct((rows, count /...  6.36 us
  transfers between devices with their start and end apart: 11, of which 3 were waited for; matrix products, arithmetic and copies ran while one was open for 0% of the time, Pallas kernels for 17%

profile of v10, /device:TPU:2, one launch (start us, length us, event | category | flops | bytes accessed | tf_op | source)
XLA Modules:
  0.0 169.4 jit_solution(3550840105389808254)
XLA Ops:
  0.6 0.0 copy-start
  0.6 15.5 %head.1 = (f32[56,4096]{1,0:T(8,128)}, f32[1,4096]{1,0:T(1,128)}, bf16[112,4096]{1,0:T(8,128)(2,1)}, f32[56,2048]{1,0:T(8,128)}) custom-call(f32[1728,128]{1,0:T(8,128)} %bitcast.12, s32[1,4096]{1,0:T(1,128)} %bitcast.13, s32[1,4096]{1,0:T(1,128)} %bitcast.14, f32[1,54]{1,0:T(1,128)} %bitcast.15), custom_call_target="tpu_custom_call" | custom-call | tf_op jit(solution)/shard_map/head/pallas_call | solution.py:196
  16.2 1.2 copy-done.5
  17.3 0.7 copy-done.7
  18.1 6.4 %sort.1.refs_1_ = f32[56,2048]{1,0:T(8,128)S(1)} custom-call(bf16[112,4096]{1,0:T(8,128)(2,1)S(1)} %copy-done.5, f32[1,4096]{1,0:T(1,128)S(1)} %copy-done.7), custom_call_target="tpu_custom_call" | custom-call | flops 1879048192 | bytes 917504 | tf_op jit(solution)/shard_map/sort/pallas_call | solution.py:256
  24.4 4.6 %collective-permute-start.1 = (f32[56,2048]{1,0:T(8,128)S(1)}, f32[56,2048]{1,0:T(8,128)S(1)}, u32[]{:S(2)}, u32[]{:S(2)}) collective-permute-start(f32[56,2048]{1,0:T(8,128)S(1)} %sort.1.refs_1_), channel_id=1, source_target_pairs={{0,1},{1,0},{2,3},{3,2},{4,5},{5,4},{6,7},{7,6},{8,9},{9,8},{10,11... | collective-permute-start | bytes 1376264 | tf_op jit(solution)/shard_map/ppermute | solution.py:25
  29.1 0.1 collective-permute-start
  29.1 0.2 collective-permute-start.2
  29.4 1.8 %collective-permute-start.3 = (f32[56,2048]{1,0:T(8,128)S(1)}, f32[56,2048]{1,0:T(8,128)S(1)}, u32[]{:S(2)}, u32[]{:S(2)}) collective-permute-start(f32[56,2048]{1,0:T(8,128)S(1)} %copy-done.6), channel_id=1, source_target_pairs={{0,2},{1,3},{2,0},{3,1},{4,6},{5,7},{6,4},{7,5},{8,10},{9,11},{10,... | collective-permute-start | bytes 1376264 | tf_op jit(solution)/shard_map/ppermute | solution.py:25
  31.2 0.1 constant_dynamic-slice_fusion
  31.3 0.1 copy.14
  31.3 0.1 broadcast_in_dim.3
  31.4 0.1 broadcast_in_dim_reshape.3.refs_6_
  31.6 0.1 tile.10.refs_7_
  31.7 0.0 collective-permute-done.1.refs_3_
  31.7 0.0 collective-permute-done.refs_2_
  31.7 11.6 %collect.3 = (f32[56,12288]{1,0:T(8,128)S(1)}, bf16[64,256,256]{2,1,0:T(8,128)(2,1)S(1)}, f32[64,16,128]{2,1,0:T(8,128)S(1)}, f32[8,128]{1,0:T(8,128)S(1)}, f32[8,128]{1,0:T(8,128)S(1)}) custom-call(f32[56,2048]{1,0:T(8,128)S(1)} %copy-done.6, f32[56,2048]{1,0:T(8,128)S(1)} %sort.1.refs_1_, f32[56,2048]{1,0:T(8,128)S(1)} %collective-permute-done.refs_2_, ...), custom_call_target="tpu_custom_call" | custom-call | flops 2650800128 | tf_op jit(solution)/shard_map/collect/pallas_call | solution.py:415
  43.3 0.0 collective-permute-done.2.refs_1_
  43.3 8.5 %collective-permute-done.3.refs_0_ = f32[56,2048]{1,0:T(8,128)S(1)} collective-permute-done((f32[56,2048]{1,0:T(8,128)S(1)}, f32[56,2048]{1,0:T(8,128)S(1)}, u32[]{:S(2)}, u32[]{:S(2)}) %collective-permute-start.3) | collective-permute-done | bytes 458784 | tf_op jit(solution)/shard_map/ppermute | solution.py:25
  51.8 0.0 collective-permute-start.4
  51.8 0.5 collective-permute-start.5
  52.3 6.2 %collect.4 = (f32[56,12288]{1,0:T(8,128)S(1)}, bf16[32,256,256]{2,1,0:T(8,128)(2,1)S(1)}, f32[32,16,128]{2,1,0:T(8,128)S(1)}, f32[8,128]{1,0:T(8,128)S(1)}) custom-call(f32[56,2048]{1,0:T(8,128)S(1)} %collective-permute-done.3.refs_0_, f32[56,2048]{1,0:T(8,128)S(1)} %collective-permute-done.2.refs_1_, f32[32,128]{1,0:T(8,128)S(1)} %bitcast.10), custom_call_target="tpu_custom_call" | custom-call | flops 1325400064 | tf_op jit(solution)/shard_map/collect/pallas_call | solution.py:415
  58.6 0.0 copy-start.1
  58.6 0.0 copy-start.2
  58.6 0.0 copy-start.3
  58.6 0.0 collective-permute-done.4.refs_0_
  58.6 0.0 collective-permute-done.5.refs_1_
  58.6 6.2 %collect.5 = (f32[56,12288]{1,0:T(8,128)S(1)}, bf16[32,256,256]{2,1,0:T(8,128)(2,1)S(1)}, f32[32,16,128]{2,1,0:T(8,128)S(1)}, f32[8,128]{1,0:T(8,128)S(1)}) custom-call(f32[56,2048]{1,0:T(8,128)S(1)} %collective-permute-done.4.refs_0_, f32[56,2048]{1,0:T(8,128)S(1)} %collective-permute-done.5.refs_1_, f32[32,128]{1,0:T(8,128)S(1)} %bitcast.11), custom_call_target="tpu_custom_call" | custom-call | flops 1325400064 | tf_op jit(solution)/shard_map/collect/pallas_call | solution.py:415
  64.8 54.6 %middle.1 = (f32[56,4096]{1,0:T(8,128)S(1)}, bf16[48,128,256]{2,1,0:T(8,128)(2,1)S(1)}) custom-call(f32[56,12288]{1,0:T(8,128)S(1)} %get-tuple-element.43.refs_0_, f32[56,12288]{1,0:T(8,128)S(1)} %get-tuple-element.45.refs_1_, f32[56,12288]{1,0:T(8,128)S(1)} %get-tuple-element.46.refs_2_, f32[1728,128]{1,0:T(8,128)S(1)} %bitcast.8, f32[32,128]{1,0:T(8,128)S(1)} %copy-done.2, ...), custom_call_target="tpu_custom_call" | custom-call | tf_op jit(solution)/shard_map/middle/pallas_call | solution.py:789
  119.5 2.6 %project.5 = f32[56,2048]{1,0:T(8,128)S(1)} custom-call(bf16[48,128,256]{2,1,0:T(8,128)(2,1)S(1)} %get-tuple-element.64.refs_0_, bf16[32,256,256]{2,1,0:T(8,128)(2,1)S(1)} %get-tuple-element.53.refs_1_, f32[32,16,128]{2,1,0:T(8,128)S(1)} %get-tuple-element.54.refs_2_, f32[8,128]{1,0:T(8,128)S(1)} %get-tuple-element.55.refs_3_), custom_call_target="tpu_custom_call" | custom-call | flops 1325400064 | tf_op jit(solution)/shard_map/project/pallas_call | solution.py:520
  122.1 0.1 collective-permute-start.6
  122.1 2.3 %project.6 = f32[56,2048]{1,0:T(8,128)S(1)} custom-call(bf16[48,128,256]{2,1,0:T(8,128)(2,1)S(1)} %get-tuple-element.64.refs_0_, bf16[32,256,256]{2,1,0:T(8,128)(2,1)S(1)} %get-tuple-element.57.refs_1_, f32[32,16,128]{2,1,0:T(8,128)S(1)} %get-tuple-element.58.refs_2_, f32[8,128]{1,0:T(8,128)S(1)} %get-tuple-element.59.refs_3_), custom_call_target="tpu_custom_call" | custom-call | flops 1325400064 | tf_op jit(solution)/shard_map/project/pallas_call | solution.py:520
  124.4 0.0 collective-permute-done.6
  124.4 0.1 add.12
  124.5 2.2 %project.7 = f32[56,2048]{1,0:T(8,128)S(1)} custom-call(bf16[48,128,256]{2,1,0:T(8,128)(2,1)S(1)} %get-tuple-element.64.refs_0_, bf16[32,256,256]{2,1,0:T(8,128)(2,1)S(1)} %get-tuple-element.53.refs_1_, f32[32,16,128]{2,1,0:T(8,128)S(1)} %get-tuple-element.54.refs_2_, f32[8,128]{1,0:T(8,128)S(1)} %get-tuple-element.55.refs_3_), custom_call_target="tpu_custom_call" | custom-call | flops 1325400064 | tf_op jit(solution)/shard_map/project/pallas_call | solution.py:520
  126.8 0.9 collective-permute-start.7
  127.6 2.4 %project.8 = f32[56,2048]{1,0:T(8,128)S(1)} custom-call(bf16[48,128,256]{2,1,0:T(8,128)(2,1)S(1)} %get-tuple-element.64.refs_0_, bf16[32,256,256]{2,1,0:T(8,128)(2,1)S(1)} %get-tuple-element.57.refs_1_, f32[32,16,128]{2,1,0:T(8,128)S(1)} %get-tuple-element.58.refs_2_, f32[8,128]{1,0:T(8,128)S(1)} %get-tuple-element.59.refs_3_), custom_call_target="tpu_custom_call" | custom-call | flops 1325400064 | tf_op jit(solution)/shard_map/project/pallas_call | solution.py:520
  130.1 0.0 collective-permute-done.7
  130.1 0.1 add.13
  130.2 8.6 %project.9 = (f32[56,4096]{1,0:T(8,128)S(1)}, f32[56,4096]{1,0:T(8,128)S(1)}, f32[1728,128]{1,0:T(8,128)}) custom-call(bf16[48,128,256]{2,1,0:T(8,128)(2,1)S(1)} %get-tuple-element.64.refs_0_, bf16[64,256,256]{2,1,0:T(8,128)(2,1)S(1)} %get-tuple-element.65.refs_1_, f32[64,16,128]{2,1,0:T(8,128)S(1)} %get-tuple-element.66.refs_2_, ...), custom_call_target="tpu_custom_call" | custom-call | flops 2650800128 | tf_op jit(solution)/shard_map/project/pallas_call | solution.py:520
  138.7 0.1 collective-permute-start.8
  138.8 0.1 collective-permute-start.10
  138.9 2.0 %collective-permute-start.9 = (f32[56,2048]{1,0:T(8,128)S(1)}, f32[56,2048]{1,0:T(8,128)S(1)}, u32[]{:S(2)}, u32[]{:S(2)}) collective-permute-start(f32[56,2048]{1,0:T(8,128)S(1)} %add.13), channel_id=1, source_target_pairs={{0,2},{1,3},{2,0},{3,1},{4,6},{5,7},{6,4},{7,5},{8,10},{9,11},{10,... | collective-permute-start | bytes 1376264 | tf_op jit(solution)/shard_map/ppermute | solution.py:25
  140.9 11.4 %collective-permute-done.10.refs_2_ = f32[56,2048]{1,0:T(8,128)S(1)} collective-permute-done((f32[56,2048]{1,0:T(8,128)S(1)}, f32[56,2048]{1,0:T(8,128)S(1)}, u32[]{:S(2)}, u32[]{:S(2)}) %collective-permute-start.10) | collective-permute-done | bytes 458784 | tf_op jit(solution)/shard_map/ppermute | solution.py:25
  152.3 0.0 collective-permute-done.8.refs_1_
  152.3 5.8 %unsort.2.refs_3_ = f32[56,4096]{1,0:T(8,128)S(1)} custom-call(f32[1,4096]{1,0:T(1,128)S(1)} %copy-done.8, f32[56,4096]{1,0:T(8,128)S(1)} %get-tuple-element.70.refs_0_, f32[56,4096]{1,0:T(8,128)S(1)} %collective-permute-done.8.refs_1_, f32[56,2048]{1,0:T(8,128)S(1)} %collective-permute-done.10.refs_2_), custom_call_target="tpu_custom_call" | custom-call | flops 1879048192 | bytes 917504 | tf_op jit(solution)/shard_map/unsort/pallas_call | solution.py:315
  158.1 3.5 %collective-permute-done.9.refs_2_ = f32[56,2048]{1,0:T(8,128)S(1)} collective-permute-done((f32[56,2048]{1,0:T(8,128)S(1)}, f32[56,2048]{1,0:T(8,128)S(1)}, u32[]{:S(2)}, u32[]{:S(2)}) %collective-permute-start.9) | collective-permute-done | bytes 458784 | tf_op jit(solution)/shard_map/ppermute | solution.py:25
  161.6 7.8 %unsort.3 = f32[1728,128]{1,0:T(8,128)} custom-call(f32[1,4096]{1,0:T(1,128)S(1)} %copy-done.8, f32[56,4096]{1,0:T(8,128)S(1)} %get-tuple-element.70.refs_0_, f32[56,4096]{1,0:T(8,128)S(1)} %collective-permute-done.8.refs_1_, f32[56,2048]{1,0:T(8,128)S(1)} %collective-permute-done.9.refs_2_, f32[56,4096]{1,0:T(8,128)S(1)} %unsort.2.refs_3_, ...), custom_call_target="tpu_custom_call" | custom-call | flops 1879048192 | bytes 917504 | tf_op jit(solution)/shard_map/unsort/pallas_call | solution.py:315
  (18 shorter events, 0.1 us)
Async XLA Ops:
  0.6 30.5 %copy-start = (f32[128,128]{1,0:T(8,128)S(1)}, f32[128,128]{1,0:T(8,128)}, u32[]{:S(2)}) copy-start(f32[128,128]{1,0:T(8,128)} %param.14) | copy-start | bytes 196612
  16.2 1.2 copy-start.5
  17.3 0.7 copy-start.7
  18.1 11.0 %copy-start.6 = (f32[56,2048]{1,0:T(8,128)S(1)}, f32[56,2048]{1,0:T(8,128)}, u32[]{:S(2)}) copy-start(f32[56,2048]{1,0:T(8,128)} %get-tuple-element.40.refs_0_) | copy-start | bytes 1376260
  18.1 13.3 %copy-start.10 = (s32[128]{0:T(128)S(1)}, s32[128]{0:T(128)}, u32[]{:S(2)}) copy-start(s32[128]{0:T(128)} %param.19) | copy-start | bytes 1540
  18.1 13.5 %copy-start.9 = (f32[54,54]{1,0:T(8,128)S(1)}, f32[54,54]{1,0:T(8,128)}, u32[]{:S(2)}) copy-start(f32[54,54]{1,0:T(8,128)} %param.16) | copy-start | bytes 34996
  24.4 7.3 %collective-permute-start.1 = (f32[56,2048]{1,0:T(8,128)S(1)}, f32[56,2048]{1,0:T(8,128)S(1)}, u32[]{:S(2)}, u32[]{:S(2)}) collective-permute-start(f32[56,2048]{1,0:T(8,128)S(1)} %sort.1.refs_1_), channel_id=1, source_target_pairs={{0,1},{1,0},{2,3},{3,2},{4,5},{5,4},{6,7},{7,6},{8,9},{9,8},{10,11... | collective-permute-start | bytes 1376264 | tf_op jit(solution)/shard_map/ppermute | solution.py:25
  29.1 2.7 %collective-permute-start = (f32[56,2048]{1,0:T(8,128)S(1)}, f32[56,2048]{1,0:T(8,128)S(1)}, u32[]{:S(2)}, u32[]{:S(2)}) collective-permute-start(f32[56,2048]{1,0:T(8,128)S(1)} %copy-done.6), channel_id=1, source_target_pairs={{0,1},{1,0},{2,3},{3,2},{4,5},{5,4},{6,7},{7,6},{8,9},{9,8},{10,11... | collective-permute-start | bytes 1376264 | tf_op jit(solution)/shard_map/ppermute | solution.py:25
  29.1 14.2 %collective-permute-start.2 = (f32[56,2048]{1,0:T(8,128)S(1)}, f32[56,2048]{1,0:T(8,128)S(1)}, u32[]{:S(2)}, u32[]{:S(2)}) collective-permute-start(f32[56,2048]{1,0:T(8,128)S(1)} %sort.1.refs_1_), channel_id=1, source_target_pairs={{0,2},{1,3},{2,0},{3,1},{4,6},{5,7},{6,4},{7,5},{8,10},{9,11},{10,... | collective-permute-start | bytes 1376264 | tf_op jit(solution)/shard_map/ppermute | solution.py:25
  29.4 22.5 %collective-permute-start.3 = (f32[56,2048]{1,0:T(8,128)S(1)}, f32[56,2048]{1,0:T(8,128)S(1)}, u32[]{:S(2)}, u32[]{:S(2)}) collective-permute-start(f32[56,2048]{1,0:T(8,128)S(1)} %copy-done.6), channel_id=1, source_target_pairs={{0,2},{1,3},{2,0},{3,1},{4,6},{5,7},{6,4},{7,5},{8,10},{9,11},{10,... | collective-permute-start | bytes 1376264 | tf_op jit(solution)/shard_map/ppermute | solution.py:25
  51.8 6.8 %collective-permute-start.4 = (f32[56,2048]{1,0:T(8,128)S(1)}, f32[56,2048]{1,0:T(8,128)S(1)}, u32[]{:S(2)}, u32[]{:S(2)}) collective-permute-start(f32[56,2048]{1,0:T(8,128)S(1)} %collective-permute-done.3.refs_0_), channel_id=1, source_target_pairs={{0,1},{1,0},{2,3},{3,2},{4,5},{5,4},{6,7},{7,6},{8,9},{9,8},{10,11... | collective-permute-start | bytes 1376264 | tf_op jit(solution)/shard_map/ppermute | solution.py:25
  51.8 6.8 %collective-permute-start.5 = (f32[56,2048]{1,0:T(8,128)S(1)}, f32[56,2048]{1,0:T(8,128)S(1)}, u32[]{:S(2)}, u32[]{:S(2)}) collective-permute-start(f32[56,2048]{1,0:T(8,128)S(1)} %collective-permute-done.2.refs_1_), channel_id=1, source_target_pairs={{0,1},{1,0},{2,3},{3,2},{4,5},{5,4},{6,7},{7,6},{8,9},{9,8},{10,11... | collective-permute-start | bytes 1376264 | tf_op jit(solution)/shard_map/ppermute | solution.py:25
  58.6 6.3 %copy-start.1 = (f32[54,32,128]{2,1,0:T(8,128)S(1)}, f32[54,32,128]{2,1,0:T(8,128)}, u32[]{:S(2)}) copy-start(f32[54,32,128]{2,1,0:T(8,128)} %param.11) | copy-start | bytes 2654212
  58.6 6.3 %copy-start.2 = (f32[32,128]{1,0:T(8,128)S(1)}, f32[32,128]{1,0:T(8,128)}, u32[]{:S(2)}) copy-start(f32[32,128]{1,0:T(8,128)} %refs_4_) | copy-start | bytes 49156
  58.6 6.3 %copy-start.3 = (f32[32,128]{1,0:T(8,128)S(1)}, f32[32,128]{1,0:T(8,128)}, u32[]{:S(2)}) copy-start(f32[32,128]{1,0:T(8,128)} %refs_5_) | copy-start | bytes 49156
  122.1 2.4 %collective-permute-start.6 = (f32[56,2048]{1,0:T(8,128)S(1)}, f32[56,2048]{1,0:T(8,128)S(1)}, u32[]{:S(2)}, u32[]{:S(2)}) collective-permute-start(f32[56,2048]{1,0:T(8,128)S(1)} %project.5), channel_id=1, source_target_pairs={{0,1},{1,0},{2,3},{3,2},{4,5},{5,4},{6,7},{7,6},{8,9},{9,8},{10,11... | collective-permute-start | bytes 1376264 | tf_op jit(solution)/shard_map/ppermute | solution.py:25
  126.8 3.3 %collective-permute-start.7 = (f32[56,2048]{1,0:T(8,128)S(1)}, f32[56,2048]{1,0:T(8,128)S(1)}, u32[]{:S(2)}, u32[]{:S(2)}) collective-permute-start(f32[56,2048]{1,0:T(8,128)S(1)} %project.7), channel_id=1, source_target_pairs={{0,1},{1,0},{2,3},{3,2},{4,5},{5,4},{6,7},{7,6},{8,9},{9,8},{10,11... | collective-permute-start | bytes 1376264 | tf_op jit(solution)/shard_map/ppermute | solution.py:25
  130.2 22.1 %copy-start.8 = (f32[1,4096]{1,0:T(1,128)S(1)}, f32[1,4096]{1,0:T(1,128)}, u32[]{:S(2)}) copy-start(f32[1,4096]{1,0:T(1,128)} %get-tuple-element.39.rank_ref) | copy-start | bytes 49156
  138.7 13.5 %collective-permute-start.8 = (f32[56,4096]{1,0:T(8,128)S(1)}, f32[56,4096]{1,0:T(8,128)S(1)}, u32[]{:S(2)}, u32[]{:S(2)}) collective-permute-start(f32[56,4096]{1,0:T(8,128)S(1)} %get-tuple-element.71), channel_id=1, source_target_pairs={{0,1},{1,0},{2,3},{3,2},{4,5},{5,4},{6,7},{7,6},{8,9},{9,8},{10,11... | collective-permute-start | bytes 2752520 | tf_op jit(solution)/shard_map/ppermute | solution.py:25
  138.8 13.5 %collective-permute-start.10 = (f32[56,2048]{1,0:T(8,128)S(1)}, f32[56,2048]{1,0:T(8,128)S(1)}, u32[]{:S(2)}, u32[]{:S(2)}) collective-permute-start(f32[56,2048]{1,0:T(8,128)S(1)} %add.12), channel_id=1, source_target_pairs={{0,2},{1,3},{2,0},{3,1},{4,6},{5,7},{6,4},{7,5},{8,10},{9,11},{10,... | collective-permute-start | bytes 1376264 | tf_op jit(solution)/shard_map/ppermute | solution.py:25
  138.9 22.7 %collective-permute-start.9 = (f32[56,2048]{1,0:T(8,128)S(1)}, f32[56,2048]{1,0:T(8,128)S(1)}, u32[]{:S(2)}, u32[]{:S(2)}) collective-permute-start(f32[56,2048]{1,0:T(8,128)S(1)} %add.13), channel_id=1, source_target_pairs={{0,2},{1,3},{2,0},{3,1},{4,6},{5,7},{6,4},{7,5},{8,10},{9,11},{10,... | collective-permute-start | bytes 1376264 | tf_op jit(solution)/shard_map/ppermute | solution.py:25
  152.3 9.3 %copy-start.4 = (f32[56,4096]{1,0:T(8,128)S(1)}, f32[56,4096]{1,0:T(8,128)}, u32[]{:S(2)}) copy-start(f32[56,4096]{1,0:T(8,128)} %get-tuple-element.74.refs_4_) | copy-start | bytes 2752516

commit v11 on v10

--- a/solution.py
+++ b/solution.py
@@ -95,9 +95,6 @@
         carry = carry + jnp.sum(hot, axis=1, keepdims=True)
 
 
-HALO_ORDER = {2: lambda n: (), 3: lambda n: range(1, n - 1), 0: lambda n: (), 1: lambda n: sorted({0, n - 1})}
-
-
 def head_kernel(grid_shape, cells, nshape, tiles, span, *refs):
     given, (t_ref, rank_ref, parts_ref, half_ref), refs = refs[:4], refs[4:8], refs[8:]
     les_ref, map_ref, shape_ref, diff_ref, key_ref, table_ref, *refs = refs
@@ -162,9 +159,17 @@
     number = jnp.where(row == lax.broadcasted_iota(jnp.int32, (species, species), 1), diff_ref[...], 0.0)
     number = jnp.sum(number, axis=1, keepdims=True)
     lane = lax.broadcasted_iota(jnp.int32, (species, LANES), 1)
-    for n in (2, 3, 0, 1):
-        pl.when(sides[n ^ 1][0])(copies[n].wait_recv)
-        for x, y in [(x, y) for x in HALO_ORDER[n](nx) for y in range(ny)]:
+    edge_y, edge_x = sorted({0, ny - 1}), sorted({0, nx - 1})
+    phases = [
+        ((), [(x, y) for x in range(1, nx - 1) for y in range(1, ny - 1)]),
+        ((2, 3), [(x, y) for x in range(1, nx - 1) for y in edge_y]),
+        ((0, 1), [(x, y) for x in edge_x for y in range(ny)]),
+    ]
+    done = 0
+    for sources, places in phases:
+        for n in sources:
+            pl.when(sides[n ^ 1][0])(copies[n].wait_recv)
+        for x, y in places:
             here = line(x, y)
             around = line(x + 1, y) if x < nx - 1 else halos[1][y, :species]
             around = around + (line(x - 1, y) if x else halos[0][y, :species])
@@ -174,17 +179,15 @@
             around = around + jnp.where(lane > 0, pltpu.roll(here, 1, 1), 0.0)
             place = (x * ny + y) * LANES
             t_ref[:species, place : place + LANES] = here + number * (around - 6.0 * here)
-        planes = list(HALO_ORDER[n](nx))
-        for x in planes:
-            piece = slice(x * ny * LANES, (x + 1) * ny * LANES)
+        for x, y in places:
+            piece = slice((x * ny + y) * LANES, (x * ny + y + 1) * LANES)
             value = t_ref[:, piece]
             high = value.astype(BF16).astype(F32)
             parts_ref[:, piece] = jnp.concatenate([high, value - high], axis=0).astype(BF16)
-        if planes and ny * LANES == CHUNK:
-            last = n == 1
-            sort_tiles(parts_ref, rank_ref, table_ref[...] if last else None, half_ref, 0, planes, last and nx > 2)
-    if ny * LANES != CHUNK:
-        sort_tiles(parts_ref, rank_ref, table_ref[...], half_ref, 0)
+        if places:
+            done += len(places)
+            table = table_ref[...] if done == nx * ny else None
+            sort_tiles(parts_ref, rank_ref, table, half_ref, 0, [x * ny + y for x, y in places], done > len(places))
     for n, (there, _) in enumerate(sides):
         pl.when(there)(copies[n].wait_send)
 
@@ -222,18 +225,23 @@
 CHUNK = 2 * TILE
 
 
-def sort_tiles(parts, rank_ref, steps, out_ref, first, pieces=None, more=False):
+def sort_tiles(parts, rank_ref, steps, out_ref, first, lines=None, more=False):
     rows = out_ref.shape[0]
-    count = rank_ref.shape[1]
+    lines = list(range(rank_ref.shape[1] // LANES)) if lines is None else lines
+    groups = [lines[n : n + CHUNK // LANES] for n in range(0, len(lines), CHUNK // LANES)]
+
+    def pick(ref, group):
+        if group == list(range(group[0], group[-1] + 1)):
+            return ref[:, group[0] * LANES : (group[-1] + 1) * LANES]
+        return jnp.concatenate([ref[:, n * LANES : (n + 1) * LANES] for n in group], axis=1)
 
     def step(n, _):
         here = (first + n) * TILE
         total = jnp.zeros((2 * rows, TILE), F32)
-        for k in range(count // CHUNK) if pieces is None else pieces:
-            piece = slice(k * CHUNK, (k + 1) * CHUNK)
-            ids = lax.broadcasted_iota(jnp.int32, (TILE, CHUNK), 0) + here
-            hot = rows_equal(ids.astype(F32), rank_ref[:, piece])
-            total = total + lax.dot_general(parts[:, piece], hot, NT, preferred_element_type=F32)
+        for group in groups:
+            ids = lax.broadcasted_iota(jnp.int32, (TILE, len(group) * LANES), 0) + here
+            hot = rows_equal(ids.astype(F32), pick(rank_ref, group))
+            total = total + lax.dot_general(pick(parts, group), hot, NT, preferred_element_type=F32)
         total = total[:rows] + total[rows:]
         place = pl.ds(pl.multiple_of(n * TILE, TILE), TILE)
         if more:
@@ -462,7 +470,7 @@
         out_ref[full * LANES :, :] = turn(full)[:rest]
 
 
-def project_kernel(bins, pairs, lists, state_rows, part, *refs):
+def project_kernel(bins, pairs, lists, state_rows, part, first, *refs):
     parts, weights, tiles, *refs = refs
     sources, refs = refs[:lists], refs[lists:]
     mean = refs.pop(0) if state_rows else None
@@ -489,7 +497,7 @@
                 tile = steps[number, 7, k].astype(jnp.int32)
                 block = jnp.minimum(k - tile, whole_blocks - 1)
                 local = jnp.clip(block - base, 0, blocks - 1)
-                block = block + number * whole_blocks
+                block = block + (first + number) * whole_blocks
                 valid = k < pairs
                 if part is not None:
                     valid = valid & ((k < middle) == (part == 0))
@@ -509,7 +517,7 @@
     lax.fori_loop(start, stop, step, 0)
 
 
-def project_call(parts, collected, rows, count, bins, ntiles, mean=None, state_rows=0, part=None):
+def project_call(parts, collected, rows, count, bins, ntiles, mean=None, state_rows=0, part=None, first=0):
     weights, tiles, *sources = collected
     lists = len(sources)
     pairs = count // LANES + ntiles - 1
@@ -518,7 +526,7 @@
     if extra:
         scratch += [pltpu.VMEM((mean.size // LANES, LANES), F32), pltpu.VMEM((LANES, LANES), F32)]
     return pl.pallas_call(
-        functools.partial(project_kernel, bins, pairs, lists, state_rows, part),
+        functools.partial(project_kernel, bins, pairs, lists, state_rows, part, first),
         out_shape=[jax.ShapeDtypeStruct((rows, count if part is None else count // 2), F32)] * lists
         + [jax.ShapeDtypeStruct((state_rows, LANES), F32)] * len(extra),
         in_specs=[VMEM] * (3 + lists + len(extra)),
@@ -855,8 +863,15 @@
         there, parts = lax.optimization_barrier((there, parts))
         ends.append(swap(there, "cross", bits[-1]))
     low, high = ends
-    *here, cmc_out = project_call(parts, near, rows, count, bins, ntiles, fresh, species * bins)
-    total = [here[0]] + [swap(piece, "cross", bit) for bit, piece in zip(bits[:-1], here[1:])]
+    weights, tiles, *keys = near
+    pieces = []
+    for n, bit in enumerate(bits[:-1], 1):
+        (piece,) = project_call(parts, [weights, tiles, keys[n]], rows, count, bins, ntiles, first=n)
+        pieces.append(swap(piece, "cross", bit))
+    here, cmc_out = project_call(
+        parts, [weights, tiles, keys[0]], rows, count, bins, ntiles, fresh, species * bins
+    )
+    total = [here] + pieces
     before = unsort_call(total, low, rank, None, None)
     les_out = unsort_call(total, high, rank, before, flat)
     return (les_out.reshape(les_state.shape), cmc_out.reshape(species, bins, cells))

time: 170 us -> 161 us (0.947)
  waiting for transfers between devices: 23.3 us -> 16.4 us
  starting transfers between devices: 10.3 us -> 6.69 us
  Pallas kernels: 132 us -> 135 us
    ppermute x11, waiting for transfers between devices: 23.3 us -> 16.4 us  [swap(): return lax.ppermute(array, axis, [(i, i ^ bit) for i in range(count)])]
    ppermute x11, starting transfers between devices: 10.3 us -> 6.69 us  [swap(): return lax.ppermute(array, axis, [(i, i ^ bit) for i in range(count)])]
    pallas_call x5 -> x6, Pallas kernels: 18.1 us -> 19.5 us  [project_call(): pl.pallas_call(functools.partial(project_kernel, bins, pairs, lists, stat...]
  transfers between devices with their start and end apart: 11 -> 11, of which waited for: 3 -> 3; matrix products, arithmetic and copies ran while one was open for 0% -> 0% of each run, Pallas kernels for 17% -> 22%
where the time goes in v11:
time: 161 us
  Pallas kernels  135 us (84%)
  waiting for transfers between devices  16.4 us (10%)
  starting transfers between devices  6.69 us (4%)
  local copies, waits for them, and re-layouts  2.43 us (2%)
    pallas_call x1, Pallas kernels, middle_call(): pl.pallas_call(kernel, out_shape=[jax.ShapeDtypeStruct((rows, width), F32...  54.6 us
    pallas_call x3, Pallas kernels, collect_call(): pl.pallas_call(functools.partial(collect_kernel, species, bins, per_tile,...  23.9 us
    pallas_call x6, Pallas kernels, project_call(): pl.pallas_call(functools.partial(project_kernel, bins, pairs, lists, stat...  19.5 us
    pallas_call x1, Pallas kernels, head_call(): pl.pallas_call(functools.partial(head_kernel, (species, nx, ny), cells, n...  16.5 us
    ppermute x11, waiting for transfers between devices, swap(): return lax.ppermute(array, axis, [(i, i ^ bit) for i in range(count)])  16.4 us
    pallas_call x2, Pallas kernels, unsort_call(): pl.pallas_call(functools.partial(unsort_kernel, half, len(wholes) + 1), g...  13.7 us
    ppermute x11, starting transfers between devices, swap(): return lax.ppermute(array, axis, [(i, i ^ bit) for i in range(count)])  6.69 us
    pallas_call x1, Pallas kernels, sort_call(): pl.pallas_call(sort_kernel, out_shape=jax.ShapeDtypeStruct((rows, count /...  6.36 us
  transfers between devices with their start and end apart: 11, of which 3 were waited for; matrix products, arithmetic and copies ran while one was open for 0% of the time, Pallas kernels for 22%

profile of v11, /device:TPU:2, one launch (start us, length us, event | category | flops | bytes accessed | tf_op | source)
XLA Modules:
  0.0 161.1 jit_solution(11098247232844396284)
XLA Ops:
  0.6 0.0 copy-start
  0.6 16.5 %head.1 = (f32[56,4096]{1,0:T(8,128)}, f32[1,4096]{1,0:T(1,128)}, bf16[112,4096]{1,0:T(8,128)(2,1)}, f32[56,2048]{1,0:T(8,128)}) custom-call(f32[1728,128]{1,0:T(8,128)} %bitcast.12, s32[1,4096]{1,0:T(1,128)} %bitcast.13, s32[1,4096]{1,0:T(1,128)} %bitcast.14, f32[1,54]{1,0:T(1,128)} %bitcast.15), custom_call_target="tpu_custom_call" | custom-call | tf_op jit(solution)/shard_map/head/pallas_call | solution.py:199
  17.2 1.2 copy-done.5
  18.4 0.7 copy-done.7
  19.1 6.4 %sort.1.refs_1_ = f32[56,2048]{1,0:T(8,128)S(1)} custom-call(bf16[112,4096]{1,0:T(8,128)(2,1)S(1)} %copy-done.5, f32[1,4096]{1,0:T(1,128)S(1)} %copy-done.7), custom_call_target="tpu_custom_call" | custom-call | flops 1879048192 | bytes 917504 | tf_op jit(solution)/shard_map/sort/pallas_call | solution.py:264
  25.5 0.9 collective-permute-start.1
  26.4 0.1 collective-permute-start
  26.5 1.1 collective-permute-start.2
  27.6 1.0 collective-permute-start.3
  28.5 0.1 constant_dynamic-slice_fusion
  28.6 0.1 copy.14
  28.7 0.1 broadcast_in_dim.3
  28.8 0.1 broadcast_in_dim_reshape.3.refs_6_
  28.9 0.1 tile.10.refs_7_
  29.1 0.0 collective-permute-done.1.refs_3_
  29.1 0.0 collective-permute-done.refs_2_
  29.1 11.5 %collect.3 = (f32[56,12288]{1,0:T(8,128)S(1)}, bf16[64,256,256]{2,1,0:T(8,128)(2,1)S(1)}, f32[64,16,128]{2,1,0:T(8,128)S(1)}, f32[8,128]{1,0:T(8,128)S(1)}, f32[8,128]{1,0:T(8,128)S(1)}) custom-call(f32[56,2048]{1,0:T(8,128)S(1)} %copy-done.6, f32[56,2048]{1,0:T(8,128)S(1)} %sort.1.refs_1_, f32[56,2048]{1,0:T(8,128)S(1)} %collective-permute-done.refs_2_, ...), custom_call_target="tpu_custom_call" | custom-call | flops 2650800128 | tf_op jit(solution)/shard_map/collect/pallas_call | solution.py:423
  40.6 0.0 collective-permute-done.2.refs_1_
  40.6 8.6 %collective-permute-done.3.refs_0_ = f32[56,2048]{1,0:T(8,128)S(1)} collective-permute-done((f32[56,2048]{1,0:T(8,128)S(1)}, f32[56,2048]{1,0:T(8,128)S(1)}, u32[]{:S(2)}, u32[]{:S(2)}) %collective-permute-start.3) | collective-permute-done | bytes 458784 | tf_op jit(solution)/shard_map/ppermute | solution.py:25
  49.2 0.0 collective-permute-start.4
  49.2 0.5 collective-permute-start.5
  49.7 6.2 %collect.4 = (f32[56,12288]{1,0:T(8,128)S(1)}, bf16[32,256,256]{2,1,0:T(8,128)(2,1)S(1)}, f32[32,16,128]{2,1,0:T(8,128)S(1)}, f32[8,128]{1,0:T(8,128)S(1)}) custom-call(f32[56,2048]{1,0:T(8,128)S(1)} %collective-permute-done.3.refs_0_, f32[56,2048]{1,0:T(8,128)S(1)} %collective-permute-done.2.refs_1_, f32[32,128]{1,0:T(8,128)S(1)} %bitcast.10), custom_call_target="tpu_custom_call" | custom-call | flops 1325400064 | tf_op jit(solution)/shard_map/collect/pallas_call | solution.py:423
  55.9 0.0 copy-start.1
  55.9 0.0 copy-start.2
  55.9 0.0 copy-start.3
  55.9 0.0 collective-permute-done.4.refs_0_
  55.9 0.0 collective-permute-done.5.refs_1_
  55.9 6.2 %collect.5 = (f32[56,12288]{1,0:T(8,128)S(1)}, bf16[32,256,256]{2,1,0:T(8,128)(2,1)S(1)}, f32[32,16,128]{2,1,0:T(8,128)S(1)}, f32[8,128]{1,0:T(8,128)S(1)}) custom-call(f32[56,2048]{1,0:T(8,128)S(1)} %collective-permute-done.4.refs_0_, f32[56,2048]{1,0:T(8,128)S(1)} %collective-permute-done.5.refs_1_, f32[32,128]{1,0:T(8,128)S(1)} %bitcast.11), custom_call_target="tpu_custom_call" | custom-call | flops 1325400064 | tf_op jit(solution)/shard_map/collect/pallas_call | solution.py:423
  62.1 54.6 %middle.1 = (f32[56,4096]{1,0:T(8,128)S(1)}, bf16[48,128,256]{2,1,0:T(8,128)(2,1)S(1)}) custom-call(f32[56,12288]{1,0:T(8,128)S(1)} %get-tuple-element.42.refs_0_, f32[56,12288]{1,0:T(8,128)S(1)} %get-tuple-element.44.refs_1_, f32[56,12288]{1,0:T(8,128)S(1)} %get-tuple-element.45.refs_2_, f32[1728,128]{1,0:T(8,128)S(1)} %bitcast.8, f32[32,128]{1,0:T(8,128)S(1)} %copy-done.2, ...), custom_call_target="tpu_custom_call" | custom-call | tf_op jit(solution)/shard_map/middle/pallas_call | solution.py:797
  116.7 2.6 %project.6 = f32[56,2048]{1,0:T(8,128)S(1)} custom-call(bf16[48,128,256]{2,1,0:T(8,128)(2,1)S(1)} %get-tuple-element.63.refs_0_, bf16[32,256,256]{2,1,0:T(8,128)(2,1)S(1)} %get-tuple-element.52.refs_1_, f32[32,16,128]{2,1,0:T(8,128)S(1)} %get-tuple-element.53.refs_2_, f32[8,128]{1,0:T(8,128)S(1)} %get-tuple-element.54.refs_3_), custom_call_target="tpu_custom_call" | custom-call | flops 1325400064 | tf_op jit(solution)/shard_map/project/pallas_call | solution.py:528
  119.3 0.1 collective-permute-start.6
  119.4 2.3 %project.7 = f32[56,2048]{1,0:T(8,128)S(1)} custom-call(bf16[48,128,256]{2,1,0:T(8,128)(2,1)S(1)} %get-tuple-element.63.refs_0_, bf16[32,256,256]{2,1,0:T(8,128)(2,1)S(1)} %get-tuple-element.56.refs_1_, f32[32,16,128]{2,1,0:T(8,128)S(1)} %get-tuple-element.57.refs_2_, f32[8,128]{1,0:T(8,128)S(1)} %get-tuple-element.58.refs_3_), custom_call_target="tpu_custom_call" | custom-call | flops 1325400064 | tf_op jit(solution)/shard_map/project/pallas_call | solution.py:528
  121.7 0.1 add.12
  121.8 2.4 %project.8 = f32[56,2048]{1,0:T(8,128)S(1)} custom-call(bf16[48,128,256]{2,1,0:T(8,128)(2,1)S(1)} %get-tuple-element.63.refs_0_, bf16[32,256,256]{2,1,0:T(8,128)(2,1)S(1)} %get-tuple-element.52.refs_1_, f32[32,16,128]{2,1,0:T(8,128)S(1)} %get-tuple-element.53.refs_2_, f32[8,128]{1,0:T(8,128)S(1)} %get-tuple-element.54.refs_3_), custom_call_target="tpu_custom_call" | custom-call | flops 1325400064 | tf_op jit(solution)/shard_map/project/pallas_call | solution.py:528
  124.2 0.9 collective-permute-start.7
  125.1 2.2 %project.9 = f32[56,2048]{1,0:T(8,128)S(1)} custom-call(bf16[48,128,256]{2,1,0:T(8,128)(2,1)S(1)} %get-tuple-element.63.refs_0_, bf16[32,256,256]{2,1,0:T(8,128)(2,1)S(1)} %get-tuple-element.56.refs_1_, f32[32,16,128]{2,1,0:T(8,128)S(1)} %get-tuple-element.57.refs_2_, f32[8,128]{1,0:T(8,128)S(1)} %get-tuple-element.58.refs_3_), custom_call_target="tpu_custom_call" | custom-call | flops 1325400064 | tf_op jit(solution)/shard_map/project/pallas_call | solution.py:528
  127.3 0.0 collective-permute-done.7
  127.3 0.1 add.13
  127.4 3.0 %project.11 = f32[56,4096]{1,0:T(8,128)S(1)} custom-call(bf16[48,128,256]{2,1,0:T(8,128)(2,1)S(1)} %get-tuple-element.63.refs_0_, bf16[64,256,256]{2,1,0:T(8,128)(2,1)S(1)} %get-tuple-element.64.refs_1_, f32[64,16,128]{2,1,0:T(8,128)S(1)} %get-tuple-element.65.refs_2_, f32[8,128]{1,0:T(8,128)S(1)} %get-tuple-element.69.refs_3_), custom_call_target="tpu_custom_call" | custom-call | flops 1325400064 | tf_op jit(solution)/shard_map/project/pallas_call | solution.py:528
  130.4 0.1 collective-permute-start.8
  130.5 0.5 collective-permute-start.10
  131.0 1.5 collective-permute-start.9
  132.5 7.0 %project.10 = (f32[56,4096]{1,0:T(8,128)S(1)}, f32[1728,128]{1,0:T(8,128)}) custom-call(bf16[48,128,256]{2,1,0:T(8,128)(2,1)S(1)} %get-tuple-element.63.refs_0_, bf16[64,256,256]{2,1,0:T(8,128)(2,1)S(1)} %get-tuple-element.64.refs_1_, f32[64,16,128]{2,1,0:T(8,128)S(1)} %get-tuple-element.65.refs_2_, f32[8,128]{1,0:T(8,128)S(1)} %get-tuple-element.66.refs_3_, ...), custom_call_target="tpu_custom_call" | custom-call | flops 1325400064 | tf_op jit(solution)/shard_map/project/pallas_call | solution.py:528
  139.6 4.4 %collective-permute-done.10.refs_2_ = f32[56,2048]{1,0:T(8,128)S(1)} collective-permute-done((f32[56,2048]{1,0:T(8,128)S(1)}, f32[56,2048]{1,0:T(8,128)S(1)}, u32[]{:S(2)}, u32[]{:S(2)}) %collective-permute-start.10) | collective-permute-done | bytes 458784 | tf_op jit(solution)/shard_map/ppermute | solution.py:25
  143.9 0.0 collective-permute-done.8.refs_1_
  143.9 5.8 %unsort.2.refs_3_ = f32[56,4096]{1,0:T(8,128)S(1)} custom-call(f32[1,4096]{1,0:T(1,128)S(1)} %copy-done.8, f32[56,4096]{1,0:T(8,128)S(1)} %get-tuple-element.68.refs_0_, f32[56,4096]{1,0:T(8,128)S(1)} %collective-permute-done.8.refs_1_, f32[56,2048]{1,0:T(8,128)S(1)} %collective-permute-done.10.refs_2_), custom_call_target="tpu_custom_call" | custom-call | flops 1879048192 | bytes 917504 | tf_op jit(solution)/shard_map/unsort/pallas_call | solution.py:323
  149.7 3.5 %collective-permute-done.9.refs_2_ = f32[56,2048]{1,0:T(8,128)S(1)} collective-permute-done((f32[56,2048]{1,0:T(8,128)S(1)}, f32[56,2048]{1,0:T(8,128)S(1)}, u32[]{:S(2)}, u32[]{:S(2)}) %collective-permute-start.9) | collective-permute-done | bytes 458784 | tf_op jit(solution)/shard_map/ppermute | solution.py:25
  153.2 7.8 %unsort.3 = f32[1728,128]{1,0:T(8,128)} custom-call(f32[1,4096]{1,0:T(1,128)S(1)} %copy-done.8, f32[56,4096]{1,0:T(8,128)S(1)} %get-tuple-element.68.refs_0_, f32[56,4096]{1,0:T(8,128)S(1)} %collective-permute-done.8.refs_1_, f32[56,2048]{1,0:T(8,128)S(1)} %collective-permute-done.9.refs_2_, f32[56,4096]{1,0:T(8,128)S(1)} %unsort.2.refs_3_, ...), custom_call_target="tpu_custom_call" | custom-call | flops 1879048192 | bytes 917504 | tf_op jit(solution)/shard_map/unsort/pallas_call | solution.py:323
  (19 shorter events, 0.1 us)
Async XLA Ops:
  0.6 27.9 %copy-start = (f32[128,128]{1,0:T(8,128)S(1)}, f32[128,128]{1,0:T(8,128)}, u32[]{:S(2)}) copy-start(f32[128,128]{1,0:T(8,128)} %param.14) | copy-start | bytes 196612
  17.2 1.2 copy-start.5
  18.4 0.7 copy-start.7
  19.1 7.3 %copy-start.6 = (f32[56,2048]{1,0:T(8,128)S(1)}, f32[56,2048]{1,0:T(8,128)}, u32[]{:S(2)}) copy-start(f32[56,2048]{1,0:T(8,128)} %get-tuple-element.39.refs_0_) | copy-start | bytes 1376260
  19.1 9.6 %copy-start.10 = (s32[128]{0:T(128)S(1)}, s32[128]{0:T(128)}, u32[]{:S(2)}) copy-start(s32[128]{0:T(128)} %param.19) | copy-start | bytes 1540
  19.1 9.8 %copy-start.9 = (f32[54,54]{1,0:T(8,128)S(1)}, f32[54,54]{1,0:T(8,128)}, u32[]{:S(2)}) copy-start(f32[54,54]{1,0:T(8,128)} %param.16) | copy-start | bytes 34996
  25.5 3.6 %collective-permute-start.1 = (f32[56,2048]{1,0:T(8,128)S(1)}, f32[56,2048]{1,0:T(8,128)S(1)}, u32[]{:S(2)}, u32[]{:S(2)}) collective-permute-start(f32[56,2048]{1,0:T(8,128)S(1)} %sort.1.refs_1_), channel_id=1, source_target_pairs={{0,1},{1,0},{2,3},{3,2},{4,5},{5,4},{6,7},{7,6},{8,9},{9,8},{10,11... | collective-permute-start | bytes 1376264 | tf_op jit(solution)/shard_map/ppermute | solution.py:25
  26.4 2.7 %collective-permute-start = (f32[56,2048]{1,0:T(8,128)S(1)}, f32[56,2048]{1,0:T(8,128)S(1)}, u32[]{:S(2)}, u32[]{:S(2)}) collective-permute-start(f32[56,2048]{1,0:T(8,128)S(1)} %copy-done.6), channel_id=1, source_target_pairs={{0,1},{1,0},{2,3},{3,2},{4,5},{5,4},{6,7},{7,6},{8,9},{9,8},{10,11... | collective-permute-start | bytes 1376264 | tf_op jit(solution)/shard_map/ppermute | solution.py:25
  26.5 14.1 %collective-permute-start.2 = (f32[56,2048]{1,0:T(8,128)S(1)}, f32[56,2048]{1,0:T(8,128)S(1)}, u32[]{:S(2)}, u32[]{:S(2)}) collective-permute-start(f32[56,2048]{1,0:T(8,128)S(1)} %sort.1.refs_1_), channel_id=1, source_target_pairs={{0,2},{1,3},{2,0},{3,1},{4,6},{5,7},{6,4},{7,5},{8,10},{9,11},{10,... | collective-permute-start | bytes 1376264 | tf_op jit(solution)/shard_map/ppermute | solution.py:25
  27.6 21.6 %collective-permute-start.3 = (f32[56,2048]{1,0:T(8,128)S(1)}, f32[56,2048]{1,0:T(8,128)S(1)}, u32[]{:S(2)}, u32[]{:S(2)}) collective-permute-start(f32[56,2048]{1,0:T(8,128)S(1)} %copy-done.6), channel_id=1, source_target_pairs={{0,2},{1,3},{2,0},{3,1},{4,6},{5,7},{6,4},{7,5},{8,10},{9,11},{10,... | collective-permute-start | bytes 1376264 | tf_op jit(solution)/shard_map/ppermute | solution.py:25
  49.2 6.7 %collective-permute-start.4 = (f32[56,2048]{1,0:T(8,128)S(1)}, f32[56,2048]{1,0:T(8,128)S(1)}, u32[]{:S(2)}, u32[]{:S(2)}) collective-permute-start(f32[56,2048]{1,0:T(8,128)S(1)} %collective-permute-done.3.refs_0_), channel_id=1, source_target_pairs={{0,1},{1,0},{2,3},{3,2},{4,5},{5,4},{6,7},{7,6},{8,9},{9,8},{10,11... | collective-permute-start | bytes 1376264 | tf_op jit(solution)/shard_map/ppermute | solution.py:25
  49.2 6.7 %collective-permute-start.5 = (f32[56,2048]{1,0:T(8,128)S(1)}, f32[56,2048]{1,0:T(8,128)S(1)}, u32[]{:S(2)}, u32[]{:S(2)}) collective-permute-start(f32[56,2048]{1,0:T(8,128)S(1)} %collective-permute-done.2.refs_1_), channel_id=1, source_target_pairs={{0,1},{1,0},{2,3},{3,2},{4,5},{5,4},{6,7},{7,6},{8,9},{9,8},{10,11... | collective-permute-start | bytes 1376264 | tf_op jit(solution)/shard_map/ppermute | solution.py:25
  55.9 6.2 %copy-start.1 = (f32[54,32,128]{2,1,0:T(8,128)S(1)}, f32[54,32,128]{2,1,0:T(8,128)}, u32[]{:S(2)}) copy-start(f32[54,32,128]{2,1,0:T(8,128)} %param.11) | copy-start | bytes 2654212
  55.9 6.2 %copy-start.2 = (f32[32,128]{1,0:T(8,128)S(1)}, f32[32,128]{1,0:T(8,128)}, u32[]{:S(2)}) copy-start(f32[32,128]{1,0:T(8,128)} %refs_4_) | copy-start | bytes 49156
  55.9 6.2 %copy-start.3 = (f32[32,128]{1,0:T(8,128)S(1)}, f32[32,128]{1,0:T(8,128)}, u32[]{:S(2)}) copy-start(f32[32,128]{1,0:T(8,128)} %refs_5_) | copy-start | bytes 49156
  119.3 2.4 %collective-permute-start.6 = (f32[56,2048]{1,0:T(8,128)S(1)}, f32[56,2048]{1,0:T(8,128)S(1)}, u32[]{:S(2)}, u32[]{:S(2)}) collective-permute-start(f32[56,2048]{1,0:T(8,128)S(1)} %project.6), channel_id=1, source_target_pairs={{0,1},{1,0},{2,3},{3,2},{4,5},{5,4},{6,7},{7,6},{8,9},{9,8},{10,11... | collective-permute-start | bytes 1376264 | tf_op jit(solution)/shard_map/ppermute | solution.py:25
  124.2 3.1 %collective-permute-start.7 = (f32[56,2048]{1,0:T(8,128)S(1)}, f32[56,2048]{1,0:T(8,128)S(1)}, u32[]{:S(2)}, u32[]{:S(2)}) collective-permute-start(f32[56,2048]{1,0:T(8,128)S(1)} %project.8), channel_id=1, source_target_pairs={{0,1},{1,0},{2,3},{3,2},{4,5},{5,4},{6,7},{7,6},{8,9},{9,8},{10,11... | collective-permute-start | bytes 1376264 | tf_op jit(solution)/shard_map/ppermute | solution.py:25
  130.4 13.5 %collective-permute-start.8 = (f32[56,4096]{1,0:T(8,128)S(1)}, f32[56,4096]{1,0:T(8,128)S(1)}, u32[]{:S(2)}, u32[]{:S(2)}) collective-permute-start(f32[56,4096]{1,0:T(8,128)S(1)} %project.11), channel_id=1, source_target_pairs={{0,1},{1,0},{2,3},{3,2},{4,5},{5,4},{6,7},{7,6},{8,9},{9,8},{10,11... | collective-permute-start | bytes 2752520 | tf_op jit(solution)/shard_map/ppermute | solution.py:25
  130.5 13.4 %collective-permute-start.10 = (f32[56,2048]{1,0:T(8,128)S(1)}, f32[56,2048]{1,0:T(8,128)S(1)}, u32[]{:S(2)}, u32[]{:S(2)}) collective-permute-start(f32[56,2048]{1,0:T(8,128)S(1)} %add.12), channel_id=1, source_target_pairs={{0,2},{1,3},{2,0},{3,1},{4,6},{5,7},{6,4},{7,5},{8,10},{9,11},{10,... | collective-permute-start | bytes 1376264 | tf_op jit(solution)/shard_map/ppermute | solution.py:25
  131.0 22.2 %collective-permute-start.9 = (f32[56,2048]{1,0:T(8,128)S(1)}, f32[56,2048]{1,0:T(8,128)S(1)}, u32[]{:S(2)}, u32[]{:S(2)}) collective-permute-start(f32[56,2048]{1,0:T(8,128)S(1)} %add.13), channel_id=1, source_target_pairs={{0,2},{1,3},{2,0},{3,1},{4,6},{5,7},{6,4},{7,5},{8,10},{9,11},{10,... | collective-permute-start | bytes 1376264 | tf_op jit(solution)/shard_map/ppermute | solution.py:25
  132.5 11.4 %copy-start.8 = (f32[1,4096]{1,0:T(1,128)S(1)}, f32[1,4096]{1,0:T(1,128)}, u32[]{:S(2)}) copy-start(f32[1,4096]{1,0:T(1,128)} %get-tuple-element.38.rank_ref) | copy-start | bytes 49156
  143.9 9.3 %copy-start.4 = (f32[56,4096]{1,0:T(8,128)S(1)}, f32[56,4096]{1,0:T(8,128)}, u32[]{:S(2)}) copy-start(f32[56,4096]{1,0:T(8,128)} %get-tuple-element.72.refs_4_) | copy-start | bytes 2752516

commit v12 on v11

--- a/solution.py
+++ b/solution.py
@@ -17,7 +17,7 @@
 TILE = 256
 HALF = 64
 GROUP = 16
-LAG = (3, 6, 9)
+LAG = (5, 9, 14)
 
 
 def swap(array, axis, bit):
@@ -470,13 +470,13 @@
         out_ref[full * LANES :, :] = turn(full)[:rest]
 
 
-def project_kernel(bins, pairs, lists, state_rows, part, first, *refs):
+def project_kernel(pairs, lists, state_rows, part, first, *refs):
     parts, weights, tiles, *refs = refs
     sources, refs = refs[:lists], refs[lists:]
     mean = refs.pop(0) if state_rows else None
     outs, refs = refs[:lists], refs[lists:]
     state_ref = refs.pop(0) if state_rows else None
-    steps, sems, *turning = refs
+    steps, sems = refs
     copies = fetch_rows(sources, steps, sems)
     rows, count = outs[0].shape
     blocks = count // LANES
@@ -486,7 +486,7 @@
     for out in outs:
         out[...] = jnp.zeros_like(out)
     if state_rows:
-        turn_back(mean, state_ref, bins, *turning)
+        state_ref[...] = mean[...]
     for copy in copies:
         copy.wait()
 
@@ -517,16 +517,14 @@
     lax.fori_loop(start, stop, step, 0)
 
 
-def project_call(parts, collected, rows, count, bins, ntiles, mean=None, state_rows=0, part=None, first=0):
+def project_call(parts, collected, rows, count, ntiles, mean=None, state_rows=0, part=None, first=0):
     weights, tiles, *sources = collected
     lists = len(sources)
     pairs = count // LANES + ntiles - 1
     extra = [] if mean is None else [mean]
     scratch = [pltpu.SMEM((lists, 8, LANES), F32), pltpu.SemaphoreType.DMA((lists,))]
-    if extra:
-        scratch += [pltpu.VMEM((mean.size // LANES, LANES), F32), pltpu.VMEM((LANES, LANES), F32)]
     return pl.pallas_call(
-        functools.partial(project_kernel, bins, pairs, lists, state_rows, part, first),
+        functools.partial(project_kernel, pairs, lists, state_rows, part, first),
         out_shape=[jax.ShapeDtypeStruct((rows, count if part is None else count // 2), F32)] * lists
         + [jax.ShapeDtypeStruct((state_rows, LANES), F32)] * len(extra),
         in_specs=[VMEM] * (3 + lists + len(extra)),
@@ -540,8 +538,8 @@
 
 def middle_kernel(species, bins, chunk, refs_in, refs_out, scratch):
     *accs, cmc_ref, diss_ref, rate_ref, count_ref, matrix_ref = refs_in
-    fresh_ref, parts_ref = refs_out
-    next_ref, far_ref, nat, quads, turned, side_out, load, outward, hopped, summed, got, state_ref, edge_out, edge_in, side_in, pick_ref, third_ref, send, recv, side_send, side_recv = scratch
+    state_out, parts_ref = refs_out
+    fresh_ref, next_ref, far_ref, nat, quads, turned, side_out, load, outward, hopped, summed, got, state_ref, edge_out, edge_in, side_in, pick_ref, third_ref, send, recv, side_send, side_recv = scratch
     rows, width = fresh_ref.shape
     steps = width // chunk
     slab, nslab = lax.axis_index("slab"), lax.axis_size("slab")
@@ -769,6 +767,7 @@
         return 0
 
     lax.fori_loop(0, steps + LAG[2], step, 0)
+    turn_back(fresh_ref, state_out, bins, quads, turned)
 
     def finish(c, _):
         pl.when(has_outer)(lambda: to_outer(c).wait_send())
@@ -786,7 +785,7 @@
     pl.when(has_down)(to_down.wait_send)
 
 
-def middle_call(accs, cmc, diss, rate, count, matrix, species, bins, chunk=512):
+def middle_call(accs, cmc, diss, rate, count, matrix, species, bins, chunk=256):
     rows, width = accs[0].shape[0], count.shape[1]
     steps = width // chunk
     given = len(accs) + 5
@@ -797,12 +796,12 @@
     return pl.pallas_call(
         kernel,
         out_shape=[
-            jax.ShapeDtypeStruct((rows, width), F32),
+            jax.ShapeDtypeStruct(cmc.shape, F32),
             jax.ShapeDtypeStruct((3 * width // TILE, 2 * HALF, TILE), BF16),
         ],
         in_specs=[VMEM] * len(accs) + [pl.BlockSpec(memory_space=pl.ANY)] * 3 + [VMEM] * 2,
         out_specs=[VMEM] * 2,
-        scratch_shapes=[pltpu.VMEM((rows, width), F32)] * 2
+        scratch_shapes=[pltpu.VMEM((rows, width), F32)] * 3
         + [pltpu.VMEM((rows * bins, LANES), F32), pltpu.VMEM((rows * width // LANES, LANES), F32)]
         + [pltpu.VMEM((LANES, LANES), F32), pltpu.VMEM((2, rows, LANES), F32), pltpu.SemaphoreType.DMA((3,))]
         + [pltpu.VMEM((rows, width), F32)] * 5
@@ -849,16 +848,16 @@
         acc, *collected = collect_call([pair], table, species, bins, per_tile, ntiles)
         accs.append(acc)
         far.append(collected)
-    fresh, parts = middle_call(accs, *terms, species, bins)
+    state, parts = middle_call(accs, *terms, species, bins)
 
     ends = []
     for part in range(2):
         pieces = []
         for bit, collected in zip(bits[:-1], far[1:]):
-            (piece,) = project_call(parts, collected, rows, count, bins, ntiles, part=part)
+            (piece,) = project_call(parts, collected, rows, count, ntiles, part=part)
             piece, parts = lax.optimization_barrier((piece, parts))
             pieces.append(swap(piece, "cross", bit))
-        (there,) = project_call(parts, far[0], rows, count, bins, ntiles, part=part)
+        (there,) = project_call(parts, far[0], rows, count, ntiles, part=part)
         there = sum(pieces, there)
         there, parts = lax.optimization_barrier((there, parts))
         ends.append(swap(there, "cross", bits[-1]))
@@ -866,11 +865,9 @@
     weights, tiles, *keys = near
     pieces = []
     for n, bit in enumerate(bits[:-1], 1):
-        (piece,) = project_call(parts, [weights, tiles, keys[n]], rows, count, bins, ntiles, first=n)
+        (piece,) = project_call(parts, [weights, tiles, keys[n]], rows, count, ntiles, first=n)
         pieces.append(swap(piece, "cross", bit))
-    here, cmc_out = project_call(
-        parts, [weights, tiles, keys[0]], rows, count, bins, ntiles, fresh, species * bins
-    )
+    here, cmc_out = project_call(parts, [weights, tiles, keys[0]], rows, count, ntiles, state, species * bins)
     total = [here] + pieces
     before = unsort_call(total, low, rank, None, None)
     les_out = unsort_call(total, high, rank, before, flat)

time: 161 us -> 161 us (level)
  Pallas kernels: 135 us -> 131 us
  waiting for transfers between devices: 16.4 us -> 19.5 us
    pallas_call x7, Pallas kernels: 74.1 us -> 70.9 us  [the longest x1 54.5 us: middle_call(): pl.pallas_call(kernel, out_shape=[jax.ShapeDtypeStruct(cmc.shape, F32), j...]
    ppermute x11, waiting for transfers between devices: 16.4 us -> 19.5 us  [swap(): return lax.ppermute(array, axis, [(i, i ^ bit) for i in range(count)])]
  transfers between devices with their start and end apart: 11 -> 11, of which waited for: 3 -> 3; matrix products, arithmetic and copies ran while one was open for 0% -> 0% of each run, Pallas kernels for 22% -> 20%
where the time goes in v12:
time: 161 us
  Pallas kernels  131 us (81%)
  waiting for transfers between devices  19.5 us (12%)
  starting transfers between devices  6.69 us (4%)
  local copies, waits for them, and re-layouts  2.43 us (2%)
    pallas_call x1, Pallas kernels, middle_call(): pl.pallas_call(kernel, out_shape=[jax.ShapeDtypeStruct(cmc.shape, F32), j...  54.5 us
    pallas_call x3, Pallas kernels, collect_call(): pl.pallas_call(functools.partial(collect_kernel, species, bins, per_tile,...  23.9 us
    ppermute x11, waiting for transfers between devices, swap(): return lax.ppermute(array, axis, [(i, i ^ bit) for i in range(count)])  19.5 us
    pallas_call x1, Pallas kernels, head_call(): pl.pallas_call(functools.partial(head_kernel, (species, nx, ny), cells, n...  16.5 us
    pallas_call x6, Pallas kernels, project_call(): pl.pallas_call(functools.partial(project_kernel, pairs, lists, state_rows...  16.4 us
    pallas_call x2, Pallas kernels, unsort_call(): pl.pallas_call(functools.partial(unsort_kernel, half, len(wholes) + 1), g...  13.7 us
    ppermute x11, starting transfers between devices, swap(): return lax.ppermute(array, axis, [(i, i ^ bit) for i in range(count)])  6.69 us
    pallas_call x1, Pallas kernels, sort_call(): pl.pallas_call(sort_kernel, out_shape=jax.ShapeDtypeStruct((rows, count /...  6.36 us
  transfers between devices with their start and end apart: 11, of which 3 were waited for; matrix products, arithmetic and copies ran while one was open for 0% of the time, Pallas kernels for 20%

profile of v12, /device:TPU:2, one launch (start us, length us, event | category | flops | bytes accessed | tf_op | source)
XLA Modules:
  0.0 161.0 jit_solution(1677572176463519223)
XLA Ops:
  0.6 0.0 copy-start
  0.6 16.5 %head.1 = (f32[56,4096]{1,0:T(8,128)}, f32[1,4096]{1,0:T(1,128)}, bf16[112,4096]{1,0:T(8,128)(2,1)}, f32[56,2048]{1,0:T(8,128)}) custom-call(f32[1728,128]{1,0:T(8,128)} %bitcast.12, s32[1,4096]{1,0:T(1,128)} %bitcast.13, s32[1,4096]{1,0:T(1,128)} %bitcast.14, f32[1,54]{1,0:T(1,128)} %bitcast.15), custom_call_target="tpu_custom_call" | custom-call | tf_op jit(solution)/shard_map/head/pallas_call | solution.py:199
  17.2 1.2 copy-done.5
  18.4 0.7 copy-done.7
  19.1 6.4 %sort.1.refs_1_ = f32[56,2048]{1,0:T(8,128)S(1)} custom-call(bf16[112,4096]{1,0:T(8,128)(2,1)S(1)} %copy-done.5, f32[1,4096]{1,0:T(1,128)S(1)} %copy-done.7), custom_call_target="tpu_custom_call" | custom-call | flops 1879048192 | bytes 917504 | tf_op jit(solution)/shard_map/sort/pallas_call | solution.py:264
  25.5 0.9 collective-permute-start.1
  26.4 0.1 collective-permute-start
  26.5 1.1 collective-permute-start.2
  27.6 1.0 collective-permute-start.3
  28.5 0.1 constant_dynamic-slice_fusion
  28.6 0.1 copy.14
  28.7 0.1 broadcast_in_dim.3
  28.8 0.1 broadcast_in_dim_reshape.3.refs_6_
  28.9 0.1 tile.10.refs_7_
  29.1 0.0 collective-permute-done.1.refs_3_
  29.1 0.0 collective-permute-done.refs_2_
  29.1 11.5 %collect.3 = (f32[56,12288]{1,0:T(8,128)S(1)}, bf16[64,256,256]{2,1,0:T(8,128)(2,1)S(1)}, f32[64,16,128]{2,1,0:T(8,128)S(1)}, f32[8,128]{1,0:T(8,128)S(1)}, f32[8,128]{1,0:T(8,128)S(1)}) custom-call(f32[56,2048]{1,0:T(8,128)S(1)} %copy-done.6, f32[56,2048]{1,0:T(8,128)S(1)} %sort.1.refs_1_, f32[56,2048]{1,0:T(8,128)S(1)} %collective-permute-done.refs_2_, ...), custom_call_target="tpu_custom_call" | custom-call | flops 2650800128 | tf_op jit(solution)/shard_map/collect/pallas_call | solution.py:423
  40.6 0.0 collective-permute-done.2.refs_1_
  40.6 8.6 %collective-permute-done.3.refs_0_ = f32[56,2048]{1,0:T(8,128)S(1)} collective-permute-done((f32[56,2048]{1,0:T(8,128)S(1)}, f32[56,2048]{1,0:T(8,128)S(1)}, u32[]{:S(2)}, u32[]{:S(2)}) %collective-permute-start.3) | collective-permute-done | bytes 458784 | tf_op jit(solution)/shard_map/ppermute | solution.py:25
  49.2 0.0 collective-permute-start.4
  49.2 0.5 collective-permute-start.5
  49.7 6.2 %collect.4 = (f32[56,12288]{1,0:T(8,128)S(1)}, bf16[32,256,256]{2,1,0:T(8,128)(2,1)S(1)}, f32[32,16,128]{2,1,0:T(8,128)S(1)}, f32[8,128]{1,0:T(8,128)S(1)}) custom-call(f32[56,2048]{1,0:T(8,128)S(1)} %collective-permute-done.3.refs_0_, f32[56,2048]{1,0:T(8,128)S(1)} %collective-permute-done.2.refs_1_, f32[32,128]{1,0:T(8,128)S(1)} %bitcast.10), custom_call_target="tpu_custom_call" | custom-call | flops 1325400064 | tf_op jit(solution)/shard_map/collect/pallas_call | solution.py:423
  55.9 0.0 copy-start.1
  55.9 0.0 copy-start.2
  55.9 0.0 copy-start.3
  55.9 0.0 collective-permute-done.4.refs_0_
  55.9 0.0 collective-permute-done.5.refs_1_
  55.9 6.2 %collect.5 = (f32[56,12288]{1,0:T(8,128)S(1)}, bf16[32,256,256]{2,1,0:T(8,128)(2,1)S(1)}, f32[32,16,128]{2,1,0:T(8,128)S(1)}, f32[8,128]{1,0:T(8,128)S(1)}) custom-call(f32[56,2048]{1,0:T(8,128)S(1)} %collective-permute-done.4.refs_0_, f32[56,2048]{1,0:T(8,128)S(1)} %collective-permute-done.5.refs_1_, f32[32,128]{1,0:T(8,128)S(1)} %bitcast.11), custom_call_target="tpu_custom_call" | custom-call | flops 1325400064 | tf_op jit(solution)/shard_map/collect/pallas_call | solution.py:423
  62.1 54.5 %middle.1 = (f32[1728,128]{1,0:T(8,128)S(1)}, bf16[48,128,256]{2,1,0:T(8,128)(2,1)S(1)}) custom-call(f32[56,12288]{1,0:T(8,128)S(1)} %get-tuple-element.42.refs_0_, f32[56,12288]{1,0:T(8,128)S(1)} %get-tuple-element.44.refs_1_, f32[56,12288]{1,0:T(8,128)S(1)} %get-tuple-element.45.refs_2_, f32[1728,128]{1,0:T(8,128)S(1)} %bitcast.8, ...), custom_call_target="tpu_custom_call" | custom-call | tf_op jit(solution)/shard_map/middle/pallas_call | solution.py:796
  116.6 2.8 %project.6 = f32[56,2048]{1,0:T(8,128)S(1)} custom-call(bf16[48,128,256]{2,1,0:T(8,128)(2,1)S(1)} %get-tuple-element.63.refs_0_, bf16[32,256,256]{2,1,0:T(8,128)(2,1)S(1)} %get-tuple-element.52.refs_1_, f32[32,16,128]{2,1,0:T(8,128)S(1)} %get-tuple-element.53.refs_2_, f32[8,128]{1,0:T(8,128)S(1)} %get-tuple-element.54.refs_3_), custom_call_target="tpu_custom_call" | custom-call | flops 1325400064 | tf_op jit(solution)/shard_map/project/pallas_call | solution.py:526
  119.4 0.1 collective-permute-start.6
  119.5 2.3 %project.7 = f32[56,2048]{1,0:T(8,128)S(1)} custom-call(bf16[48,128,256]{2,1,0:T(8,128)(2,1)S(1)} %get-tuple-element.63.refs_0_, bf16[32,256,256]{2,1,0:T(8,128)(2,1)S(1)} %get-tuple-element.56.refs_1_, f32[32,16,128]{2,1,0:T(8,128)S(1)} %get-tuple-element.57.refs_2_, f32[8,128]{1,0:T(8,128)S(1)} %get-tuple-element.58.refs_3_), custom_call_target="tpu_custom_call" | custom-call | flops 1325400064 | tf_op jit(solution)/shard_map/project/pallas_call | solution.py:526
  121.8 0.0 collective-permute-done.6
  121.8 0.1 add.12
  121.8 2.2 %project.8 = f32[56,2048]{1,0:T(8,128)S(1)} custom-call(bf16[48,128,256]{2,1,0:T(8,128)(2,1)S(1)} %get-tuple-element.63.refs_0_, bf16[32,256,256]{2,1,0:T(8,128)(2,1)S(1)} %get-tuple-element.52.refs_1_, f32[32,16,128]{2,1,0:T(8,128)S(1)} %get-tuple-element.53.refs_2_, f32[8,128]{1,0:T(8,128)S(1)} %get-tuple-element.54.refs_3_), custom_call_target="tpu_custom_call" | custom-call | flops 1325400064 | tf_op jit(solution)/shard_map/project/pallas_call | solution.py:526
  124.1 0.9 collective-permute-start.7
  125.0 2.2 %project.9 = f32[56,2048]{1,0:T(8,128)S(1)} custom-call(bf16[48,128,256]{2,1,0:T(8,128)(2,1)S(1)} %get-tuple-element.63.refs_0_, bf16[32,256,256]{2,1,0:T(8,128)(2,1)S(1)} %get-tuple-element.56.refs_1_, f32[32,16,128]{2,1,0:T(8,128)S(1)} %get-tuple-element.57.refs_2_, f32[8,128]{1,0:T(8,128)S(1)} %get-tuple-element.58.refs_3_), custom_call_target="tpu_custom_call" | custom-call | flops 1325400064 | tf_op jit(solution)/shard_map/project/pallas_call | solution.py:526
  127.2 0.0 collective-permute-done.7
  127.2 0.1 add.13
  127.3 3.0 %project.11 = f32[56,4096]{1,0:T(8,128)S(1)} custom-call(bf16[48,128,256]{2,1,0:T(8,128)(2,1)S(1)} %get-tuple-element.63.refs_0_, bf16[64,256,256]{2,1,0:T(8,128)(2,1)S(1)} %get-tuple-element.64.refs_1_, f32[64,16,128]{2,1,0:T(8,128)S(1)} %get-tuple-element.65.refs_2_, f32[8,128]{1,0:T(8,128)S(1)} %get-tuple-element.69.refs_3_), custom_call_target="tpu_custom_call" | custom-call | flops 1325400064 | tf_op jit(solution)/shard_map/project/pallas_call | solution.py:526
  130.3 0.1 collective-permute-start.8
  130.4 0.1 collective-permute-start.10
  130.5 2.0 %collective-permute-start.9 = (f32[56,2048]{1,0:T(8,128)S(1)}, f32[56,2048]{1,0:T(8,128)S(1)}, u32[]{:S(2)}, u32[]{:S(2)}) collective-permute-start(f32[56,2048]{1,0:T(8,128)S(1)} %add.13), channel_id=1, source_target_pairs={{0,2},{1,3},{2,0},{3,1},{4,6},{5,7},{6,4},{7,5},{8,10},{9,11},{10,... | collective-permute-start | bytes 1376264 | tf_op jit(solution)/shard_map/ppermute | solution.py:25
  132.5 3.9 %project.10 = (f32[56,4096]{1,0:T(8,128)S(1)}, f32[1728,128]{1,0:T(8,128)}) custom-call(bf16[48,128,256]{2,1,0:T(8,128)(2,1)S(1)} %get-tuple-element.63.refs_0_, bf16[64,256,256]{2,1,0:T(8,128)(2,1)S(1)} %get-tuple-element.64.refs_1_, f32[64,16,128]{2,1,0:T(8,128)S(1)} %get-tuple-element.65.refs_2_, f32[8,128]{1,0:T(8,128)S(1)} %get-tuple-element.66.refs_3_, ...), custom_call_target="tpu_custom_call" | custom-call | flops 1325400064 | tf_op jit(solution)/shard_map/project/pallas_call | solution.py:526
  136.4 7.5 %collective-permute-done.10.refs_2_ = f32[56,2048]{1,0:T(8,128)S(1)} collective-permute-done((f32[56,2048]{1,0:T(8,128)S(1)}, f32[56,2048]{1,0:T(8,128)S(1)}, u32[]{:S(2)}, u32[]{:S(2)}) %collective-permute-start.10) | collective-permute-done | bytes 458784 | tf_op jit(solution)/shard_map/ppermute | solution.py:25
  143.9 5.8 %unsort.2.refs_3_ = f32[56,4096]{1,0:T(8,128)S(1)} custom-call(f32[1,4096]{1,0:T(1,128)S(1)} %copy-done.8, f32[56,4096]{1,0:T(8,128)S(1)} %get-tuple-element.68.refs_0_, f32[56,4096]{1,0:T(8,128)S(1)} %collective-permute-done.8.refs_1_, f32[56,2048]{1,0:T(8,128)S(1)} %collective-permute-done.10.refs_2_), custom_call_target="tpu_custom_call" | custom-call | flops 1879048192 | bytes 917504 | tf_op jit(solution)/shard_map/unsort/pallas_call | solution.py:323
  149.7 3.5 %collective-permute-done.9.refs_2_ = f32[56,2048]{1,0:T(8,128)S(1)} collective-permute-done((f32[56,2048]{1,0:T(8,128)S(1)}, f32[56,2048]{1,0:T(8,128)S(1)}, u32[]{:S(2)}, u32[]{:S(2)}) %collective-permute-start.9) | collective-permute-done | bytes 458784 | tf_op jit(solution)/shard_map/ppermute | solution.py:25
  153.1 7.8 %unsort.3 = f32[1728,128]{1,0:T(8,128)} custom-call(f32[1,4096]{1,0:T(1,128)S(1)} %copy-done.8, f32[56,4096]{1,0:T(8,128)S(1)} %get-tuple-element.68.refs_0_, f32[56,4096]{1,0:T(8,128)S(1)} %collective-permute-done.8.refs_1_, f32[56,2048]{1,0:T(8,128)S(1)} %collective-permute-done.9.refs_2_, f32[56,4096]{1,0:T(8,128)S(1)} %unsort.2.refs_3_, ...), custom_call_target="tpu_custom_call" | custom-call | flops 1879048192 | bytes 917504 | tf_op jit(solution)/shard_map/unsort/pallas_call | solution.py:323
  (19 shorter events, 0.1 us)
Async XLA Ops:
  0.6 27.9 %copy-start = (f32[128,128]{1,0:T(8,128)S(1)}, f32[128,128]{1,0:T(8,128)}, u32[]{:S(2)}) copy-start(f32[128,128]{1,0:T(8,128)} %param.14) | copy-start | bytes 196612
  17.2 1.2 copy-start.5
  18.4 0.7 copy-start.7
  19.1 7.3 %copy-start.6 = (f32[56,2048]{1,0:T(8,128)S(1)}, f32[56,2048]{1,0:T(8,128)}, u32[]{:S(2)}) copy-start(f32[56,2048]{1,0:T(8,128)} %get-tuple-element.39.refs_0_) | copy-start | bytes 1376260
  19.1 9.6 %copy-start.10 = (s32[128]{0:T(128)S(1)}, s32[128]{0:T(128)}, u32[]{:S(2)}) copy-start(s32[128]{0:T(128)} %param.19) | copy-start | bytes 1540
  19.1 9.8 %copy-start.9 = (f32[54,54]{1,0:T(8,128)S(1)}, f32[54,54]{1,0:T(8,128)}, u32[]{:S(2)}) copy-start(f32[54,54]{1,0:T(8,128)} %param.16) | copy-start | bytes 34996
  25.5 3.6 %collective-permute-start.1 = (f32[56,2048]{1,0:T(8,128)S(1)}, f32[56,2048]{1,0:T(8,128)S(1)}, u32[]{:S(2)}, u32[]{:S(2)}) collective-permute-start(f32[56,2048]{1,0:T(8,128)S(1)} %sort.1.refs_1_), channel_id=1, source_target_pairs={{0,1},{1,0},{2,3},{3,2},{4,5},{5,4},{6,7},{7,6},{8,9},{9,8},{10,11... | collective-permute-start | bytes 1376264 | tf_op jit(solution)/shard_map/ppermute | solution.py:25
  26.4 2.7 %collective-permute-start = (f32[56,2048]{1,0:T(8,128)S(1)}, f32[56,2048]{1,0:T(8,128)S(1)}, u32[]{:S(2)}, u32[]{:S(2)}) collective-permute-start(f32[56,2048]{1,0:T(8,128)S(1)} %copy-done.6), channel_id=1, source_target_pairs={{0,1},{1,0},{2,3},{3,2},{4,5},{5,4},{6,7},{7,6},{8,9},{9,8},{10,11... | collective-permute-start | bytes 1376264 | tf_op jit(solution)/shard_map/ppermute | solution.py:25
  26.5 14.1 %collective-permute-start.2 = (f32[56,2048]{1,0:T(8,128)S(1)}, f32[56,2048]{1,0:T(8,128)S(1)}, u32[]{:S(2)}, u32[]{:S(2)}) collective-permute-start(f32[56,2048]{1,0:T(8,128)S(1)} %sort.1.refs_1_), channel_id=1, source_target_pairs={{0,2},{1,3},{2,0},{3,1},{4,6},{5,7},{6,4},{7,5},{8,10},{9,11},{10,... | collective-permute-start | bytes 1376264 | tf_op jit(solution)/shard_map/ppermute | solution.py:25
  27.6 21.6 %collective-permute-start.3 = (f32[56,2048]{1,0:T(8,128)S(1)}, f32[56,2048]{1,0:T(8,128)S(1)}, u32[]{:S(2)}, u32[]{:S(2)}) collective-permute-start(f32[56,2048]{1,0:T(8,128)S(1)} %copy-done.6), channel_id=1, source_target_pairs={{0,2},{1,3},{2,0},{3,1},{4,6},{5,7},{6,4},{7,5},{8,10},{9,11},{10,... | collective-permute-start | bytes 1376264 | tf_op jit(solution)/shard_map/ppermute | solution.py:25
  49.2 6.7 %collective-permute-start.4 = (f32[56,2048]{1,0:T(8,128)S(1)}, f32[56,2048]{1,0:T(8,128)S(1)}, u32[]{:S(2)}, u32[]{:S(2)}) collective-permute-start(f32[56,2048]{1,0:T(8,128)S(1)} %collective-permute-done.3.refs_0_), channel_id=1, source_target_pairs={{0,1},{1,0},{2,3},{3,2},{4,5},{5,4},{6,7},{7,6},{8,9},{9,8},{10,11... | collective-permute-start | bytes 1376264 | tf_op jit(solution)/shard_map/ppermute | solution.py:25
  49.2 6.7 %collective-permute-start.5 = (f32[56,2048]{1,0:T(8,128)S(1)}, f32[56,2048]{1,0:T(8,128)S(1)}, u32[]{:S(2)}, u32[]{:S(2)}) collective-permute-start(f32[56,2048]{1,0:T(8,128)S(1)} %collective-permute-done.2.refs_1_), channel_id=1, source_target_pairs={{0,1},{1,0},{2,3},{3,2},{4,5},{5,4},{6,7},{7,6},{8,9},{9,8},{10,11... | collective-permute-start | bytes 1376264 | tf_op jit(solution)/shard_map/ppermute | solution.py:25
  55.9 6.2 %copy-start.1 = (f32[54,32,128]{2,1,0:T(8,128)S(1)}, f32[54,32,128]{2,1,0:T(8,128)}, u32[]{:S(2)}) copy-start(f32[54,32,128]{2,1,0:T(8,128)} %param.11) | copy-start | bytes 2654212
  55.9 6.2 %copy-start.2 = (f32[32,128]{1,0:T(8,128)S(1)}, f32[32,128]{1,0:T(8,128)}, u32[]{:S(2)}) copy-start(f32[32,128]{1,0:T(8,128)} %refs_4_) | copy-start | bytes 49156
  55.9 6.2 %copy-start.3 = (f32[32,128]{1,0:T(8,128)S(1)}, f32[32,128]{1,0:T(8,128)}, u32[]{:S(2)}) copy-start(f32[32,128]{1,0:T(8,128)} %refs_5_) | copy-start | bytes 49156
  119.4 2.4 %collective-permute-start.6 = (f32[56,2048]{1,0:T(8,128)S(1)}, f32[56,2048]{1,0:T(8,128)S(1)}, u32[]{:S(2)}, u32[]{:S(2)}) collective-permute-start(f32[56,2048]{1,0:T(8,128)S(1)} %project.6), channel_id=1, source_target_pairs={{0,1},{1,0},{2,3},{3,2},{4,5},{5,4},{6,7},{7,6},{8,9},{9,8},{10,11... | collective-permute-start | bytes 1376264 | tf_op jit(solution)/shard_map/ppermute | solution.py:25
  124.1 3.1 %collective-permute-start.7 = (f32[56,2048]{1,0:T(8,128)S(1)}, f32[56,2048]{1,0:T(8,128)S(1)}, u32[]{:S(2)}, u32[]{:S(2)}) collective-permute-start(f32[56,2048]{1,0:T(8,128)S(1)} %project.8), channel_id=1, source_target_pairs={{0,1},{1,0},{2,3},{3,2},{4,5},{5,4},{6,7},{7,6},{8,9},{9,8},{10,11... | collective-permute-start | bytes 1376264 | tf_op jit(solution)/shard_map/ppermute | solution.py:25
  130.3 13.5 %collective-permute-start.8 = (f32[56,4096]{1,0:T(8,128)S(1)}, f32[56,4096]{1,0:T(8,128)S(1)}, u32[]{:S(2)}, u32[]{:S(2)}) collective-permute-start(f32[56,4096]{1,0:T(8,128)S(1)} %project.11), channel_id=1, source_target_pairs={{0,1},{1,0},{2,3},{3,2},{4,5},{5,4},{6,7},{7,6},{8,9},{9,8},{10,11... | collective-permute-start | bytes 2752520 | tf_op jit(solution)/shard_map/ppermute | solution.py:25
  130.4 13.5 %collective-permute-start.10 = (f32[56,2048]{1,0:T(8,128)S(1)}, f32[56,2048]{1,0:T(8,128)S(1)}, u32[]{:S(2)}, u32[]{:S(2)}) collective-permute-start(f32[56,2048]{1,0:T(8,128)S(1)} %add.12), channel_id=1, source_target_pairs={{0,2},{1,3},{2,0},{3,1},{4,6},{5,7},{6,4},{7,5},{8,10},{9,11},{10,... | collective-permute-start | bytes 1376264 | tf_op jit(solution)/shard_map/ppermute | solution.py:25
  130.5 22.7 %collective-permute-start.9 = (f32[56,2048]{1,0:T(8,128)S(1)}, f32[56,2048]{1,0:T(8,128)S(1)}, u32[]{:S(2)}, u32[]{:S(2)}) collective-permute-start(f32[56,2048]{1,0:T(8,128)S(1)} %add.13), channel_id=1, source_target_pairs={{0,2},{1,3},{2,0},{3,1},{4,6},{5,7},{6,4},{7,5},{8,10},{9,11},{10,... | collective-permute-start | bytes 1376264 | tf_op jit(solution)/shard_map/ppermute | solution.py:25
  132.5 11.4 %copy-start.8 = (f32[1,4096]{1,0:T(1,128)S(1)}, f32[1,4096]{1,0:T(1,128)}, u32[]{:S(2)}) copy-start(f32[1,4096]{1,0:T(1,128)} %get-tuple-element.38.rank_ref) | copy-start | bytes 49156
  143.8 9.3 %copy-start.4 = (f32[56,4096]{1,0:T(8,128)S(1)}, f32[56,4096]{1,0:T(8,128)}, u32[]{:S(2)}) copy-start(f32[56,4096]{1,0:T(8,128)} %get-tuple-element.72.refs_4_) | copy-start | bytes 2752516
